TPU v7x, 128 devices: a whole 4x4x4 slice. The times are simulated.
128 devices in a mesh: dp: 8 (over z_hi, x), fsdp: 16 (over z_lo, y, core).
Axes of the slice: x: 4, y: 4, z: 4 (z_hi: 2, z_lo: 2; z = z_hi * 2 + z_lo), core: 2. Of those that a mesh axis runs over, the one named last changes fastest.
Arguments:
- long_in: bfloat16 [65536, 768], P(('dp', 'fsdp')), may hold values from -6 to 6
- glob_in: bfloat16 [4096, 768], P(('dp', 'fsdp')), may hold values from -6 to 6
- cot_long: bfloat16 [65536, 768], P(('dp', 'fsdp')), may hold values from -6 to 6
- cot_glob: bfloat16 [4096, 768], P(('dp', 'fsdp')), may hold values from -6 to 6
- teacher: bfloat16 [65536, 768], P(('dp', 'fsdp')), may hold values from -12 to 12
- w_qkv: bfloat16 [768, 2304], P(('dp', 'fsdp')), may hold values from -0.21875 to 0.21875
- w_attn: bfloat16 [768, 768], P(('dp', 'fsdp')), may hold values from -0.875 to 0.875
- w_in: bfloat16 [768, 3072], P(('dp', 'fsdp')), may hold values from -0.21875 to 0.21875
- w_out: bfloat16 [3072, 768], P(('dp', 'fsdp')), may hold values from -0.109375 to 0.109375
- norm_gains: bfloat16 [768, 2], P(('dp', 'fsdp')), may hold values from 0.25 to 1.75
- norm_biases: bfloat16 [768, 2], P(('dp', 'fsdp')), may hold values from -1.5 to 1.5
- rel_bias: float32 [171, 12], replicated, may hold values from -5 to 5
- lengths: int32 [32], P('dp'), may hold values from 1024 to 2048, as said below
- block_order: int32 [8, 64], P('dp'), may hold values from 0 to 63, each once within a row
- global_pos: int32 [4096], P('dp'), may hold values from 0 to 2047, as said below
- rel_labels: int32 [169], replicated, may hold values from 0 to 168, each once
- loss_mask: int32 [65536], P(('dp', 'fsdp')), may hold values 0 or 1
Outputs:
- out_long: bfloat16 [65536, 768], P(('dp', 'fsdp'))
- out_glob: bfloat16 [4096, 768], P(('dp', 'fsdp'))
- loss: float32 [], replicated
- grad_long: float32 [65536, 768], P(('dp', 'fsdp'))
- grad_glob: float32 [4096, 768], P(('dp', 'fsdp'))
- grad_qkv: float32 [768, 2304], P(('dp', 'fsdp'))
- grad_attn: float32 [768, 768], P(('dp', 'fsdp'))
- grad_in: float32 [768, 3072], P(('dp', 'fsdp'))
- grad_out: float32 [3072, 768], P(('dp', 'fsdp'))
- grad_gains: float32 [768, 2], P(('dp', 'fsdp'))
- grad_biases: float32 [768, 2], P(('dp', 'fsdp'))
- grad_rel: float32 [171, 12], replicated
Inputs may be any that keep to these rules, and one draw needn't show every extreme that they name: `lengths`: a sequence's real tokens fill its first slots; at least one sequence of all has 2048. `block_order`: each row is a permutation of the group's block numbers. `global_pos`: the k-th global token of a sequence is anchored at a position from k * 16 to k * 16 + 15. `rel_labels`: a permutation of the labels.
All inputs are finite; a program needn't handle non-finite values. No bound on the sum of `loss_mask` on one device may be relied on, other than what follows from the above.
Results may differ from a plain program's by a relative error of at most 0.018.
Values may be sent and summed in bfloat16 or wider, within the bound.
No kernel may reach another device: no remote copies, remote signals or barrier semaphores. Data moves between devices by JAX's collectives and lax.ppermute only.
A program may use at most 320 MiB of HBM per device.

v0:
```python
import math

import jax
import jax.numpy as jnp
from jax import lax
from jax.sharding import PartitionSpec as P

D = 768
HEADS = 12
HEAD = 64
RADIUS = 84
LABELS = 169
BLOCK = 128
SEQ_BLOCKS = 16
GLOBAL_EVERY = 16
GSEQ = 128


EPS = 1e-05
MASKED = -1e30
HIGHEST = lax.Precision.HIGHEST


def joined(value, axis, join):
    pieces = jax.tree.map(lambda part: lax.all_gather(part, axis), value)
    head = jax.tree.map(lambda part: part[0], pieces)
    tail = jax.tree.map(lambda part: part[1:], pieces)
    so_far, _ = lax.scan(lambda so_far, piece: (join(so_far, piece), None), head, tail)
    return so_far


def norm_rows(values, gain, shift):
    centre = jnp.mean(values, -1, keepdims=True)
    centred = values - centre
    spread = jnp.mean(centred * centred, -1, keepdims=True)
    factor = lax.rsqrt(spread + EPS)
    normal = centred * factor
    return (normal * gain + shift, normal, factor)


def norm_back(grad, normal, factor, gain):
    scaled = grad * gain
    first = jnp.mean(scaled, -1, keepdims=True)
    second = jnp.mean(scaled * normal, -1, keepdims=True)
    return (
        factor * (scaled - first - normal * second),
        jnp.sum(grad * normal, 0),
        jnp.sum(grad, 0),
    )


def combine(first, second):
    summit = jnp.maximum(first[0], second[0])
    return (summit, first[1] * jnp.exp(first[0] - summit) + second[1] * jnp.exp(second[0] - summit))


def shards(
    long_in,
    glob_in,
    cot_long,
    cot_glob,
    teacher,
    w_qkv,
    w_attn,
    w_in,
    w_out,
    norm_gains,
    norm_biases,
    rel_bias,
    lengths,
    block_order,
    global_pos,
    rel_labels,
    loss_mask,
):
    scale = 1.0 / math.sqrt(HEAD)
    block_count = long_in.shape[0] // BLOCK
    row_count = block_count * BLOCK
    own_globals = glob_in.shape[0]
    group_globals = global_pos.shape[0]
    seq_count = lengths.shape[0]
    width = BLOCK + 2 * RADIUS
    order = block_order[0]
    member = lax.axis_index("fsdp")
    first_own = member * own_globals
    my_ids = lax.dynamic_slice_in_dim(order, member * block_count, block_count)
    seq_ids = my_ids // SEQ_BLOCKS
    bins = my_ids % SEQ_BLOCKS
    seq_range = jnp.arange(seq_count)
    my_lens = jnp.sum(jnp.where(seq_ids[:, None] == seq_range[None, :], lengths[None, :], 0), 1)
    query_pos = bins[:, None] * BLOCK + jnp.arange(BLOCK)[None, :]
    query_valid = query_pos < my_lens[:, None]
    glob_seq = jnp.arange(group_globals) // GSEQ
    glob_lens = jnp.sum(jnp.where(glob_seq[:, None] == seq_range[None, :], lengths[None, :], 0), 1)
    glob_valid = global_pos < glob_lens
    anchor_run = global_pos // GLOBAL_EVERY
    weights = (w_qkv, w_attn, w_in, w_out, norm_gains, norm_biases)
    qkv_full, attn_full, in_full, out_full, gain_full, shift_full = (
        lax.all_gather(weights[0], ("dp", "fsdp"), axis=0, tiled=True),
        lax.all_gather(weights[1], ("dp", "fsdp"), axis=0, tiled=True),
        lax.all_gather(weights[2], ("dp", "fsdp"), axis=0, tiled=True),
        lax.all_gather(weights[3], ("dp", "fsdp"), axis=0, tiled=True),
        lax.all_gather(weights[4], ("dp", "fsdp"), axis=0, tiled=True),
        lax.all_gather(weights[5], ("dp", "fsdp"), axis=0, tiled=True),
    )
    gain_table = gain_full.astype(jnp.float32)
    shift_table = shift_full.astype(jnp.float32)
    stacked = jnp.concatenate([long_in, glob_in], 0).astype(jnp.float32)
    normed_one, base_one, factor_one = norm_rows(stacked, gain_table[:, 0], shift_table[:, 0])
    acts_one = normed_one.astype(jnp.bfloat16)
    projected = jnp.dot(acts_one, qkv_full, preferred_element_type=jnp.float32).astype(jnp.bfloat16)
    long_proj = projected[:row_count]
    glob_proj = projected[row_count:]
    query = long_proj[:, :D].reshape(block_count, BLOCK, HEADS, HEAD)
    keyval = long_proj[:, D:].reshape(block_count, BLOCK, 2 * D)
    own_key = long_proj[:, D : 2 * D].reshape(row_count, HEADS, HEAD)
    own_value = long_proj[:, 2 * D :].reshape(row_count, HEADS, HEAD)
    group_proj = lax.all_gather(glob_proj, "fsdp", axis=0, tiled=True)
    glob_query = group_proj[:, :D].reshape(group_globals, HEADS, HEAD)
    glob_key = group_proj[:, D : 2 * D].reshape(group_globals, HEADS, HEAD)
    glob_value = group_proj[:, 2 * D :].reshape(group_globals, HEADS, HEAD)
    my_query = glob_proj[:, :D].reshape(own_globals, HEADS, HEAD)
    piece = lax.all_gather(keyval, "fsdp", axis=0, tiled=True)
    to_left = ((order[None, :] == my_ids[:, None] - 1) & (bins[:, None] > 0)).astype(jnp.bfloat16)
    to_right = ((order[None, :] == my_ids[:, None] + 1) & (bins[:, None] < SEQ_BLOCKS - 1)).astype(
        jnp.bfloat16
    )
    left_rim = jnp.einsum(
        "jc,crd->jrd", to_left, piece[:, BLOCK - RADIUS :], preferred_element_type=jnp.float32
    )
    right_rim = jnp.einsum(
        "jc,crd->jrd", to_right, piece[:, :RADIUS], preferred_element_type=jnp.float32
    )
    left_rim, right_rim = (left_rim, right_rim)
    window = jnp.concatenate(
        [left_rim.astype(jnp.bfloat16), keyval, right_rim.astype(jnp.bfloat16)], 1
    )
    window_key = window[..., :D].reshape(block_count, width, HEADS, HEAD)
    window_value = window[..., D:].reshape(block_count, width, HEADS, HEAD)
    key_pos = bins[:, None] * BLOCK - RADIUS + jnp.arange(width)[None, :]
    key_valid = (key_pos >= 0) & (key_pos < my_lens[:, None])
    offsets = jnp.arange(width)[None, :] - jnp.arange(BLOCK)[:, None]
    inside = (offsets >= 0) & (offsets <= 2 * RADIUS)
    picker = (rel_labels[:, None] == jnp.arange(LABELS)[None, :]).astype(jnp.float32)
    label_table = jnp.dot(picker, rel_bias[:LABELS], precision=HIGHEST)
    band_bias = jnp.transpose(label_table[jnp.clip(offsets, 0, 2 * RADIUS)], (2, 0, 1))
    local_mask = inside[None, None] & key_valid[:, None, None, :]
    same_seq = seq_ids[:, None] == glob_seq[None, :]
    owning = (query_pos[:, :, None] // GLOBAL_EVERY == anchor_run[None, None, :]) & same_seq[
        :, None, :
    ]
    remote_mask = (same_seq & glob_valid[None, :])[:, None, None, :]
    own_bias = rel_bias[LABELS]
    other_bias = rel_bias[LABELS + 1]
    remote_bias = jnp.where(
        owning[:, None], own_bias[None, :, None, None], other_bias[None, :, None, None]
    )

    def long_scores():
        local = (
            jnp.einsum("bihd,bthd->bhit", query, window_key, preferred_element_type=jnp.float32)
            * scale
            + band_bias[None]
        )
        remote = (
            jnp.einsum("bihd,ghd->bhig", query, glob_key, preferred_element_type=jnp.float32)
            * scale
            + remote_bias
        )
        return (jnp.where(local_mask, local, MASKED), jnp.where(remote_mask, remote, MASKED))

    local_s, remote_s = long_scores()
    summit = jnp.maximum(jnp.max(local_s, -1), jnp.max(remote_s, -1))[..., None]
    local_e = jnp.exp(local_s - summit)
    remote_e = jnp.exp(remote_s - summit)
    row_total = jnp.sum(local_e, -1, keepdims=True) + jnp.sum(remote_e, -1, keepdims=True)
    long_lse = summit + jnp.log(row_total)
    local_p = (local_e / row_total).astype(jnp.bfloat16)
    remote_p = (remote_e / row_total).astype(jnp.bfloat16)
    long_out = jnp.einsum(
        "bhit,bthd->bihd", local_p, window_value, preferred_element_type=jnp.float32
    )
    long_out = long_out + jnp.einsum(
        "bhig,ghd->bihd", remote_p, glob_value, preferred_element_type=jnp.float32
    )
    long_out = long_out.reshape(row_count, D).astype(jnp.bfloat16)
    key_seq = jnp.broadcast_to(seq_ids[:, None], (block_count, BLOCK)).reshape(row_count)
    key_run = query_pos.reshape(row_count) // GLOBAL_EVERY
    cross_mask = (glob_seq[:, None] == key_seq[None, :]) & query_valid.reshape(row_count)[None, :]
    cross_own = (anchor_run[:, None] == key_run[None, :]) & (glob_seq[:, None] == key_seq[None, :])
    cross_bias = jnp.where(cross_own[None], own_bias[:, None, None], other_bias[:, None, None])
    my_seq = lax.dynamic_slice_in_dim(glob_seq, first_own, own_globals)
    self_mask = (my_seq[:, None] == glob_seq[None, :]) & glob_valid[None, :]

    def cross_scores():
        scores = (
            jnp.einsum("ihd,jhd->hij", glob_query, own_key, preferred_element_type=jnp.float32)
            * scale
            + cross_bias
        )
        return jnp.where(cross_mask[None], scores, MASKED)

    def self_scores():
        scores = (
            jnp.einsum("ihd,jhd->hij", my_query, glob_key, preferred_element_type=jnp.float32)
            * scale
        )
        return jnp.where(self_mask[None], scores, MASKED)

    cross_s = cross_scores()
    cross_top = jnp.max(cross_s, -1)
    cross_sum = jnp.sum(
        jnp.where(cross_mask[None], jnp.exp(cross_s - cross_top[..., None]), 0.0), -1
    )
    self_s = self_scores()
    self_top = jnp.max(self_s, -1)
    self_sum = jnp.sum(jnp.exp(self_s - self_top[..., None]), -1)
    padded_top = lax.dynamic_update_slice_in_dim(
        jnp.full((HEADS, group_globals), MASKED, jnp.float32), self_top, first_own, 1
    )
    padded_sum = lax.dynamic_update_slice_in_dim(
        jnp.zeros((HEADS, group_globals), jnp.float32), self_sum, first_own, 1
    )
    part_top, part_sum = combine((cross_top, cross_sum), (padded_top, padded_sum))
    glob_top, glob_total = joined((part_top, part_sum), "fsdp", combine)
    glob_lse = glob_top + jnp.log(glob_total)
    my_lse = lax.dynamic_slice_in_dim(glob_lse, first_own, own_globals, 1)
    cross_p = jnp.where(cross_mask[None], jnp.exp(cross_s - glob_lse[..., None]), 0.0).astype(
        jnp.bfloat16
    )
    self_p = jnp.exp(self_s - my_lse[..., None]).astype(jnp.bfloat16)
    summed_part = jnp.einsum(
        "hij,jhd->ihd", cross_p, own_value, preferred_element_type=jnp.float32
    ).reshape(group_globals, D)
    mine = jnp.einsum(
        "hij,jhd->ihd", self_p, glob_value, preferred_element_type=jnp.float32
    ).reshape(own_globals, D)
    summed_part = lax.dynamic_update_slice_in_dim(
        summed_part,
        lax.dynamic_slice_in_dim(summed_part, first_own, own_globals, 0) + mine,
        first_own,
        0,
    )
    glob_out = lax.psum_scatter(
        summed_part.astype(jnp.bfloat16), "fsdp", scatter_dimension=0, tiled=True
    )
    mixed = jnp.concatenate([long_out, glob_out], 0)
    middle = stacked + jnp.dot(mixed, attn_full, preferred_element_type=jnp.float32)
    normed_two, base_two, factor_two = norm_rows(middle, gain_table[:, 1], shift_table[:, 1])
    acts_two = normed_two.astype(jnp.bfloat16)
    inner = jnp.dot(acts_two, in_full, preferred_element_type=jnp.float32)
    hidden_full, gelu_back = jax.vjp(lambda values: jax.nn.gelu(values, approximate=False), inner)
    hidden = hidden_full.astype(jnp.bfloat16)
    result = middle + jnp.dot(hidden, out_full, preferred_element_type=jnp.float32)
    weighting = (query_valid.reshape(row_count) & (loss_mask == 1)).astype(jnp.float32)
    error = result[:row_count] - teacher.astype(jnp.float32)
    loss_sum, count = lax.psum(
        (jnp.sum(weighting[:, None] * error * error), jnp.sum(weighting)), ("dp", "fsdp")
    )
    loss = loss_sum / count
    grad_result = jnp.concatenate(
        [
            cot_long.astype(jnp.float32) + 2.0 * weighting[:, None] * error / count,
            cot_glob.astype(jnp.float32),
        ],
        0,
    )
    qkv_full, attn_full, in_full, out_full, gain_full, shift_full = (
        lax.all_gather(weights[0], ("dp", "fsdp"), axis=0, tiled=True),
        lax.all_gather(weights[1], ("dp", "fsdp"), axis=0, tiled=True),
        lax.all_gather(weights[2], ("dp", "fsdp"), axis=0, tiled=True),
        lax.all_gather(weights[3], ("dp", "fsdp"), axis=0, tiled=True),
        lax.all_gather(weights[4], ("dp", "fsdp"), axis=0, tiled=True),
        lax.all_gather(weights[5], ("dp", "fsdp"), axis=0, tiled=True),
    )
    gain_table = gain_full.astype(jnp.float32)
    grad_z = grad_result.astype(jnp.bfloat16)
    grad_wout = jnp.dot(hidden.T, grad_z, preferred_element_type=jnp.float32)
    grad_hidden = jnp.dot(grad_z, out_full.T, preferred_element_type=jnp.float32)
    grad_inner = gelu_back(grad_hidden)[0].astype(jnp.bfloat16)
    grad_win = jnp.dot(acts_two.T, grad_inner, preferred_element_type=jnp.float32)
    grad_acts_two = jnp.dot(grad_inner, in_full.T, preferred_element_type=jnp.float32)
    back_two, gain_grad_two, shift_grad_two = norm_back(
        grad_acts_two, base_two, factor_two, gain_table[:, 1]
    )
    grad_middle = grad_result + back_two
    grad_branch = grad_middle.astype(jnp.bfloat16)
    grad_wattn = jnp.dot(mixed.T, grad_branch, preferred_element_type=jnp.float32)
    grad_mixed = jnp.dot(grad_branch, attn_full.T, preferred_element_type=jnp.float32).astype(
        jnp.bfloat16
    )
    grad_long_out = grad_mixed[:row_count].reshape(block_count, BLOCK, HEADS, HEAD)
    grad_glob_out = grad_mixed[row_count:]
    local_s, remote_s = long_scores()
    local_f = jnp.exp(local_s - long_lse)
    remote_f = jnp.exp(remote_s - long_lse)
    local_dp = jnp.einsum(
        "bihd,bthd->bhit", grad_long_out, window_value, preferred_element_type=jnp.float32
    )
    remote_dp = jnp.einsum(
        "bihd,ghd->bhig", grad_long_out, glob_value, preferred_element_type=jnp.float32
    )
    delta = jnp.sum(local_f * local_dp, -1, keepdims=True) + jnp.sum(
        remote_f * remote_dp, -1, keepdims=True
    )
    local_ds = (local_f * (local_dp - delta)).astype(jnp.bfloat16)
    remote_ds = (remote_f * (remote_dp - delta)).astype(jnp.bfloat16)
    grad_query = (
        jnp.einsum("bhit,bthd->bihd", local_ds, window_key, preferred_element_type=jnp.float32)
        + jnp.einsum("bhig,ghd->bihd", remote_ds, glob_key, preferred_element_type=jnp.float32)
    ) * scale
    grad_window_key = (
        jnp.einsum("bhit,bihd->bthd", local_ds, query, preferred_element_type=jnp.float32) * scale
    )
    grad_window_value = jnp.einsum(
        "bhit,bihd->bthd",
        local_f.astype(jnp.bfloat16),
        grad_long_out,
        preferred_element_type=jnp.float32,
    )
    grad_gkey = (
        jnp.einsum("bhig,bihd->ghd", remote_ds, query, preferred_element_type=jnp.float32) * scale
    )
    grad_gvalue = jnp.einsum(
        "bhig,bihd->ghd",
        remote_f.astype(jnp.bfloat16),
        grad_long_out,
        preferred_element_type=jnp.float32,
    )
    band_grad = jnp.sum(local_ds.astype(jnp.float32), 0)
    skewed = jnp.pad(band_grad.reshape(HEADS, BLOCK * width), ((0, 0), (0, BLOCK))).reshape(
        HEADS, BLOCK, width + 1
    )[:, :, :LABELS]
    grad_table = jnp.sum(skewed, 1)
    remote_grad = remote_ds.astype(jnp.float32)
    grad_own = jnp.sum(jnp.where(owning[:, None], remote_grad, 0.0), (0, 2, 3))
    grad_other = jnp.sum(jnp.where(owning[:, None], 0.0, remote_grad), (0, 2, 3))
    group_grad_out = lax.all_gather(grad_glob_out, "fsdp", axis=0, tiled=True).reshape(
        group_globals, HEADS, HEAD
    )
    my_grad_out = grad_glob_out.reshape(own_globals, HEADS, HEAD)
    cross_s = cross_scores()
    cross_f = jnp.where(cross_mask[None], jnp.exp(cross_s - glob_lse[..., None]), 0.0)
    cross_dp = jnp.einsum(
        "ihd,jhd->hij", group_grad_out, own_value, preferred_element_type=jnp.float32
    )
    self_s = self_scores()
    self_f = jnp.exp(self_s - my_lse[..., None])
    self_dp = jnp.einsum(
        "ihd,jhd->hij", my_grad_out, glob_value, preferred_element_type=jnp.float32
    )
    part_delta = jnp.sum(cross_f * cross_dp, -1)
    part_delta = lax.dynamic_update_slice_in_dim(
        part_delta,
        lax.dynamic_slice_in_dim(part_delta, first_own, own_globals, 1)
        + jnp.sum(self_f * self_dp, -1),
        first_own,
        1,
    )
    glob_delta = lax.psum(part_delta, "fsdp")
    my_delta = lax.dynamic_slice_in_dim(glob_delta, first_own, own_globals, 1)
    cross_ds = (cross_f * (cross_dp - glob_delta[..., None])).astype(jnp.bfloat16)
    self_ds = (self_f * (self_dp - my_delta[..., None])).astype(jnp.bfloat16)
    grad_own_key = (
        jnp.einsum("hij,ihd->jhd", cross_ds, glob_query, preferred_element_type=jnp.float32) * scale
    )
    grad_own_value = jnp.einsum(
        "hij,ihd->jhd",
        cross_f.astype(jnp.bfloat16),
        group_grad_out,
        preferred_element_type=jnp.float32,
    )
    grad_gquery = (
        jnp.einsum("hij,jhd->ihd", cross_ds, own_key, preferred_element_type=jnp.float32) * scale
    )
    self_query = (
        jnp.einsum("hij,jhd->ihd", self_ds, glob_key, preferred_element_type=jnp.float32) * scale
    )
    grad_gquery = lax.dynamic_update_slice_in_dim(
        grad_gquery,
        lax.dynamic_slice_in_dim(grad_gquery, first_own, own_globals, 0) + self_query,
        first_own,
        0,
    )
    grad_gkey = (
        grad_gkey
        + jnp.einsum("hij,ihd->jhd", self_ds, my_query, preferred_element_type=jnp.float32) * scale
    )
    grad_gvalue = grad_gvalue + jnp.einsum(
        "hij,ihd->jhd", self_f.astype(jnp.bfloat16), my_grad_out, preferred_element_type=jnp.float32
    )
    cross_grad = cross_ds.astype(jnp.float32)
    grad_own = grad_own + jnp.sum(jnp.where(cross_own[None], cross_grad, 0.0), (1, 2))
    grad_other = grad_other + jnp.sum(jnp.where(cross_own[None], 0.0, cross_grad), (1, 2))
    glob_sums = (
        grad_gquery.reshape(group_globals, D),
        grad_gkey.reshape(group_globals, D),
        grad_gvalue.reshape(group_globals, D),
    )
    query_total, key_total, value_total = (
        lax.psum_scatter(
            glob_sums[0].astype(jnp.bfloat16), "fsdp", scatter_dimension=0, tiled=True
        ).astype(jnp.float32),
        lax.psum_scatter(
            glob_sums[1].astype(jnp.bfloat16), "fsdp", scatter_dimension=0, tiled=True
        ).astype(jnp.float32),
        lax.psum_scatter(
            glob_sums[2].astype(jnp.bfloat16), "fsdp", scatter_dimension=0, tiled=True
        ).astype(jnp.float32),
    )
    glob_grad_proj = jnp.concatenate([query_total, key_total, value_total], 1).astype(jnp.bfloat16)
    grad_window = jnp.concatenate(
        [
            grad_window_key.reshape(block_count, width, D),
            grad_window_value.reshape(block_count, width, D),
        ],
        -1,
    )
    grad_left = grad_window[:, :RADIUS]
    grad_right = grad_window[:, RADIUS + BLOCK :]

    def spread(start, count_rows):
        from_right = ((order[:, None] == my_ids[None, :] - 1) & (bins[None, :] > 0)).astype(
            jnp.float32
        )
        from_left = (
            (order[:, None] == my_ids[None, :] + 1) & (bins[None, :] < SEQ_BLOCKS - 1)
        ).astype(jnp.float32)
        upper = jnp.einsum("cj,jrd->crd", from_right, grad_left, precision=HIGHEST)
        lower = jnp.einsum("cj,jrd->crd", from_left, grad_right, precision=HIGHEST)
        return jnp.pad(upper, ((0, 0), (BLOCK - RADIUS, 0), (0, 0))) + jnp.pad(
            lower, ((0, 0), (0, BLOCK - RADIUS), (0, 0))
        )

    rim_grad = lax.psum_scatter(
        spread(jnp.int32(0), block_count * lax.axis_size("fsdp")).astype(jnp.bfloat16),
        "fsdp",
        scatter_dimension=0,
        tiled=True,
    ).astype(jnp.float32)
    cross_kv = jnp.concatenate(
        [grad_own_key.reshape(row_count, D), grad_own_value.reshape(row_count, D)], 1
    ).reshape(block_count, BLOCK, 2 * D)
    own_grad = grad_window[:, RADIUS : RADIUS + BLOCK] + rim_grad + cross_kv
    long_grad_proj = jnp.concatenate(
        [grad_query.reshape(row_count, D), own_grad.reshape(row_count, 2 * D)], 1
    ).astype(jnp.bfloat16)
    grad_proj = jnp.concatenate([long_grad_proj, glob_grad_proj], 0)
    grad_wqkv = jnp.dot(acts_one.T, grad_proj, preferred_element_type=jnp.float32)
    grad_acts_one = jnp.dot(grad_proj, qkv_full.T, preferred_element_type=jnp.float32)
    back_one, gain_grad_one, shift_grad_one = norm_back(
        grad_acts_one, base_one, factor_one, gain_table[:, 0]
    )
    grad_input = grad_middle + back_one
    label_grad = jnp.dot(picker.T, grad_table.T, precision=HIGHEST)
    rel_grad = jnp.concatenate([label_grad, grad_own[None], grad_other[None]], 0)
    rel_total = lax.psum(rel_grad, ("dp", "fsdp"))
    grad_parts = (
        grad_wqkv,
        grad_wattn,
        grad_win,
        grad_wout,
        jnp.stack([gain_grad_one, gain_grad_two], 1),
        jnp.stack([shift_grad_one, shift_grad_two], 1),
    )
    qkv_grad, attn_grad, in_grad, out_grad, gains_grad, biases_grad = (
        lax.psum_scatter(grad_parts[0], ("dp", "fsdp"), scatter_dimension=0, tiled=True),
        lax.psum_scatter(grad_parts[1], ("dp", "fsdp"), scatter_dimension=0, tiled=True),
        lax.psum_scatter(grad_parts[2], ("dp", "fsdp"), scatter_dimension=0, tiled=True),
        lax.psum_scatter(grad_parts[3], ("dp", "fsdp"), scatter_dimension=0, tiled=True),
        lax.psum_scatter(grad_parts[4], ("dp", "fsdp"), scatter_dimension=0, tiled=True),
        lax.psum_scatter(grad_parts[5], ("dp", "fsdp"), scatter_dimension=0, tiled=True),
    )
    return (
        result[:row_count].astype(jnp.bfloat16),
        result[row_count:].astype(jnp.bfloat16),
        loss,
        grad_input[:row_count],
        grad_input[row_count:],
        qkv_grad,
        attn_grad,
        in_grad,
        out_grad,
        gains_grad,
        biases_grad,
        rel_total,
    )


def solution(mesh):
    in_specs = (
        P(("dp", "fsdp"), None),
        P(("dp", "fsdp"), None),
        P(("dp", "fsdp"), None),
        P(("dp", "fsdp"), None),
        P(("dp", "fsdp"), None),
        P(("dp", "fsdp"), None),
        P(("dp", "fsdp"), None),
        P(("dp", "fsdp"), None),
        P(("dp", "fsdp"), None),
        P(("dp", "fsdp"), None),
        P(("dp", "fsdp"), None),
        P(),
        P("dp"),
        P("dp", None),
        P("dp"),
        P(),
        P(("dp", "fsdp")),
    )
    out_specs = (
        P(("dp", "fsdp"), None),
        P(("dp", "fsdp"), None),
        P(),
        P(("dp", "fsdp"), None),
        P(("dp", "fsdp"), None),
        P(("dp", "fsdp"), None),
        P(("dp", "fsdp"), None),
        P(("dp", "fsdp"), None),
        P(("dp", "fsdp"), None),
        P(("dp", "fsdp"), None),
        P(("dp", "fsdp"), None),
        P(),
    )
    return jax.shard_map(shards, mesh=mesh, in_specs=in_specs, out_specs=out_specs, check_vma=False)
```

profile of v0, /device:TPU:1, one launch (start us, length us, event | category | flops | bytes accessed | tf_op | source)
XLA Modules:
  0.0 2617.4 jit_solution(2852482211274871386)
XLA Ops:
  8.0 179.5 %all-gather.2 = bf16[128,6,2]{1,2,0:T(2,128)(2,1)S(1)} all-gather(bf16[1,6,2]{1,2,0:T(2,128)(2,1)} %bitcast.317), channel_id=1, replica_groups=mesh['dp'=8,'fsdp'=16] {'dp','fsdp'}, dimensions={0}, use_global_device_ids=true | all-gather | bytes 3096 | tf_op jit(solution)/shard_map/all_gather | solution.py:103
  187.6 169.8 %all-gather.3 = bf16[128,6,2]{1,2,0:T(2,128)(2,1)S(1)} all-gather(bf16[1,6,2]{1,2,0:T(2,128)(2,1)} %bitcast.318), channel_id=1, replica_groups=mesh['dp'=8,'fsdp'=16] {'dp','fsdp'}, dimensions={0}, use_global_device_ids=true | all-gather | bytes 3096 | tf_op jit(solution)/shard_map/all_gather | solution.py:104
  361.7 6.7 reshape.769
  387.2 17.2 all-gather.18.cloned.1.call-done
  422.3 19.5 all-gather.6
  442.7 17.9 all-gather.5
  461.4 12.4 while.12
  495.2 65.7 %psum.29 = f32[]{:T(128)} all-reduce(f32[]{:T(128)} %convert_reduce_fusion.2), channel_id=1, replica_groups=mesh['dp'=8,'fsdp'=16] {'dp','fsdp'}, use_global_device_ids=true, to_apply=%region_20.21 | all-reduce | flops 1 | bytes 8 | tf_op jit(solution)/shard_map/psum | solution.py:257
  562.0 124.8 %gather_fusion = f32[37888,12]{1,0:T(8,128)} fusion(f32[169,12]{1,0:T(8,128)S(1)} %fusion.100, s32[37888]{0:T(1024)S(1)} %broadcast_clamp_fusion), kind=kCustom, calls=%fused_computation | custom fusion | bytes 3788800 | tf_op jit(solution)/shard_map/gather | solution.py:146
  686.9 12.2 copy.416
  704.1 96.4 %all-gather.26.cloned.1.call-done = bf16[128,6,3072]{2,1,0:T(8,128)(2,1)} async-done(((bf16[1,6,3072]{2,1,0:T(8,128)(2,1)}), bf16[128,6,3072]{2,1,0:T(8,128)(2,1)}) %all-gather.26.cloned.1.call-update) | async-done | bytes 4718608 | tf_op jit(solution)/shard_map/all_gather | solution.py:101
  800.5 7.7 reshape.777
  808.3 6.7 fusion.182
  815.0 44.0 %reduce-scatter.27.cloned.1.call-done = bf16[32,768]{1,0:T(8,128)(2,1)} async-done(((bf16[512,768]{1,0:T(8,128)(2,1)}), bf16[32,768]{1,0:T(8,128)(2,1)}) %reduce-scatter.27.cloned.1.call-update) | async-done | bytes 49168
  860.0 134.9 %all-gather.16.cloned.1.call-done = bf16[64,128,1536]{2,1,0:T(8,128)(2,1)} async-done(((bf16[4,128,1536]{2,1,0:T(8,128)(2,1)}), bf16[64,128,1536]{2,1,0:T(8,128)(2,1)}) %all-gather.16.cloned.1.call-update) | async-done | bytes 25165840 | tf_op jit(solution)/shard_map/all_gather | solution.py:123
  995.0 19.0 fusion.175
  1014.0 16.0 fusion.43
  1032.4 7.3 fusion.46
  1059.0 8.2 fusion.17
  1076.2 19.4 multiply_convert_fusion.2
  1095.7 100.8 %all-gather.20.cloned.1.call-done = bf16[3072,768]{1,0:T(8,128)(2,1)} async-done(((bf16[24,768]{1,0:T(8,128)(2,1)}), bf16[3072,768]{1,0:T(8,128)(2,1)}) %all-gather.20.cloned.1.call-update) | async-done | bytes 4718608 | tf_op jit(solution)/shard_map/all_gather | solution.py:102
  1196.4 6.2 convolution_add_fusion
  1205.7 9.1 add_convert_fusion.1
  1226.3 7.1 fusion.35
  1244.5 10.5 fusion.13
  1274.3 17.5 fusion.50
  1291.8 113.1 %add_convert_fusion = bf16[64,128,1536]{2,0,1:T(8,128)(2,1)S(1)} fusion(f32[64,84,1536]{2,0,1:T(8,128)} %fusion.50, f32[4,84,1536]{2,1,0:T(8,128)} %get-tuple-element.103, pred[64,4,1]{0,1,2:T(4,128)(4,1)S(1)} %copy-done.162), kind=kOutput, calls=%fused_computation.6 | convolution fusion | flops 421527552 | bytes 60260608 | tf_op jit(solution)/shard_map/jit(_pad)/pad | solution.py:431
  1404.9 43.2 %copy.448 = bf16[64,128,1536]{2,1,0:T(8,128)(2,1)} copy(bf16[64,128,1536]{2,0,1:T(8,128)(2,1)S(1)} %add_convert_fusion) | data formatting | bytes 50331648 | tf_op jit(solution)/shard_map/convert_element_type | solution.py:436
  1449.1 22.5 all_gather.56
  1472.9 6.9 fusion.27
  1484.8 9.8 multiply_reduce_fusion
  1494.9 50.6 %psum.30 = f32[12,512]{1,0:T(8,128)S(1)} all-reduce(f32[12,512]{1,0:T(8,128)S(1)} %dynamic_update_slice.18), channel_id=1, replica_groups=mesh['dp'=8,'fsdp'=16] {'fsdp'}, use_global_device_ids=true, to_apply=%region_28.29 | all-reduce | flops 6144 | bytes 49152 | tf_op jit(solution)/shard_map/psum | solution.py:360
  1545.6 14.0 fusion.11
  1563.4 6.4 dynamic_update_slice.19
  1573.7 12.6 fusion.9
  1591.8 10.0 fusion.104
  1602.9 7.9 convolution_bitcast_fusion
  1636.5 7.2 fusion.170
  1649.1 61.3 %reduce-scatter.19.cloned.1.call-done = bf16[32,768]{1,0:T(8,128)(2,1)} async-done(((bf16[512,768]{1,0:T(8,128)(2,1)}), bf16[32,768]{1,0:T(8,128)(2,1)}) %reduce-scatter.19.cloned.1.call-update) | async-done | bytes 49168 | tf_op jit(solution)/shard_map/reduce_scatter | solution.py:401
  1710.4 62.2 %reduce-scatter.21.cloned.1.call-done = bf16[32,768]{1,0:T(8,128)(2,1)} async-done(((bf16[512,768]{1,0:T(8,128)(2,1)}), bf16[32,768]{1,0:T(8,128)(2,1)}) %reduce-scatter.21.cloned.1.call-update) | async-done | bytes 49168 | tf_op jit(solution)/shard_map/reduce_scatter | solution.py:404
  1772.7 7.6 fusion.166
  1780.2 373.5 %fusion.172 = (f32[8,2304]{1,0:T(8,128)S(1)}, f32[8,768]{1,0:T(8,128)S(1)}, f32[8,3072]{1,0:T(8,128)S(1)}) fusion(f32[768,2304]{1,0:T(8,128)} %fusion.166, f32[768,768]{1,0:T(8,128)} %fusion.95, f32[768,3072]{1,0:T(8,128)} %fusion.170), kind=kCustom, calls=%all-reduce-scatter.3 | all-reduce-scatter fusion | flops 6291457 | bytes 19070976
  2165.6 13.0 collective-permute-start.54
  2267.8 7.1 collective-permute-start.25
  2380.4 66.4 %all-reduce.11 = (f32[]{:T(128)}, f32[768,2]{0,1:T(2,128)S(1)}, f32[768,2]{0,1:T(2,128)S(1)}, f32[171,12]{0,1:T(8,128)}) all-reduce(f32[]{:T(128)} %get-tuple-element.111, f32[768,2]{0,1:T(2,128)S(1)} %pad_maximum_fusion.8, f32[768,2]{0,1:T(2,128)S(1)} %pad_maximum_fusion.9, ...), channel_id=1, replica_groups=mesh['dp'=8,'fsdp'=16] {'dp','fsdp'}, use_global_device_ids=true, to_apply=%region_18.19 | all-reduce | flops 5125 | bytes 41000 | tf_op jit(solution)/shard_map/psum | solution.py:257
  2490.2 26.5 %concatenate.50 = f32[262,768]{1,0:T(8,128)S(1)} concatenate(f32[6,768]{1,0:T(8,128)S(1)} %collective-permute-done.63, f32[8,768]{1,0:T(8,128)} %copy-done.140, f32[8,768]{1,0:T(8,128)} %copy-done.141, f32[8,768]{1,0:T(8,128)} %copy-done.142, f32[8,768]{1,0:T(8,128)} %copy-done.143, f32[8,768]{1,0:T(8,128)} %copy-done.144, f32[8,768]{1,0:T(8,128)} %copy-done.145, ...), dimensions={0} | concatenate | bytes 1609728
  2530.9 29.1 %concatenate.49 = f32[262,2304]{1,0:T(8,128)S(1)} concatenate(f32[6,2304]{1,0:T(8,128)S(1)} %copy-done.111, f32[8,2304]{1,0:T(8,128)S(1)} %copy-done.105, f32[8,2304]{1,0:T(8,128)S(1)} %copy-done.107, f32[8,2304]{1,0:T(8,128)S(1)} %copy-done.109, f32[8,2304]{1,0:T(8,128)} %collective-permute-done.27, f32[8,2304]{1,0:T(8,128)} %collective-permute-done.26, ...), dimensions={0} | concatenate | bytes 4829184
  2577.0 31.5 %concatenate.51 = f32[262,3072]{1,0:T(8,128)S(1)} concatenate(f32[6,3072]{1,0:T(8,128)} %copy-done.75, f32[8,3072]{1,0:T(8,128)S(1)} %copy-done.74, f32[8,3072]{1,0:T(8,128)} %copy-done.76, f32[8,3072]{1,0:T(8,128)} %copy-done.77, f32[8,3072]{1,0:T(8,128)} %copy-done.78, f32[8,3072]{1,0:T(8,128)} %copy-done.79, f32[8,3072]{1,0:T(8,128)} %copy-done.80, f32[8,3072]{1,0:T(8,128)} %copy-done.81, ...), dimensions={0} | concatenate | bytes 6438912
  (868 shorter events, 489.6 us)
Async XLA Ops:
  7.2 354.5 %all-gather.22.cloned.1.call-start = ((), (), s32[]{:S(2)}) async-start(), calls=%async_computation.14 | async-start | bytes 4755456 | tf_op jit(solution)/shard_map/all_gather | solution.py:99
  7.9 396.5 %all-gather.18.cloned.1.call-start = ((), (), s32[]{:S(2)}) async-start(), calls=%async_computation.7 | async-start | bytes 2506752 | tf_op jit(solution)/shard_map/all_gather | solution.py:118
  374.9 325.5 %all-gather.24.cloned.1.call-start = ((), (), s32[]{:S(2)}) async-start(), calls=%async_computation.15 | async-start | bytes 1585152 | tf_op jit(solution)/shard_map/all_gather | solution.py:100
  375.7 424.8 %all-gather.26.cloned.1.call-start = ((), (), s32[]{:S(2)}) async-start(), calls=%async_computation.16 | async-start | bytes 6340608 | tf_op jit(solution)/shard_map/all_gather | solution.py:101
  376.3 482.8 %reduce-scatter.27.cloned.1.call-start = ((), (), s32[]{:S(2)}) async-start(), calls=%async_computation.17 | async-start | bytes 835584
  489.0 506.0 %all-gather.16.cloned.1.call-start = ((), (), s32[]{:S(2)}) async-start(), calls=%async_computation.6 | async-start | bytes 26738688 | tf_op jit(solution)/shard_map/all_gather | solution.py:123
  491.7 704.7 %all-gather.20.cloned.1.call-start = ((), (), s32[]{:S(2)}) async-start(), calls=%async_computation.8 | async-start | bytes 4755456 | tf_op jit(solution)/shard_map/all_gather | solution.py:102
  492.5 1151.3 %reduce-scatter.17.cloned.1.call-start = ((), (), s32[]{:S(2)}) async-start(), calls=%async_computation.9 | async-start | bytes 26738688 | tf_op jit(solution)/shard_map/reduce_scatter | solution.py:435
  1448.1 201.0 %reduce-scatter.23.cloned.1.call-start = ((), (), s32[]{:S(2)}) async-start(), calls=%async_computation.12 | async-start | bytes 835584 | tf_op jit(solution)/shard_map/reduce_scatter | solution.py:407
  1545.6 164.8 %reduce-scatter.19.cloned.1.call-start = ((), (), s32[]{:S(2)}) async-start(), calls=%async_computation.10 | async-start | bytes 835584 | tf_op jit(solution)/shard_map/reduce_scatter | solution.py:401
  1573.6 199.0 %reduce-scatter.21.cloned.1.call-start = ((), (), s32[]{:S(2)}) async-start(), calls=%async_computation.11 | async-start | bytes 835584 | tf_op jit(solution)/shard_map/reduce_scatter | solution.py:404
  1591.5 1017.7 %reduce-scatter.25.cloned.1.call-start = ((), (), s32[]{:S(2)}) async-start(), calls=%async_computation.13 | async-start | bytes 9510912 | tf_op jit(solution)/shard_map/reduce_scatter | solution.py:470
  2160.3 18.3 collective-permute-start.58
  2161.6 20.8 collective-permute-start.57
  2163.0 22.9 collective-permute-start.56
  2164.3 24.4 collective-permute-start.55
  2165.6 25.4 collective-permute-start.54
  2194.9 29.1 %collective-permute-start.47 = (f32[8,768]{1,0:T(8,128)S(1)}, f32[8,768]{1,0:T(8,128)}, u32[]{:S(2)}, u32[]{:S(2)}) collective-permute-start(f32[8,768]{1,0:T(8,128)S(1)} %get-tuple-element.78), channel_id=1, source_target_pairs={{0,16},{1,17},{2,18},{3,19},{4,20},{5,21},{6,22},{7,23},{8,24},{9,... | collective-permute-start | bytes 73736
  2197.4 30.1 %collective-permute-start.46 = (f32[8,768]{1,0:T(8,128)S(1)}, f32[8,768]{1,0:T(8,128)}, u32[]{:S(2)}, u32[]{:S(2)}) collective-permute-start(f32[8,768]{1,0:T(8,128)S(1)} %get-tuple-element.78), channel_id=1, source_target_pairs={{0,15},{1,16},{2,17},{3,18},{4,19},{5,20},{6,21},{7,22},{8,23},{9,... | collective-permute-start | bytes 73736
  2199.4 29.5 %collective-permute-start.45 = (f32[8,768]{1,0:T(8,128)S(1)}, f32[8,768]{1,0:T(8,128)}, u32[]{:S(2)}, u32[]{:S(2)}) collective-permute-start(f32[8,768]{1,0:T(8,128)S(1)} %get-tuple-element.78), channel_id=1, source_target_pairs={{0,14},{1,15},{2,16},{3,17},{4,18},{5,19},{6,20},{7,21},{8,22},{9,... | collective-permute-start | bytes 73736
  2204.8 26.1 collective-permute-start.44
  2206.8 27.3 %collective-permute-start.43 = (f32[8,768]{1,0:T(8,128)S(1)}, f32[8,768]{1,0:T(8,128)}, u32[]{:S(2)}, u32[]{:S(2)}) collective-permute-start(f32[8,768]{1,0:T(8,128)S(1)} %get-tuple-element.78), channel_id=1, source_target_pairs={{0,12},{1,13},{2,14},{3,15},{4,16},{5,17},{6,18},{7,19},{8,20},{9,... | collective-permute-start | bytes 73736
  2263.8 22.4 collective-permute-start.27
  2265.9 22.8 collective-permute-start.26
  2267.8 23.7 collective-permute-start.25
  2299.6 18.1 collective-permute-start.16
  2301.5 19.2 collective-permute-start.15
  2303.1 21.2 collective-permute-start.14
  2305.5 20.9 collective-permute-start.13
  2367.3 85.0 %collective-permute-start.88 = (f32[8,3072]{1,0:T(8,128)S(1)}, f32[8,3072]{1,0:T(8,128)S(1)}, u32[]{:S(2)}, u32[]{:S(2)}) collective-permute-start(f32[8,3072]{1,0:T(8,128)S(1)} %get-tuple-element.79), channel_id=1, source_target_pairs={{0,25},{1,26},{2,27},{3,28},{4,29},{5,30},{6,31},{7,32},{8,33},{9,... | collective-permute-start | bytes 294920
  2371.2 84.6 %collective-permute-start.87 = (f32[8,3072]{1,0:T(8,128)S(1)}, f32[8,3072]{1,0:T(8,128)S(1)}, u32[]{:S(2)}, u32[]{:S(2)}) collective-permute-start(f32[8,3072]{1,0:T(8,128)S(1)} %get-tuple-element.79), channel_id=1, source_target_pairs={{0,24},{1,25},{2,26},{3,27},{4,28},{5,29},{6,30},{7,31},{8,32},{9,... | collective-permute-start | bytes 294920
  2373.2 86.4 %collective-permute-start.86 = (f32[8,3072]{1,0:T(8,128)S(1)}, f32[8,3072]{1,0:T(8,128)S(1)}, u32[]{:S(2)}, u32[]{:S(2)}) collective-permute-start(f32[8,3072]{1,0:T(8,128)S(1)} %get-tuple-element.79), channel_id=1, source_target_pairs={{0,23},{1,24},{2,25},{3,26},{4,27},{5,28},{6,29},{7,30},{8,31},{9,... | collective-permute-start | bytes 294920
  2375.8 87.0 %collective-permute-start.85 = (f32[8,3072]{1,0:T(8,128)S(1)}, f32[8,3072]{1,0:T(8,128)S(1)}, u32[]{:S(2)}, u32[]{:S(2)}) collective-permute-start(f32[8,3072]{1,0:T(8,128)S(1)} %get-tuple-element.79), channel_id=1, source_target_pairs={{0,22},{1,23},{2,24},{3,25},{4,26},{5,27},{6,28},{7,29},{8,30},{9,... | collective-permute-start | bytes 294920
  2379.0 89.1 %collective-permute-start.84 = (f32[8,3072]{1,0:T(8,128)S(1)}, f32[8,3072]{1,0:T(8,128)S(1)}, u32[]{:S(2)}, u32[]{:S(2)}) collective-permute-start(f32[8,3072]{1,0:T(8,128)S(1)} %get-tuple-element.79), channel_id=1, source_target_pairs={{0,21},{1,22},{2,23},{3,24},{4,25},{5,26},{6,27},{7,28},{8,29},{9,... | collective-permute-start | bytes 294920
  2452.3 19.4 collective-permute-start.83
  2455.9 19.3 collective-permute-start.82
  2459.6 19.8 collective-permute-start.81
  2462.8 19.1 collective-permute-start.80
  2471.7 45.0 %collective-permute-start.78 = (f32[8,3072]{1,0:T(8,128)S(1)}, f32[8,3072]{1,0:T(8,128)S(1)}, u32[]{:S(2)}, u32[]{:S(2)}) collective-permute-start(f32[8,3072]{1,0:T(8,128)S(1)} %get-tuple-element.79), channel_id=1, source_target_pairs={{0,15},{1,16},{2,17},{3,18},{4,19},{5,20},{6,21},{7,22},{8,23},{9,... | collective-permute-start | bytes 294920
  2475.1 44.0 %collective-permute-start.77 = (f32[8,3072]{1,0:T(8,128)S(1)}, f32[8,3072]{1,0:T(8,128)S(1)}, u32[]{:S(2)}, u32[]{:S(2)}) collective-permute-start(f32[8,3072]{1,0:T(8,128)S(1)} %get-tuple-element.79), channel_id=1, source_target_pairs={{0,14},{1,15},{2,16},{3,17},{4,18},{5,19},{6,20},{7,21},{8,22},{9,... | collective-permute-start | bytes 294920
  2479.4 41.1 %collective-permute-start.76 = (f32[8,3072]{1,0:T(8,128)S(1)}, f32[8,3072]{1,0:T(8,128)S(1)}, u32[]{:S(2)}, u32[]{:S(2)}) collective-permute-start(f32[8,3072]{1,0:T(8,128)S(1)} %get-tuple-element.79), channel_id=1, source_target_pairs={{0,13},{1,14},{2,15},{3,16},{4,17},{5,18},{6,19},{7,20},{8,21},{9,... | collective-permute-start | bytes 294920
  2481.9 42.3 %collective-permute-start.75 = (f32[8,3072]{1,0:T(8,128)S(1)}, f32[8,3072]{1,0:T(8,128)S(1)}, u32[]{:S(2)}, u32[]{:S(2)}) collective-permute-start(f32[8,3072]{1,0:T(8,128)S(1)} %get-tuple-element.79), channel_id=1, source_target_pairs={{0,12},{1,13},{2,14},{3,15},{4,16},{5,17},{6,18},{7,19},{8,20},{9,... | collective-permute-start | bytes 294920
  2485.9 40.5 %collective-permute-start.74 = (f32[8,3072]{1,0:T(8,128)S(1)}, f32[8,3072]{1,0:T(8,128)S(1)}, u32[]{:S(2)}, u32[]{:S(2)}) collective-permute-start(f32[8,3072]{1,0:T(8,128)S(1)} %get-tuple-element.79), channel_id=1, source_target_pairs={{0,11},{1,12},{2,13},{3,14},{4,15},{5,16},{6,17},{7,18},{8,19},{9,... | collective-permute-start | bytes 294920
  2516.7 43.3 %collective-permute-start.73 = (f32[8,3072]{1,0:T(8,128)S(1)}, f32[8,3072]{1,0:T(8,128)S(1)}, u32[]{:S(2)}, u32[]{:S(2)}) collective-permute-start(f32[8,3072]{1,0:T(8,128)S(1)} %get-tuple-element.79), channel_id=1, source_target_pairs={{0,10},{1,11},{2,12},{3,13},{4,14},{5,15},{6,16},{7,17},{8,18},{9,... | collective-permute-start | bytes 294920
  2519.2 43.6 %collective-permute-start.72 = (f32[8,3072]{1,0:T(8,128)S(1)}, f32[8,3072]{1,0:T(8,128)S(1)}, u32[]{:S(2)}, u32[]{:S(2)}) collective-permute-start(f32[8,3072]{1,0:T(8,128)S(1)} %get-tuple-element.79), channel_id=1, source_target_pairs={{0,9},{1,10},{2,11},{3,12},{4,13},{5,14},{6,15},{7,16},{8,17},{9,1... | collective-permute-start | bytes 294920
  2520.5 46.1 %collective-permute-start.71 = (f32[8,3072]{1,0:T(8,128)S(1)}, f32[8,3072]{1,0:T(8,128)S(1)}, u32[]{:S(2)}, u32[]{:S(2)}) collective-permute-start(f32[8,3072]{1,0:T(8,128)S(1)} %get-tuple-element.79), channel_id=1, source_target_pairs={{0,8},{1,9},{2,10},{3,11},{4,12},{5,13},{6,14},{7,15},{8,16},{9,17... | collective-permute-start | bytes 294920
  2524.2 45.6 %collective-permute-start.70 = (f32[8,3072]{1,0:T(8,128)S(1)}, f32[8,3072]{1,0:T(8,128)S(1)}, u32[]{:S(2)}, u32[]{:S(2)}) collective-permute-start(f32[8,3072]{1,0:T(8,128)S(1)} %get-tuple-element.79), channel_id=1, source_target_pairs={{0,7},{1,8},{2,9},{3,10},{4,11},{5,12},{6,13},{7,14},{8,15},{9,16}... | collective-permute-start | bytes 294920
  2526.5 46.1 %collective-permute-start.69 = (f32[8,3072]{1,0:T(8,128)S(1)}, f32[8,3072]{1,0:T(8,128)S(1)}, u32[]{:S(2)}, u32[]{:S(2)}) collective-permute-start(f32[8,3072]{1,0:T(8,128)S(1)} %get-tuple-element.79), channel_id=1, source_target_pairs={{0,6},{1,7},{2,8},{3,9},{4,10},{5,11},{6,12},{7,13},{8,14},{9,15},... | collective-permute-start | bytes 294920
  (281 other events, 8669.0 us)
Sparse Core Ops, SparseCore 0:
  9.7 202.3 all-gather.21
  375.1 29.3 all-gather.17
  406.2 193.0 all-gather.23
  600.9 199.6 all-gather.25
  802.7 56.2 reduce-scatter.26
  861.3 133.6 all-gather.15
  996.8 199.5 all-gather.19
  1448.2 140.1 reduce-scatter.16
  1590.9 57.6 reduce-scatter.22
  1650.8 59.5 reduce-scatter.18
  1712.9 59.7 reduce-scatter.20
  1775.4 653.7 reduce-scatter.24
where the time goes:
time: 2630 us; the launch traced here: 2620 us
  blocking collectives  965 us (37%)
  waiting for transfers between devices  520 us (20%)
  local copies, waits for them, and re-layouts  435 us (17%)
  matrix products  330 us (13%)
  starting transfers between devices  258 us (10%)
  other arithmetic  88.2 us (3%)
    unnamed x1, blocking collectives  374 us
    unnamed x97, starting transfers between devices  257 us
    all_gather x1, blocking collectives, shards(): lax.all_gather(weights[4], ('dp', 'fsdp'), axis=0, tiled=True)  180 us
    all_gather x1, blocking collectives, shards(): lax.all_gather(weights[5], ('dp', 'fsdp'), axis=0, tiled=True)  170 us
    gather x2, local copies, waits for them, and re-layouts, shards(): label_table[jnp.clip(offsets, 0, 2 * RADIUS)]  137 us
    all_gather x1, waiting for transfers between devices, shards(): piece = lax.all_gather(keyval, 'fsdp', axis=0, tiled=True)  135 us
    psum x2, blocking collectives, shards(): lax.psum((jnp.sum(weighting[:, None] * error * error), jnp.sum(weighting)...  132 us
    unnamed x461, local copies, waits for them, and re-layouts  129 us
  transfers between devices with their start and end apart: 108, of which 7 were waited for; matrix products, arithmetic and copies ran while one was open for 36% of the time, Pallas kernels for 0%

commit v1 on v0

v1 whole, which is shorter than its diff:
```python
import math

import jax
import jax.numpy as jnp
from jax import lax
from jax.sharding import PartitionSpec as P

D = 768
HEADS = 12
HEAD = 64
RADIUS = 84
LABELS = 169
BLOCK = 128
SEQ_BLOCKS = 16
GLOBAL_EVERY = 16
GSEQ = 128
ROWS = 512
EXT = 896
EPS = 1e-05
MASKED = -1e30
HIGHEST = lax.Precision.HIGHEST
BOTH = ("dp", "fsdp")
f32 = jnp.float32
bf16 = jnp.bfloat16

QUADS = [[4 * i + j for j in range(4)] for i in range(4)]
SAME_CORE = [[4 * g + 2 * p + c for p in range(2) for g in range(32)] for c in range(2)]
SWAP = [(i, i ^ 1) for i in range(16)]
TO_RIGHT = [(i, i + 1) for i in range(16) if i % 4 < 3]
TO_LEFT = [(i, i - 1) for i in range(16) if i % 4 > 0]


def exchange(value, axis, groups=None):
    return lax.all_to_all(value, axis, 0, 0, axis_index_groups=groups, tiled=True)


def swap(value):
    return lax.ppermute(value, "fsdp", SWAP)


def pieces(rows):
    width = rows.shape[-1]
    return rows.reshape(4, 16, 8, width).transpose(1, 0, 2, 3).reshape(64, 8, width)


def unpieces(value):
    width = value.shape[-1]
    return value.reshape(16, 4, 8, width).transpose(1, 0, 2, 3).reshape(ROWS, width)


def reorder(rows, index):
    spread = exchange(pieces(rows), "fsdp")
    return unpieces(exchange(spread[index], "fsdp"))


def norm_rows(values, gain, shift):
    centre = jnp.mean(values, -1, keepdims=True)
    centred = values - centre
    spread = jnp.mean(centred * centred, -1, keepdims=True)
    factor = lax.rsqrt(spread + EPS)
    normal = centred * factor
    return (normal * gain + shift, normal, factor)


def norm_back(grad, normal, factor, gain):
    scaled = grad * gain
    first = jnp.mean(scaled, -1, keepdims=True)
    second = jnp.mean(scaled * normal, -1, keepdims=True)
    return factor * (scaled - first - normal * second)


def split3(value):
    high = value.astype(bf16)
    rest = value - high.astype(f32)
    mid = rest.astype(bf16)
    low = (rest - mid.astype(f32)).astype(bf16)
    return jnp.concatenate([high, mid, low], -1)


def join3(value, count):
    value = value.astype(f32)
    return value[..., :count] + value[..., count : 2 * count] + value[..., 2 * count : 3 * count]


def dot(a, b):
    return jnp.dot(a, b, preferred_element_type=f32)


def reduce_columns(grad, core):
    keep = lax.dynamic_index_in_dim(grad, core, 1, keepdims=False)
    send = lax.dynamic_index_in_dim(grad, 1 - core, 1, keepdims=False)
    total = keep + swap(send.astype(bf16)).astype(f32)
    parts = exchange(total.astype(bf16).reshape(64, 24, D), BOTH, SAME_CORE)
    mine = jnp.sum(parts.astype(f32), 0)
    return exchange(mine.reshape(4, 6, D), "fsdp", QUADS)


def shards(
    long_in,
    glob_in,
    cot_long,
    cot_glob,
    teacher,
    w_qkv,
    w_attn,
    w_in,
    w_out,
    norm_gains,
    norm_biases,
    rel_bias,
    lengths,
    block_order,
    global_pos,
    rel_labels,
    loss_mask,
):
    scale = 1.0 / math.sqrt(HEAD)
    member = lax.axis_index("fsdp")
    core = member % 2
    quarter = member % 4
    seq = member // 4
    order = block_order[0]
    slots = jnp.arange(64)
    inverse = jnp.sum(jnp.where(order[None, :] == slots[:, None], slots[None, :], 0), 1)
    length = jnp.sum(jnp.where(jnp.arange(4) == seq, lengths, 0))
    anchors = lax.dynamic_slice_in_dim(global_pos, seq * GSEQ, GSEQ)

    my_ids = lax.dynamic_slice_in_dim(order, member * 4, 4)
    my_lens = jnp.sum(
        jnp.where(my_ids[:, None] // SEQ_BLOCKS == jnp.arange(4)[None, :], lengths[None, :], 0), 1
    )
    slot_pos = (my_ids % SEQ_BLOCKS)[:, None] * BLOCK + jnp.arange(BLOCK)[None, :]
    slot_weight = ((slot_pos < my_lens[:, None]).reshape(ROWS) & (loss_mask == 1)).astype(jnp.int32)
    my_count = jnp.sum(slot_weight)

    high = (my_count // 16).astype(bf16)
    low = (my_count % 16).astype(bf16)
    extra = jnp.concatenate(
        [
            norm_gains,
            norm_biases,
            jnp.broadcast_to(jnp.stack([high, low]), (6, 2)),
            jnp.zeros((6, 122), bf16),
        ],
        1,
    )
    first = lax.all_gather(
        jnp.concatenate([w_qkv, w_attn, extra], 1), "fsdp", axis_index_groups=QUADS, axis=0, tiled=True
    )
    second = lax.all_gather(w_in, "fsdp", axis_index_groups=QUADS, axis=0, tiled=True)
    first_part = jnp.concatenate(
        [lax.dynamic_slice_in_dim(first, quarter * D, D, 1), first[:, 4 * D :]], 1
    )
    second_part = lax.dynamic_slice_in_dim(second, quarter * D, D, 1)
    mine_one = exchange(
        jnp.broadcast_to(first_part[None], (64, 24, EXT)), BOTH, SAME_CORE
    ).reshape(2, D, EXT)
    other_one = swap(mine_one[..., :D])
    extras = mine_one[..., D:].reshape(2, 32, 24, 128)[0].reshape(D, 128)
    del extras
    side = mine_one[0, :, D:].astype(f32)
    even = jnp.where(core == 0, mine_one[..., :D], other_one)
    odd = jnp.where(core == 0, other_one, mine_one[..., :D])
    wq, wv = even[0], even[1]
    wk, wa = odd[0], odd[1]
    gain1, gain2, shift1, shift2 = side[:, 0], side[:, 1], side[:, 2], side[:, 3]
    count = jnp.sum(
        jnp.where(jnp.arange(D) % 6 == 0, side[:, 4] * 16.0 + side[:, 5], 0.0)
    )
    mine_two = exchange(
        jnp.broadcast_to(second_part[None], (64, 24, D)), BOTH, SAME_CORE
    ).reshape(2, D, D)
    other_two = swap(mine_two)
    even = jnp.where(core == 0, mine_two, other_two)
    odd = jnp.where(core == 0, other_two, mine_two)
    win = jnp.concatenate([even[0], odd[0], even[1], odd[1]], 1)
    half_keep = lax.dynamic_slice_in_dim(w_out, core * 384, 384, 1)
    half_send = lax.dynamic_slice_in_dim(w_out, (1 - core) * 384, 384, 1)
    half_got = swap(half_send)
    pair_rows = jnp.where(
        core == 0,
        jnp.concatenate([half_keep, half_got], 0),
        jnp.concatenate([half_got, half_keep], 0),
    )
    mine_three = exchange(jnp.broadcast_to(pair_rows[None], (64, 48, 384)), BOTH, SAME_CORE)
    mine_three = mine_three.reshape(2, 32, 48, 384).transpose(1, 0, 2, 3).reshape(4 * D, 384)
    other_three = swap(mine_three)
    wout = jnp.where(
        core == 0,
        jnp.concatenate([mine_three, other_three], 1),
        jnp.concatenate([other_three, mine_three], 1),
    )

    natural = reorder(long_in, inverse)
    packed = jnp.concatenate(
        [
            cot_long,
            teacher,
            jnp.broadcast_to(slot_weight[:, None], (ROWS, 128)).astype(bf16),
        ],
        1,
    )
    packed = reorder(packed, inverse)
    cot_nat = packed[:, :D].astype(f32)
    teach_nat = packed[:, D : 2 * D].astype(f32)
    weighting = packed[:, 2 * D].astype(f32)
    globs = lax.all_gather(
        jnp.concatenate([glob_in, cot_glob], 1), "fsdp", axis_index_groups=QUADS, axis=0, tiled=True
    )
    left = lax.ppermute(natural[ROWS - BLOCK :], "fsdp", TO_RIGHT)
    right = lax.ppermute(natural[:BLOCK], "fsdp", TO_LEFT)
    inputs = jnp.concatenate([left, natural, right, globs[:, :D]], 0).astype(f32)
    normed_one, base_one, factor_one = norm_rows(inputs, gain1, shift1)
    acts_one = normed_one.astype(bf16)
    wqkv = jnp.concatenate([wq, wk, wv], 1)
    proj = dot(acts_one, wqkv).astype(bf16)

    def heads(value):
        return value.reshape(value.shape[0], HEADS, HEAD)

    query = heads(proj[128:640, :D]).reshape(4, BLOCK, HEADS, HEAD)
    keys = heads(proj[:768, D : 2 * D])
    values = heads(proj[:768, 2 * D :])
    gquery = heads(proj[768:, :D])
    gkey = heads(proj[768:, D : 2 * D])
    gvalue = heads(proj[768:, 2 * D :])
    start = quarter * ROWS
    key_pos = start - BLOCK + jnp.arange(768)
    key_ok = (key_pos >= 0) & (key_pos < length)
    glob_ok = anchors < length
    window_key = jnp.stack([keys[128 * j : 128 * j + 384] for j in range(4)])
    window_value = jnp.stack([values[128 * j : 128 * j + 384] for j in range(4)])
    window_ok = jnp.stack([key_ok[128 * j : 128 * j + 384] for j in range(4)])
    picker = (rel_labels[:, None] == jnp.arange(LABELS)[None, :]).astype(f32)
    label_table = jnp.dot(picker, rel_bias[:LABELS], precision=HIGHEST)
    line = jnp.full((HEADS, 512), MASKED, f32)
    line = lax.dynamic_update_slice(line, label_table.T, (0, 44))
    band = jnp.stack([jnp.roll(line, r, 1)[:, :384] for r in range(BLOCK)], 1)
    query_run = (start + jnp.arange(ROWS)) // GLOBAL_EVERY
    owning = (query_run[:, None] == jnp.arange(GSEQ)[None, :]).reshape(4, BLOCK, GSEQ)
    own_bias = rel_bias[LABELS]
    other_bias = rel_bias[LABELS + 1]
    remote_bias = jnp.where(
        owning[:, None], own_bias[None, :, None, None], other_bias[None, :, None, None]
    )

    def long_scores():
        local = (
            jnp.einsum("bihd,bthd->bhit", query, window_key, preferred_element_type=f32) * scale
            + band[None]
        )
        remote = (
            jnp.einsum("bihd,ghd->bhig", query, gkey, preferred_element_type=f32) * scale
            + remote_bias
        )
        return jnp.concatenate(
            [
                jnp.where(window_ok[:, None, None, :], local, MASKED),
                jnp.where(glob_ok[None, None, None, :], remote, MASKED),
            ],
            -1,
        )

    scores = long_scores()
    summit = jnp.max(scores, -1, keepdims=True)
    powers = jnp.exp(scores - summit)
    total = jnp.sum(powers, -1, keepdims=True)
    long_lse = summit + jnp.log(total)
    probs = (powers / total).astype(bf16)
    long_out = jnp.einsum(
        "bhit,bthd->bihd", probs[..., :384], window_value, preferred_element_type=f32
    ) + jnp.einsum("bhig,ghd->bihd", probs[..., 384:], gvalue, preferred_element_type=f32)
    long_out = long_out.reshape(ROWS, D).astype(bf16)

    cross_key = jnp.concatenate([keys[128:640], gkey], 0)
    cross_value = jnp.concatenate([values[128:640], gvalue], 0)
    own_glob = jnp.arange(GSEQ) // 32 == quarter
    cross_ok = jnp.concatenate([key_ok[128:640], glob_ok & own_glob])
    cross_own = query_run[None, :] == jnp.arange(GSEQ)[:, None]
    cross_bias = jnp.concatenate(
        [
            jnp.where(cross_own[None], own_bias[:, None, None], other_bias[:, None, None]),
            jnp.zeros((HEADS, GSEQ, GSEQ), f32),
        ],
        -1,
    )

    def cross_scores():
        return jnp.where(
            cross_ok[None, None, :],
            jnp.einsum("ihd,jhd->hij", gquery, cross_key, preferred_element_type=f32) * scale
            + cross_bias,
            MASKED,
        )

    scores = cross_scores()
    top = jnp.max(scores, -1, keepdims=True)
    powers = jnp.exp(scores - top)
    total = jnp.sum(powers, -1, keepdims=True)
    part_lse = (top + jnp.log(total))[..., 0].T
    part_out = jnp.einsum(
        "hij,jhd->ihd", (powers / total).astype(bf16), cross_value, preferred_element_type=f32
    ).reshape(GSEQ, D)
    sent = jnp.concatenate(
        [part_out.astype(bf16), split3(part_lse), jnp.zeros((GSEQ, 92), bf16)], 1
    )
    got = exchange(jnp.broadcast_to(sent[None], (4, GSEQ, EXT)).reshape(4 * GSEQ, EXT), "fsdp", QUADS)
    got = got.reshape(4, GSEQ, EXT)
    lses = join3(got[..., D:], HEADS)
    high = jnp.max(lses, 0)
    glob_lse = high + jnp.log(jnp.sum(jnp.exp(lses - high), 0))
    shares = jnp.exp(lses - glob_lse)
    glob_out = jnp.sum(
        got[..., :D].astype(f32) * jnp.repeat(shares, HEAD, axis=-1), 0
    ).astype(bf16)

    mixed = jnp.concatenate([long_out, glob_out], 0)
    middle = inputs[jnp.r_[128:640, 768:896]] + dot(mixed, wa)
    normed_two, base_two, factor_two = norm_rows(middle, gain2, shift2)
    acts_two = normed_two.astype(bf16)
    inner = dot(acts_two, win)
    hidden_full, gelu_back = jax.vjp(lambda v: jax.nn.gelu(v, approximate=False), inner)
    hidden = hidden_full.astype(bf16)
    result = middle + dot(hidden, wout)
    error = result[:ROWS] - teach_nat
    loss_sum = jnp.sum(weighting[:, None] * error * error)
    grad_result = jnp.concatenate(
        [cot_nat + 2.0 * weighting[:, None] * error / count, globs[:, D:].astype(f32)], 0
    )
    owned = jnp.concatenate([jnp.ones((ROWS,), f32), own_glob.astype(f32)])[:, None]
    owned_bf = owned.astype(bf16)
    grad_z = grad_result.astype(bf16)
    grad_wout = dot(hidden.T, grad_z * owned_bf)
    grad_hidden = dot(grad_z, wout.T)
    grad_inner = gelu_back(grad_hidden)[0].astype(bf16)
    grad_win = dot(acts_two.T, grad_inner * owned_bf)
    grad_acts = dot(grad_inner, win.T)
    gain_grad_two = jnp.sum(grad_acts * base_two * owned, 0)
    shift_grad_two = jnp.sum(grad_acts * owned, 0)
    grad_middle = grad_result + norm_back(grad_acts, base_two, factor_two, gain2)
    grad_branch = grad_middle.astype(bf16)
    grad_wattn = dot(mixed.T, grad_branch * owned_bf)
    grad_mixed = dot(grad_branch, wa.T).astype(bf16)

    grad_long_out = heads(grad_mixed[:ROWS]).reshape(4, BLOCK, HEADS, HEAD)
    grad_glob_out = heads(grad_mixed[ROWS:])
    probs = jnp.exp(long_scores() - long_lse)
    dp = jnp.concatenate(
        [
            jnp.einsum("bihd,bthd->bhit", grad_long_out, window_value, preferred_element_type=f32),
            jnp.einsum("bihd,ghd->bhig", grad_long_out, gvalue, preferred_element_type=f32),
        ],
        -1,
    )
    delta = jnp.sum(probs * dp, -1, keepdims=True)
    ds = (probs * (dp - delta)).astype(bf16)
    probs = probs.astype(bf16)
    grad_query = (
        jnp.einsum("bhit,bthd->bihd", ds[..., :384], window_key, preferred_element_type=f32)
        + jnp.einsum("bhig,ghd->bihd", ds[..., 384:], gkey, preferred_element_type=f32)
    ) * scale
    win_dk = jnp.einsum("bhit,bihd->bthd", ds[..., :384], query, preferred_element_type=f32) * scale
    win_dv = jnp.einsum(
        "bhit,bihd->bthd", probs[..., :384], grad_long_out, preferred_element_type=f32
    )
    dgk = jnp.einsum("bhig,bihd->ghd", ds[..., 384:], query, preferred_element_type=f32) * scale
    dgv = jnp.einsum("bhig,bihd->ghd", probs[..., 384:], grad_long_out, preferred_element_type=f32)
    band_grad = jnp.sum(ds[..., :384].astype(f32), 0)
    skewed = jnp.pad(band_grad.reshape(HEADS, BLOCK * 384), ((0, 0), (0, BLOCK))).reshape(
        HEADS, BLOCK, 385
    )
    grad_table = jnp.sum(skewed, 1)[:, 44 : 44 + LABELS]
    remote = ds[..., 384:].astype(f32)
    grad_own = jnp.sum(jnp.where(owning[:, None], remote, 0.0), (0, 2, 3))
    grad_other = jnp.sum(jnp.where(owning[:, None], 0.0, remote), (0, 2, 3))
    gdelta = jnp.sum(
        heads(grad_mixed[ROWS:]).astype(f32) * heads(glob_out).astype(f32), -1
    )
    probs = jnp.exp(cross_scores() - glob_lse.T[..., None])
    dp = jnp.einsum("ihd,jhd->hij", grad_glob_out, cross_value, preferred_element_type=f32)
    ds = (probs * (dp - gdelta.T[..., None])).astype(bf16)
    probs = probs.astype(bf16)
    dgq = jnp.einsum("hij,jhd->ihd", ds, cross_key, preferred_element_type=f32) * scale
    cross_dk = jnp.einsum("hij,ihd->jhd", ds, gquery, preferred_element_type=f32) * scale
    cross_dv = jnp.einsum("hij,ihd->jhd", probs, grad_glob_out, preferred_element_type=f32)
    remote = ds[..., :ROWS].astype(f32)
    grad_own = grad_own + jnp.sum(jnp.where(cross_own[None], remote, 0.0), (1, 2))
    grad_other = grad_other + jnp.sum(jnp.where(cross_own[None], 0.0, remote), (1, 2))

    def gather_rows(windows, cross):
        rows = jnp.zeros((768, HEADS, HEAD), f32)
        for j in range(4):
            rows = rows.at[128 * j : 128 * j + 384].add(windows[j])
        return rows.at[128:640].add(cross[:ROWS]).reshape(768, D)

    dk = jnp.concatenate([gather_rows(win_dk, cross_dk), (dgk + cross_dk[ROWS:]).reshape(GSEQ, D)])
    dv = jnp.concatenate([gather_rows(win_dv, cross_dv), (dgv + cross_dv[ROWS:]).reshape(GSEQ, D)])
    dq = jnp.concatenate(
        [
            jnp.zeros((BLOCK, D), f32),
            grad_query.reshape(ROWS, D),
            jnp.zeros((BLOCK, D), f32),
            dgq.reshape(GSEQ, D),
        ]
    )
    grad_proj = jnp.concatenate([dq, dk, dv], 1).astype(bf16)
    grad_wqkv = dot(acts_one.T, grad_proj)
    grad_acts = dot(grad_proj, wqkv.T)
    gain_grad_one = jnp.sum(grad_acts * base_one, 0)
    shift_grad_one = jnp.sum(grad_acts, 0)
    back = norm_back(grad_acts, base_one, factor_one, gain1)
    from_left = lax.ppermute(back[640:768].astype(bf16), "fsdp", TO_RIGHT).astype(f32)
    from_right = lax.ppermute(back[:128].astype(bf16), "fsdp", TO_LEFT).astype(f32)
    grad_nat = grad_middle[:ROWS] + back[128:640]
    grad_nat = grad_nat.at[:128].add(from_left).at[384:].add(from_right)
    grad_long = reorder(grad_nat.astype(bf16), order).astype(f32)
    glob_parts = exchange(back[768:].reshape(4 * 32, D), "fsdp", QUADS).reshape(4, 32, D)
    grad_glob = lax.dynamic_slice_in_dim(grad_middle, ROWS + quarter * 32, 32, 0) + jnp.sum(
        glob_parts, 0
    )
    out_long = reorder(result[:ROWS].astype(bf16), order)
    out_glob = lax.dynamic_slice_in_dim(result, ROWS + quarter * 32, 32, 0).astype(bf16)

    one = jnp.concatenate([grad_wqkv, grad_wattn], 1).reshape(D, 2, 2, D).transpose(1, 2, 0, 3)
    one = reduce_columns(one, core)
    two = reduce_columns(grad_win.reshape(D, 2, 2, D).transpose(1, 2, 0, 3), core)
    qkv_grad = one[:3].transpose(1, 0, 2).reshape(6, 3 * D)
    attn_grad = one[3]
    in_grad = two.transpose(1, 0, 2).reshape(6, 4 * D)
    keep = lax.dynamic_slice_in_dim(grad_wout, core * 384, 384, 1)
    send = lax.dynamic_slice_in_dim(grad_wout, (1 - core) * 384, 384, 1)
    total = (keep + swap(send.astype(bf16)).astype(f32)).astype(bf16)
    total = total.reshape(32, 2, 48, 384).transpose(1, 0, 2, 3).reshape(64, 48, 384)
    mine = jnp.sum(exchange(total, BOTH, SAME_CORE).astype(f32), 0)
    other = swap(mine)
    halves = jnp.where(
        core == 0, jnp.concatenate([mine, other], 1), jnp.concatenate([other, mine], 1)
    )
    out_grad = lax.dynamic_slice_in_dim(halves, core * 24, 24, 0)
    label_grad = jnp.dot(picker.T, grad_table.T, precision=HIGHEST)
    rel_grad = jnp.concatenate([label_grad, grad_own[None], grad_other[None]], 0)
    norm_grads = jnp.stack([gain_grad_one, gain_grad_two, shift_grad_one, shift_grad_two], 1)
    rel_total, norm_total, loss_total = lax.psum((rel_grad, norm_grads, loss_sum), BOTH)
    mine_norm = lax.dynamic_slice_in_dim(
        norm_total, (lax.axis_index("dp") * 16 + member) * 6, 6, 0
    )
    return (
        out_long,
        out_glob,
        loss_total / count,
        grad_long,
        grad_glob,
        qkv_grad,
        attn_grad,
        in_grad,
        out_grad,
        mine_norm[:, :2],
        mine_norm[:, 2:],
        rel_total,
    )


def solution(mesh):
    rows = P(BOTH, None)
    in_specs = (rows,) * 11 + (P(), P("dp"), P("dp", None), P("dp"), P(), P(BOTH))
    out_specs = (rows, rows, P(), rows, rows, rows, rows, rows, rows, rows, rows, P())
    return jax.shard_map(shards, mesh=mesh, in_specs=in_specs, out_specs=out_specs, check_vma=False)
```

time: 2630 us -> 959 us (0.36)
  blocking collectives: 965 us -> 150 us
  waiting for transfers between devices: 520 us -> 79.9 us
  matrix products: 330 us -> 138 us
  local copies, waits for them, and re-layouts: 435 us -> 294 us
  starting transfers between devices: 258 us -> 132 us
  other arithmetic: 88.2 us -> 140 us
    unnamed x1 -> x0, blocking collectives: 374 us -> none
    all_gather x6 -> x0, waiting for transfers between devices: 349 us -> none  [the longest x1 135 us: shards(): piece = lax.all_gather(keyval, 'fsdp', axis=0, tiled=True)]
    all_gather x5 -> x3, blocking collectives: 409 us -> 77.6 us  [the longest x1 29.7 us: shards(): lax.all_gather(jnp.concatenate([glob_in, cot_glob], 1), 'fsdp', axis_inde...]
    unnamed x97 -> x0, starting transfers between devices: 257 us -> none
    gather x2 -> x5, local copies, waits for them, and re-layouts: 137 us -> 13 us  [the longest x4 9.65 us: reorder(): return unpieces(exchange(spread[index], 'fsdp'))]
    reduce_scatter x5 -> x0, waiting for transfers between devices: 124 us -> none  [the longest x1 62.2 us: shards(): lax.psum_scatter(glob_sums[1].astype(jnp.bfloat16), 'fsdp', scatter_dimen...]
    all_to_all x0 -> x18, starting transfers between devices: none -> 119 us  [exchange(): lax.all_to_all(value, axis, 0, 0, axis_index_groups=groups, tiled=True)]
    pad x1 -> x0, matrix products: 113 us -> none  [spread(): jnp.pad(upper, ((0, 0), (BLOCK - RADIUS, 0), (0, 0)))]
  transfers between devices with their start and end apart: 108 -> 30, of which waited for: 7 -> 10; matrix products, arithmetic and copies ran while one was open for 36% -> 45% of each run, Pallas kernels for 0% -> 0%
where the time goes in v1:
time: 959 us; the launch traced here: 943 us
  local copies, waits for them, and re-layouts  294 us (31%)
  blocking collectives  150 us (16%)
  other arithmetic  140 us (15%)
  matrix products  138 us (14%)
  starting transfers between devices  132 us (14%)
  waiting for transfers between devices  79.9 us (8%)
    all_to_all x18, starting transfers between devices, exchange(): lax.all_to_all(value, axis, 0, 0, axis_index_groups=groups, tiled=True)  119 us
    unnamed x512, local copies, waits for them, and re-layouts  100 us
    dot_general x12, matrix products, dot(): return jnp.dot(a, b, preferred_element_type=f32)  97.4 us
    all_to_all x18, waiting for transfers between devices, exchange(): lax.all_to_all(value, axis, 0, 0, axis_index_groups=groups, tiled=True)  79.8 us
    psum x1, blocking collectives, shards(): lax.psum((rel_grad, norm_grads, loss_sum), BOTH)  72.6 us
    slice x127, local copies, waits for them, and re-layouts, shards(): band = jnp.stack([jnp.roll(line, r, 1)[:, :384] for r in range(BLOCK)], 1)  61.7 us
    sub x1, other arithmetic, shards(): ds = (probs * (dp - delta)).astype(bf16)  41.8 us
    all_gather x1, blocking collectives, shards(): lax.all_gather(jnp.concatenate([glob_in, cot_glob], 1), 'fsdp', axis_inde...  29.7 us
  transfers between devices with their start and end apart: 30, of which 10 were waited for; matrix products, arithmetic and copies ran while one was open for 45% of the time, Pallas kernels for 0%

profile of v1, /device:TPU:1, one launch (start us, length us, event | category | flops | bytes accessed | tf_op | source)
XLA Modules:
  0.0 942.5 jit_solution(18045819323352895346)
XLA Ops:
  2.8 7.3 all-to-all-start
  136.0 5.7 all-to-all-start.1
  145.8 9.0 all-to-all-done.1
  154.8 4.3 all-to-all-start.8
  159.0 25.0 %all-gather.1 = bf16[4,6,3072]{2,1,0:T(8,128)(2,1)S(1)} all-gather(bf16[1,6,3072]{2,1,0:T(8,128)(2,1)} %bitcast.916), channel_id=1, replica_groups={{0,1,2,3},{4,5,6,7},{8,9,10,11},{12,13,14,15},{16,17,18,19},{20,21,22,2..., dimensions={0}, use_global_device_ids=true | all-gather | bytes 184320 | tf_op jit(solution)/shard_map/all_gather | solution.py:150
  193.9 10.0 %all-to-all-start.4 = ((bf16[64,24,768]{2,1,0:T(8,128)(2,1)}), bf16[64,24,768]{2,1,0:T(8,128)(2,1)}, u32[]{:S(2)}, u32[]{:S(2)}) async-start(bf16[64,24,768]{2,1,0:T(8,128)(2,1)} %broadcast_in_dim.287), calls=%async_computation.4 | async-start | bytes 4718592 | tf_op jit(solution)/shard_map/all_to_all | solution.py:34
  210.5 23.0 %all-gather = bf16[4,6,3200]{2,1,0:T(8,128)(2,1)S(1)} all-gather(bf16[1,6,3200]{2,1,0:T(8,128)(2,1)S(1)} %bitcast.911), channel_id=1, replica_groups={{0,1,2,3},{4,5,6,7},{8,9,10,11},{12,13,14,15},{16,17,18,19},{20,21,22,2..., dimensions={0}, use_global_device_ids=true | all-gather | bytes 192000 | tf_op jit(solution)/shard_map/all_gather | solution.py:147
  238.4 9.6 %all-to-all-start.5 = ((bf16[64,48,384]{2,1,0:T(8,128)(2,1)}), bf16[64,48,384]{2,1,0:T(8,128)(2,1)S(1)}, u32[]{:S(2)}, u32[]{:S(2)}) async-start(bf16[64,48,384]{2,1,0:T(8,128)(2,1)} %broadcast_in_dim.288), calls=%async_computation.5 | async-start | bytes 4718592 | tf_op jit(solution)/shard_map/all_to_all | solution.py:34
  256.1 21.8 %all-to-all-done.5 = bf16[64,48,384]{2,1,0:T(8,128)(2,1)S(1)} async-done(((bf16[64,48,384]{2,1,0:T(8,128)(2,1)}), bf16[64,48,384]{2,1,0:T(8,128)(2,1)S(1)}, u32[]{:S(2)}, u32[]{:S(2)}) %all-to-all-start.5) | async-done | bytes 2359328 | tf_op jit(solution)/shard_map/all_to_all | solution.py:34
  280.4 8.0 all-to-all-start.2
  293.6 29.7 %all_gather.9 = bf16[128,1536]{1,0:T(8,128)(2,1)S(1)} all-gather(bf16[32,1536]{1,0:T(8,128)(2,1)S(1)} %pad_maximum_fusion.29), channel_id=1, replica_groups={{0,1,2,3},{4,5,6,7},{8,9,10,11},{12,13,14,15},{16,17,18,19},{20,21,22,2..., dimensions={0}, use_global_device_ids=true | all-gather | bytes 491520 | tf_op jit(solution)/shard_map/all_gather | solution.py:207
  341.0 5.2 all-to-all-start.9
  346.7 4.1 copy.240
  380.4 5.1 convolution_convert_fusion
  405.8 12.7 %all-to-all-start.3 = ((bf16[4,128,896]{1,2,0:T(8,128)(2,1)}), bf16[4,128,896]{1,2,0:T(8,128)(2,1)S(1)}, u32[]{:S(2)}, u32[]{:S(2)}) async-start(bf16[4,128,896]{1,2,0:T(8,128)(2,1)} %broadcast_in_dim.285), calls=%async_computation.3 | async-start | bytes 1835008 | tf_op jit(solution)/shard_map/all_to_all | solution.py:34
  434.8 5.9 fusion.3
  443.2 4.3 fusion.15
  456.9 25.3 %multiply_convert_fusion.1 = (bf16[640,3072]{1,0:T(8,128)(2,1)}, f32[640,3072]{1,0:T(8,128)}, f32[640,3072]{1,0:T(8,128)}) fusion(bf16[768,768]{1,0:T(8,128)(2,1)S(1)} %copy-done.85, bf16[768,768]{1,0:T(8,128)(2,1)S(1)} %copy-done.86, bf16[768,768]{1,0:T(8,128)(2,1)S(1)} %copy-done.84, bf16[768,768]{1,0:T(8,128)(2,1)S(1)} %copy-done.87, ...), kind=kOutput, calls=%fused_computation.22 | convolution fusion | flops 3169026048 | bytes 26356736 | tf_op jit(solution)/shard_map/dot_general | solution.py:86
  482.3 8.3 convolution_add_fusion
  493.5 13.3 %add_convert_fusion = bf16[640,3072]{1,0:T(8,128)(2,1)} fusion(f32[640,3072]{1,0:T(8,128)} %get-tuple-element.185, f32[640,3072]{1,0:T(8,128)} %get-tuple-element.246, bf16[3072,384]{1,0:T(8,128)(2,1)} %collective-permute-done.5, bf16[3072,384]{1,0:T(8,128)(2,1)} %bitcast.185, pred[]{:T(512)S(6)} %eq.122, f32[128,768]{1,0:T(8,128)S(1)} %copy-done.83, ...), kind=kOutput, calls=%fused_computation.21 | convolution fusion | flops 3070623744 | bytes 26345472 | tf_op jit(solution)/shard_map/dot_general | solution.py:86
  506.7 8.6 multiply_reduce_fusion.6
  522.1 5.0 fusion.118
  527.3 4.5 fusion.47
  536.6 41.8 %multiply_convert_fusion = bf16[4,12,128,512]{3,2,1,0:T(8,128)(2,1)S(1)} fusion(f32[4,12,128,128]{3,2,1,0:T(8,128)} %convolution_bitcast_fusion, f32[4,12,128,384]{3,2,1,0:T(8,128)} %fusion.118, f32[4,12,128]{2,1,0:T(8,128)S(1)} %log_add_fusion, f32[4,12,128,128]{3,2,1,0:T(8,128)} %copy-done.20, f32[4,12,128,384]{3,2,1,0:T(8,128)} %copy-done), kind=kOutput, calls=%fused_computation.8 | output fusion | flops 31463936 | bytes 31481856 | tf_op jit(solution)/shard_map/sub | solution.py:356
  596.3 5.9 multiply_reduce_fusion.1
  605.8 3.9 collective-permute-start.6
  612.5 4.7 all-to-all-start.12
  621.2 8.1 fusion.317
  629.3 8.7 pad_maximum_fusion.2
  638.0 13.1 %reshape.989 = f32[768,2,2,768]{3,2,1,0:T(2,128)} reshape(f32[768,3072]{1,0:T(8,128)} %pad_maximum_fusion.2) | data formatting | bytes 18874368 | tf_op jit(solution)/shard_map/reshape | solution.py:424
  659.8 8.3 all-to-all-done.6
  668.1 4.2 all-to-all-start.10
  672.2 6.4 constant_dynamic-slice_fusion.3
  686.3 4.4 all-to-all-start.7
  690.7 8.7 fusion.21
  699.4 13.1 %reshape.993 = f32[768,2,2,768]{3,2,1,0:T(2,128)} reshape(f32[768,3072]{1,0:T(8,128)} %fusion.21) | data formatting | bytes 18874368 | tf_op jit(solution)/shard_map/reshape | solution.py:426
  712.5 6.4 constant_dynamic-slice_fusion.1
  722.6 5.8 all-to-all-start.11
  728.4 6.3 constant_dynamic-slice_fusion.4
  742.3 8.6 all-to-all-start.13
  750.9 6.9 fusion.107
  763.0 4.5 constant_dynamic-slice_fusion.2
  771.0 9.6 %all-to-all-done.13 = bf16[64,24,768]{2,1,0:T(8,128)(2,1)S(1)} async-done(((bf16[64,24,768]{2,1,0:T(8,128)(2,1)}), bf16[64,24,768]{2,1,0:T(8,128)(2,1)S(1)}, u32[]{:S(2)}, u32[]{:S(2)}) %all-to-all-start.13) | async-done | bytes 2359328 | tf_op jit(solution)/shard_map/all_to_all | solution.py:34
  782.1 8.4 all-to-all-start.15
  799.0 20.1 %all-to-all-done.15 = bf16[64,24,768]{2,1,0:T(8,128)(2,1)} async-done(((bf16[64,24,768]{2,1,0:T(8,128)(2,1)}), bf16[64,24,768]{2,1,0:T(8,128)(2,1)}, u32[]{:S(2)}, u32[]{:S(2)}) %all-to-all-start.15) | async-done | bytes 2359328 | tf_op jit(solution)/shard_map/all_to_all | solution.py:34
  819.1 7.9 all-to-all-start.17
  839.4 72.6 %all-reduce.133 = (f32[]{:T(128)}, f32[768,4]{0,1:T(4,128)S(1)}, f32[171,12]{0,1:T(8,128)}) all-reduce(f32[]{:T(128)} %get-tuple-element.215, f32[768,4]{0,1:T(4,128)S(1)} %pad_maximum_fusion.32, f32[171,12]{0,1:T(8,128)S(1)} %pad_maximum_fusion.31), channel_id=1, replica_groups=mesh['dp'=8,'fsdp'=16] {'dp','fsdp'}, use_global_device_ids=true, to_apply=%region_17.18 | all-reduce | flops 5125 | bytes 41000 | tf_op jit(solution)/shard_map/psum | solution.py:443
  931.5 4.2 all-to-all-start.16
  (889 shorter events, 385.4 us)
Async XLA Ops:
  2.8 130.3 %all-to-all-start = ((bf16[64,8,768]{2,1,0:T(8,128)(2,1)}), bf16[64,8,768]{2,1,0:T(8,128)(2,1)}, u32[]{:S(2)}, u32[]{:S(2)}) async-start(bf16[64,8,768]{2,1,0:T(8,128)(2,1)} %bitcast.2), calls=%async_computation | async-start | bytes 1572864 | tf_op jit(solution)/shard_map/all_to_all | solution.py:34
  10.8 225.1 %collective-permute-start.4 = (bf16[24,384]{1,0:T(8,128)(2,1)}, bf16[24,384]{1,0:T(8,128)(2,1)}, u32[]{:S(2)}, u32[]{:S(2)}) collective-permute-start(bf16[24,384]{1,0:T(8,128)(2,1)} %get-tuple-element.229), channel_id=1, source_target_pairs={{0,1},{1,0},{2,3},{3,2},{4,5},{5,4},{6,7},{7,6},{8,9},{9,8},{10,11... | collective-permute-start | bytes 55304 | tf_op jit(solution)/shard_map/ppermute | solution.py:38
  82.6 46.2 %copy-start.117 = (f32[12,440]{1,0:T(8,128)S(1)}, f32[12,440]{1,0:T(8,128)}, u32[]{:S(2)}) copy-start(f32[12,440]{1,0:T(8,128)} %pad_slice_fusion.55) | copy-start | bytes 63364
  82.6 46.3 %copy-start.116 = (f32[12,439]{1,0:T(8,128)S(1)}, f32[12,439]{1,0:T(8,128)}, u32[]{:S(2)}) copy-start(f32[12,439]{1,0:T(8,128)} %pad_slice_fusion.54) | copy-start | bytes 63220
  82.6 46.4 %copy-start.115 = (f32[12,438]{1,0:T(8,128)S(1)}, f32[12,438]{1,0:T(8,128)}, u32[]{:S(2)}) copy-start(f32[12,438]{1,0:T(8,128)} %pad_slice_fusion.53) | copy-start | bytes 63076
  82.6 46.4 %copy-start.114 = (f32[12,437]{1,0:T(8,128)S(1)}, f32[12,437]{1,0:T(8,128)}, u32[]{:S(2)}) copy-start(f32[12,437]{1,0:T(8,128)} %pad_slice_fusion.52) | copy-start | bytes 62932
  82.7 46.5 %copy-start.113 = (f32[12,436]{1,0:T(8,128)S(1)}, f32[12,436]{1,0:T(8,128)}, u32[]{:S(2)}) copy-start(f32[12,436]{1,0:T(8,128)} %pad_slice_fusion.51) | copy-start | bytes 62788
  82.7 46.6 %copy-start.112 = (f32[12,435]{1,0:T(8,128)S(1)}, f32[12,435]{1,0:T(8,128)}, u32[]{:S(2)}) copy-start(f32[12,435]{1,0:T(8,128)} %pad_slice_fusion.50) | copy-start | bytes 62644
  82.7 46.6 %copy-start.111 = (f32[12,434]{1,0:T(8,128)S(1)}, f32[12,434]{1,0:T(8,128)}, u32[]{:S(2)}) copy-start(f32[12,434]{1,0:T(8,128)} %pad_slice_fusion.49) | copy-start | bytes 62500
  82.7 46.7 %copy-start.110 = (f32[12,433]{1,0:T(8,128)S(1)}, f32[12,433]{1,0:T(8,128)}, u32[]{:S(2)}) copy-start(f32[12,433]{1,0:T(8,128)} %pad_slice_fusion.48) | copy-start | bytes 62356
  82.7 46.8 %copy-start.109 = (f32[12,432]{1,0:T(8,128)S(1)}, f32[12,432]{1,0:T(8,128)}, u32[]{:S(2)}) copy-start(f32[12,432]{1,0:T(8,128)} %pad_slice_fusion.47) | copy-start | bytes 62212
  82.7 46.8 %copy-start.108 = (f32[12,431]{1,0:T(8,128)S(1)}, f32[12,431]{1,0:T(8,128)}, u32[]{:S(2)}) copy-start(f32[12,431]{1,0:T(8,128)} %pad_slice_fusion.46) | copy-start | bytes 62068
  82.7 46.9 %copy-start.107 = (f32[12,430]{1,0:T(8,128)S(1)}, f32[12,430]{1,0:T(8,128)}, u32[]{:S(2)}) copy-start(f32[12,430]{1,0:T(8,128)} %pad_slice_fusion.45) | copy-start | bytes 61924
  82.7 47.0 %copy-start.106 = (f32[12,429]{1,0:T(8,128)S(1)}, f32[12,429]{1,0:T(8,128)}, u32[]{:S(2)}) copy-start(f32[12,429]{1,0:T(8,128)} %pad_slice_fusion.44) | copy-start | bytes 61780
  136.0 18.7 %all-to-all-start.1 = ((bf16[64,8,768]{2,1,0:T(8,128)(2,1)}), bf16[64,8,768]{2,1,0:T(8,128)(2,1)S(1)}, u32[]{:S(2)}, u32[]{:S(2)}) async-start(bf16[64,8,768]{2,1,0:T(8,128)(2,1)} %gather_fusion), calls=%async_computation.1 | async-start | bytes 1572864 | tf_op jit(solution)/shard_map/all_to_all | solution.py:34
  154.8 174.5 %copy-start.38 = (bf16[64,8,768]{2,1,0:T(8,128)(2,1)}, bf16[64,8,768]{2,1,0:T(8,128)(2,1)S(1)}, u32[]{:S(2)}) copy-start(bf16[64,8,768]{2,1,0:T(8,128)(2,1)S(1)} %all-to-all-done.1) | copy-start | bytes 2359300
  154.8 37.2 %all-to-all-start.8 = ((bf16[64,8,1664]{2,1,0:T(8,128)(2,1)}), bf16[64,8,1664]{2,1,0:T(8,128)(2,1)S(1)}, u32[]{:S(2)}, u32[]{:S(2)}) async-start(bf16[64,8,1664]{2,1,0:T(8,128)(2,1)} %bitcast.196), calls=%async_computation.8 | async-start | bytes 3407872 | tf_op jit(solution)/shard_map/all_to_all | solution.py:34
  193.9 42.8 %all-to-all-start.4 = ((bf16[64,24,768]{2,1,0:T(8,128)(2,1)}), bf16[64,24,768]{2,1,0:T(8,128)(2,1)}, u32[]{:S(2)}, u32[]{:S(2)}) async-start(bf16[64,24,768]{2,1,0:T(8,128)(2,1)} %broadcast_in_dim.287), calls=%async_computation.4 | async-start | bytes 4718592 | tf_op jit(solution)/shard_map/all_to_all | solution.py:34
  238.4 39.5 %all-to-all-start.5 = ((bf16[64,48,384]{2,1,0:T(8,128)(2,1)}), bf16[64,48,384]{2,1,0:T(8,128)(2,1)S(1)}, u32[]{:S(2)}, u32[]{:S(2)}) async-start(bf16[64,48,384]{2,1,0:T(8,128)(2,1)} %broadcast_in_dim.288), calls=%async_computation.5 | async-start | bytes 4718592 | tf_op jit(solution)/shard_map/all_to_all | solution.py:34
  280.4 60.6 %all-to-all-start.2 = ((bf16[64,24,896]{2,1,0:T(8,128)(2,1)}), bf16[64,24,896]{2,1,0:T(8,128)(2,1)S(1)}, u32[]{:S(2)}, u32[]{:S(2)}) async-start(bf16[64,24,896]{2,1,0:T(8,128)(2,1)} %broadcast_in_dim.190), calls=%async_computation.2 | async-start | bytes 5505024 | tf_op jit(solution)/shard_map/all_to_all | solution.py:34
  327.7 44.0 %collective-permute-start.3 = (bf16[2,768,768]{2,1,0:T(8,128)(2,1)}, bf16[2,768,768]{2,1,0:T(8,128)(2,1)}, u32[]{:S(2)}, u32[]{:S(2)}) collective-permute-start(bf16[2,768,768]{2,1,0:T(8,128)(2,1)} %bitcast.178), channel_id=1, source_target_pairs={{0,1},{1,0},{2,3},{3,2},{4,5},{5,4},{6,7},{7,6},{8,9},{9,8},{10,11... | collective-permute-start | bytes 7077896 | tf_op jit(solution)/shard_map/ppermute | solution.py:38
  330.0 24.0 %collective-permute-start.1 = (bf16[128,768]{1,0:T(8,128)(2,1)}, bf16[128,768]{1,0:T(8,128)(2,1)}, u32[]{:S(2)}, u32[]{:S(2)}) collective-permute-start(bf16[128,768]{1,0:T(8,128)(2,1)} %get-tuple-element.225), channel_id=1, source_target_pairs={{1,0},{2,1},{3,2},{5,4},{6,5},{7,6},{9,8},{10,9},{11,10},{13,12},{... | collective-permute-start | bytes 589832 | tf_op jit(solution)/shard_map/ppermute | solution.py:211
  332.3 21.7 %collective-permute-start = (bf16[128,768]{1,0:T(8,128)(2,1)}, bf16[128,768]{1,0:T(8,128)(2,1)}, u32[]{:S(2)}, u32[]{:S(2)}) collective-permute-start(bf16[128,768]{1,0:T(8,128)(2,1)} %get-tuple-element.224), channel_id=1, source_target_pairs={{0,1},{1,2},{2,3},{4,5},{5,6},{6,7},{8,9},{9,10},{10,11},{12,13},{... | collective-permute-start | bytes 589832 | tf_op jit(solution)/shard_map/ppermute | solution.py:210
  341.0 28.2 %all-to-all-start.9 = ((bf16[64,8,1664]{2,1,0:T(8,128)(2,1)}), bf16[64,8,1664]{2,1,0:T(8,128)(2,1)}, u32[]{:S(2)}, u32[]{:S(2)}) async-start(bf16[64,8,1664]{2,1,0:T(8,128)(2,1)} %gather_fusion.3), calls=%async_computation.9 | async-start | bytes 3407872 | tf_op jit(solution)/shard_map/all_to_all | solution.py:34
  353.8 23.1 %collective-permute-start.2 = (bf16[2,768,768]{2,1,0:T(8,128)(2,1)}, bf16[2,768,768]{2,1,0:T(8,128)(2,1)}, u32[]{:S(2)}, u32[]{:S(2)}) collective-permute-start(bf16[2,768,768]{2,1,0:T(8,128)(2,1)} %slice.2078), channel_id=1, source_target_pairs={{0,1},{1,0},{2,3},{3,2},{4,5},{5,4},{6,7},{7,6},{8,9},{9,8},{10,11... | collective-permute-start | bytes 7077896 | tf_op jit(solution)/shard_map/ppermute | solution.py:38
  363.6 118.6 %collective-permute-start.5 = (bf16[3072,384]{1,0:T(8,128)(2,1)}, bf16[3072,384]{1,0:T(8,128)(2,1)}, u32[]{:S(2)}, u32[]{:S(2)}) collective-permute-start(bf16[3072,384]{1,0:T(8,128)(2,1)} %bitcast.185), channel_id=1, source_target_pairs={{0,1},{1,0},{2,3},{3,2},{4,5},{5,4},{6,7},{7,6},{8,9},{9,8},{10,11... | collective-permute-start | bytes 7077896 | tf_op jit(solution)/shard_map/ppermute | solution.py:38
  405.8 45.4 %all-to-all-start.3 = ((bf16[4,128,896]{1,2,0:T(8,128)(2,1)}), bf16[4,128,896]{1,2,0:T(8,128)(2,1)S(1)}, u32[]{:S(2)}, u32[]{:S(2)}) async-start(bf16[4,128,896]{1,2,0:T(8,128)(2,1)} %broadcast_in_dim.285), calls=%async_computation.3 | async-start | bytes 1835008 | tf_op jit(solution)/shard_map/all_to_all | solution.py:34
  454.2 61.1 %copy-start.9 = (f32[640,768]{1,0:T(8,128)}, f32[640,768]{1,0:T(8,128)S(1)}, u32[]{:S(2)}) copy-start(f32[640,768]{1,0:T(8,128)S(1)} %get-tuple-element.187) | copy-start | bytes 5898244
  535.0 48.2 %slice-start.3 = ((s8[6291456]{0:T(1024)(128)(4,1)}), s8[4194304]{0:T(1024)(128)(4,1)S(1)}, s32[]{:S(2)}) async-start(s8[6291456]{0:T(1024)(128)(4,1)} %bitcast.835), calls=%async_computation.21 | async-start | bytes 8388608
  536.6 46.6 %slice-start.4 = ((s8[6291456]{0:T(1024)(128)(4,1)}), s8[2097152]{0:T(1024)(128)(4,1)S(1)}, s32[]{:S(2)}) async-start(s8[6291456]{0:T(1024)(128)(4,1)} %bitcast.835), calls=%async_computation.22 | async-start | bytes 4194304
  605.8 50.9 %collective-permute-start.6 = (bf16[128,768]{1,0:T(8,128)(2,1)}, bf16[128,768]{1,0:T(8,128)(2,1)}, u32[]{:S(2)}, u32[]{:S(2)}) collective-permute-start(bf16[128,768]{1,0:T(8,128)(2,1)} %get-tuple-element.223), channel_id=1, source_target_pairs={{0,1},{1,2},{2,3},{4,5},{5,6},{6,7},{8,9},{9,10},{10,11},{12,13},{... | collective-permute-start | bytes 589832 | tf_op jit(solution)/shard_map/ppermute | solution.py:412
  609.7 48.0 %collective-permute-start.7 = (bf16[128,768]{1,0:T(8,128)(2,1)}, bf16[128,768]{1,0:T(8,128)(2,1)}, u32[]{:S(2)}, u32[]{:S(2)}) collective-permute-start(bf16[128,768]{1,0:T(8,128)(2,1)} %get-tuple-element.222), channel_id=1, source_target_pairs={{1,0},{2,1},{3,2},{5,4},{6,5},{7,6},{9,8},{10,9},{11,10},{13,12},{... | collective-permute-start | bytes 589832 | tf_op jit(solution)/shard_map/ppermute | solution.py:413
  612.5 38.7 %all-to-all-start.12 = ((f32[4,32,768]{2,1,0:T(8,128)}), f32[4,32,768]{2,1,0:T(8,128)}, u32[]{:S(2)}, u32[]{:S(2)}) async-start(f32[4,32,768]{2,1,0:T(8,128)} %bitcast.901), calls=%async_computation.12 | async-start | bytes 786432 | tf_op jit(solution)/shard_map/all_to_all | solution.py:34
  651.2 16.9 %all-to-all-start.6 = ((bf16[64,8,768]{2,1,0:T(8,128)(2,1)}), bf16[64,8,768]{2,1,0:T(8,128)(2,1)S(1)}, u32[]{:S(2)}, u32[]{:S(2)}) async-start(bf16[64,8,768]{2,1,0:T(8,128)(2,1)} %bitcast.188), calls=%async_computation.6 | async-start | bytes 1572864 | tf_op jit(solution)/shard_map/all_to_all | solution.py:34
  668.1 17.3 %all-to-all-start.10 = ((bf16[64,8,768]{2,1,0:T(8,128)(2,1)}), bf16[64,8,768]{2,1,0:T(8,128)(2,1)S(1)}, u32[]{:S(2)}, u32[]{:S(2)}) async-start(bf16[64,8,768]{2,1,0:T(8,128)(2,1)} %bitcast.235), calls=%async_computation.10 | async-start | bytes 1572864 | tf_op jit(solution)/shard_map/all_to_all | solution.py:34
  680.5 54.3 %collective-permute-start.8 = (bf16[2,768,768]{2,1,0:T(8,128)(2,1)}, bf16[2,768,768]{2,1,0:T(8,128)(2,1)}, u32[]{:S(2)}, u32[]{:S(2)}) collective-permute-start(bf16[2,768,768]{2,1,0:T(8,128)(2,1)} %bitcast.828), channel_id=1, source_target_pairs={{0,1},{1,0},{2,3},{3,2},{4,5},{5,4},{6,7},{7,6},{8,9},{9,8},{10,11... | collective-permute-start | bytes 7077896 | tf_op jit(solution)/shard_map/ppermute | solution.py:38
  686.3 36.3 %all-to-all-start.7 = ((bf16[64,8,768]{2,1,0:T(8,128)(2,1)}), bf16[64,8,768]{2,1,0:T(8,128)(2,1)S(1)}, u32[]{:S(2)}, u32[]{:S(2)}) async-start(bf16[64,8,768]{2,1,0:T(8,128)(2,1)} %gather_fusion.2), calls=%async_computation.7 | async-start | bytes 1572864 | tf_op jit(solution)/shard_map/all_to_all | solution.py:34
  720.8 46.6 %collective-permute-start.9 = (bf16[2,768,768]{2,1,0:T(8,128)(2,1)}, bf16[2,768,768]{2,1,0:T(8,128)(2,1)}, u32[]{:S(2)}, u32[]{:S(2)}) collective-permute-start(bf16[2,768,768]{2,1,0:T(8,128)(2,1)} %bitcast.829), channel_id=1, source_target_pairs={{0,1},{1,0},{2,3},{3,2},{4,5},{5,4},{6,7},{7,6},{8,9},{9,8},{10,11... | collective-permute-start | bytes 7077896 | tf_op jit(solution)/shard_map/ppermute | solution.py:38
  722.6 18.8 %all-to-all-start.11 = ((bf16[64,8,768]{2,1,0:T(8,128)(2,1)}), bf16[64,8,768]{2,1,0:T(8,128)(2,1)S(1)}, u32[]{:S(2)}, u32[]{:S(2)}) async-start(bf16[64,8,768]{2,1,0:T(8,128)(2,1)} %gather_fusion.4), calls=%async_computation.11 | async-start | bytes 1572864 | tf_op jit(solution)/shard_map/all_to_all | solution.py:34
  742.3 38.4 %all-to-all-start.13 = ((bf16[64,24,768]{2,1,0:T(8,128)(2,1)}), bf16[64,24,768]{2,1,0:T(8,128)(2,1)S(1)}, u32[]{:S(2)}, u32[]{:S(2)}) async-start(bf16[64,24,768]{2,1,0:T(8,128)(2,1)} %bitcast.851), calls=%async_computation.13 | async-start | bytes 4718592 | tf_op jit(solution)/shard_map/all_to_all | solution.py:34
  762.3 31.5 %collective-permute-start.10 = (bf16[3072,384]{1,0:T(8,128)(2,1)}, bf16[3072,384]{1,0:T(8,128)(2,1)}, u32[]{:S(2)}, u32[]{:S(2)}) collective-permute-start(bf16[3072,384]{1,0:T(8,128)(2,1)} %dynamic-slice_convert_fusion), channel_id=1, source_target_pairs={{0,1},{1,0},{2,3},{3,2},{4,5},{5,4},{6,7},{7,6},{8,9},{9,8},{10,11... | collective-permute-start | bytes 7077896 | tf_op jit(solution)/shard_map/ppermute | solution.py:38
  782.1 37.0 %all-to-all-start.15 = ((bf16[64,24,768]{2,1,0:T(8,128)(2,1)}), bf16[64,24,768]{2,1,0:T(8,128)(2,1)}, u32[]{:S(2)}, u32[]{:S(2)}) async-start(bf16[64,24,768]{2,1,0:T(8,128)(2,1)} %bitcast.850), calls=%async_computation.15 | async-start | bytes 4718592 | tf_op jit(solution)/shard_map/all_to_all | solution.py:34
  819.1 105.1 %all-to-all-start.17 = ((bf16[64,48,384]{2,1,0:T(8,128)(2,1)}), bf16[64,48,384]{2,1,0:T(8,128)(2,1)}, u32[]{:S(2)}, u32[]{:S(2)}) async-start(bf16[64,48,384]{2,1,0:T(8,128)(2,1)} %bitcast.257), calls=%async_computation.17 | async-start | bytes 4718592 | tf_op jit(solution)/shard_map/all_to_all | solution.py:34
  836.6 81.4 %copy-start.49 = (bf16[64,8,768]{2,1,0:T(8,128)(2,1)S(1)}, bf16[64,8,768]{2,1,0:T(8,128)(2,1)}, u32[]{:S(2)}) copy-start(bf16[64,8,768]{2,1,0:T(8,128)(2,1)} %copy-done.48) | copy-start | bytes 2359300
  836.6 82.4 %copy-start.54 = (bf16[64,8,768]{2,1,0:T(8,128)(2,1)S(1)}, bf16[64,8,768]{2,1,0:T(8,128)(2,1)}, u32[]{:S(2)}) copy-start(bf16[64,8,768]{2,1,0:T(8,128)(2,1)} %copy-done.53) | copy-start | bytes 2359300
  924.2 7.3 all-to-all-start.14
  930.8 8.9 collective-permute-start.11
  931.5 7.6 all-to-all-start.16
  (170 other events, 1983.0 us)

commit v2 on v1

v2 whole, which is shorter than its diff:
```python
import jax
import jax.numpy as jnp
from jax import lax
from jax.experimental import pallas as pl
from jax.experimental.pallas import tpu as pltpu
from jax.sharding import PartitionSpec as P

D = 768
HEADS = 12
HEAD = 64
RADIUS = 84
LABELS = 169
BLOCK = 128
SEQ_BLOCKS = 16
GLOBAL_EVERY = 16
GSEQ = 128
ROWS = 512
EXT = 896
EPS = 1e-05
MASKED = -1e30
HIGHEST = lax.Precision.HIGHEST
BOTH = ("dp", "fsdp")
f32 = jnp.float32
bf16 = jnp.bfloat16

QUADS = [[4 * i + j for j in range(4)] for i in range(4)]
SAME_CORE = [[4 * g + 2 * p + c for p in range(2) for g in range(32)] for c in range(2)]
SWAP = [(i, i ^ 1) for i in range(16)]
TO_RIGHT = [(i, i + 1) for i in range(16) if i % 4 < 3]
TO_LEFT = [(i, i - 1) for i in range(16) if i % 4 > 0]


def exchange(value, axis, groups=None):
    return lax.all_to_all(value, axis, 0, 0, axis_index_groups=groups, tiled=True)


def swap(value):
    return lax.ppermute(value, "fsdp", SWAP)


def pieces(rows):
    width = rows.shape[-1]
    return rows.reshape(4, 16, 8, width).transpose(1, 0, 2, 3).reshape(64, 8, width)


def unpieces(value):
    width = value.shape[-1]
    return value.reshape(16, 4, 8, width).transpose(1, 0, 2, 3).reshape(ROWS, width)


def reorder(rows, index):
    spread = exchange(pieces(rows), "fsdp")
    return unpieces(exchange(spread[index], "fsdp"))


def split3(value):
    high = value.astype(bf16)
    rest = value - high.astype(f32)
    mid = rest.astype(bf16)
    low = (rest - mid.astype(f32)).astype(bf16)
    return jnp.concatenate([high, mid, low], 0)


def join3(value):
    value = value.astype(f32)
    return value[:, :HEADS] + value[:, HEADS : 2 * HEADS] + value[:, 2 * HEADS : 3 * HEADS]


def reduce_columns(keep, send):
    total = keep.astype(f32) + swap(send).astype(f32)
    parts = exchange(total.astype(bf16).reshape(64, 24, D), BOTH, SAME_CORE)
    mine = jnp.sum(parts.astype(f32), 0)
    return exchange(mine.reshape(4, 6, D), "fsdp", QUADS)


def dot_nn(a, b):
    return lax.dot_general(a, b, (((1,), (0,)), ((), ())), preferred_element_type=f32)


def dot_nt(a, b):
    return lax.dot_general(a, b, (((1,), (1,)), ((), ())), preferred_element_type=f32)


def dot_tn(a, b):
    return lax.dot_general(a, b, (((0,), (0,)), ((), ())), preferred_element_type=f32)


def whole(shape):
    zeros = (0,) * len(shape)
    return pl.BlockSpec(shape, lambda *_: zeros, pipeline_mode=pl.Buffered(1))


SCALARS = pl.BlockSpec(memory_space=pltpu.SMEM)


def params(megabytes):
    return pltpu.CompilerParams(vmem_limit_bytes=megabytes << 20)


def normalise(values):
    centre = jnp.mean(values, -1, keepdims=True)
    centred = values - centre
    spread = jnp.mean(centred * centred, -1, keepdims=True)
    factor = lax.rsqrt(spread + EPS)
    return centred * factor, factor


def project_kernel(left, nat, right, globs, norms, even, odd, rows_out, acts_out, proj_out):
    rows_out[:128] = left[...]
    rows_out[128:640] = nat[...]
    rows_out[640:768] = right[...]
    rows_out[768:] = globs[:, :D]
    normal, _ = normalise(rows_out[...].astype(f32))
    acts = (normal * norms[0:1] + norms[2:3]).astype(bf16)
    acts_out[...] = acts
    proj_out[:, :D] = dot_nn(acts, even[0]).astype(bf16)
    proj_out[:, D : 2 * D] = dot_nn(acts, odd[0]).astype(bf16)
    proj_out[:, 2 * D :] = dot_nn(acts, even[1]).astype(bf16)


def project(left, nat, right, globs, norms, even, odd):
    return pl.pallas_call(
        project_kernel,
        out_shape=(
            jax.ShapeDtypeStruct((EXT, D), bf16),
            jax.ShapeDtypeStruct((EXT, D), bf16),
            jax.ShapeDtypeStruct((EXT, 3 * D), bf16),
        ),
        compiler_params=params(50),
        name="project",
    )(left, nat, right, globs, norms, even, odd)


def stack_heads(rows):
    first = lax.broadcasted_iota(jnp.int32, rows.shape, 1) < HEAD
    zero = jnp.zeros_like(rows)
    return jnp.concatenate([jnp.where(first, rows, zero), jnp.where(first, zero, rows)], 0)


def merge_heads(value):
    first = lax.broadcasted_iota(jnp.int32, (128, 128), 0) < HEAD
    return jnp.where(first, value[:, :128], value[:, 128:]).T


def band_tile(line):
    tiles = []
    for head in range(2):
        spread = jnp.broadcast_to(line[head : head + 1], (BLOCK, 512))
        rolled = pltpu.roll(spread, 0, 1, stride=1, stride_axis=0)
        tiles.append(
            jnp.concatenate([rolled[:, 128 * i : 128 * i + 128].T for i in range(3)], 0)
        )
    return jnp.concatenate(tiles, 1)


def pair_row(first, second):
    lane = lax.broadcasted_iota(jnp.int32, (1, 256), 1)
    return jnp.where(lane < 128, first, second)


def long_owned(run):
    key = lax.broadcasted_iota(jnp.int32, (128, 256), 0)
    lane = lax.broadcasted_iota(jnp.int32, (128, 256), 1)
    return key == run + lax.shift_right_logical(lane & 127, 4)


def cross_owned(run):
    key = lax.broadcasted_iota(jnp.int32, (ROWS, 256), 0)
    lane = lax.broadcasted_iota(jnp.int32, (ROWS, 256), 1)
    return run + lax.shift_right_logical(key, 4) == (lane & 127)


def attend_kernel(
    place, table, line, key_mask, self_mask, q, k, v, out, lse, glob_out, glob_lse, band
):
    pair = pl.program_id(0)
    run = place[0] * 32
    own = pair_row(table[0, 2 * pair], table[0, 2 * pair + 1])
    other = pair_row(table[1, 2 * pair], table[1, 2 * pair + 1])
    band[...] = band_tile(line[0])
    values = v[...].T
    for j in range(4):
        low = 128 * j
        query = stack_heads(q[128 + low : 256 + low, :] * 0.125)
        near = dot_nt(k[low : low + 384, :], query) + (band[...] + key_mask[low : low + 384, :])
        far = dot_nt(k[768:, :], query) + (
            jnp.where(long_owned(run + 8 * j), own, other) + key_mask[768:, :]
        )
        top = jnp.maximum(jnp.max(near, 0, keepdims=True), jnp.max(far, 0, keepdims=True))
        near = jnp.exp(near - top)
        far = jnp.exp(far - top)
        total = jnp.sum(near, 0, keepdims=True) + jnp.sum(far, 0, keepdims=True)
        share = 1.0 / total
        got = dot_nn(values[:, low : low + 384], (near * share).astype(bf16)) + dot_nn(
            values[:, 768:], (far * share).astype(bf16)
        )
        out[low : low + 128, :] = merge_heads(got).astype(bf16)
        lse[0, j : j + 1, :] = top + jnp.log(total)
    query = stack_heads(q[768:, :] * 0.125)
    near = dot_nt(k[128:640, :], query) + (
        jnp.where(cross_owned(run), own, other) + key_mask[128:640, :]
    )
    far = dot_nt(k[768:, :], query) + self_mask[...]
    top = jnp.maximum(jnp.max(near, 0, keepdims=True), jnp.max(far, 0, keepdims=True))
    near = jnp.exp(near - top)
    far = jnp.exp(far - top)
    total = jnp.sum(near, 0, keepdims=True) + jnp.sum(far, 0, keepdims=True)
    share = 1.0 / total
    got = dot_nn(values[:, 128:640], (near * share).astype(bf16)) + dot_nn(
        values[:, 768:], (far * share).astype(bf16)
    )
    first = lax.broadcasted_iota(jnp.int32, (128, 128), 0) < HEAD
    glob_out[...] = jnp.where(first, got[:, :128], got[:, 128:]).astype(bf16)
    glob_lse[0] = top + jnp.log(total)


def column(width, offset):
    return pl.BlockSpec((width, 128), lambda h: (0, h + offset))


def attend(place, table, line, key_mask, self_mask, proj):
    return pl.pallas_call(
        attend_kernel,
        grid=(6,),
        in_specs=[
            SCALARS,
            SCALARS,
            pl.BlockSpec((1, 2, 512), lambda h: (h, 0, 0)),
            whole((EXT, 256)),
            whole((128, 256)),
            column(EXT, 0),
            column(EXT, 6),
            column(EXT, 12),
        ],
        out_specs=[
            column(ROWS, 0),
            pl.BlockSpec((1, 4, 256), lambda h: (h, 0, 0)),
            pl.BlockSpec((128, 128), lambda h: (h, 0)),
            pl.BlockSpec((1, 1, 256), lambda h: (h, 0, 0)),
        ],
        out_shape=(
            jax.ShapeDtypeStruct((ROWS, D), bf16),
            jax.ShapeDtypeStruct((6, 4, 256), f32),
            jax.ShapeDtypeStruct((D, 128), bf16),
            jax.ShapeDtypeStruct((6, 1, 256), f32),
        ),
        scratch_shapes=[pltpu.VMEM((384, 256), f32)],
        compiler_params=params(40),
        name="attend",
    )(place, table, line, key_mask, self_mask, proj, proj, proj)


def fold_band(tile):
    rows = jnp.concatenate([tile[128 * i : 128 * i + 128].T for i in range(3)], 1)
    rows = jnp.concatenate([rows, jnp.zeros((BLOCK, 128), f32)], 1)
    total = rows[:8]
    for a in range(1, 16):
        total = total + pltpu.roll(rows[8 * a : 8 * a + 8], 512 - 8 * a, 1)
    row = lax.broadcasted_iota(jnp.int32, (8, 512), 0)
    for bit in (1, 2, 4):
        total = jnp.where((row & bit) != 0, pltpu.roll(total, 512 - bit, 1), total)
    return jnp.sum(total, 0, keepdims=True)


def attend_back_kernel(
    place,
    table,
    line,
    key_mask,
    self_mask,
    q,
    k,
    v,
    grad,
    lse,
    glob_out,
    glob_lse,
    dq,
    dk,
    dv,
    rel,
    band,
    band_sum,
    key_sum,
    value_sum,
):
    pair = pl.program_id(0)
    run = place[0] * 32
    own = pair_row(table[0, 2 * pair], table[0, 2 * pair + 1])
    other = pair_row(table[1, 2 * pair], table[1, 2 * pair + 1])
    band[...] = band_tile(line[0])
    keys = k[...].T
    band_sum[...] = jnp.zeros_like(band_sum)
    key_sum[...] = jnp.zeros_like(key_sum)
    value_sum[...] = jnp.zeros_like(value_sum)
    owned_sum = jnp.zeros((1, 256), f32)
    other_sum = jnp.zeros((1, 256), f32)
    dq[:128] = jnp.zeros((128, 128), bf16)
    dq[640:768] = jnp.zeros((128, 128), bf16)
    for j in range(4):
        low = 128 * j
        query = stack_heads(q[128 + low : 256 + low, :] * 0.125)
        back = stack_heads(grad[low : low + 128, :])
        near = dot_nt(k[low : low + 384, :], query) + (band[...] + key_mask[low : low + 384, :])
        owned = long_owned(run + 8 * j)
        far = dot_nt(k[768:, :], query) + (jnp.where(owned, own, other) + key_mask[768:, :])
        top = lse[0, j : j + 1, :]
        near = jnp.exp(near - top)
        far = jnp.exp(far - top)
        near_d = dot_nt(v[low : low + 384, :], back)
        far_d = dot_nt(v[768:, :], back)
        delta = jnp.sum(near * near_d, 0, keepdims=True) + jnp.sum(far * far_d, 0, keepdims=True)
        near_d = (near * (near_d - delta)).astype(bf16)
        far_d = (far * (far_d - delta)).astype(bf16)
        key_sum[low : low + 384, :] += dot_nn(near_d, query)
        value_sum[low : low + 384, :] += dot_nn(near.astype(bf16), back)
        key_sum[768:, :] += dot_nn(far_d, query)
        value_sum[768:, :] += dot_nn(far.astype(bf16), back)
        got = dot_nn(keys[:, low : low + 384], near_d) + dot_nn(keys[:, 768:], far_d)
        dq[128 + low : 256 + low, :] = (merge_heads(got) * 0.125).astype(bf16)
        band_sum[...] += near_d.astype(f32)
        far_d = far_d.astype(f32)
        owned_sum += jnp.sum(jnp.where(owned, far_d, 0.0), 0, keepdims=True)
        other_sum += jnp.sum(jnp.where(owned, 0.0, far_d), 0, keepdims=True)
    query = stack_heads(q[768:, :] * 0.125)
    back = stack_heads(grad[ROWS:, :])
    owned = cross_owned(run)
    near = dot_nt(k[128:640, :], query) + (jnp.where(owned, own, other) + key_mask[128:640, :])
    far = dot_nt(k[768:, :], query) + self_mask[...]
    top = glob_lse[0]
    near = jnp.exp(near - top)
    far = jnp.exp(far - top)
    near_d = dot_nt(v[128:640, :], back)
    far_d = dot_nt(v[768:, :], back)
    product = grad[ROWS:, :].astype(f32).T * glob_out[...].astype(f32)
    delta = jnp.concatenate(
        [
            jnp.sum(product[:HEAD], 0, keepdims=True),
            jnp.sum(product[HEAD:], 0, keepdims=True),
        ],
        1,
    )
    near_d = (near * (near_d - delta)).astype(bf16)
    far_d = (far * (far_d - delta)).astype(bf16)
    key_sum[128:640, :] += dot_nn(near_d, query)
    value_sum[128:640, :] += dot_nn(near.astype(bf16), back)
    key_sum[768:, :] += dot_nn(far_d, query)
    value_sum[768:, :] += dot_nn(far.astype(bf16), back)
    got = dot_nn(keys[:, 128:640], near_d) + dot_nn(keys[:, 768:], far_d)
    dq[768:, :] = (merge_heads(got) * 0.125).astype(bf16)
    near_d = near_d.astype(f32)
    owned_sum += jnp.sum(jnp.where(owned, near_d, 0.0), 0, keepdims=True)
    other_sum += jnp.sum(jnp.where(owned, 0.0, near_d), 0, keepdims=True)
    dk[...] = key_sum[...].astype(bf16)
    dv[...] = value_sum[...].astype(bf16)
    rel[0] = jnp.zeros((8, 512), f32)
    for head in range(2):
        lanes = slice(128 * head, 128 * head + 128)
        rel[0, head : head + 1, :] = fold_band(band_sum[:, lanes])
        rel[0, 2 + head : 3 + head, :128] = owned_sum[:, lanes]
        rel[0, 4 + head : 5 + head, :128] = other_sum[:, lanes]


def attend_back(place, table, line, key_mask, self_mask, proj, grad, lse, glob_out, glob_lse):
    return pl.pallas_call(
        attend_back_kernel,
        grid=(6,),
        in_specs=[
            SCALARS,
            SCALARS,
            pl.BlockSpec((1, 2, 512), lambda h: (h, 0, 0)),
            whole((EXT, 256)),
            whole((128, 256)),
            column(EXT, 0),
            column(EXT, 6),
            column(EXT, 12),
            column(640, 0),
            pl.BlockSpec((1, 4, 256), lambda h: (h, 0, 0)),
            pl.BlockSpec((128, 128), lambda h: (h, 0)),
            pl.BlockSpec((1, 1, 256), lambda h: (h, 0, 0)),
        ],
        out_specs=[
            column(EXT, 0),
            column(EXT, 0),
            column(EXT, 0),
            pl.BlockSpec((1, 8, 512), lambda h: (h, 0, 0)),
        ],
        out_shape=(
            jax.ShapeDtypeStruct((EXT, D), bf16),
            jax.ShapeDtypeStruct((EXT, D), bf16),
            jax.ShapeDtypeStruct((EXT, D), bf16),
            jax.ShapeDtypeStruct((6, 8, 512), f32),
        ),
        scratch_shapes=[
            pltpu.VMEM((384, 256), f32),
            pltpu.VMEM((384, 256), f32),
            pltpu.VMEM((EXT, 128), f32),
            pltpu.VMEM((EXT, 128), f32),
        ],
        compiler_params=params(48),
        name="attend_back",
    )(place, table, line, key_mask, self_mask, proj, proj, proj, grad, lse, glob_out, glob_lse)


def feed_kernel(
    place,
    coef,
    rows,
    long_out,
    parts,
    shares,
    packed,
    globs,
    norms,
    wa,
    win,
    wout,
    result_out,
    loss_out,
    glob_out,
    middle_grad_out,
    mixed_grad_out,
    wattn_grad,
    win_send,
    win_keep,
    wout_send,
    wout_keep,
    norm_grads,
    mixed,
    acts,
    normal,
    total,
    hidden,
    slope,
    grad_z,
    grad_acts,
    factor,
):
    step = pl.program_id(0)
    core = place[1]
    quarter = place[0]
    forward = step < 4
    late = jnp.maximum(step - 4, 0)
    chunk = jnp.where(
        forward, step, jnp.where(late < 2, 2 * late + 1 - core, 2 * (late - 2) + core)
    )

    def owned():
        row = lax.broadcasted_iota(jnp.int32, (640, 1), 0)
        first = ROWS + quarter * 32
        return (row < ROWS) | ((row >= first) & (row < first + 32))

    @pl.when(step == 0)
    def _():
        mixed[:ROWS] = long_out[...]
        for pair in range(6):
            sums = jnp.zeros((128, 128), f32)
            top = lax.broadcasted_iota(jnp.int32, (128, 128), 0) < HEAD
            for source in range(4):
                share = jnp.where(
                    top,
                    shares[source, 2 * pair : 2 * pair + 1, :],
                    shares[source, 2 * pair + 1 : 2 * pair + 2, :],
                )
                sums = sums + parts[source, 128 * pair : 128 * pair + 128, :].astype(f32) * share
            glob_out[128 * pair : 128 * pair + 128, :] = sums.astype(bf16)
            mixed[ROWS:, 128 * pair : 128 * pair + 128] = sums.T.astype(bf16)
        middle = dot_nn(mixed[...], wa[...])
        middle = middle + jnp.concatenate(
            [rows[128:640].astype(f32), rows[768:].astype(f32)], 0
        )
        total[...] = middle
        base, scale = normalise(middle)
        normal[...] = base
        factor[...] = scale
        acts[...] = (base * norms[1:2] + norms[3:4]).astype(bf16)

    @pl.when(forward)
    def _():
        inner = dot_nn(acts[...], win[0])
        half = 0.5 + 0.5 * lax.erf(inner * 0.7071067811865476)
        slope[chunk] = half + inner * (jnp.exp(-0.5 * inner * inner) * 0.3989422804014327)
        bits = (inner * half).astype(bf16)
        hidden[chunk] = bits
        total[...] += dot_nn(bits, wout[...])

    @pl.when(step == 3)
    def _():
        result = total[...]
        result_out[...] = result.astype(bf16)
        weight = packed[:, 2 * D : 2 * D + 1].astype(f32)
        error = result[:ROWS] - packed[:, D : 2 * D].astype(f32)
        masked = weight * error
        loss_out[...] = jnp.broadcast_to(
            jnp.sum(jnp.sum(masked * error, 0, keepdims=True), 1, keepdims=True), (8, 128)
        )
        grad = jnp.concatenate(
            [packed[:, :D].astype(f32) + coef[0] * masked, globs[:, D:].astype(f32)], 0
        )
        total[...] = grad
        grad_z[...] = grad.astype(bf16)
        grad_acts[...] = jnp.zeros_like(grad_acts)

    @pl.when(step >= 4)
    def _():
        keep_rows = owned()
        grad_inner = (dot_nt(grad_z[...], wout[...]) * slope[chunk]).astype(bf16)
        zeros = jnp.zeros_like(grad_inner)
        grad_acts[...] += dot_nt(grad_inner, win[0])
        part = dot_tn(acts[...], jnp.where(keep_rows, grad_inner, zeros)).astype(bf16)

        @pl.when(late < 2)
        def _():
            win_send[0] = part

        @pl.when(late >= 2)
        def _():
            win_keep[0] = part

        part = dot_tn(hidden[chunk], jnp.where(keep_rows, grad_z[...], zeros)).astype(bf16)
        first = core == 0
        wout_keep[...] = jnp.where(first, part[:, :384], part[:, 384:])
        wout_send[...] = jnp.where(first, part[:, 384:], part[:, :384])

    @pl.when(step == 7)
    def _():
        keep_rows = owned()
        grad = grad_acts[...]
        base = normal[...]
        mine = jnp.where(keep_rows, grad, 0.0)
        norm_grads[0:1, :] = jnp.sum(mine * base, 0, keepdims=True)
        norm_grads[1:2, :] = jnp.sum(mine, 0, keepdims=True)
        scaled = grad * norms[1:2]
        first = jnp.mean(scaled, -1, keepdims=True)
        second = jnp.mean(scaled * base, -1, keepdims=True)
        middle = total[...] + factor[...] * (scaled - first - base * second)
        middle_grad_out[...] = middle
        branch = middle.astype(bf16)
        mixed_grad_out[...] = dot_nt(branch, wa[...]).astype(bf16)
        wattn_grad[...] = dot_tn(
            mixed[...], jnp.where(keep_rows, branch, jnp.zeros_like(branch))
        ).astype(bf16)


def feed(place, coef, rows, long_out, parts, shares, packed, globs, norms, wa, win, wout):
    def chunk(t, place):
        late = jnp.maximum(t - 4, 0)
        core = place[1]
        back = jnp.where(late < 2, 2 * late + 1 - core, 2 * (late - 2) + core)
        return jnp.where(t < 4, t, back)

    def back_chunk(t, place):
        return chunk(jnp.maximum(t, 4), place)

    def fixed(shape):
        zeros = (0,) * len(shape)
        return pl.BlockSpec(shape, lambda t, place: zeros, pipeline_mode=pl.Buffered(1))

    return pl.pallas_call(
        feed_kernel,
        grid_spec=pltpu.PrefetchScalarGridSpec(
            num_scalar_prefetch=1,
            grid=(8,),
            in_specs=[
                SCALARS,
                fixed((EXT, D)),
                fixed((ROWS, D)),
                fixed((4, 816, 128)),
                fixed((4, 16, 128)),
                fixed((ROWS, 2 * D + 128)),
                fixed((128, 2 * D)),
                fixed((8, D)),
                fixed((D, D)),
                pl.BlockSpec((1, D, D), lambda t, place: (chunk(t, place), 0, 0)),
                pl.BlockSpec((D, D), lambda t, place: (chunk(t, place), 0)),
            ],
            out_specs=[
                fixed((640, D)),
                fixed((8, 128)),
                fixed((D, 128)),
                fixed((640, D)),
                fixed((640, D)),
                fixed((D, D)),
                pl.BlockSpec((1, D, D), lambda t, place: (jnp.clip(t - 4, 0, 1), 0, 0)),
                pl.BlockSpec((1, D, D), lambda t, place: (jnp.clip(t - 6, 0, 1), 0, 0)),
                pl.BlockSpec((D, 384), lambda t, place: (back_chunk(t, place), 0)),
                pl.BlockSpec((D, 384), lambda t, place: (back_chunk(t, place), 0)),
                fixed((8, D)),
            ],
            scratch_shapes=[
                pltpu.VMEM((640, D), bf16),
                pltpu.VMEM((640, D), bf16),
                pltpu.VMEM((640, D), f32),
                pltpu.VMEM((640, D), f32),
                pltpu.VMEM((4, 640, D), bf16),
                pltpu.VMEM((4, 640, D), f32),
                pltpu.VMEM((640, D), bf16),
                pltpu.VMEM((640, D), f32),
                pltpu.VMEM((640, 1), f32),
            ],
        ),
        out_shape=(
            jax.ShapeDtypeStruct((640, D), bf16),
            jax.ShapeDtypeStruct((8, 128), f32),
            jax.ShapeDtypeStruct((D, 128), bf16),
            jax.ShapeDtypeStruct((640, D), f32),
            jax.ShapeDtypeStruct((640, D), bf16),
            jax.ShapeDtypeStruct((D, D), bf16),
            jax.ShapeDtypeStruct((2, D, D), bf16),
            jax.ShapeDtypeStruct((2, D, D), bf16),
            jax.ShapeDtypeStruct((4 * D, 384), bf16),
            jax.ShapeDtypeStruct((4 * D, 384), bf16),
            jax.ShapeDtypeStruct((8, D), f32),
        ),
        compiler_params=params(60),
        name="feed",
    )(place, coef, rows, long_out, parts, shares, packed, globs, norms, wa, win, wout)


def project_back_kernel(
    place, rows, acts, dq, dk, dv, norms, even, odd, middle_grad, wattn_grad,
    send, keep, nat, left, right, globs, norm_grads,
):
    core = place[1]
    both = acts[...]
    grads = (dot_tn(both, dq[...]), dot_tn(both, dk[...]), dot_tn(both, dv[...]))
    parts = [part.astype(bf16) for part in grads] + [wattn_grad[...]]

    @pl.when(core == 0)
    def _():
        keep[0], keep[1], send[0], send[1] = parts[0], parts[2], parts[1], parts[3]

    @pl.when(core == 1)
    def _():
        keep[0], keep[1], send[0], send[1] = parts[1], parts[3], parts[0], parts[2]

    grad = dot_nt(dq[...], even[0]) + dot_nt(dk[...], odd[0]) + dot_nt(dv[...], even[1])
    base, factor = normalise(rows[...].astype(f32))
    norm_grads[0:1, :] = jnp.sum(grad * base, 0, keepdims=True)
    norm_grads[1:2, :] = jnp.sum(grad, 0, keepdims=True)
    scaled = grad * norms[0:1]
    first = jnp.mean(scaled, -1, keepdims=True)
    second = jnp.mean(scaled * base, -1, keepdims=True)
    back = factor * (scaled - first - base * second)
    nat[...] = back[128:640] + middle_grad[:ROWS]
    left[...] = back[:128].astype(bf16)
    right[...] = back[640:768].astype(bf16)
    globs[...] = back[768:]


def project_back(place, rows, acts, dq, dk, dv, norms, even, odd, middle_grad, wattn_grad):
    vm = pl.BlockSpec(memory_space=pltpu.VMEM)
    return pl.pallas_call(
        project_back_kernel,
        in_specs=[SCALARS] + [vm] * 10,
        out_shape=(
            jax.ShapeDtypeStruct((2, D, D), bf16),
            jax.ShapeDtypeStruct((2, D, D), bf16),
            jax.ShapeDtypeStruct((ROWS, D), f32),
            jax.ShapeDtypeStruct((128, D), bf16),
            jax.ShapeDtypeStruct((128, D), bf16),
            jax.ShapeDtypeStruct((128, D), f32),
            jax.ShapeDtypeStruct((8, D), f32),
        ),
        compiler_params=params(56),
        name="project_back",
    )(place, rows, acts, dq, dk, dv, norms, even, odd, middle_grad, wattn_grad)


def shards(
    long_in,
    glob_in,
    cot_long,
    cot_glob,
    teacher,
    w_qkv,
    w_attn,
    w_in,
    w_out,
    norm_gains,
    norm_biases,
    rel_bias,
    lengths,
    block_order,
    global_pos,
    rel_labels,
    loss_mask,
):
    member = lax.axis_index("fsdp")
    core = member % 2
    quarter = member % 4
    seq = member // 4
    order = block_order[0]
    slots = jnp.arange(64)
    inverse = jnp.sum(jnp.where(order[None, :] == slots[:, None], slots[None, :], 0), 1)
    length = jnp.sum(jnp.where(jnp.arange(4) == seq, lengths, 0))
    anchors = lax.dynamic_slice_in_dim(global_pos, seq * GSEQ, GSEQ)

    my_ids = lax.dynamic_slice_in_dim(order, member * 4, 4)
    my_lens = jnp.sum(
        jnp.where(my_ids[:, None] // SEQ_BLOCKS == jnp.arange(4)[None, :], lengths[None, :], 0), 1
    )
    slot_pos = (my_ids % SEQ_BLOCKS)[:, None] * BLOCK + jnp.arange(BLOCK)[None, :]
    slot_weight = ((slot_pos < my_lens[:, None]).reshape(ROWS) & (loss_mask == 1)).astype(jnp.int32)
    my_count = jnp.sum(slot_weight)

    high = (my_count // 16).astype(bf16)
    low = (my_count % 16).astype(bf16)
    extra = jnp.concatenate(
        [
            norm_gains,
            norm_biases,
            jnp.broadcast_to(jnp.stack([high, low]), (6, 2)),
            jnp.zeros((6, 122), bf16),
        ],
        1,
    )
    first = lax.all_gather(
        jnp.concatenate([w_qkv, w_attn, extra], 1), "fsdp", axis_index_groups=QUADS, axis=0, tiled=True
    )
    second = lax.all_gather(w_in, "fsdp", axis_index_groups=QUADS, axis=0, tiled=True)
    first_part = jnp.concatenate(
        [lax.dynamic_slice_in_dim(first, quarter * D, D, 1), first[:, 4 * D :]], 1
    )
    second_part = lax.dynamic_slice_in_dim(second, quarter * D, D, 1)
    mine_one = exchange(
        jnp.broadcast_to(first_part[None], (64, 24, EXT)), BOTH, SAME_CORE
    ).reshape(2, D, EXT)
    other_one = swap(mine_one[..., :D])
    side = mine_one[0, :, D:].astype(f32)
    even = jnp.where(core == 0, mine_one[..., :D], other_one)
    odd = jnp.where(core == 0, other_one, mine_one[..., :D])
    wa = odd[1]
    count = jnp.sum(
        jnp.where(jnp.arange(D) % 6 == 0, side[:, 4] * 16.0 + side[:, 5], 0.0)
    )
    mine_two = exchange(
        jnp.broadcast_to(second_part[None], (64, 24, D)), BOTH, SAME_CORE
    ).reshape(2, D, D)
    other_two = swap(mine_two)
    even2 = jnp.where(core == 0, mine_two, other_two)
    odd2 = jnp.where(core == 0, other_two, mine_two)
    win = jnp.stack([even2[0], odd2[0], even2[1], odd2[1]])
    half_keep = lax.dynamic_slice_in_dim(w_out, core * 384, 384, 1)
    half_send = lax.dynamic_slice_in_dim(w_out, (1 - core) * 384, 384, 1)
    half_got = swap(half_send)
    pair_rows = jnp.where(
        core == 0,
        jnp.concatenate([half_keep, half_got], 0),
        jnp.concatenate([half_got, half_keep], 0),
    )
    mine_three = exchange(jnp.broadcast_to(pair_rows[None], (64, 48, 384)), BOTH, SAME_CORE)
    mine_three = mine_three.reshape(2, 32, 48, 384).transpose(1, 0, 2, 3).reshape(4 * D, 384)
    other_three = swap(mine_three)
    wout = jnp.where(
        core == 0,
        jnp.concatenate([mine_three, other_three], 1),
        jnp.concatenate([other_three, mine_three], 1),
    )

    natural = reorder(long_in, inverse)
    packed = jnp.concatenate(
        [
            cot_long,
            teacher,
            jnp.broadcast_to(slot_weight[:, None], (ROWS, 128)).astype(bf16),
        ],
        1,
    )
    packed = reorder(packed, inverse)
    globs = lax.all_gather(
        jnp.concatenate([glob_in, cot_glob], 1), "fsdp", axis_index_groups=QUADS, axis=0, tiled=True
    )
    left = lax.ppermute(natural[ROWS - BLOCK :], "fsdp", TO_RIGHT)
    right = lax.ppermute(natural[:BLOCK], "fsdp", TO_LEFT)
    norms = jnp.concatenate([side[:, :4].T, jnp.zeros((4, D), f32)], 0)
    rows, acts, proj = project(left, natural, right, globs, norms, even, odd)

    start = quarter * ROWS
    place = jnp.stack([quarter, core]).astype(jnp.int32)
    key_pos = start - BLOCK + jnp.arange(768)
    key_ok = (key_pos >= 0) & (key_pos < length)
    glob_ok = anchors < length
    own_glob = jnp.arange(GSEQ) // 32 == quarter
    key_mask = jnp.broadcast_to(
        jnp.where(jnp.concatenate([key_ok, glob_ok]), 0.0, MASKED)[:, None], (EXT, 256)
    )
    self_mask = jnp.broadcast_to(jnp.where(glob_ok & own_glob, 0.0, MASKED)[:, None], (GSEQ, 256))
    picker = (rel_labels[:, None] == jnp.arange(LABELS)[None, :]).astype(f32)
    label_table = jnp.dot(picker, rel_bias[:LABELS], precision=HIGHEST)
    line = jnp.full((HEADS, 512), MASKED, f32)
    line = lax.dynamic_update_slice(line, label_table.T, (0, 44)).reshape(6, 2, 512)
    table = rel_bias[LABELS:]
    long_out, long_lse, part_out, part_lse = attend(place, table, line, key_mask, self_mask, proj)

    sent = jnp.concatenate(
        [part_out, split3(part_lse.reshape(HEADS, 128)), jnp.zeros((12, 128), bf16)], 0
    )
    got = exchange(jnp.broadcast_to(sent[None], (4, 816, 128)), "fsdp", QUADS)
    lses = join3(got[:, D:])
    high = jnp.max(lses, 0)
    glob_lse = high + jnp.log(jnp.sum(jnp.exp(lses - high), 0))
    shares = jnp.pad(jnp.exp(lses - glob_lse), ((0, 0), (0, 4), (0, 0)))
    glob_lse = glob_lse.reshape(6, 1, 256)

    (
        result,
        loss_sum,
        glob_out,
        grad_middle,
        grad_mixed,
        wattn_grad,
        win_send,
        win_keep,
        wout_send,
        wout_keep,
        norm_two,
    ) = feed(
        place, (2.0 / count)[None], rows, long_out, got, shares, packed, globs, norms, wa, win, wout
    )
    loss_sum = loss_sum[0, 0]
    dq, dk, dv, rel = attend_back(
        place, table, line, key_mask, self_mask, proj, grad_mixed, long_lse, glob_out, glob_lse
    )
    one_send, one_keep, grad_nat, back_left, back_right, back_glob, norm_one = project_back(
        place, rows, acts, dq, dk, dv, norms, even, odd, grad_middle, wattn_grad
    )
    grad_table = rel[:, :2, 44 : 44 + LABELS].reshape(HEADS, LABELS)
    grad_own = jnp.sum(rel[:, 2:4, :128], -1).reshape(HEADS)
    grad_other = jnp.sum(rel[:, 4:6, :128], -1).reshape(HEADS)
    from_left = lax.ppermute(back_right, "fsdp", TO_RIGHT).astype(f32)
    from_right = lax.ppermute(back_left, "fsdp", TO_LEFT).astype(f32)
    grad_nat = grad_nat.at[:128].add(from_left).at[384:].add(from_right)
    grad_long = reorder(grad_nat.astype(bf16), order).astype(f32)
    glob_parts = exchange(back_glob.reshape(4 * 32, D), "fsdp", QUADS).reshape(4, 32, D)
    grad_glob = lax.dynamic_slice_in_dim(grad_middle, ROWS + quarter * 32, 32, 0) + jnp.sum(
        glob_parts, 0
    )
    out_long = reorder(result[:ROWS], order)
    out_glob = lax.dynamic_slice_in_dim(result, ROWS + quarter * 32, 32, 0)

    one = reduce_columns(one_keep, one_send)
    two = reduce_columns(win_keep, win_send)
    qkv_grad = one[:3].transpose(1, 0, 2).reshape(6, 3 * D)
    attn_grad = one[3]
    in_grad = two.transpose(1, 0, 2).reshape(6, 4 * D)
    total = (wout_keep.astype(f32) + swap(wout_send).astype(f32)).astype(bf16)
    total = total.reshape(32, 2, 48, 384).transpose(1, 0, 2, 3).reshape(64, 48, 384)
    mine = jnp.sum(exchange(total, BOTH, SAME_CORE).astype(f32), 0)
    other = swap(mine)
    halves = jnp.where(
        core == 0, jnp.concatenate([mine, other], 1), jnp.concatenate([other, mine], 1)
    )
    out_grad = lax.dynamic_slice_in_dim(halves, core * 24, 24, 0)
    label_grad = jnp.dot(picker.T, grad_table.T, precision=HIGHEST)
    rel_grad = jnp.concatenate([label_grad, grad_own[None], grad_other[None]], 0)
    norm_grads = jnp.stack([norm_one[0], norm_two[0], norm_one[1], norm_two[1]], 1)
    rel_total, norm_total, loss_total = lax.psum((rel_grad, norm_grads, loss_sum), BOTH)
    mine_norm = lax.dynamic_slice_in_dim(
        norm_total, (lax.axis_index("dp") * 16 + member) * 6, 6, 0
    )
    return (
        out_long,
        out_glob,
        loss_total / count,
        grad_long,
        grad_glob,
        qkv_grad,
        attn_grad,
        in_grad,
        out_grad,
        mine_norm[:, :2],
        mine_norm[:, 2:],
        rel_total,
    )


def solution(mesh):
    rows = P(BOTH, None)
    in_specs = (rows,) * 11 + (P(), P("dp"), P("dp", None), P("dp"), P(), P(BOTH))
    out_specs = (rows, rows, P(), rows, rows, rows, rows, rows, rows, rows, rows, P())
    return jax.shard_map(shards, mesh=mesh, in_specs=in_specs, out_specs=out_specs, check_vma=False)
```

time: 959 us -> 676 us (0.70)
  local copies, waits for them, and re-layouts: 294 us -> 53.6 us
  matrix products: 138 us -> 0.41 us
  waiting for transfers between devices: 79.9 us -> 183 us
  Pallas kernels: 0 us -> 102 us
  other arithmetic: 140 us -> 42.6 us
    dot_general x30 -> x0, matrix products: 137 us -> none  [the longest x12 97.4 us: dot(): return jnp.dot(a, b, preferred_element_type=f32)]
    pallas_call x0 -> x5, Pallas kernels: none -> 102 us  [the longest x1 40 us: feed(): pl.pallas_call(feed_kernel, grid_spec=pltpu.PrefetchScalarGridSpec(num_sc...]
    all_to_all x18, waiting for transfers between devices: 79.8 us -> 174 us  [exchange(): lax.all_to_all(value, axis, 0, 0, axis_index_groups=groups, tiled=True)]
    unnamed x512 -> x95, local copies, waits for them, and re-layouts: 100 us -> 12.9 us
    slice x156 -> x6, local copies, waits for them, and re-layouts: 84.9 us -> 1.73 us  [the longest x1 1.2 us: shards(): loss_sum = loss_sum[0, 0]]
    sub x1 -> x0, other arithmetic: 41.8 us -> none  [shards(): ds = (probs * (dp - delta)).astype(bf16)]
    reshape x3, local copies, waits for them, and re-layouts: 29.8 us -> 0.04 us  [the longest x1 0.02 us: shards(): lax.dynamic_update_slice(line, label_table.T, (0, 44)).reshape(6, 2, 512)]
    reduce_sum x13 -> x2, other arithmetic: 18.8 us -> 0.72 us  [the longest x1 0.63 us: shards(): my_count = jnp.sum(slot_weight)]
  transfers between devices with their start and end apart: 30 -> 30, of which waited for: 10 -> 17; matrix products, arithmetic and copies ran while one was open for 45% -> 11% of each run, Pallas kernels for 0% -> 4%
where the time goes in v2:
time: 676 us; the launch traced here: 667 us
  waiting for transfers between devices  183 us (27%)
  blocking collectives  154 us (23%)
  starting transfers between devices  123 us (18%)
  Pallas kernels  102 us (15%)
  local copies, waits for them, and re-layouts  53.6 us (8%)
  other arithmetic  42.6 us (6%)
  between operations  7.67 us (1%)
    all_to_all x18, waiting for transfers between devices, exchange(): lax.all_to_all(value, axis, 0, 0, axis_index_groups=groups, tiled=True)  174 us
    all_to_all x18, starting transfers between devices, exchange(): lax.all_to_all(value, axis, 0, 0, axis_index_groups=groups, tiled=True)  108 us
    psum x1, blocking collectives, shards(): lax.psum((rel_grad, norm_grads, loss_sum), BOTH)  81.5 us
    pallas_call x1, Pallas kernels, feed(): pl.pallas_call(feed_kernel, grid_spec=pltpu.PrefetchScalarGridSpec(num_sc...  40 us
    all_gather x1, blocking collectives, shards(): lax.all_gather(w_in, 'fsdp', axis_index_groups=QUADS, axis=0, tiled=True)  25 us
    all_gather x1, blocking collectives, shards(): lax.all_gather(jnp.concatenate([glob_in, cot_glob], 1), 'fsdp', axis_inde...  24.3 us
    all_gather x1, blocking collectives, shards(): lax.all_gather(jnp.concatenate([w_qkv, w_attn, extra], 1), 'fsdp', axis_i...  23.3 us
    pallas_call x1, Pallas kernels, attend_back(): pl.pallas_call(attend_back_kernel, grid=(6,), in_specs=[SCALARS, SCALARS,...  21.4 us
  transfers between devices with their start and end apart: 30, of which 17 were waited for; matrix products, arithmetic and copies ran while one was open for 11% of the time, Pallas kernels for 4%

profile of v2, /device:TPU:1, one launch (start us, length us, event | category | flops | bytes accessed | tf_op | source)
XLA Modules:
  0.0 666.9 jit_solution(10887076390760849954)
XLA Ops:
  2.8 7.5 %all-to-all-start.1 = ((bf16[64,8,768]{2,1,0:T(8,128)(2,1)}), bf16[64,8,768]{2,1,0:T(8,128)(2,1)S(1)}, u32[]{:S(2)}, u32[]{:S(2)}) async-start(bf16[64,8,768]{2,1,0:T(8,128)(2,1)} %bitcast.13), calls=%async_computation.1 | async-start | bytes 1572864 | tf_op jit(solution)/shard_map/all_to_all | solution.py:34
  10.5 12.8 %all-to-all-done.1 = bf16[64,8,768]{2,1,0:T(8,128)(2,1)S(1)} async-done(((bf16[64,8,768]{2,1,0:T(8,128)(2,1)}), bf16[64,8,768]{2,1,0:T(8,128)(2,1)S(1)}, u32[]{:S(2)}, u32[]{:S(2)}) %all-to-all-start.1) | async-done | bytes 786464 | tf_op jit(solution)/shard_map/all_to_all | solution.py:34
  24.7 4.2 all-to-all-start.2
  31.5 10.6 %all-to-all-done.2 = bf16[64,8,768]{2,1,0:T(8,128)(2,1)S(1)} async-done(((bf16[64,8,768]{2,1,0:T(8,128)(2,1)}), bf16[64,8,768]{2,1,0:T(8,128)(2,1)S(1)}, u32[]{:S(2)}, u32[]{:S(2)}) %all-to-all-start.2) | async-done | bytes 786464 | tf_op jit(solution)/shard_map/all_to_all | solution.py:34
  42.9 4.2 all-to-all-start.4
  47.1 25.0 %all-gather.1 = bf16[4,6,3072]{2,1,0:T(8,128)(2,1)S(1)} all-gather(bf16[1,6,3072]{2,1,0:T(8,128)(2,1)S(1)} %bitcast.134), channel_id=1, replica_groups={{0,1,2,3},{4,5,6,7},{8,9,10,11},{12,13,14,15},{16,17,18,19},{20,21,22,2..., dimensions={0}, use_global_device_ids=true | all-gather | bytes 184320 | tf_op jit(solution)/shard_map/all_gather | solution.py:721
  74.1 9.7 %all-to-all-start.6 = ((bf16[64,24,768]{2,1,0:T(8,128)(2,1)}), bf16[64,24,768]{2,1,0:T(8,128)(2,1)S(1)}, u32[]{:S(2)}, u32[]{:S(2)}) async-start(bf16[64,24,768]{2,1,0:T(8,128)(2,1)} %broadcast_in_dim.136), calls=%async_computation.6 | async-start | bytes 4718592 | tf_op jit(solution)/shard_map/all_to_all | solution.py:34
  85.3 28.4 %all-to-all-done.6 = bf16[64,24,768]{2,1,0:T(8,128)(2,1)S(1)} async-done(((bf16[64,24,768]{2,1,0:T(8,128)(2,1)}), bf16[64,24,768]{2,1,0:T(8,128)(2,1)S(1)}, u32[]{:S(2)}, u32[]{:S(2)}) %all-to-all-start.6) | async-done | bytes 2359328 | tf_op jit(solution)/shard_map/all_to_all | solution.py:34
  115.8 8.0 %all-to-all-start.7 = ((bf16[64,48,384]{2,1,0:T(8,128)(2,1)}), bf16[64,48,384]{2,1,0:T(8,128)(2,1)S(1)}, u32[]{:S(2)}, u32[]{:S(2)}) async-start(bf16[64,48,384]{2,1,0:T(8,128)(2,1)} %broadcast_in_dim.137), calls=%async_computation.7 | async-start | bytes 4718592 | tf_op jit(solution)/shard_map/all_to_all | solution.py:34
  127.6 23.3 %all-gather = bf16[4,6,3200]{2,1,0:T(8,128)(2,1)S(1)} all-gather(bf16[1,6,3200]{2,1,0:T(8,128)(2,1)S(1)} %bitcast.132), channel_id=1, replica_groups={{0,1,2,3},{4,5,6,7},{8,9,10,11},{12,13,14,15},{16,17,18,19},{20,21,22,2..., dimensions={0}, use_global_device_ids=true | all-gather | bytes 192000 | tf_op jit(solution)/shard_map/all_gather | solution.py:718
  155.1 10.5 %all-to-all-start = ((bf16[64,24,896]{2,1,0:T(8,128)(2,1)}), bf16[64,24,896]{2,1,0:T(8,128)(2,1)S(1)}, u32[]{:S(2)}, u32[]{:S(2)}) async-start(bf16[64,24,896]{2,1,0:T(8,128)(2,1)} %broadcast_in_dim.72), calls=%async_computation | async-start | bytes 5505024 | tf_op jit(solution)/shard_map/all_to_all | solution.py:34
  166.9 3.5 gather_fusion.1
  170.4 29.1 %all-to-all-done = bf16[64,24,896]{2,1,0:T(8,128)(2,1)S(1)} async-done(((bf16[64,24,896]{2,1,0:T(8,128)(2,1)}), bf16[64,24,896]{2,1,0:T(8,128)(2,1)S(1)}, u32[]{:S(2)}, u32[]{:S(2)}) %all-to-all-start) | async-done | bytes 2752544 | tf_op jit(solution)/shard_map/all_to_all | solution.py:34
  199.5 6.3 all-to-all-start.5
  207.5 24.3 %all_gather.10.globs = bf16[128,1536]{1,0:T(8,128)(2,1)S(1)} all-gather(bf16[32,1536]{1,0:T(8,128)(2,1)S(1)} %pad_maximum_fusion.2), channel_id=1, replica_groups={{0,1,2,3},{4,5,6,7},{8,9,10,11},{12,13,14,15},{16,17,18,19},{20,21,22,2..., dimensions={0}, use_global_device_ids=true | all-gather | bytes 491520 | tf_op jit(solution)/shard_map/all_gather | solution.py:771
  233.8 4.2 collective-permute-start
  244.9 2.9 copy.94
  253.1 4.3 broadcast_select_fusion.2
  257.4 8.5 %project.1 = (bf16[896,768]{1,0:T(8,128)(2,1)S(1)}, bf16[896,768]{1,0:T(8,128)(2,1)}, bf16[896,2304]{1,0:T(8,128)(2,1)}) custom-call(bf16[128,768]{1,0:T(8,128)(2,1)S(1)} %collective-permute-done.left, bf16[512,768]{1,0:T(8,128)(2,1)S(1)} %bitcast.110, bf16[128,768]{1,0:T(8,128)(2,1)S(1)} %collective-permute-done.1.right, ...), custom_call_target="tpu_custom_call" | custom-call | tf_op jit(solution)/shard_map/project/pallas_call | solution.py:122
  268.6 15.6 %attend.1 = (bf16[512,768]{1,0:T(8,128)(2,1)S(1)}, f32[6,4,256]{2,1,0:T(4,128)S(1)}, bf16[768,128]{1,0:T(8,128)(2,1)S(1)}, f32[6,1,256]{2,1,0:T(1,128)S(1)}) custom-call(s32[2]{0:T(128)S(1)} %pad_add_fusion.place, f32[2,12]{1,0:T(2,128)S(1)} %copy.105.table, f32[6,2,512]{2,1,0:T(2,128)S(1)} %reshape.394.line, f32[896,256]{1,0:T(8,128)S(1)} %broadcast_in_dim.129.key_mask, ...), custom_call_target="tpu_custom_call" | custom-call | tf_op jit(solution)/shard_map/attend/pallas_call | solution.py:222
  286.5 4.1 all-to-all-start.3
  290.7 7.7 %maximum_select_fusion.wout = bf16[3072,768]{1,0:T(8,128)(2,1)} fusion(bf16[3072,384]{1,0:T(8,128)(2,1)} %collective-permute-done.5, bf16[3072,384]{1,0:T(8,128)(2,1)} %bitcast.36, pred[]{:T(512)S(6)} %eq.89), kind=kLoop, calls=%fused_computation.5 | loop fusion | flops 21233664 | bytes 9437185 | tf_op jit(solution)/shard_map/jit(_where)/select_n | solution.py:755
  302.9 40.0 %feed.1 = (bf16[640,768]{1,0:T(8,128)(2,1)}, f32[8,128]{1,0:T(8,128)}, bf16[768,128]{1,0:T(8,128)(2,1)}, f32[640,768]{1,0:T(8,128)}, bf16[640,768]{1,0:T(8,128)(...) custom-call(s32[2]{0:T(128)} %copy-done.9, ...), custom_call_target="tpu_custom_call" | custom-call | tf_op jit(solution)/shard_map/feed/pallas_call | solution.py:559
  345.0 21.4 %attend_back.1 = (bf16[896,768]{1,0:T(8,128)(2,1)S(1)}, bf16[896,768]{1,0:T(8,128)(2,1)S(1)}, bf16[896,768]{1,0:T(8,128)(2,1)}, f32[6,8,512]{2,1,0:T(8,128)S(1)}) custom-call(s32[2]{0:T(128)S(1)} %copy-done.10, f32[2,12]{1,0:T(2,128)S(1)} %copy.105.table, f32[6,2,512]{2,1,0:T(2,128)S(1)} %reshape.394.line, f32[896,256]{1,0:T(8,128)S(1)} %broadcast_in_dim.129.key_mask, ...), custom_call_target="tpu_custom_call" | custom-call | tf_op jit(solution)/shard_map/attend_back/pallas_call | solution.py:365
  368.6 16.7 %project_back.1 = (bf16[2,768,768]{2,1,0:T(8,128)(2,1)}, bf16[2,768,768]{2,1,0:T(8,128)(2,1)}, f32[512,768]{1,0:T(8,128)}, bf16[128,768]{1,0:T(8,128)(2,1)}, bf1...) custom-call(s32[2]{0:T(128)} %copy-done.9, bf16[896,768]{1,0:T(8,128)(2,1)} %copy-done.1, ...), custom_call_target="tpu_custom_call" | custom-call | tf_op jit(solution)/shard_map/project_back/pallas_call | solution.py:653
  385.3 4.3 all-to-all-start.12
  390.8 5.4 all-to-all-done.12
  397.0 4.3 all-to-all-start.8
  401.3 3.5 collective-permute-start.6
  407.0 5.5 collective-permute-done.6
  415.8 4.8 all-to-all-start.10
  422.1 11.5 %all-to-all-done.10 = bf16[64,8,768]{2,1,0:T(8,128)(2,1)S(1)} async-done(((bf16[64,8,768]{2,1,0:T(8,128)(2,1)}), bf16[64,8,768]{2,1,0:T(8,128)(2,1)S(1)}, u32[]{:S(2)}, u32[]{:S(2)}) %all-to-all-start.10) | async-done | bytes 786464 | tf_op jit(solution)/shard_map/all_to_all | solution.py:34
  433.6 4.2 all-to-all-start.9
  439.5 11.3 %all-to-all-done.9 = bf16[64,8,768]{2,1,0:T(8,128)(2,1)S(1)} async-done(((bf16[64,8,768]{2,1,0:T(8,128)(2,1)}), bf16[64,8,768]{2,1,0:T(8,128)(2,1)S(1)}, u32[]{:S(2)}, u32[]{:S(2)}) %all-to-all-start.9) | async-done | bytes 786464 | tf_op jit(solution)/shard_map/all_to_all | solution.py:34
  450.9 4.1 all-to-all-start.11
  455.0 3.0 add_convert_fusion
  459.7 8.4 %all-to-all-done.11 = bf16[64,8,768]{2,1,0:T(8,128)(2,1)S(1)} async-done(((bf16[64,8,768]{2,1,0:T(8,128)(2,1)}), bf16[64,8,768]{2,1,0:T(8,128)(2,1)S(1)}, u32[]{:S(2)}, u32[]{:S(2)}) %all-to-all-start.11) | async-done | bytes 786464 | tf_op jit(solution)/shard_map/all_to_all | solution.py:34
  469.0 8.1 %all-to-all-start.17 = ((bf16[64,48,384]{2,1,0:T(8,128)(2,1)}), bf16[64,48,384]{2,1,0:T(8,128)(2,1)S(1)}, u32[]{:S(2)}, u32[]{:S(2)}) async-start(bf16[64,48,384]{2,1,0:T(8,128)(2,1)} %bitcast.116), calls=%async_computation.17 | async-start | bytes 4718592 | tf_op jit(solution)/shard_map/all_to_all | solution.py:34
  477.7 4.4 add_convert_fusion.2
  482.1 24.8 %all-to-all-done.17 = bf16[64,48,384]{2,1,0:T(8,128)(2,1)S(1)} async-done(((bf16[64,48,384]{2,1,0:T(8,128)(2,1)}), bf16[64,48,384]{2,1,0:T(8,128)(2,1)S(1)}, u32[]{:S(2)}, u32[]{:S(2)}) %all-to-all-start.17) | async-done | bytes 2359328 | tf_op jit(solution)/shard_map/all_to_all | solution.py:34
  506.9 8.3 %all-to-all-start.13 = ((bf16[64,24,768]{2,1,0:T(8,128)(2,1)}), bf16[64,24,768]{2,1,0:T(8,128)(2,1)}, u32[]{:S(2)}, u32[]{:S(2)}) async-start(bf16[64,24,768]{2,1,0:T(8,128)(2,1)} %bitcast.53), calls=%async_computation.13 | async-start | bytes 4718592 | tf_op jit(solution)/shard_map/all_to_all | solution.py:34
  515.3 4.4 add_convert_fusion.1
  519.7 24.3 %all-to-all-done.13 = bf16[64,24,768]{2,1,0:T(8,128)(2,1)} async-done(((bf16[64,24,768]{2,1,0:T(8,128)(2,1)}), bf16[64,24,768]{2,1,0:T(8,128)(2,1)}, u32[]{:S(2)}, u32[]{:S(2)}) %all-to-all-start.13) | async-done | bytes 2359328 | tf_op jit(solution)/shard_map/all_to_all | solution.py:34
  544.0 7.9 %all-to-all-start.15 = ((bf16[64,24,768]{2,1,0:T(8,128)(2,1)}), bf16[64,24,768]{2,1,0:T(8,128)(2,1)}, u32[]{:S(2)}, u32[]{:S(2)}) async-start(bf16[64,24,768]{2,1,0:T(8,128)(2,1)} %bitcast.57), calls=%async_computation.15 | async-start | bytes 4718592 | tf_op jit(solution)/shard_map/all_to_all | solution.py:34
  555.5 81.5 %all-reduce.3 = (f32[]{:T(128)}, f32[768,4]{0,1:T(4,128)S(1)}, f32[171,12]{0,1:T(8,128)}) all-reduce(f32[]{:T(128)} %bitcast.45, f32[768,4]{0,1:T(4,128)S(1)} %pad_maximum_fusion.5, f32[171,12]{0,1:T(8,128)S(1)} %pad_maximum_fusion.4), channel_id=1, replica_groups=mesh['dp'=8,'fsdp'=16] {'dp','fsdp'}, use_global_device_ids=true, to_apply=%region_7.8 | all-reduce | flops 5125 | bytes 41000 | tf_op jit(solution)/shard_map/psum | solution.py:858
  649.2 3.3 all-to-all-start.14
  655.8 4.2 all-to-all-start.16
  660.6 2.7 all-to-all-done.16
  (224 shorter events, 82.0 us)
Async XLA Ops:
  2.8 26.1 %copy-start.38 = (s32[4]{0:T(128)S(1)}, s32[4]{0:T(128)}, u32[]{:S(2)}) copy-start(s32[4]{0:T(128)} %param.33) | copy-start | bytes 52
  2.8 27.0 %copy-start.36 = (s32[512]{0:T(512)S(1)}, s32[512]{0:T(512)}, u32[]{:S(2)}) copy-start(s32[512]{0:T(512)} %param.37) | copy-start | bytes 6148
  2.8 27.2 %copy-start.26 = (bf16[512,768]{1,0:T(8,128)(2,1)S(1)}, bf16[512,768]{1,0:T(8,128)(2,1)}, u32[]{:S(2)}) copy-start(bf16[512,768]{1,0:T(8,128)(2,1)} %param.25) | copy-start | bytes 2359300
  2.8 27.2 %copy-start.27 = (bf16[512,768]{1,0:T(8,128)(2,1)S(1)}, bf16[512,768]{1,0:T(8,128)(2,1)}, u32[]{:S(2)}) copy-start(bf16[512,768]{1,0:T(8,128)(2,1)} %param.23) | copy-start | bytes 2359300
  2.8 20.5 %all-to-all-start.1 = ((bf16[64,8,768]{2,1,0:T(8,128)(2,1)}), bf16[64,8,768]{2,1,0:T(8,128)(2,1)S(1)}, u32[]{:S(2)}, u32[]{:S(2)}) async-start(bf16[64,8,768]{2,1,0:T(8,128)(2,1)} %bitcast.13), calls=%async_computation.1 | async-start | bytes 1572864 | tf_op jit(solution)/shard_map/all_to_all | solution.py:34
  24.7 17.3 %all-to-all-start.2 = ((bf16[64,8,768]{2,1,0:T(8,128)(2,1)}), bf16[64,8,768]{2,1,0:T(8,128)(2,1)S(1)}, u32[]{:S(2)}, u32[]{:S(2)}) async-start(bf16[64,8,768]{2,1,0:T(8,128)(2,1)} %gather_fusion), calls=%async_computation.2 | async-start | bytes 1572864 | tf_op jit(solution)/shard_map/all_to_all | solution.py:34
  31.5 15.7 %copy-start.31 = (bf16[6,3072]{1,0:T(8,128)(2,1)S(1)}, bf16[6,3072]{1,0:T(8,128)(2,1)}, u32[]{:S(2)}) copy-start(bf16[6,3072]{1,0:T(8,128)(2,1)} %param.28) | copy-start | bytes 110596
  42.9 29.3 %all-to-all-start.4 = ((bf16[64,8,1664]{2,1,0:T(8,128)(2,1)}), bf16[64,8,1664]{2,1,0:T(8,128)(2,1)S(1)}, u32[]{:S(2)}, u32[]{:S(2)}) async-start(bf16[64,8,1664]{2,1,0:T(8,128)(2,1)} %bitcast.27), calls=%async_computation.4 | async-start | bytes 3407872 | tf_op jit(solution)/shard_map/all_to_all | solution.py:34
  74.1 39.6 %all-to-all-start.6 = ((bf16[64,24,768]{2,1,0:T(8,128)(2,1)}), bf16[64,24,768]{2,1,0:T(8,128)(2,1)S(1)}, u32[]{:S(2)}, u32[]{:S(2)}) async-start(bf16[64,24,768]{2,1,0:T(8,128)(2,1)} %broadcast_in_dim.136), calls=%async_computation.6 | async-start | bytes 4718592 | tf_op jit(solution)/shard_map/all_to_all | solution.py:34
  83.9 1.4 collective-permute-start.4
  115.8 37.0 %all-to-all-start.7 = ((bf16[64,48,384]{2,1,0:T(8,128)(2,1)}), bf16[64,48,384]{2,1,0:T(8,128)(2,1)S(1)}, u32[]{:S(2)}, u32[]{:S(2)}) async-start(bf16[64,48,384]{2,1,0:T(8,128)(2,1)} %broadcast_in_dim.137), calls=%async_computation.7 | async-start | bytes 4718592 | tf_op jit(solution)/shard_map/all_to_all | solution.py:34
  154.6 12.1 %copy-start.35 = (f32[171,12]{0,1:T(8,128)S(1)}, f32[171,12]{0,1:T(8,128)}, u32[]{:S(2)}) copy-start(f32[171,12]{0,1:T(8,128)} %param.32) | copy-start | bytes 24628
  154.7 12.1 %copy-start.43 = (s32[169]{0:T(256)S(1)}, s32[169]{0:T(256)}, u32[]{:S(2)}) copy-start(s32[169]{0:T(256)} %param.36) | copy-start | bytes 2032
  155.1 44.5 %all-to-all-start = ((bf16[64,24,896]{2,1,0:T(8,128)(2,1)}), bf16[64,24,896]{2,1,0:T(8,128)(2,1)S(1)}, u32[]{:S(2)}, u32[]{:S(2)}) async-start(bf16[64,24,896]{2,1,0:T(8,128)(2,1)} %broadcast_in_dim.72), calls=%async_computation | async-start | bytes 5505024 | tf_op jit(solution)/shard_map/all_to_all | solution.py:34
  165.5 82.3 %collective-permute-start.3 = (bf16[2,768,768]{2,1,0:T(8,128)(2,1)}, bf16[2,768,768]{2,1,0:T(8,128)(2,1)}, u32[]{:S(2)}, u32[]{:S(2)}) collective-permute-start(bf16[2,768,768]{2,1,0:T(8,128)(2,1)} %bitcast.117), channel_id=1, source_target_pairs={{0,1},{1,0},{2,3},{3,2},{4,5},{5,4},{6,7},{7,6},{8,9},{9,8},{10,11... | collective-permute-start | bytes 7077896 | tf_op jit(solution)/shard_map/ppermute | solution.py:38
  170.4 37.1 %copy-start.29 = (bf16[32,768]{1,0:T(8,128)(2,1)S(1)}, bf16[32,768]{1,0:T(8,128)(2,1)}, u32[]{:S(2)}) copy-start(bf16[32,768]{1,0:T(8,128)(2,1)} %param.24) | copy-start | bytes 147460
  170.4 37.1 %copy-start.30 = (bf16[32,768]{1,0:T(8,128)(2,1)S(1)}, bf16[32,768]{1,0:T(8,128)(2,1)}, u32[]{:S(2)}) copy-start(bf16[32,768]{1,0:T(8,128)(2,1)} %param.22) | copy-start | bytes 147460
  199.5 33.9 %copy-start.12 = (bf16[64,24,896]{2,1,0:T(8,128)(2,1)}, bf16[64,24,896]{2,1,0:T(8,128)(2,1)S(1)}, u32[]{:S(2)}) copy-start(bf16[64,24,896]{2,1,0:T(8,128)(2,1)S(1)} %all-to-all-done) | copy-start | bytes 8257540
  199.5 45.4 %all-to-all-start.5 = ((bf16[64,8,1664]{2,1,0:T(8,128)(2,1)}), bf16[64,8,1664]{2,1,0:T(8,128)(2,1)}, u32[]{:S(2)}, u32[]{:S(2)}) async-start(bf16[64,8,1664]{2,1,0:T(8,128)(2,1)} %gather_fusion.1), calls=%async_computation.5 | async-start | bytes 3407872 | tf_op jit(solution)/shard_map/all_to_all | solution.py:34
  231.9 25.5 %copy-start.2 = (bf16[128,1536]{1,0:T(8,128)(2,1)}, bf16[128,1536]{1,0:T(8,128)(2,1)S(1)}, u32[]{:S(2)}) copy-start(bf16[128,1536]{1,0:T(8,128)(2,1)S(1)} %all_gather.10.globs) | copy-start | bytes 1179652
  233.4 19.2 %collective-permute-start.2 = (bf16[2,768,768]{2,1,0:T(8,128)(2,1)}, bf16[2,768,768]{2,1,0:T(8,128)(2,1)}, u32[]{:S(2)}, u32[]{:S(2)}) collective-permute-start(bf16[2,768,768]{2,1,0:T(8,128)(2,1)} %slice.193), channel_id=1, source_target_pairs={{0,1},{1,0},{2,3},{3,2},{4,5},{5,4},{6,7},{7,6},{8,9},{9,8},{10,11... | collective-permute-start | bytes 7077896 | tf_op jit(solution)/shard_map/ppermute | solution.py:38
  233.7 32.5 %copy-start.9 = (s32[2]{0:T(128)}, s32[2]{0:T(128)S(1)}, u32[]{:S(2)}) copy-start(s32[2]{0:T(128)S(1)} %pad_add_fusion.place) | copy-start | bytes 28
  233.8 23.6 %collective-permute-start = (bf16[128,768]{1,0:T(8,128)(2,1)S(1)}, bf16[128,768]{1,0:T(8,128)(2,1)S(1)}, u32[]{:S(2)}, u32[]{:S(2)}) collective-permute-start(bf16[128,768]{1,0:T(8,128)(2,1)S(1)} %get-tuple-element.116), channel_id=1, source_target_pairs={{0,1},{1,2},{2,3},{4,5},{5,6},{6,7},{8,9},{9,10},{10,11},{12,13},{... | collective-permute-start | bytes 589832 | tf_op jit(solution)/shard_map/ppermute | solution.py:774
  238.0 19.4 %collective-permute-start.1 = (bf16[128,768]{1,0:T(8,128)(2,1)S(1)}, bf16[128,768]{1,0:T(8,128)(2,1)S(1)}, u32[]{:S(2)}, u32[]{:S(2)}) collective-permute-start(bf16[128,768]{1,0:T(8,128)(2,1)S(1)} %get-tuple-element.115), channel_id=1, source_target_pairs={{1,0},{2,1},{3,2},{5,4},{6,5},{7,6},{9,8},{10,9},{11,10},{13,12},{... | collective-permute-start | bytes 589832 | tf_op jit(solution)/shard_map/ppermute | solution.py:775
  241.6 49.1 %collective-permute-start.5 = (bf16[3072,384]{1,0:T(8,128)(2,1)}, bf16[3072,384]{1,0:T(8,128)(2,1)}, u32[]{:S(2)}, u32[]{:S(2)}) collective-permute-start(bf16[3072,384]{1,0:T(8,128)(2,1)} %bitcast.36), channel_id=1, source_target_pairs={{0,1},{1,0},{2,3},{3,2},{4,5},{5,4},{6,7},{7,6},{8,9},{9,8},{10,11... | collective-permute-start | bytes 7077896 | tf_op jit(solution)/shard_map/ppermute | solution.py:38
  243.2 14.2 %copy-start.7 = (f32[8,768]{1,0:T(8,128)}, f32[8,768]{1,0:T(8,128)S(1)}, u32[]{:S(2)}) copy-start(f32[8,768]{1,0:T(8,128)S(1)} %concatenate.61.clone.norms) | copy-start | bytes 73732
  265.9 18.3 %copy-start.1 = (bf16[896,768]{1,0:T(8,128)(2,1)}, bf16[896,768]{1,0:T(8,128)(2,1)S(1)}, u32[]{:S(2)}) copy-start(bf16[896,768]{1,0:T(8,128)(2,1)S(1)} %get-tuple-element.65.rows) | copy-start | bytes 4128772
  286.5 15.4 %all-to-all-start.3 = ((bf16[4,816,128]{2,1,0:T(8,128)(2,1)}), bf16[4,816,128]{2,1,0:T(8,128)(2,1)S(1)}, u32[]{:S(2)}, u32[]{:S(2)}) async-start(bf16[4,816,128]{2,1,0:T(8,128)(2,1)} %broadcast_in_dim.134), calls=%async_computation.3 | async-start | bytes 1671168 | tf_op jit(solution)/shard_map/all_to_all | solution.py:34
  302.9 40.0 %copy-start.10 = (s32[2]{0:T(128)S(1)}, s32[2]{0:T(128)}, u32[]{:S(2)}) copy-start(s32[2]{0:T(128)} %copy-done.9) | copy-start | bytes 28
  368.6 21.2 %copy-start.28 = (bf16[640,768]{1,0:T(8,128)(2,1)S(1)}, bf16[640,768]{1,0:T(8,128)(2,1)}, u32[]{:S(2)}) copy-start(bf16[640,768]{1,0:T(8,128)(2,1)} %get-tuple-element.70) | copy-start | bytes 2949124
  385.3 10.9 %all-to-all-start.12 = ((f32[4,32,768]{2,1,0:T(8,128)}), f32[4,32,768]{2,1,0:T(8,128)S(1)}, u32[]{:S(2)}, u32[]{:S(2)}) async-start(f32[4,32,768]{2,1,0:T(8,128)} %bitcast.130), calls=%async_computation.12 | async-start | bytes 786432 | tf_op jit(solution)/shard_map/all_to_all | solution.py:34
  389.7 65.4 %collective-permute-start.10 = (bf16[3072,384]{1,0:T(8,128)(2,1)}, bf16[3072,384]{1,0:T(8,128)(2,1)}, u32[]{:S(2)}, u32[]{:S(2)}) collective-permute-start(bf16[3072,384]{1,0:T(8,128)(2,1)} %get-tuple-element.90), channel_id=1, source_target_pairs={{0,1},{1,0},{2,3},{3,2},{4,5},{5,4},{6,7},{7,6},{8,9},{9,8},{10,11... | collective-permute-start | bytes 7077896 | tf_op jit(solution)/shard_map/ppermute | solution.py:38
  389.8 15.0 %copy-start.41 = (bf16[128,768]{1,0:T(8,128)(2,1)S(1)}, bf16[128,768]{1,0:T(8,128)(2,1)}, u32[]{:S(2)}) copy-start(bf16[128,768]{1,0:T(8,128)(2,1)} %get-tuple-element.83) | copy-start | bytes 589828
  389.8 22.7 %copy-start.22 = (f32[512,768]{1,0:T(8,128)S(1)}, f32[512,768]{1,0:T(8,128)}, u32[]{:S(2)}) copy-start(f32[512,768]{1,0:T(8,128)} %get-tuple-element.81) | copy-start | bytes 4718596
  397.0 18.8 %all-to-all-start.8 = ((bf16[64,8,768]{2,1,0:T(8,128)(2,1)}), bf16[64,8,768]{2,1,0:T(8,128)(2,1)S(1)}, u32[]{:S(2)}, u32[]{:S(2)}) async-start(bf16[64,8,768]{2,1,0:T(8,128)(2,1)} %bitcast.39), calls=%async_computation.8 | async-start | bytes 1572864 | tf_op jit(solution)/shard_map/all_to_all | solution.py:34
  401.3 11.2 %collective-permute-start.6 = (bf16[128,768]{1,0:T(8,128)(2,1)S(1)}, bf16[128,768]{1,0:T(8,128)(2,1)S(1)}, u32[]{:S(2)}, u32[]{:S(2)}) collective-permute-start(bf16[128,768]{1,0:T(8,128)(2,1)S(1)} %copy-done.42), channel_id=1, source_target_pairs={{0,1},{1,2},{2,3},{4,5},{5,6},{6,7},{8,9},{9,10},{10,11},{12,13},{... | collective-permute-start | bytes 589832 | tf_op jit(solution)/shard_map/ppermute | solution.py:831
  404.8 9.8 %collective-permute-start.7 = (bf16[128,768]{1,0:T(8,128)(2,1)S(1)}, bf16[128,768]{1,0:T(8,128)(2,1)S(1)}, u32[]{:S(2)}, u32[]{:S(2)}) collective-permute-start(bf16[128,768]{1,0:T(8,128)(2,1)S(1)} %copy-done.41), channel_id=1, source_target_pairs={{1,0},{2,1},{3,2},{5,4},{6,5},{7,6},{9,8},{10,9},{11,10},{13,12},{... | collective-permute-start | bytes 589832 | tf_op jit(solution)/shard_map/ppermute | solution.py:832
  415.8 17.8 %all-to-all-start.10 = ((bf16[64,8,768]{2,1,0:T(8,128)(2,1)}), bf16[64,8,768]{2,1,0:T(8,128)(2,1)S(1)}, u32[]{:S(2)}, u32[]{:S(2)}) async-start(bf16[64,8,768]{2,1,0:T(8,128)(2,1)} %bitcast.48), calls=%async_computation.10 | async-start | bytes 1572864 | tf_op jit(solution)/shard_map/all_to_all | solution.py:34
  433.6 17.3 %all-to-all-start.9 = ((bf16[64,8,768]{2,1,0:T(8,128)(2,1)}), bf16[64,8,768]{2,1,0:T(8,128)(2,1)S(1)}, u32[]{:S(2)}, u32[]{:S(2)}) async-start(bf16[64,8,768]{2,1,0:T(8,128)(2,1)} %gather_fusion.2), calls=%async_computation.9 | async-start | bytes 1572864 | tf_op jit(solution)/shard_map/all_to_all | solution.py:34
  437.8 39.9 %collective-permute-start.8 = (bf16[2,768,768]{2,1,0:T(8,128)(2,1)}, bf16[2,768,768]{2,1,0:T(8,128)(2,1)}, u32[]{:S(2)}, u32[]{:S(2)}) collective-permute-start(bf16[2,768,768]{2,1,0:T(8,128)(2,1)} %get-tuple-element.86), channel_id=1, source_target_pairs={{0,1},{1,0},{2,3},{3,2},{4,5},{5,4},{6,7},{7,6},{8,9},{9,8},{10,11... | collective-permute-start | bytes 7077896 | tf_op jit(solution)/shard_map/ppermute | solution.py:38
  450.9 17.3 %all-to-all-start.11 = ((bf16[64,8,768]{2,1,0:T(8,128)(2,1)}), bf16[64,8,768]{2,1,0:T(8,128)(2,1)S(1)}, u32[]{:S(2)}, u32[]{:S(2)}) async-start(bf16[64,8,768]{2,1,0:T(8,128)(2,1)} %gather_fusion.3), calls=%async_computation.11 | async-start | bytes 1572864 | tf_op jit(solution)/shard_map/all_to_all | solution.py:34
  469.0 37.9 %all-to-all-start.17 = ((bf16[64,48,384]{2,1,0:T(8,128)(2,1)}), bf16[64,48,384]{2,1,0:T(8,128)(2,1)S(1)}, u32[]{:S(2)}, u32[]{:S(2)}) async-start(bf16[64,48,384]{2,1,0:T(8,128)(2,1)} %bitcast.116), calls=%async_computation.17 | async-start | bytes 4718592 | tf_op jit(solution)/shard_map/all_to_all | solution.py:34
  477.1 38.2 %collective-permute-start.9 = (bf16[2,768,768]{2,1,0:T(8,128)(2,1)}, bf16[2,768,768]{2,1,0:T(8,128)(2,1)}, u32[]{:S(2)}, u32[]{:S(2)}) collective-permute-start(bf16[2,768,768]{2,1,0:T(8,128)(2,1)} %get-tuple-element.88), channel_id=1, source_target_pairs={{0,1},{1,0},{2,3},{3,2},{4,5},{5,4},{6,7},{7,6},{8,9},{9,8},{10,11... | collective-permute-start | bytes 7077896 | tf_op jit(solution)/shard_map/ppermute | solution.py:38
  506.9 37.1 %all-to-all-start.13 = ((bf16[64,24,768]{2,1,0:T(8,128)(2,1)}), bf16[64,24,768]{2,1,0:T(8,128)(2,1)}, u32[]{:S(2)}, u32[]{:S(2)}) async-start(bf16[64,24,768]{2,1,0:T(8,128)(2,1)} %bitcast.53), calls=%async_computation.13 | async-start | bytes 4718592 | tf_op jit(solution)/shard_map/all_to_all | solution.py:34
  544.0 105.2 %all-to-all-start.15 = ((bf16[64,24,768]{2,1,0:T(8,128)(2,1)}), bf16[64,24,768]{2,1,0:T(8,128)(2,1)}, u32[]{:S(2)}, u32[]{:S(2)}) async-start(bf16[64,24,768]{2,1,0:T(8,128)(2,1)} %bitcast.57), calls=%async_computation.15 | async-start | bytes 4718592 | tf_op jit(solution)/shard_map/all_to_all | solution.py:34
  645.7 18.3 %collective-permute-start.11 = (f32[48,384]{1,0:T(8,128)S(1)}, f32[48,384]{1,0:T(8,128)S(1)}, u32[]{:S(2)}, u32[]{:S(2)}) collective-permute-start(f32[48,384]{1,0:T(8,128)S(1)} %convert_reduce_fusion), channel_id=1, source_target_pairs={{0,1},{1,0},{2,3},{3,2},{4,5},{5,4},{6,7},{7,6},{8,9},{9,8},{10,11... | collective-permute-start | bytes 221192 | tf_op jit(solution)/shard_map/ppermute | solution.py:38
  649.2 6.6 all-to-all-start.14
  655.8 7.6 %all-to-all-start.16 = ((f32[4,6,768]{2,1,0:T(8,128)}), f32[4,6,768]{2,1,0:T(8,128)S(1)}, u32[]{:S(2)}, u32[]{:S(2)}) async-start(f32[4,6,768]{2,1,0:T(8,128)} %reshape.413), calls=%async_computation.16 | async-start | bytes 196608 | tf_op jit(solution)/shard_map/all_to_all | solution.py:34
  (26 other events, 120.4 us)

commit v3 on v2

--- a/solution.py
+++ b/solution.py
@@ -30,12 +30,186 @@
 TO_LEFT = [(i, i - 1) for i in range(16) if i % 4 > 0]
 
 
+def flip(device, axis, step):
+    if axis == "x":
+        return device ^ (step << 4)
+    if axis == "y":
+        return device ^ (step << 1)
+    return device ^ ((step >> 1) << 6) ^ ((step & 1) << 3)
+
+
+PARTNERS = {
+    axis: [[(i, flip(i, axis, step)) for i in range(128)] for step in (1, 2, 3)] for axis in "xyz"
+}
+
+
 def exchange(value, axis, groups=None):
     return lax.all_to_all(value, axis, 0, 0, axis_index_groups=groups, tiled=True)
 
 
 def swap(value):
     return lax.ppermute(value, "fsdp", SWAP)
+
+
+def relay(values, axis):
+    return [lax.ppermute(value, BOTH, pairs) for value, pairs in zip(values, PARTNERS[axis])]
+
+
+def after(value, *others):
+    return lax.optimization_barrier((value,) + others)[0]
+
+
+ANY = pl.BlockSpec(memory_space=pl.ANY)
+SCALARS = pl.BlockSpec(memory_space=pltpu.SMEM)
+
+
+def cost(microseconds):
+    return pl.CostEstimate(
+        flops=int(microseconds * 1.1e9),
+        bytes_accessed=int(microseconds * 3.6e6),
+        transcendentals=0,
+    )
+
+
+def place_parts(spot, parts, shapes, moves, name):
+    def kernel(spot_ref, *refs):
+        ins, outs = refs[:4], refs[4:]
+        for k in range(4):
+            for source, which, target in moves(spot_ref[0] ^ k):
+                outs[which][target] = ins[k][source]
+
+    vm = pl.BlockSpec(memory_space=pltpu.VMEM)
+    return pl.pallas_call(
+        kernel,
+        in_specs=[SCALARS] + [vm] * 4,
+        out_specs=[vm] * len(shapes),
+        out_shape=[jax.ShapeDtypeStruct(shape, bf16) for shape in shapes],
+        compiler_params=params(32),
+        cost_estimate=cost(2),
+        name=name,
+    )(spot, *parts)
+
+
+def gather_axis(spot, value, axis, shapes, moves, name):
+    return place_parts(spot, [value] + relay([value] * 3, axis), shapes, moves, name)
+
+
+def encode(value):
+    high = value.astype(bf16)
+    return high, (value - high.astype(f32)).astype(bf16)
+
+
+def fold_parts(spot, parts, starts, length, name):
+    count = parts[0].shape[0] // 4 * 4
+    extra = parts[0].shape[0] - count
+    size = count // 4
+
+    def kernel(spot_ref, *refs):
+        ins, outs = refs[: len(parts)], refs[len(parts) :]
+        for k in range(4):
+            for i, start in enumerate(starts(spot_ref[0] ^ k)):
+                total = ins[0][pl.ds(start, length)].astype(f32)
+                for other in ins[1:]:
+                    total = total + other[pl.ds(start, length)].astype(f32)
+                outs[k][i * length : (i + 1) * length] = total.astype(bf16)
+        if extra:
+            small = [ref[count, :8].astype(f32) + ref[count, 8:16].astype(f32) for ref in ins]
+            small = [small[i] + small[i + 1] for i in range(0, len(ins), 2)]
+            high, low = encode(small[0] if len(small) == 1 else small[0] + small[1])
+            for out in outs:
+                out[size, :8] = high
+                out[size, 8:16] = low
+                out[size, 16:] = jnp.zeros((8, D), bf16)
+
+    vm = pl.BlockSpec(memory_space=pltpu.VMEM)
+    return pl.pallas_call(
+        kernel,
+        in_specs=[SCALARS] + [vm] * len(parts),
+        out_specs=[vm] * 4,
+        out_shape=[jax.ShapeDtypeStruct((size + extra, 24, D), bf16)] * 4,
+        compiler_params=params(32),
+        cost_estimate=cost(2),
+        name=name,
+    )(spot, *parts)
+
+
+def add_pairs(pairs, name):
+    def kernel(*refs):
+        for i in range(len(pairs)):
+            ours, theirs = refs[2 * i][...].astype(f32), refs[2 * i + 1][...].astype(f32)
+            refs[2 * len(pairs) + i][...] = (ours + theirs).astype(bf16)
+
+    block = pl.BlockSpec((384, D), lambda i: (i, 0))
+    return pl.pallas_call(
+        kernel,
+        grid=(4,),
+        in_specs=[block] * (2 * len(pairs)),
+        out_specs=[block] * len(pairs),
+        out_shape=[jax.ShapeDtypeStruct((2 * D, D), bf16)] * len(pairs),
+        compiler_params=params(32),
+        cost_estimate=cost(4),
+        name=name,
+    )(*[part.reshape(2 * D, D) for pair in pairs for part in pair])
+
+
+def scatter_axis(spot, parts, axis, starts, length, name):
+    cut = fold_parts(spot, parts, starts, length, name)
+    return [cut[0]] + relay(cut[1:], axis)
+
+
+def pack_rows(result, nat, from_left, from_right):
+    def kernel(result_ref, nat_ref, left_ref, right_ref, out):
+        for block in range(4):
+            rows = slice(128 * block, 128 * block + 128)
+            grad = nat_ref[rows]
+            if block == 0:
+                grad = grad + left_ref[...].astype(f32)
+            if block == 3:
+                grad = grad + right_ref[...].astype(f32)
+            for piece in range(16):
+                low = 8 * piece
+                out[4 * piece + block, :, D:] = grad[low : low + 8].astype(bf16)
+                out[4 * piece + block, :, :D] = result_ref[
+                    128 * block + low : 128 * block + low + 8
+                ]
+
+    vm = pl.BlockSpec(memory_space=pltpu.VMEM)
+    return pl.pallas_call(
+        kernel,
+        in_specs=[vm] * 4,
+        out_specs=vm,
+        out_shape=jax.ShapeDtypeStruct((64, 8, 2 * D), bf16),
+        compiler_params=params(32),
+        cost_estimate=cost(3),
+        name="pack_rows",
+    )(result, nat, from_left, from_right)
+
+
+def unpack_rows(value):
+    def kernel(value_ref, long_ref, grad_ref):
+        for block in range(4):
+            for piece in range(16):
+                low = 128 * block + 8 * piece
+                long_ref[low : low + 8] = value_ref[4 * piece + block, :, :D]
+                grad_ref[low : low + 8] = value_ref[4 * piece + block, :, D:].astype(f32)
+
+    vm = pl.BlockSpec(memory_space=pltpu.VMEM)
+    return pl.pallas_call(
+        kernel,
+        in_specs=[vm],
+        out_specs=[vm] * 2,
+        out_shape=[jax.ShapeDtypeStruct((ROWS, D), bf16), jax.ShapeDtypeStruct((ROWS, D), f32)],
+        compiler_params=params(32),
+        cost_estimate=cost(3),
+        name="unpack_rows",
+    )(value)
+
+
+def total_of(parts):
+    total = parts[0].astype(f32)
+    for part in parts[1:]:
+        total = total + part.astype(f32)
+    return total
 
 
 def pieces(rows):
@@ -66,13 +240,6 @@
     return value[:, :HEADS] + value[:, HEADS : 2 * HEADS] + value[:, 2 * HEADS : 3 * HEADS]
 
 
-def reduce_columns(keep, send):
-    total = keep.astype(f32) + swap(send).astype(f32)
-    parts = exchange(total.astype(bf16).reshape(64, 24, D), BOTH, SAME_CORE)
-    mine = jnp.sum(parts.astype(f32), 0)
-    return exchange(mine.reshape(4, 6, D), "fsdp", QUADS)
-
-
 def dot_nn(a, b):
     return lax.dot_general(a, b, (((1,), (0,)), ((), ())), preferred_element_type=f32)
 
@@ -88,9 +255,6 @@
 def whole(shape):
     zeros = (0,) * len(shape)
     return pl.BlockSpec(shape, lambda *_: zeros, pipeline_mode=pl.Buffered(1))
-
-
-SCALARS = pl.BlockSpec(memory_space=pltpu.SMEM)
 
 
 def params(megabytes):
@@ -105,7 +269,24 @@
     return centred * factor, factor
 
 
-def project_kernel(left, nat, right, globs, norms, even, odd, rows_out, acts_out, proj_out):
+def load_quarters(core, mine, other, target, sems, count):
+    copies = []
+    for p in range(2):
+        copies.append(pltpu.make_async_copy(mine.at[p, :, pl.ds(0, D)], target.at[2 * p + core], sems.at[2 * p]))
+        copies.append(
+            pltpu.make_async_copy(
+                other.at[p, :, pl.ds(0, D)], target.at[2 * p + 1 - core], sems.at[2 * p + 1]
+            )
+        )
+    for copy in copies:
+        copy.start()
+    return copies
+
+
+def project_kernel(
+    place, left, nat, right, globs, norms, mine, other, rows_out, acts_out, proj_out, w, sems
+):
+    copies = load_quarters(place[1], mine, other, w, sems, 4)
     rows_out[:128] = left[...]
     rows_out[128:640] = nat[...]
     rows_out[640:768] = right[...]
@@ -113,22 +294,27 @@
     normal, _ = normalise(rows_out[...].astype(f32))
     acts = (normal * norms[0:1] + norms[2:3]).astype(bf16)
     acts_out[...] = acts
-    proj_out[:, :D] = dot_nn(acts, even[0]).astype(bf16)
-    proj_out[:, D : 2 * D] = dot_nn(acts, odd[0]).astype(bf16)
-    proj_out[:, 2 * D :] = dot_nn(acts, even[1]).astype(bf16)
-
-
-def project(left, nat, right, globs, norms, even, odd):
+    for copy in copies:
+        copy.wait()
+    for i in range(3):
+        proj_out[:, i * D : i * D + D] = dot_nn(acts, w[i]).astype(bf16)
+
+
+def project(place, left, nat, right, globs, norms, mine, other):
+    vm = pl.BlockSpec(memory_space=pltpu.VMEM)
     return pl.pallas_call(
         project_kernel,
+        in_specs=[SCALARS] + [vm] * 5 + [ANY] * 2,
+        scratch_shapes=[pltpu.VMEM((4, D, D), bf16), pltpu.SemaphoreType.DMA((4,))],
         out_shape=(
             jax.ShapeDtypeStruct((EXT, D), bf16),
             jax.ShapeDtypeStruct((EXT, D), bf16),
             jax.ShapeDtypeStruct((EXT, 3 * D), bf16),
         ),
         compiler_params=params(50),
+        cost_estimate=cost(9),
         name="project",
-    )(left, nat, right, globs, norms, even, odd)
+    )(place, left, nat, right, globs, norms, mine, other)
 
 
 def stack_heads(rows):
@@ -246,6 +432,7 @@
         ),
         scratch_shapes=[pltpu.VMEM((384, 256), f32)],
         compiler_params=params(40),
+        cost_estimate=cost(15),
         name="attend",
     )(place, table, line, key_mask, self_mask, proj, proj, proj)
 
@@ -398,6 +585,7 @@
             pltpu.VMEM((EXT, 128), f32),
         ],
         compiler_params=params(48),
+        cost_estimate=cost(21),
         name="attend_back",
     )(place, table, line, key_mask, self_mask, proj, proj, proj, grad, lse, glob_out, glob_lse)
 
@@ -412,9 +600,11 @@
     packed,
     globs,
     norms,
-    wa,
-    win,
     wout,
+    first_mine,
+    first_other,
+    in_mine,
+    in_other,
     result_out,
     loss_out,
     glob_out,
@@ -435,9 +625,18 @@
     grad_z,
     grad_acts,
     factor,
+    wa,
+    win,
+    sem,
+    sems,
 ):
     step = pl.program_id(0)
     core = place[1]
+
+
+    def attn_copy(source):
+        return pltpu.make_async_copy(source.at[1, :, pl.ds(0, D)], wa, sem)
+
     quarter = place[0]
     forward = step < 4
     late = jnp.maximum(step - 4, 0)
@@ -452,6 +651,15 @@
 
     @pl.when(step == 0)
     def _():
+        @pl.when(core == 1)
+        def _():
+            attn_copy(first_mine).start()
+
+        @pl.when(core == 0)
+        def _():
+            attn_copy(first_other).start()
+
+        load_quarters(core, in_mine, in_other, win, sems, 4)
         mixed[:ROWS] = long_out[...]
         for pair in range(6):
             sums = jnp.zeros((128, 128), f32)
@@ -465,6 +673,7 @@
                 sums = sums + parts[source, 128 * pair : 128 * pair + 128, :].astype(f32) * share
             glob_out[128 * pair : 128 * pair + 128, :] = sums.astype(bf16)
             mixed[ROWS:, 128 * pair : 128 * pair + 128] = sums.T.astype(bf16)
+        attn_copy(first_mine).wait()
         middle = dot_nn(mixed[...], wa[...])
         middle = middle + jnp.concatenate(
             [rows[128:640].astype(f32), rows[768:].astype(f32)], 0
@@ -474,10 +683,12 @@
         normal[...] = base
         factor[...] = scale
         acts[...] = (base * norms[1:2] + norms[3:4]).astype(bf16)
+        for p in range(4):
+            pltpu.make_async_copy(in_mine.at[0, :, pl.ds(0, D)], win.at[0], sems.at[p]).wait()
 
     @pl.when(forward)
     def _():
-        inner = dot_nn(acts[...], win[0])
+        inner = dot_nn(acts[...], win[chunk])
         half = 0.5 + 0.5 * lax.erf(inner * 0.7071067811865476)
         slope[chunk] = half + inner * (jnp.exp(-0.5 * inner * inner) * 0.3989422804014327)
         bits = (inner * half).astype(bf16)
@@ -506,7 +717,7 @@
         keep_rows = owned()
         grad_inner = (dot_nt(grad_z[...], wout[...]) * slope[chunk]).astype(bf16)
         zeros = jnp.zeros_like(grad_inner)
-        grad_acts[...] += dot_nt(grad_inner, win[0])
+        grad_acts[...] += dot_nt(grad_inner, win[chunk])
         part = dot_tn(acts[...], jnp.where(keep_rows, grad_inner, zeros)).astype(bf16)
 
         @pl.when(late < 2)
@@ -517,10 +728,12 @@
         def _():
             win_keep[0] = part
 
-        part = dot_tn(hidden[chunk], jnp.where(keep_rows, grad_z[...], zeros)).astype(bf16)
-        first = core == 0
-        wout_keep[...] = jnp.where(first, part[:, :384], part[:, 384:])
-        wout_send[...] = jnp.where(first, part[:, 384:], part[:, :384])
+        part = dot_tn(hidden[chunk], jnp.where(keep_rows, grad_z[...], zeros))
+        part = part.reshape(8, 2, 2, 24, D)
+        for p in range(2):
+            even, odd = part[:, p, 0], part[:, p, 1]
+            wout_keep[p] = jnp.where(core == 0, even, odd).astype(bf16)
+            wout_send[p] = jnp.where(core == 0, odd, even).astype(bf16)
 
     @pl.when(step == 7)
     def _():
@@ -542,7 +755,7 @@
         ).astype(bf16)
 
 
-def feed(place, coef, rows, long_out, parts, shares, packed, globs, norms, wa, win, wout):
+def feed(place, coef, rows, long_out, parts, shares, packed, globs, norms, *weights):
     def chunk(t, place):
         late = jnp.maximum(t - 4, 0)
         core = place[1]
@@ -570,9 +783,11 @@
                 fixed((ROWS, 2 * D + 128)),
                 fixed((128, 2 * D)),
                 fixed((8, D)),
-                fixed((D, D)),
-                pl.BlockSpec((1, D, D), lambda t, place: (chunk(t, place), 0, 0)),
                 pl.BlockSpec((D, D), lambda t, place: (chunk(t, place), 0)),
+                ANY,
+                ANY,
+                ANY,
+                ANY,
             ],
             out_specs=[
                 fixed((640, D)),
@@ -583,8 +798,8 @@
                 fixed((D, D)),
                 pl.BlockSpec((1, D, D), lambda t, place: (jnp.clip(t - 4, 0, 1), 0, 0)),
                 pl.BlockSpec((1, D, D), lambda t, place: (jnp.clip(t - 6, 0, 1), 0, 0)),
-                pl.BlockSpec((D, 384), lambda t, place: (back_chunk(t, place), 0)),
-                pl.BlockSpec((D, 384), lambda t, place: (back_chunk(t, place), 0)),
+                pl.BlockSpec((2, 8, 24, D), lambda t, place: (0, back_chunk(t, place), 0, 0)),
+                pl.BlockSpec((2, 8, 24, D), lambda t, place: (0, back_chunk(t, place), 0, 0)),
                 fixed((8, D)),
             ],
             scratch_shapes=[
@@ -597,6 +812,10 @@
                 pltpu.VMEM((640, D), bf16),
                 pltpu.VMEM((640, D), f32),
                 pltpu.VMEM((640, 1), f32),
+                pltpu.VMEM((D, D), bf16),
+                pltpu.VMEM((4, D, D), bf16),
+                pltpu.SemaphoreType.DMA,
+                pltpu.SemaphoreType.DMA((4,)),
             ],
         ),
         out_shape=(
@@ -608,36 +827,57 @@
             jax.ShapeDtypeStruct((D, D), bf16),
             jax.ShapeDtypeStruct((2, D, D), bf16),
             jax.ShapeDtypeStruct((2, D, D), bf16),
-            jax.ShapeDtypeStruct((4 * D, 384), bf16),
-            jax.ShapeDtypeStruct((4 * D, 384), bf16),
+            jax.ShapeDtypeStruct((2, 32, 24, D), bf16),
+            jax.ShapeDtypeStruct((2, 32, 24, D), bf16),
             jax.ShapeDtypeStruct((8, D), f32),
         ),
         compiler_params=params(60),
+        cost_estimate=cost(43),
         name="feed",
-    )(place, coef, rows, long_out, parts, shares, packed, globs, norms, wa, win, wout)
+    )(place, coef, rows, long_out, parts, shares, packed, globs, norms, *weights)
 
 
 def project_back_kernel(
-    place, rows, acts, dq, dk, dv, norms, even, odd, middle_grad, wattn_grad,
-    send, keep, nat, left, right, globs, norm_grads,
+    place, rows, acts, dq, dk, dv, norms, middle_grad, wattn_grad, rel, norm_two, loss,
+    mine, other, send, keep, nat, left, right, globs, w, sems, small,
 ):
     core = place[1]
+    copies = load_quarters(core, mine, other, w, sems, 4)
     both = acts[...]
-    grads = (dot_tn(both, dq[...]), dot_tn(both, dk[...]), dot_tn(both, dv[...]))
-    parts = [part.astype(bf16) for part in grads] + [wattn_grad[...]]
+    grads = [dot_tn(both, ref[...]).reshape(32, 24, D).astype(bf16) for ref in (dq, dk, dv)]
+    grads.append(wattn_grad[...].astype(f32).reshape(32, 24, D).astype(bf16))
+    first, second = slice(0, 32), slice(32, 64)
 
     @pl.when(core == 0)
     def _():
-        keep[0], keep[1], send[0], send[1] = parts[0], parts[2], parts[1], parts[3]
+        keep[first], keep[second], send[first], send[second] = grads[0], grads[2], grads[1], grads[3]
 
     @pl.when(core == 1)
     def _():
-        keep[0], keep[1], send[0], send[1] = parts[1], parts[3], parts[0], parts[2]
-
-    grad = dot_nt(dq[...], even[0]) + dot_nt(dk[...], odd[0]) + dot_nt(dv[...], even[1])
+        keep[first], keep[second], send[first], send[second] = grads[1], grads[3], grads[0], grads[2]
+
+    for copy in copies:
+        copy.wait()
+    grad = dot_nt(dq[...], w[0]) + dot_nt(dk[...], w[1]) + dot_nt(dv[...], w[2])
     base, factor = normalise(rows[...].astype(f32))
-    norm_grads[0:1, :] = jnp.sum(grad * base, 0, keepdims=True)
-    norm_grads[1:2, :] = jnp.sum(grad, 0, keepdims=True)
+    small[0:1, :] = jnp.sum(grad * base, 0, keepdims=True)
+    small[1:2, :] = jnp.sum(grad, 0, keepdims=True)
+    small[2:4, :] = norm_two[0:2, :]
+    for n in range(HEADS):
+        low = 256 * (n % 3)
+        small[4 + n // 3 : 5 + n // 3, low : low + 256] = rel[n // 2, n % 2 : n % 2 + 1, :256]
+    lane = lax.broadcasted_iota(jnp.int32, (1, 128), 1)
+    line = jnp.where(lane == 24, loss[0:1, :], small[4:5, :128])
+    for n in range(2 * HEADS):
+        head, row = n % HEADS, 2 + 2 * (n // HEADS)
+        part = rel[head // 2, row + head % 2 : row + head % 2 + 1, :128]
+        line = jnp.where(lane == n, jnp.sum(part, 1, keepdims=True), line)
+    small[4:5, :128] = line
+    high, low = encode(small[...])
+    for ref in (keep, send):
+        ref[64, :8] = high
+        ref[64, 8:16] = low
+        ref[64, 16:] = jnp.zeros((8, D), bf16)
     scaled = grad * norms[0:1]
     first = jnp.mean(scaled, -1, keepdims=True)
     second = jnp.mean(scaled * base, -1, keepdims=True)
@@ -648,23 +888,28 @@
     globs[...] = back[768:]
 
 
-def project_back(place, rows, acts, dq, dk, dv, norms, even, odd, middle_grad, wattn_grad):
+def project_back(*operands):
     vm = pl.BlockSpec(memory_space=pltpu.VMEM)
     return pl.pallas_call(
         project_back_kernel,
-        in_specs=[SCALARS] + [vm] * 10,
+        in_specs=[SCALARS] + [vm] * 11 + [ANY] * 2,
+        scratch_shapes=[
+            pltpu.VMEM((4, D, D), bf16),
+            pltpu.SemaphoreType.DMA((4,)),
+            pltpu.VMEM((8, D), f32),
+        ],
         out_shape=(
-            jax.ShapeDtypeStruct((2, D, D), bf16),
-            jax.ShapeDtypeStruct((2, D, D), bf16),
+            jax.ShapeDtypeStruct((65, 24, D), bf16),
+            jax.ShapeDtypeStruct((65, 24, D), bf16),
             jax.ShapeDtypeStruct((ROWS, D), f32),
             jax.ShapeDtypeStruct((128, D), bf16),
             jax.ShapeDtypeStruct((128, D), bf16),
             jax.ShapeDtypeStruct((128, D), f32),
-            jax.ShapeDtypeStruct((8, D), f32),
         ),
         compiler_params=params(56),
+        cost_estimate=cost(15),
         name="project_back",
-    )(place, rows, acts, dq, dk, dv, norms, even, odd, middle_grad, wattn_grad)
+    )(*operands)
 
 
 def shards(
@@ -704,78 +949,33 @@
     slot_weight = ((slot_pos < my_lens[:, None]).reshape(ROWS) & (loss_mask == 1)).astype(jnp.int32)
     my_count = jnp.sum(slot_weight)
 
-    high = (my_count // 16).astype(bf16)
-    low = (my_count % 16).astype(bf16)
-    extra = jnp.concatenate(
+    device = lax.axis_index("dp") * 16 + member
+    spot = {
+        "x": ((device >> 4) & 3)[None],
+        "y": ((device >> 1) & 3)[None],
+        "z": (((device >> 6) & 1) * 2 + ((device >> 3) & 1))[None],
+    }
+    counted = jnp.stack([my_count // 16, my_count % 16]).astype(bf16)
+    extra = jnp.concatenate([norm_gains, norm_biases, jnp.broadcast_to(counted, (6, 2))], 1)
+    extra = jnp.broadcast_to(jnp.pad(extra, ((0, 6), (0, D - 6))), (4, 12, D))
+    opening = jnp.concatenate(
         [
-            norm_gains,
-            norm_biases,
-            jnp.broadcast_to(jnp.stack([high, low]), (6, 2)),
-            jnp.zeros((6, 122), bf16),
+            jnp.concatenate([w_qkv, w_attn], 1).reshape(6, 4, D).transpose(1, 0, 2),
+            w_in.reshape(6, 4, D).transpose(1, 0, 2),
+            extra,
+            jnp.broadcast_to(jnp.concatenate([glob_in, cot_glob])[None], (4, 64, D)),
         ],
         1,
     )
-    first = lax.all_gather(
-        jnp.concatenate([w_qkv, w_attn, extra], 1), "fsdp", axis_index_groups=QUADS, axis=0, tiled=True
-    )
-    second = lax.all_gather(w_in, "fsdp", axis_index_groups=QUADS, axis=0, tiled=True)
-    first_part = jnp.concatenate(
-        [lax.dynamic_slice_in_dim(first, quarter * D, D, 1), first[:, 4 * D :]], 1
-    )
-    second_part = lax.dynamic_slice_in_dim(second, quarter * D, D, 1)
-    mine_one = exchange(
-        jnp.broadcast_to(first_part[None], (64, 24, EXT)), BOTH, SAME_CORE
-    ).reshape(2, D, EXT)
-    other_one = swap(mine_one[..., :D])
-    side = mine_one[0, :, D:].astype(f32)
-    even = jnp.where(core == 0, mine_one[..., :D], other_one)
-    odd = jnp.where(core == 0, other_one, mine_one[..., :D])
-    wa = odd[1]
-    count = jnp.sum(
-        jnp.where(jnp.arange(D) % 6 == 0, side[:, 4] * 16.0 + side[:, 5], 0.0)
-    )
-    mine_two = exchange(
-        jnp.broadcast_to(second_part[None], (64, 24, D)), BOTH, SAME_CORE
-    ).reshape(2, D, D)
-    other_two = swap(mine_two)
-    even2 = jnp.where(core == 0, mine_two, other_two)
-    odd2 = jnp.where(core == 0, other_two, mine_two)
-    win = jnp.stack([even2[0], odd2[0], even2[1], odd2[1]])
-    half_keep = lax.dynamic_slice_in_dim(w_out, core * 384, 384, 1)
-    half_send = lax.dynamic_slice_in_dim(w_out, (1 - core) * 384, 384, 1)
-    half_got = swap(half_send)
-    pair_rows = jnp.where(
-        core == 0,
-        jnp.concatenate([half_keep, half_got], 0),
-        jnp.concatenate([half_got, half_keep], 0),
-    )
-    mine_three = exchange(jnp.broadcast_to(pair_rows[None], (64, 48, 384)), BOTH, SAME_CORE)
-    mine_three = mine_three.reshape(2, 32, 48, 384).transpose(1, 0, 2, 3).reshape(4 * D, 384)
-    other_three = swap(mine_three)
-    wout = jnp.where(
-        core == 0,
-        jnp.concatenate([mine_three, other_three], 1),
-        jnp.concatenate([other_three, mine_three], 1),
-    )
-
-    natural = reorder(long_in, inverse)
-    packed = jnp.concatenate(
-        [
-            cot_long,
-            teacher,
-            jnp.broadcast_to(slot_weight[:, None], (ROWS, 128)).astype(bf16),
-        ],
-        1,
-    )
-    packed = reorder(packed, inverse)
-    globs = lax.all_gather(
-        jnp.concatenate([glob_in, cot_glob], 1), "fsdp", axis_index_groups=QUADS, axis=0, tiled=True
-    )
-    left = lax.ppermute(natural[ROWS - BLOCK :], "fsdp", TO_RIGHT)
-    right = lax.ppermute(natural[:BLOCK], "fsdp", TO_LEFT)
-    norms = jnp.concatenate([side[:, :4].T, jnp.zeros((4, D), f32)], 0)
-    rows, acts, proj = project(left, natural, right, globs, norms, even, odd)
-
+    opening = exchange(opening, "fsdp", QUADS)
+    spread_long = exchange(pieces(after(long_in, opening)), "fsdp")
+    first = jnp.concatenate([opening[:, :6].reshape(24, D), opening[:, 12:18, :128].reshape(24, 128)], 1)
+    globs = jnp.concatenate([opening[:, 24:56], opening[:, 56:]], 2).reshape(GSEQ, 2 * D)
+    wout = jnp.concatenate([w_out, jnp.zeros((24, D), bf16)], 0)
+    wout = lax.all_gather(wout, "fsdp", axis=0, tiled=True)
+    wout = wout.reshape(16, 48, D)[:, :24].reshape(384, D)
+    natural = unpieces(exchange(spread_long[inverse], "fsdp"))
+    every = slice(None)
     start = quarter * ROWS
     place = jnp.stack([quarter, core]).astype(jnp.int32)
     key_pos = start - BLOCK + jnp.arange(768)
@@ -791,12 +991,85 @@
     line = jnp.full((HEADS, 512), MASKED, f32)
     line = lax.dynamic_update_slice(line, label_table.T, (0, 44)).reshape(6, 2, 512)
     table = rel_bias[LABELS:]
+    second = opening[:, 6:12].reshape(24, D)
+    (first,) = gather_axis(
+        spot["y"], first, "y", [(2, 2, 24, EXT)], lambda s: [(..., 0, (s & 1, s >> 1))], "first_y"
+    )
+    (second,) = gather_axis(
+        spot["z"], second, "z", [(2, 2, 24, D)], lambda s: [(..., 0, (s >> 1, s & 1))], "second_z"
+    )
+    first, second = lax.optimization_barrier((first, second))
+    (first,) = gather_axis(
+        spot["z"],
+        first,
+        "z",
+        [(2, 2, 2, 2, 24, EXT)],
+        lambda s: [(..., 0, (every, s >> 1, s & 1))],
+        "first_z",
+    )
+    (second,) = gather_axis(
+        spot["x"],
+        second,
+        "x",
+        [(2, 4, 2, 24, D)],
+        lambda s: [(..., 0, (every, s))],
+        "second_x",
+    )
+    first, second, natural, key_mask, self_mask, line = lax.optimization_barrier(
+        (first, second, natural, key_mask, self_mask, line)
+    )
+    left = lax.ppermute(natural[ROWS - BLOCK :], "fsdp", TO_RIGHT)
+    right = lax.ppermute(natural[:BLOCK], "fsdp", TO_LEFT)
+    first = first.reshape(2, 2, 4, 24, EXT)
+    parts = [first] + relay([first] * 3, "x")
+    packed = jnp.concatenate(
+        [
+            cot_long,
+            teacher,
+            jnp.broadcast_to(slot_weight[:, None], (ROWS, 128)).astype(bf16),
+        ],
+        1,
+    )
+    packed = exchange(pieces(after(packed, natural)), "fsdp")
+    *parts, left, right, packed = lax.optimization_barrier((*parts, left, right, packed))
+    (first,) = place_parts(
+        spot["x"],
+        parts,
+        [(2, 2, 4, 4, 24, EXT)],
+        lambda s: [(..., 0, (every, every, s))],
+        "first_x",
+    )
+    first = first.reshape(2, D, EXT)
+    first_other = swap(first)
+    wout = lax.all_gather(after(wout, first), "dp", axis=0, tiled=True)
+    second = after(second.reshape(16, 24, D), first_other)
+    second_parts = [second] + relay([second] * 3, "y")
+    side = first[0, :, D:].astype(f32)
+    whole_count = side[:, 4] * 16.0 + side[:, 5]
+    count = jnp.sum(jnp.where(jnp.arange(D) % 6 == 0, whole_count, 0.0))
+    norms = jnp.pad(side[:, :4].T, ((0, 4), (0, 0)))
+
+    packed = exchange(packed[inverse], "fsdp")
+    rows, acts, proj = project(place, left, natural, right, globs, norms, first, first_other)
     long_out, long_lse, part_out, part_lse = attend(place, table, line, key_mask, self_mask, proj)
 
     sent = jnp.concatenate(
         [part_out, split3(part_lse.reshape(HEADS, 128)), jnp.zeros((12, 128), bf16)], 0
     )
-    got = exchange(jnp.broadcast_to(sent[None], (4, 816, 128)), "fsdp", QUADS)
+    packed = after(packed, long_out)
+    got = exchange(jnp.broadcast_to(after(sent, packed)[None], (4, 816, 128)), "fsdp", QUADS)
+    *second_parts, _ = lax.optimization_barrier((*second_parts, long_out))
+    (second,) = place_parts(
+        spot["y"],
+        second_parts,
+        [(2, 16, 2, 24, D)],
+        lambda s: [(..., 0, (s & 1, every, s >> 1))],
+        "second_y",
+    )
+    second = second.reshape(2, D, D)
+    second_other = swap(second)
+
+    packed = unpieces(packed)
     lses = join3(got[:, D:])
     high = jnp.max(lses, 0)
     glob_lse = high + jnp.log(jnp.sum(jnp.exp(lses - high), 0))
@@ -816,49 +1089,99 @@
         wout_keep,
         norm_two,
     ) = feed(
-        place, (2.0 / count)[None], rows, long_out, got, shares, packed, globs, norms, wa, win, wout
-    )
-    loss_sum = loss_sum[0, 0]
+        place,
+        (2.0 / count)[None],
+        rows,
+        long_out,
+        got,
+        shares,
+        packed,
+        globs,
+        norms,
+        wout,
+        first,
+        first_other,
+        second,
+        second_other,
+    )
     dq, dk, dv, rel = attend_back(
         place, table, line, key_mask, self_mask, proj, grad_mixed, long_lse, glob_out, glob_lse
     )
-    one_send, one_keep, grad_nat, back_left, back_right, back_glob, norm_one = project_back(
-        place, rows, acts, dq, dk, dv, norms, even, odd, grad_middle, wattn_grad
-    )
-    grad_table = rel[:, :2, 44 : 44 + LABELS].reshape(HEADS, LABELS)
-    grad_own = jnp.sum(rel[:, 2:4, :128], -1).reshape(HEADS)
-    grad_other = jnp.sum(rel[:, 4:6, :128], -1).reshape(HEADS)
-    from_left = lax.ppermute(back_right, "fsdp", TO_RIGHT).astype(f32)
-    from_right = lax.ppermute(back_left, "fsdp", TO_LEFT).astype(f32)
-    grad_nat = grad_nat.at[:128].add(from_left).at[384:].add(from_right)
-    grad_long = reorder(grad_nat.astype(bf16), order).astype(f32)
-    glob_parts = exchange(back_glob.reshape(4 * 32, D), "fsdp", QUADS).reshape(4, 32, D)
+    (two,) = add_pairs([(win_keep, swap(win_send))], "add_cores")
+    three = fold_parts(
+        spot["z"],
+        [wout_keep.reshape(64, 24, D), swap(wout_send).reshape(64, 24, D)],
+        lambda s: [((g // 4 * 2 + (s >> 1)) * 4 + g % 4) * 4 + (s & 1) * 2 for g in range(8)],
+        2,
+        "three_z",
+    )
+    dq, two, *three = lax.optimization_barrier((dq, two, *three))
+    two = exchange(two.reshape(64, 24, D), BOTH, SAME_CORE)
+    one_send, one_keep, grad_nat, back_left, back_right, back_glob = project_back(
+        place,
+        rows,
+        acts,
+        dq,
+        dk,
+        dv,
+        norms,
+        grad_middle,
+        wattn_grad,
+        rel,
+        norm_two,
+        loss_sum,
+        first,
+        first_other,
+    )
+    one = scatter_axis(
+        spot["x"],
+        [one_keep, swap(one_send)],
+        "x",
+        lambda s: [(g * 4 + s) * 4 for g in range(4)],
+        4,
+        "one_x",
+    )
+    *three, _ = lax.optimization_barrier((*three, one[0]))
+    three = [three[0]] + relay(three[1:], "z")
+    three = scatter_axis(spot["x"], three, "x", lambda s: [s * 2, (4 + s) * 2], 2, "three_x")
+    three = scatter_axis(spot["y"], three, "y", lambda s: [(s & 1) * 2 + (s >> 1)], 1, "three_y")
+    out_grad = total_of(three)[0]
+    from_left = lax.ppermute(back_right, "fsdp", TO_RIGHT)
+    from_right = lax.ppermute(back_left, "fsdp", TO_LEFT)
+    both = pack_rows(result, grad_nat, from_left, from_right)
+    both = exchange(after(both, two), "fsdp")
+    out_long, grad_long = unpack_rows(exchange(both[order], "fsdp"))
+    two = jnp.sum(two.astype(f32), 0)
+    out_glob = lax.dynamic_slice_in_dim(result, ROWS + quarter * 32, 32, 0)
+    one = scatter_axis(
+        spot["z"], one, "z", lambda s: [s * 2, (4 + s) * 2], 2, "one_z"
+    )
+    one = scatter_axis(spot["y"], one, "y", lambda s: [(s & 1) * 2 + (s >> 1)], 1, "one_y")
+    small = [part[1, :8].astype(f32) + part[1, 8:16].astype(f32) for part in one]
+    small = (small[0] + small[1]) + (small[2] + small[3])
+    one = [part[0] for part in one]
+    closing = jnp.concatenate(
+        [
+            back_glob.reshape(4, 32, D),
+            total_of(one).reshape(4, 6, D),
+            two.reshape(4, 6, D),
+            jnp.zeros((4, 4, D), f32),
+        ],
+        1,
+    )
+    closing = exchange(after(closing, out_long), "fsdp", QUADS)
     grad_glob = lax.dynamic_slice_in_dim(grad_middle, ROWS + quarter * 32, 32, 0) + jnp.sum(
-        glob_parts, 0
-    )
-    out_long = reorder(result[:ROWS], order)
-    out_glob = lax.dynamic_slice_in_dim(result, ROWS + quarter * 32, 32, 0)
-
-    one = reduce_columns(one_keep, one_send)
-    two = reduce_columns(win_keep, win_send)
+        closing[:, :32], 0
+    )
+    one, two = closing[:, 32:38], closing[:, 38:44]
     qkv_grad = one[:3].transpose(1, 0, 2).reshape(6, 3 * D)
     attn_grad = one[3]
     in_grad = two.transpose(1, 0, 2).reshape(6, 4 * D)
-    total = (wout_keep.astype(f32) + swap(wout_send).astype(f32)).astype(bf16)
-    total = total.reshape(32, 2, 48, 384).transpose(1, 0, 2, 3).reshape(64, 48, 384)
-    mine = jnp.sum(exchange(total, BOTH, SAME_CORE).astype(f32), 0)
-    other = swap(mine)
-    halves = jnp.where(
-        core == 0, jnp.concatenate([mine, other], 1), jnp.concatenate([other, mine], 1)
-    )
-    out_grad = lax.dynamic_slice_in_dim(halves, core * 24, 24, 0)
-    label_grad = jnp.dot(picker.T, grad_table.T, precision=HIGHEST)
-    rel_grad = jnp.concatenate([label_grad, grad_own[None], grad_other[None]], 0)
-    norm_grads = jnp.stack([norm_one[0], norm_two[0], norm_one[1], norm_two[1]], 1)
-    rel_total, norm_total, loss_total = lax.psum((rel_grad, norm_grads, loss_sum), BOTH)
-    mine_norm = lax.dynamic_slice_in_dim(
-        norm_total, (lax.axis_index("dp") * 16 + member) * 6, 6, 0
-    )
+    bands = small[4:].reshape(HEADS, 256)[:, 44 : 44 + LABELS]
+    label_grad = jnp.dot(picker.T, bands.T, precision=HIGHEST)
+    rel_total = jnp.concatenate([label_grad, small[4:5, :HEADS], small[4:5, HEADS : 2 * HEADS]], 0)
+    loss_total = small[4, 24]
+    mine_norm = lax.dynamic_slice_in_dim(small[:4], device * 6, 6, 1).T
     return (
         out_long,
         out_glob,
@@ -869,8 +1192,8 @@
         attn_grad,
         in_grad,
         out_grad,
-        mine_norm[:, :2],
-        mine_norm[:, 2:],
+        mine_norm[:, 0::2],
+        mine_norm[:, 1::2],
         rel_total,
     )
 

time: 676 us -> 480 us (0.71)
  blocking collectives: 154 us -> 0 us
  waiting for transfers between devices: 183 us -> 136 us
  other arithmetic: 42.6 us -> 20.4 us
  Pallas kernels: 102 us -> 121 us
  between operations: 7.67 us -> 21 us
  local copies, waits for them, and re-layouts: 53.6 us -> 44.6 us
    all_to_all x18 -> x10, waiting for transfers between devices: 174 us -> 16.8 us  [exchange(): lax.all_to_all(value, axis, 0, 0, axis_index_groups=groups, tiled=True)]
    ppermute x2 -> x38, waiting for transfers between devices: 7.54 us -> 99.2 us  [the longest x36 81.3 us: relay(): lax.ppermute(value, BOTH, pairs)]
    psum x1 -> x0, blocking collectives: 81.5 us -> none  [shards(): lax.psum((rel_grad, norm_grads, loss_sum), BOTH)]
    all_gather x3 -> x0, blocking collectives: 72.6 us -> none  [the longest x1 25 us: shards(): lax.all_gather(w_in, 'fsdp', axis_index_groups=QUADS, axis=0, tiled=True)]
    ppermute x2 -> x38, starting transfers between devices: 5.72 us -> 63.7 us  [the longest x36 58.2 us: relay(): lax.ppermute(value, BOTH, pairs)]
    all_to_all x18 -> x10, starting transfers between devices: 108 us -> 52.6 us  [exchange(): lax.all_to_all(value, axis, 0, 0, axis_index_groups=groups, tiled=True)]
    pallas_call x2 -> x17, Pallas kernels: 25.2 us -> 42.6 us  [the longest x1 16.8 us: project_back(): pl.pallas_call(project_back_kernel, in_specs=[SCALARS] + [vm] * 11 + [ANY...]
    select_n x7 -> x2, other arithmetic: 14.6 us -> 0.04 us  [the longest x1 0.04 us: shards(): natural = unpieces(exchange(spread_long[inverse], 'fsdp'))]
  transfers between devices with their start and end apart: 30 -> 57, of which waited for: 17 -> 25; matrix products, arithmetic and copies ran while one was open for 11% -> 8% of each run, Pallas kernels for 4% -> 12%
where the time goes in v3:
time: 480 us; the launch traced here: 471 us
  waiting for transfers between devices  136 us (28%)
  starting transfers between devices  127 us (26%)
  Pallas kernels  121 us (25%)
  local copies, waits for them, and re-layouts  44.6 us (9%)
  between operations  21 us (4%)
  other arithmetic  20.4 us (4%)
    ppermute x36, waiting for transfers between devices, relay(): lax.ppermute(value, BOTH, pairs)  81.3 us
    ppermute x36, starting transfers between devices, relay(): lax.ppermute(value, BOTH, pairs)  58.2 us
    all_to_all x10, starting transfers between devices, exchange(): lax.all_to_all(value, axis, 0, 0, axis_index_groups=groups, tiled=True)  52.6 us
    pallas_call x1, Pallas kernels, feed(): pl.pallas_call(feed_kernel, grid_spec=pltpu.PrefetchScalarGridSpec(num_sc...  41.4 us
    pallas_call x1, Pallas kernels, attend_back(): pl.pallas_call(attend_back_kernel, grid=(6,), in_specs=[SCALARS, SCALARS,...  21.2 us
    unnamed x102, local copies, waits for them, and re-layouts  17.4 us
    all_to_all x10, waiting for transfers between devices, exchange(): lax.all_to_all(value, axis, 0, 0, axis_index_groups=groups, tiled=True)  16.8 us
    pallas_call x1, Pallas kernels, project_back(): pl.pallas_call(project_back_kernel, in_specs=[SCALARS] + [vm] * 11 + [ANY...  16.8 us
  transfers between devices with their start and end apart: 57, of which 25 were waited for; matrix products, arithmetic and copies ran while one was open for 8% of the time, Pallas kernels for 12%

profile of v3, /device:TPU:1, one launch (start us, length us, event | category | flops | bytes accessed | tf_op | source)
XLA Modules:
  0.0 471.2 jit_solution(5031255286649200448)
XLA Ops:
  18.7 4.9 %all-to-all-start = ((bf16[4,88,768]{2,1,0:T(8,128)(2,1)}), bf16[4,88,768]{2,1,0:T(8,128)(2,1)S(1)}, u32[]{:S(2)}, u32[]{:S(2)}) async-start(bf16[4,88,768]{2,1,0:T(8,128)(2,1)} %pad_maximum_fusion.1), calls=%async_computation | async-start | bytes 1081344 | tf_op jit(solution)/shard_map/all_to_all | solution.py:47
  26.2 5.5 %all-to-all-done = bf16[4,88,768]{2,1,0:T(8,128)(2,1)S(1)} async-done(((bf16[4,88,768]{2,1,0:T(8,128)(2,1)}), bf16[4,88,768]{2,1,0:T(8,128)(2,1)S(1)}, u32[]{:S(2)}, u32[]{:S(2)}) %all-to-all-start) | async-done | bytes 540704 | tf_op jit(solution)/shard_map/all_to_all | solution.py:47
  32.7 6.8 %all-to-all-start.1 = ((bf16[64,8,768]{2,1,0:T(8,128)(2,1)}), bf16[64,8,768]{2,1,0:T(8,128)(2,1)S(1)}, u32[]{:S(2)}, u32[]{:S(2)}) async-start(bf16[64,8,768]{2,1,0:T(8,128)(2,1)} %bitcast.15), calls=%async_computation.1 | async-start | bytes 1572864 | tf_op jit(solution)/shard_map/all_to_all | solution.py:47
  41.7 3.3 collective-permute-start.4
  46.4 2.4 collective-permute-start.1
  49.3 6.4 %collective-permute-start.2 = (bf16[24,896]{1,0:T(8,128)(2,1)S(1)}, bf16[24,896]{1,0:T(8,128)(2,1)S(1)}, u32[]{:S(2)}, u32[]{:S(2)}) collective-permute-start(bf16[24,896]{1,0:T(8,128)(2,1)S(1)} %constant_dynamic-update-slice_fusion.refs_0_), channel_id=1, source_target_pairs={{0,6},{1,7},{2,4},{3,5},{4,2},{5,3},{6,0},{7,1},{8,14},{9,15},{10,... | collective-permute-start | bytes 129032 | tf_op jit(solution)/shard_map/ppermute | solution.py:55
  57.7 5.2 %all-to-all-start.2 = ((bf16[64,8,768]{2,1,0:T(8,128)(2,1)}), bf16[64,8,768]{2,1,0:T(8,128)(2,1)S(1)}, u32[]{:S(2)}, u32[]{:S(2)}) async-start(bf16[64,8,768]{2,1,0:T(8,128)(2,1)} %gather_fusion), calls=%async_computation.2 | async-start | bytes 1572864 | tf_op jit(solution)/shard_map/all_to_all | solution.py:47
  63.0 3.1 collective-permute-start.10
  69.8 2.6 collective-permute-start.7
  74.4 3.9 collective-permute-done.6.refs_1_
  78.4 5.5 %collective-permute-done.7.refs_2_ = bf16[2,2,24,896]{3,2,1,0:T(8,128)(2,1)S(1)} collective-permute-done((bf16[2,2,24,896]{3,2,1,0:T(8,128)(2,1)S(1)}, bf16[2,2,24,896]{3,2,1,0:T(8,128)(2,1)S(1)}, u32[]{:S(2)}, u32[]{:S(2)}) %collective-permute-start.7) | collective-permute-done | bytes 172064 | tf_op jit(solution)/shard_map/ppermute | solution.py:55
  86.7 4.6 all-to-all-start.3
  96.4 4.1 collective-permute-start.15
  104.4 11.5 %collective-permute-done.15.left = bf16[128,768]{1,0:T(8,128)(2,1)S(1)} collective-permute-done((bf16[128,768]{1,0:T(8,128)(2,1)}, bf16[128,768]{1,0:T(8,128)(2,1)S(1)}, u32[]{:S(2)}, u32[]{:S(2)}) %collective-permute-start.15) | collective-permute-done | bytes 196640 | tf_op jit(solution)/shard_map/ppermute | solution.py:1021
  116.3 8.9 %collective-permute-done.13.refs_2_ = bf16[2,2,4,24,896]{4,3,2,1,0:T(8,128)(2,1)} collective-permute-done((bf16[2,2,4,24,896]{4,3,2,1,0:T(8,128)(2,1)S(1)}, bf16[2,2,4,24,896]{4,3,2,1,0:T(8,128)(2,1)}, u32[]{:S(2)}, u32[]{:S(2)}) %collective-permute-start.13) | collective-permute-done | bytes 688160 | tf_op jit(solution)/shard_map/ppermute | solution.py:55
  136.7 3.4 gather_fusion.1
  140.1 5.7 %all-to-all-start.4 = ((bf16[64,8,1664]{2,1,0:T(8,128)(2,1)}), bf16[64,8,1664]{2,1,0:T(8,128)(2,1)}, u32[]{:S(2)}, u32[]{:S(2)}) async-start(bf16[64,8,1664]{2,1,0:T(8,128)(2,1)} %gather_fusion.1), calls=%async_computation.4 | async-start | bytes 3407872 | tf_op jit(solution)/shard_map/all_to_all | solution.py:47
  147.3 2.4 collective-permute-start.19
  150.2 9.2 %project.1 = (bf16[896,768]{1,0:T(8,128)(2,1)S(1)}, bf16[896,768]{1,0:T(8,128)(2,1)}, bf16[896,2304]{1,0:T(8,128)(2,1)}) custom-call(s32[2]{0:T(128)S(1)} %pad_add_fusion.place, bf16[128,768]{1,0:T(8,128)(2,1)S(1)} %collective-permute-done.15.left, bf16[512,768]{1,0:T(8,128)(2,1)S(1)} %bitcast.90, bf16[128,768]{1,0:T(8,128)(2,1)} %collective-permute-done.16.right, ...), custom_call_target="tpu_custom_call" | custom-call | flops 9900000256 | bytes 32400000 | tf_op jit(solution)/shard_map/project/pallas_call | solution.py:305
  159.5 2.7 copy-done.24
  162.1 15.6 %attend.1 = (bf16[512,768]{1,0:T(8,128)(2,1)S(1)}, f32[6,4,256]{2,1,0:T(4,128)S(1)}, bf16[768,128]{1,0:T(8,128)(2,1)S(1)}, f32[6,1,256]{2,1,0:T(1,128)S(1)}) custom-call(s32[2]{0:T(128)S(1)} %pad_add_fusion.place, f32[2,12]{1,0:T(2,128)S(1)} %copy.75.table, f32[6,2,512]{2,1,0:T(2,128)S(1)} %reshape.347.line, f32[896,256]{1,0:T(8,128)S(1)} %broadcast_in_dim.129.key_mask, ...), custom_call_target="tpu_custom_call" | custom-call | flops 16499999744 | bytes 54000000 | tf_op jit(solution)/shard_map/attend/pallas_call | solution.py:408
  177.8 3.1 collective-permute-done.18.refs_1_
  180.9 12.6 %collective-permute-done.19.refs_2_ = bf16[16,24,768]{2,1,0:T(8,128)(2,1)S(1)} collective-permute-done((bf16[16,24,768]{2,1,0:T(8,128)(2,1)S(1)}, bf16[16,24,768]{2,1,0:T(8,128)(2,1)S(1)}, u32[]{:S(2)}, u32[]{:S(2)}) %collective-permute-start.19) | collective-permute-done | bytes 589856 | tf_op jit(solution)/shard_map/ppermute | solution.py:55
  197.3 3.7 all-to-all-start.5
  202.6 2.8 copy.70
  205.4 6.8 %all-to-all-done.5.parts = bf16[4,816,128]{2,1,0:T(8,128)(2,1)S(1)} async-done(((bf16[4,816,128]{2,1,0:T(8,128)(2,1)}), bf16[4,816,128]{2,1,0:T(8,128)(2,1)S(1)}, u32[]{:S(2)}, u32[]{:S(2)}) %all-to-all-start.5) | async-done | bytes 835616 | tf_op jit(solution)/shard_map/all_to_all | solution.py:47
  213.0 8.3 %all-gather.5.cloned.1.call-done.wout = bf16[3072,768]{1,0:T(8,128)(2,1)} async-done(((bf16[384,768]{1,0:T(8,128)(2,1)}), bf16[3072,768]{1,0:T(8,128)(2,1)}) %all-gather.5.cloned.1.call-update) | async-done | bytes 4718608 | tf_op jit(solution)/shard_map/all_gather | solution.py:1044
  221.4 41.4 %feed.1 = (bf16[640,768]{1,0:T(8,128)(2,1)}, f32[8,128]{1,0:T(8,128)}, bf16[768,128]{1,0:T(8,128)(2,1)}, f32[640,768]{1,0:T(8,128)}, bf16[640,768]{1,0:T(8,128)(...) custom-call(s32[2]{0:T(128)} %copy-done.14, ...), custom_call_target="tpu_custom_call" | custom-call | flops 47300001792 | bytes 154800000 | tf_op jit(solution)/shard_map/feed/pallas_call | solution.py:772
  266.7 21.2 %attend_back.1 = (bf16[896,768]{1,0:T(8,128)(2,1)S(1)}, bf16[896,768]{1,0:T(8,128)(2,1)S(1)}, bf16[896,768]{1,0:T(8,128)(2,1)}, f32[6,8,512]{2,1,0:T(8,128)S(1)}) custom-call(s32[2]{0:T(128)S(1)} %copy-done.15, f32[2,12]{1,0:T(2,128)S(1)} %copy.75.table, f32[6,2,512]{2,1,0:T(2,128)S(1)} %reshape.347.line, f32[896,256]{1,0:T(8,128)S(1)} %broadcast_in_dim.129.key_mask, ...), custom_call_target="tpu_custom_call" | custom-call | flops 23100000256 | bytes 75600000 | tf_op jit(solution)/shard_map/attend_back/pallas_call | solution.py:552
  288.0 4.3 three_z.1
  293.2 2.3 add_cores.1
  295.4 16.8 %project_back.1 = (bf16[65,24,768]{2,1,0:T(8,128)(2,1)}, bf16[65,24,768]{2,1,0:T(8,128)(2,1)}, f32[512,768]{1,0:T(8,128)}, bf16[128,768]{1,0:T(8,128)(2,1)}, bf1...) custom-call(s32[2]{0:T(128)} %copy-done.14, bf16[896,768]{1,0:T(8,128)(2,1)} %copy-done.25, ...), custom_call_target="tpu_custom_call" | custom-call | flops 16499999744 | bytes 54000000 | tf_op jit(solution)/shard_map/project_back/pallas_call | solution.py:893
  312.9 6.7 %all-to-all-start.6 = ((bf16[64,24,768]{2,1,0:T(8,128)(2,1)}), bf16[64,24,768]{2,1,0:T(8,128)(2,1)}, u32[]{:S(2)}, u32[]{:S(2)}) async-start(bf16[64,24,768]{2,1,0:T(8,128)(2,1)} %bitcast.44), calls=%async_computation.6 | async-start | bytes 4718592 | tf_op jit(solution)/shard_map/all_to_all | solution.py:47
  319.6 3.6 collective-permute-start.24
  331.9 16.0 %collective-permute-done.24.left_ref = bf16[128,768]{1,0:T(8,128)(2,1)S(1)} collective-permute-done((bf16[128,768]{1,0:T(8,128)(2,1)}, bf16[128,768]{1,0:T(8,128)(2,1)S(1)}, u32[]{:S(2)}, u32[]{:S(2)}) %collective-permute-start.24) | collective-permute-done | bytes 196640 | tf_op jit(solution)/shard_map/ppermute | solution.py:1149
  351.2 4.5 all-to-all-start.7
  356.3 2.4 collective-permute-start.37
  361.6 3.2 collective-permute-start.28
  369.1 22.3 %collective-permute-done.37.refs_2_ = bf16[16,24,768]{2,1,0:T(8,128)(2,1)} collective-permute-done((bf16[16,24,768]{2,1,0:T(8,128)(2,1)}, bf16[16,24,768]{2,1,0:T(8,128)(2,1)}, u32[]{:S(2)}, u32[]{:S(2)}) %collective-permute-start.37) | collective-permute-done | bytes 589856 | tf_op jit(solution)/shard_map/ppermute | solution.py:55
  394.3 2.6 collective-permute-start.39
  405.9 2.6 collective-permute-done.41.refs_3_
  410.1 3.2 gather_fusion.2
  413.3 5.9 %all-to-all-start.8 = ((bf16[64,8,1536]{2,1,0:T(8,128)(2,1)}), bf16[64,8,1536]{2,1,0:T(8,128)(2,1)S(1)}, u32[]{:S(2)}, u32[]{:S(2)}) async-start(bf16[64,8,1536]{2,1,0:T(8,128)(2,1)} %gather_fusion.2), calls=%async_computation.8 | async-start | bytes 3145728 | tf_op jit(solution)/shard_map/all_to_all | solution.py:47
  419.2 2.7 collective-permute-start.44
  423.4 2.6 collective-permute-start.35
  426.0 14.6 %collective-permute-done.44 = bf16[1,24,768]{2,1,0:T(8,128)(2,1)S(1)} collective-permute-done((bf16[1,24,768]{2,1,0:T(8,128)(2,1)S(1)}, bf16[1,24,768]{2,1,0:T(8,128)(2,1)S(1)}, u32[]{:S(2)}, u32[]{:S(2)}) %collective-permute-start.44) | collective-permute-done | bytes 36896 | tf_op jit(solution)/shard_map/ppermute | solution.py:55
  446.0 4.6 all-to-all-start.9
  454.8 4.5 all-to-all-done.9
  (282 shorter events, 107.0 us)
Async XLA Ops:
  18.7 13.0 %all-to-all-start = ((bf16[4,88,768]{2,1,0:T(8,128)(2,1)}), bf16[4,88,768]{2,1,0:T(8,128)(2,1)S(1)}, u32[]{:S(2)}, u32[]{:S(2)}) async-start(bf16[4,88,768]{2,1,0:T(8,128)(2,1)} %pad_maximum_fusion.1), calls=%async_computation | async-start | bytes 1081344 | tf_op jit(solution)/shard_map/all_to_all | solution.py:47
  23.5 78.9 %all-gather.3.cloned.1.call-start = ((), (), s32[]{:S(2)}) async-start(), calls=%async_computation.10 | async-start | bytes 1253376 | tf_op jit(solution)/shard_map/all_gather | solution.py:975
  32.7 23.5 %all-to-all-start.1 = ((bf16[64,8,768]{2,1,0:T(8,128)(2,1)}), bf16[64,8,768]{2,1,0:T(8,128)(2,1)S(1)}, u32[]{:S(2)}, u32[]{:S(2)}) async-start(bf16[64,8,768]{2,1,0:T(8,128)(2,1)} %bitcast.15), calls=%async_computation.1 | async-start | bytes 1572864 | tf_op jit(solution)/shard_map/all_to_all | solution.py:47
  41.7 14.5 %collective-permute-start.4 = (bf16[24,768]{1,0:T(8,128)(2,1)S(1)}, bf16[24,768]{1,0:T(8,128)(2,1)S(1)}, u32[]{:S(2)}, u32[]{:S(2)}) collective-permute-start(bf16[24,768]{1,0:T(8,128)(2,1)S(1)} %reshape.342.refs_0_), channel_id=1, source_target_pairs={{0,64},{1,65},{2,66},{3,67},{4,68},{5,69},{6,70},{7,71},{8,72},{9,... | collective-permute-start | bytes 110600 | tf_op jit(solution)/shard_map/ppermute | solution.py:55
  45.1 17.8 %collective-permute-start = (bf16[24,896]{1,0:T(8,128)(2,1)S(1)}, bf16[24,896]{1,0:T(8,128)(2,1)S(1)}, u32[]{:S(2)}, u32[]{:S(2)}) collective-permute-start(bf16[24,896]{1,0:T(8,128)(2,1)S(1)} %constant_dynamic-update-slice_fusion.refs_0_), channel_id=1, source_target_pairs={{0,2},{1,3},{2,0},{3,1},{4,6},{5,7},{6,4},{7,5},{8,10},{9,11},{10,... | collective-permute-start | bytes 129032 | tf_op jit(solution)/shard_map/ppermute | solution.py:55
  46.4 16.6 %collective-permute-start.1 = (bf16[24,896]{1,0:T(8,128)(2,1)S(1)}, bf16[24,896]{1,0:T(8,128)(2,1)S(1)}, u32[]{:S(2)}, u32[]{:S(2)}) collective-permute-start(bf16[24,896]{1,0:T(8,128)(2,1)S(1)} %constant_dynamic-update-slice_fusion.refs_0_), channel_id=1, source_target_pairs={{0,4},{1,5},{2,6},{3,7},{4,0},{5,1},{6,2},{7,3},{8,12},{9,13},{10,... | collective-permute-start | bytes 129032 | tf_op jit(solution)/shard_map/ppermute | solution.py:55
  49.3 13.6 %collective-permute-start.2 = (bf16[24,896]{1,0:T(8,128)(2,1)S(1)}, bf16[24,896]{1,0:T(8,128)(2,1)S(1)}, u32[]{:S(2)}, u32[]{:S(2)}) collective-permute-start(bf16[24,896]{1,0:T(8,128)(2,1)S(1)} %constant_dynamic-update-slice_fusion.refs_0_), channel_id=1, source_target_pairs={{0,6},{1,7},{2,4},{3,5},{4,2},{5,3},{6,0},{7,1},{8,14},{9,15},{10,... | collective-permute-start | bytes 129032 | tf_op jit(solution)/shard_map/ppermute | solution.py:55
  57.7 26.2 %all-to-all-start.2 = ((bf16[64,8,768]{2,1,0:T(8,128)(2,1)}), bf16[64,8,768]{2,1,0:T(8,128)(2,1)S(1)}, u32[]{:S(2)}, u32[]{:S(2)}) async-start(bf16[64,8,768]{2,1,0:T(8,128)(2,1)} %gather_fusion), calls=%async_computation.2 | async-start | bytes 1572864 | tf_op jit(solution)/shard_map/all_to_all | solution.py:47
  69.8 14.1 %collective-permute-start.7 = (bf16[2,2,24,896]{3,2,1,0:T(8,128)(2,1)S(1)}, bf16[2,2,24,896]{3,2,1,0:T(8,128)(2,1)S(1)}, u32[]{:S(2)}, u32[]{:S(2)}) collective-permute-start(bf16[2,2,24,896]{3,2,1,0:T(8,128)(2,1)S(1)} %first_y.1.refs_0_), channel_id=1, source_target_pairs={{0,64},{1,65},{2,66},{3,67},{4,68},{5,69},{6,70},{7,71},{8,72},{9,... | collective-permute-start | bytes 516104 | tf_op jit(solution)/shard_map/ppermute | solution.py:55
  72.3 11.5 %collective-permute-start.8 = (bf16[2,2,24,896]{3,2,1,0:T(8,128)(2,1)S(1)}, bf16[2,2,24,896]{3,2,1,0:T(8,128)(2,1)S(1)}, u32[]{:S(2)}, u32[]{:S(2)}) collective-permute-start(bf16[2,2,24,896]{3,2,1,0:T(8,128)(2,1)S(1)} %first_y.1.refs_0_), channel_id=1, source_target_pairs={{0,72},{1,73},{2,74},{3,75},{4,76},{5,77},{6,78},{7,79},{8,64},{9,... | collective-permute-start | bytes 516104 | tf_op jit(solution)/shard_map/ppermute | solution.py:55
  86.7 40.6 %all-to-all-start.3 = ((bf16[64,8,1664]{2,1,0:T(8,128)(2,1)}), bf16[64,8,1664]{2,1,0:T(8,128)(2,1)}, u32[]{:S(2)}, u32[]{:S(2)}) async-start(bf16[64,8,1664]{2,1,0:T(8,128)(2,1)} %bitcast.110), calls=%async_computation.3 | async-start | bytes 3407872 | tf_op jit(solution)/shard_map/all_to_all | solution.py:47
  91.2 130.1 %all-gather.5.cloned.1.call-start = ((), (), s32[]{:S(2)}) async-start(), calls=%async_computation.11 | async-start | bytes 5308416 | tf_op jit(solution)/shard_map/all_gather | solution.py:1044
  91.3 25.0 %collective-permute-start.12 = (bf16[2,2,4,24,896]{4,3,2,1,0:T(8,128)(2,1)S(1)}, bf16[2,2,4,24,896]{4,3,2,1,0:T(8,128)(2,1)S(1)}, u32[]{:S(2)}, u32[]{:S(2)}) collective-permute-start(bf16[2,2,4,24,896]{4,3,2,1,0:T(8,128)(2,1)S(1)} %bitcast.99), channel_id=1, source_target_pairs={{0,16},{1,17},{2,18},{3,19},{4,20},{5,21},{6,22},{7,23},{8,24},{9,... | collective-permute-start | bytes 2064392 | tf_op jit(solution)/shard_map/ppermute | solution.py:55
  93.1 32.1 %collective-permute-start.13 = (bf16[2,2,4,24,896]{4,3,2,1,0:T(8,128)(2,1)S(1)}, bf16[2,2,4,24,896]{4,3,2,1,0:T(8,128)(2,1)}, u32[]{:S(2)}, u32[]{:S(2)}) collective-permute-start(bf16[2,2,4,24,896]{4,3,2,1,0:T(8,128)(2,1)S(1)} %bitcast.100), channel_id=1, source_target_pairs={{0,32},{1,33},{2,34},{3,35},{4,36},{5,37},{6,38},{7,39},{8,40},{9,... | collective-permute-start | bytes 2064392 | tf_op jit(solution)/shard_map/ppermute | solution.py:55
  95.1 32.2 %collective-permute-start.14 = (bf16[2,2,4,24,896]{4,3,2,1,0:T(8,128)(2,1)S(1)}, bf16[2,2,4,24,896]{4,3,2,1,0:T(8,128)(2,1)}, u32[]{:S(2)}, u32[]{:S(2)}) collective-permute-start(bf16[2,2,4,24,896]{4,3,2,1,0:T(8,128)(2,1)S(1)} %bitcast.101), channel_id=1, source_target_pairs={{0,48},{1,49},{2,50},{3,51},{4,52},{5,53},{6,54},{7,55},{8,56},{9,... | collective-permute-start | bytes 2064392 | tf_op jit(solution)/shard_map/ppermute | solution.py:55
  96.4 19.5 %collective-permute-start.15 = (bf16[128,768]{1,0:T(8,128)(2,1)}, bf16[128,768]{1,0:T(8,128)(2,1)S(1)}, u32[]{:S(2)}, u32[]{:S(2)}) collective-permute-start(bf16[128,768]{1,0:T(8,128)(2,1)} %get-tuple-element.203), channel_id=1, source_target_pairs={{0,1},{1,2},{2,3},{4,5},{5,6},{6,7},{8,9},{9,10},{10,11},{12,13},{... | collective-permute-start | bytes 589832 | tf_op jit(solution)/shard_map/ppermute | solution.py:1021
  100.5 15.8 %collective-permute-start.16 = (bf16[128,768]{1,0:T(8,128)(2,1)}, bf16[128,768]{1,0:T(8,128)(2,1)}, u32[]{:S(2)}, u32[]{:S(2)}) collective-permute-start(bf16[128,768]{1,0:T(8,128)(2,1)} %get-tuple-element.202), channel_id=1, source_target_pairs={{1,0},{2,1},{3,2},{5,4},{6,5},{7,6},{9,8},{10,9},{11,10},{13,12},{... | collective-permute-start | bytes 589832 | tf_op jit(solution)/shard_map/ppermute | solution.py:1022
  130.4 15.4 %collective-permute-start.17 = (bf16[2,768,896]{2,1,0:T(8,128)(2,1)}, bf16[2,768,896]{2,1,0:T(8,128)(2,1)}, u32[]{:S(2)}, u32[]{:S(2)}) collective-permute-start(bf16[2,768,896]{2,1,0:T(8,128)(2,1)} %bitcast.93), channel_id=1, source_target_pairs={{0,1},{1,0},{2,3},{3,2},{4,5},{5,4},{6,7},{7,6},{8,9},{9,8},{10,11... | collective-permute-start | bytes 8257544 | tf_op jit(solution)/shard_map/ppermute | solution.py:51
  140.1 55.8 %all-to-all-start.4 = ((bf16[64,8,1664]{2,1,0:T(8,128)(2,1)}), bf16[64,8,1664]{2,1,0:T(8,128)(2,1)}, u32[]{:S(2)}, u32[]{:S(2)}) async-start(bf16[64,8,1664]{2,1,0:T(8,128)(2,1)} %gather_fusion.1), calls=%async_computation.4 | async-start | bytes 3407872 | tf_op jit(solution)/shard_map/all_to_all | solution.py:47
  145.8 35.1 %collective-permute-start.18 = (bf16[16,24,768]{2,1,0:T(8,128)(2,1)S(1)}, bf16[16,24,768]{2,1,0:T(8,128)(2,1)S(1)}, u32[]{:S(2)}, u32[]{:S(2)}) collective-permute-start(bf16[16,24,768]{2,1,0:T(8,128)(2,1)S(1)} %bitcast.103), channel_id=1, source_target_pairs={{0,2},{1,3},{2,0},{3,1},{4,6},{5,7},{6,4},{7,5},{8,10},{9,11},{10,... | collective-permute-start | bytes 1769480 | tf_op jit(solution)/shard_map/ppermute | solution.py:55
  147.3 46.2 %collective-permute-start.19 = (bf16[16,24,768]{2,1,0:T(8,128)(2,1)S(1)}, bf16[16,24,768]{2,1,0:T(8,128)(2,1)S(1)}, u32[]{:S(2)}, u32[]{:S(2)}) collective-permute-start(bf16[16,24,768]{2,1,0:T(8,128)(2,1)S(1)} %bitcast.104), channel_id=1, source_target_pairs={{0,4},{1,5},{2,6},{3,7},{4,0},{5,1},{6,2},{7,3},{8,12},{9,13},{10,... | collective-permute-start | bytes 1769480 | tf_op jit(solution)/shard_map/ppermute | solution.py:55
  149.7 43.8 %collective-permute-start.20 = (bf16[16,24,768]{2,1,0:T(8,128)(2,1)S(1)}, bf16[16,24,768]{2,1,0:T(8,128)(2,1)S(1)}, u32[]{:S(2)}, u32[]{:S(2)}) collective-permute-start(bf16[16,24,768]{2,1,0:T(8,128)(2,1)S(1)} %bitcast.105), channel_id=1, source_target_pairs={{0,6},{1,7},{2,4},{3,5},{4,2},{5,3},{6,0},{7,1},{8,14},{9,15},{10,... | collective-permute-start | bytes 1769480 | tf_op jit(solution)/shard_map/ppermute | solution.py:55
  195.1 18.0 %collective-permute-start.21 = (bf16[2,768,768]{2,1,0:T(8,128)(2,1)}, bf16[2,768,768]{2,1,0:T(8,128)(2,1)}, u32[]{:S(2)}, u32[]{:S(2)}) collective-permute-start(bf16[2,768,768]{2,1,0:T(8,128)(2,1)} %bitcast.39.in_mine), channel_id=1, source_target_pairs={{0,1},{1,0},{2,3},{3,2},{4,5},{5,4},{6,7},{7,6},{8,9},{9,8},{10,11... | collective-permute-start | bytes 7077896 | tf_op jit(solution)/shard_map/ppermute | solution.py:51
  197.3 14.9 %all-to-all-start.5 = ((bf16[4,816,128]{2,1,0:T(8,128)(2,1)}), bf16[4,816,128]{2,1,0:T(8,128)(2,1)S(1)}, u32[]{:S(2)}, u32[]{:S(2)}) async-start(bf16[4,816,128]{2,1,0:T(8,128)(2,1)} %broadcast_in_dim.137), calls=%async_computation.5 | async-start | bytes 1671168 | tf_op jit(solution)/shard_map/all_to_all | solution.py:47
  262.8 25.2 %collective-permute-start.23 = (bf16[2,32,24,768]{3,2,1,0:T(8,128)(2,1)}, bf16[2,32,24,768]{3,2,1,0:T(8,128)(2,1)}, u32[]{:S(2)}, u32[]{:S(2)}) collective-permute-start(bf16[2,32,24,768]{3,2,1,0:T(8,128)(2,1)} %get-tuple-element.142), channel_id=1, source_target_pairs={{0,1},{1,0},{2,3},{3,2},{4,5},{5,4},{6,7},{7,6},{8,9},{9,8},{10,11... | collective-permute-start | bytes 7077896 | tf_op jit(solution)/shard_map/ppermute | solution.py:51
  264.3 28.9 %collective-permute-start.22 = (bf16[2,768,768]{2,1,0:T(8,128)(2,1)}, bf16[2,768,768]{2,1,0:T(8,128)(2,1)S(1)}, u32[]{:S(2)}, u32[]{:S(2)}) collective-permute-start(bf16[2,768,768]{2,1,0:T(8,128)(2,1)} %get-tuple-element.140), channel_id=1, source_target_pairs={{0,1},{1,0},{2,3},{3,2},{4,5},{5,4},{6,7},{7,6},{8,9},{9,8},{10,11... | collective-permute-start | bytes 7077896 | tf_op jit(solution)/shard_map/ppermute | solution.py:51
  312.2 12.9 %collective-permute-start.26 = (bf16[65,24,768]{2,1,0:T(8,128)(2,1)}, bf16[65,24,768]{2,1,0:T(8,128)(2,1)S(1)}, u32[]{:S(2)}, u32[]{:S(2)}) collective-permute-start(bf16[65,24,768]{2,1,0:T(8,128)(2,1)} %get-tuple-element.162), channel_id=1, source_target_pairs={{0,1},{1,0},{2,3},{3,2},{4,5},{5,4},{6,7},{7,6},{8,9},{9,8},{10,11... | collective-permute-start | bytes 7188488 | tf_op jit(solution)/shard_map/ppermute | solution.py:51
  312.9 38.3 %all-to-all-start.6 = ((bf16[64,24,768]{2,1,0:T(8,128)(2,1)}), bf16[64,24,768]{2,1,0:T(8,128)(2,1)}, u32[]{:S(2)}, u32[]{:S(2)}) async-start(bf16[64,24,768]{2,1,0:T(8,128)(2,1)} %bitcast.44), calls=%async_computation.6 | async-start | bytes 4718592 | tf_op jit(solution)/shard_map/all_to_all | solution.py:47
  319.6 28.2 %collective-permute-start.24 = (bf16[128,768]{1,0:T(8,128)(2,1)}, bf16[128,768]{1,0:T(8,128)(2,1)S(1)}, u32[]{:S(2)}, u32[]{:S(2)}) collective-permute-start(bf16[128,768]{1,0:T(8,128)(2,1)} %get-tuple-element.156), channel_id=1, source_target_pairs={{0,1},{1,2},{2,3},{4,5},{5,6},{6,7},{8,9},{9,10},{10,11},{12,13},{... | collective-permute-start | bytes 589832 | tf_op jit(solution)/shard_map/ppermute | solution.py:1149
  323.2 26.6 %collective-permute-start.25 = (bf16[128,768]{1,0:T(8,128)(2,1)}, bf16[128,768]{1,0:T(8,128)(2,1)S(1)}, u32[]{:S(2)}, u32[]{:S(2)}) collective-permute-start(bf16[128,768]{1,0:T(8,128)(2,1)} %get-tuple-element.157), channel_id=1, source_target_pairs={{1,0},{2,1},{3,2},{5,4},{6,5},{7,6},{9,8},{10,9},{11,10},{13,12},{... | collective-permute-start | bytes 589832 | tf_op jit(solution)/shard_map/ppermute | solution.py:1150
  330.7 35.1 %collective-permute-start.36 = (bf16[16,24,768]{2,1,0:T(8,128)(2,1)}, bf16[16,24,768]{2,1,0:T(8,128)(2,1)}, u32[]{:S(2)}, u32[]{:S(2)}) collective-permute-start(bf16[16,24,768]{2,1,0:T(8,128)(2,1)} %get-tuple-element.183), channel_id=1, source_target_pairs={{0,8},{1,9},{2,10},{3,11},{4,12},{5,13},{6,14},{7,15},{8,0},{9,1},... | collective-permute-start | bytes 1769480 | tf_op jit(solution)/shard_map/ppermute | solution.py:55
  351.2 58.9 %all-to-all-start.7 = ((bf16[64,8,1536]{2,1,0:T(8,128)(2,1)}), bf16[64,8,1536]{2,1,0:T(8,128)(2,1)}, u32[]{:S(2)}, u32[]{:S(2)}) async-start(bf16[64,8,1536]{2,1,0:T(8,128)(2,1)} %pack_rows.1), calls=%async_computation.7 | async-start | bytes 3145728 | tf_op jit(solution)/shard_map/all_to_all | solution.py:47
  356.3 35.2 %collective-permute-start.37 = (bf16[16,24,768]{2,1,0:T(8,128)(2,1)}, bf16[16,24,768]{2,1,0:T(8,128)(2,1)}, u32[]{:S(2)}, u32[]{:S(2)}) collective-permute-start(bf16[16,24,768]{2,1,0:T(8,128)(2,1)} %get-tuple-element.184), channel_id=1, source_target_pairs={{0,64},{1,65},{2,66},{3,67},{4,68},{5,69},{6,70},{7,71},{8,72},{9,... | collective-permute-start | bytes 1769480 | tf_op jit(solution)/shard_map/ppermute | solution.py:55
  358.7 32.7 %collective-permute-start.38 = (bf16[16,24,768]{2,1,0:T(8,128)(2,1)}, bf16[16,24,768]{2,1,0:T(8,128)(2,1)}, u32[]{:S(2)}, u32[]{:S(2)}) collective-permute-start(bf16[16,24,768]{2,1,0:T(8,128)(2,1)} %get-tuple-element.185), channel_id=1, source_target_pairs={{0,72},{1,73},{2,74},{3,75},{4,76},{5,77},{6,78},{7,79},{8,64},{9,... | collective-permute-start | bytes 1769480 | tf_op jit(solution)/shard_map/ppermute | solution.py:55
  360.1 38.8 %collective-permute-start.27 = (bf16[17,24,768]{2,1,0:T(8,128)(2,1)S(1)}, bf16[17,24,768]{2,1,0:T(8,128)(2,1)S(1)}, u32[]{:S(2)}, u32[]{:S(2)}) collective-permute-start(bf16[17,24,768]{2,1,0:T(8,128)(2,1)S(1)} %copy-done.9), channel_id=1, source_target_pairs={{0,16},{1,17},{2,18},{3,19},{4,20},{5,21},{6,22},{7,23},{8,24},{9,... | collective-permute-start | bytes 1880072 | tf_op jit(solution)/shard_map/ppermute | solution.py:55
  361.6 37.8 %collective-permute-start.28 = (bf16[17,24,768]{2,1,0:T(8,128)(2,1)S(1)}, bf16[17,24,768]{2,1,0:T(8,128)(2,1)}, u32[]{:S(2)}, u32[]{:S(2)}) collective-permute-start(bf16[17,24,768]{2,1,0:T(8,128)(2,1)S(1)} %copy-done.7), channel_id=1, source_target_pairs={{0,32},{1,33},{2,34},{3,35},{4,36},{5,37},{6,38},{7,39},{8,40},{9,... | collective-permute-start | bytes 1880072 | tf_op jit(solution)/shard_map/ppermute | solution.py:55
  365.8 33.6 %collective-permute-start.29 = (bf16[17,24,768]{2,1,0:T(8,128)(2,1)S(1)}, bf16[17,24,768]{2,1,0:T(8,128)(2,1)}, u32[]{:S(2)}, u32[]{:S(2)}) collective-permute-start(bf16[17,24,768]{2,1,0:T(8,128)(2,1)S(1)} %copy-done.5), channel_id=1, source_target_pairs={{0,48},{1,49},{2,50},{3,51},{4,52},{5,53},{6,54},{7,55},{8,56},{9,... | collective-permute-start | bytes 1880072 | tf_op jit(solution)/shard_map/ppermute | solution.py:55
  401.6 17.6 %collective-permute-start.30 = (bf16[5,24,768]{2,1,0:T(8,128)(2,1)S(1)}, bf16[5,24,768]{2,1,0:T(8,128)(2,1)S(1)}, u32[]{:S(2)}, u32[]{:S(2)}) collective-permute-start(bf16[5,24,768]{2,1,0:T(8,128)(2,1)S(1)} %get-tuple-element.168), channel_id=1, source_target_pairs={{0,8},{1,9},{2,10},{3,11},{4,12},{5,13},{6,14},{7,15},{8,0},{9,1},... | collective-permute-start | bytes 552968 | tf_op jit(solution)/shard_map/ppermute | solution.py:55
  402.0 19.9 %collective-permute-start.31 = (bf16[5,24,768]{2,1,0:T(8,128)(2,1)S(1)}, bf16[5,24,768]{2,1,0:T(8,128)(2,1)S(1)}, u32[]{:S(2)}, u32[]{:S(2)}) collective-permute-start(bf16[5,24,768]{2,1,0:T(8,128)(2,1)S(1)} %get-tuple-element.169), channel_id=1, source_target_pairs={{0,64},{1,65},{2,66},{3,67},{4,68},{5,69},{6,70},{7,71},{8,72},{9,... | collective-permute-start | bytes 552968 | tf_op jit(solution)/shard_map/ppermute | solution.py:55
  403.3 18.6 %collective-permute-start.32 = (bf16[5,24,768]{2,1,0:T(8,128)(2,1)S(1)}, bf16[5,24,768]{2,1,0:T(8,128)(2,1)S(1)}, u32[]{:S(2)}, u32[]{:S(2)}) collective-permute-start(bf16[5,24,768]{2,1,0:T(8,128)(2,1)S(1)} %get-tuple-element.170), channel_id=1, source_target_pairs={{0,72},{1,73},{2,74},{3,75},{4,76},{5,77},{6,78},{7,79},{8,64},{9,... | collective-permute-start | bytes 552968 | tf_op jit(solution)/shard_map/ppermute | solution.py:55
  408.5 14.9 %collective-permute-start.42 = (bf16[1,24,768]{2,1,0:T(8,128)(2,1)S(1)}, bf16[1,24,768]{2,1,0:T(8,128)(2,1)S(1)}, u32[]{:S(2)}, u32[]{:S(2)}) collective-permute-start(bf16[1,24,768]{2,1,0:T(8,128)(2,1)S(1)} %get-tuple-element.191), channel_id=1, source_target_pairs={{0,2},{1,3},{2,0},{3,1},{4,6},{5,7},{6,4},{7,5},{8,10},{9,11},{10,... | collective-permute-start | bytes 110600 | tf_op jit(solution)/shard_map/ppermute | solution.py:55
  408.9 17.1 %collective-permute-start.43 = (bf16[1,24,768]{2,1,0:T(8,128)(2,1)S(1)}, bf16[1,24,768]{2,1,0:T(8,128)(2,1)S(1)}, u32[]{:S(2)}, u32[]{:S(2)}) collective-permute-start(bf16[1,24,768]{2,1,0:T(8,128)(2,1)S(1)} %get-tuple-element.192), channel_id=1, source_target_pairs={{0,4},{1,5},{2,6},{3,7},{4,0},{5,1},{6,2},{7,3},{8,12},{9,13},{10,... | collective-permute-start | bytes 110600 | tf_op jit(solution)/shard_map/ppermute | solution.py:55
  413.3 31.2 %all-to-all-start.8 = ((bf16[64,8,1536]{2,1,0:T(8,128)(2,1)}), bf16[64,8,1536]{2,1,0:T(8,128)(2,1)S(1)}, u32[]{:S(2)}, u32[]{:S(2)}) async-start(bf16[64,8,1536]{2,1,0:T(8,128)(2,1)} %gather_fusion.2), calls=%async_computation.8 | async-start | bytes 3145728 | tf_op jit(solution)/shard_map/all_to_all | solution.py:47
  419.2 21.4 %collective-permute-start.44 = (bf16[1,24,768]{2,1,0:T(8,128)(2,1)S(1)}, bf16[1,24,768]{2,1,0:T(8,128)(2,1)S(1)}, u32[]{:S(2)}, u32[]{:S(2)}) collective-permute-start(bf16[1,24,768]{2,1,0:T(8,128)(2,1)S(1)} %get-tuple-element.193), channel_id=1, source_target_pairs={{0,6},{1,7},{2,4},{3,5},{4,2},{5,3},{6,0},{7,1},{8,14},{9,15},{10,... | collective-permute-start | bytes 110600 | tf_op jit(solution)/shard_map/ppermute | solution.py:55
  422.1 19.5 %collective-permute-start.33 = (bf16[2,24,768]{2,1,0:T(8,128)(2,1)S(1)}, bf16[2,24,768]{2,1,0:T(8,128)(2,1)S(1)}, u32[]{:S(2)}, u32[]{:S(2)}) collective-permute-start(bf16[2,24,768]{2,1,0:T(8,128)(2,1)S(1)} %get-tuple-element.172), channel_id=1, source_target_pairs={{0,2},{1,3},{2,0},{3,1},{4,6},{5,7},{6,4},{7,5},{8,10},{9,11},{10,... | collective-permute-start | bytes 221192 | tf_op jit(solution)/shard_map/ppermute | solution.py:55
  422.2 21.2 %collective-permute-start.34 = (bf16[2,24,768]{2,1,0:T(8,128)(2,1)S(1)}, bf16[2,24,768]{2,1,0:T(8,128)(2,1)S(1)}, u32[]{:S(2)}, u32[]{:S(2)}) collective-permute-start(bf16[2,24,768]{2,1,0:T(8,128)(2,1)S(1)} %get-tuple-element.173), channel_id=1, source_target_pairs={{0,4},{1,5},{2,6},{3,7},{4,0},{5,1},{6,2},{7,3},{8,12},{9,13},{10,... | collective-permute-start | bytes 221192 | tf_op jit(solution)/shard_map/ppermute | solution.py:55
  423.4 19.9 %collective-permute-start.35 = (bf16[2,24,768]{2,1,0:T(8,128)(2,1)S(1)}, bf16[2,24,768]{2,1,0:T(8,128)(2,1)S(1)}, u32[]{:S(2)}, u32[]{:S(2)}) collective-permute-start(bf16[2,24,768]{2,1,0:T(8,128)(2,1)S(1)} %get-tuple-element.174), channel_id=1, source_target_pairs={{0,6},{1,7},{2,4},{3,5},{4,2},{5,3},{6,0},{7,1},{8,14},{9,15},{10,... | collective-permute-start | bytes 221192 | tf_op jit(solution)/shard_map/ppermute | solution.py:55
  446.0 13.3 %all-to-all-start.9 = ((f32[4,48,768]{2,1,0:T(8,128)}), f32[4,48,768]{2,1,0:T(8,128)S(1)}, u32[]{:S(2)}, u32[]{:S(2)}) async-start(f32[4,48,768]{2,1,0:T(8,128)} %maximum_maximum_fusion), calls=%async_computation.9 | async-start | bytes 1179648 | tf_op jit(solution)/shard_map/all_to_all | solution.py:47
  (58 other events, 594.5 us)
Sparse Core Ops, SparseCore 0:
  26.6 40.8 all-gather.2
  130.5 90.7 all-gather.4

commit v4 on v3

--- a/solution.py
+++ b/solution.py
@@ -283,28 +283,54 @@
     return copies
 
 
+def quarter_copy(step, core, mine, target, sems):
+    slot = 2 * (step // 2) + jnp.where(step % 2 == core, 0, 1)
+    return pltpu.make_async_copy(mine.at[0, :, pl.ds(0, D)], target.at[step], sems.at[slot])
+
+
 def project_kernel(
     place, left, nat, right, globs, norms, mine, other, rows_out, acts_out, proj_out, w, sems
 ):
-    copies = load_quarters(place[1], mine, other, w, sems, 4)
-    rows_out[:128] = left[...]
-    rows_out[128:640] = nat[...]
-    rows_out[640:768] = right[...]
-    rows_out[768:] = globs[:, :D]
-    normal, _ = normalise(rows_out[...].astype(f32))
-    acts = (normal * norms[0:1] + norms[2:3]).astype(bf16)
-    acts_out[...] = acts
-    for copy in copies:
-        copy.wait()
-    for i in range(3):
-        proj_out[:, i * D : i * D + D] = dot_nn(acts, w[i]).astype(bf16)
+    step = pl.program_id(0)
+    core = place[1]
+
+    @pl.when(step == 0)
+    def _():
+        load_quarters(core, mine, other, w, sems, 4)
+        rows_out[:128] = left[...]
+        rows_out[128:640] = nat[...]
+        rows_out[640:768] = right[...]
+        rows_out[768:] = globs[:, :D]
+        normal, _ = normalise(rows_out[...].astype(f32))
+        acts_out[...] = (normal * norms[0:1] + norms[2:3]).astype(bf16)
+
+    quarter_copy(step, core, mine, w, sems).wait()
+    proj_out[...] = dot_nn(acts_out[...], w[step]).astype(bf16)
+
+    @pl.when(step == 2)
+    def _():
+        quarter_copy(step + 1, core, mine, w, sems).wait()
 
 
 def project(place, left, nat, right, globs, norms, mine, other):
-    vm = pl.BlockSpec(memory_space=pltpu.VMEM)
     return pl.pallas_call(
         project_kernel,
-        in_specs=[SCALARS] + [vm] * 5 + [ANY] * 2,
+        grid=(3,),
+        in_specs=[
+            SCALARS,
+            whole((128, D)),
+            whole((ROWS, D)),
+            whole((128, D)),
+            whole((128, 2 * D)),
+            whole((8, D)),
+            ANY,
+            ANY,
+        ],
+        out_specs=[
+            whole((EXT, D)),
+            whole((EXT, D)),
+            pl.BlockSpec((EXT, D), lambda i: (0, i)),
+        ],
         scratch_shapes=[pltpu.VMEM((4, D, D), bf16), pltpu.SemaphoreType.DMA((4,))],
         out_shape=(
             jax.ShapeDtypeStruct((EXT, D), bf16),
@@ -462,9 +488,7 @@
     lse,
     glob_out,
     glob_lse,
-    dq,
-    dk,
-    dv,
+    grads,
     rel,
     band,
     band_sum,
@@ -482,8 +506,8 @@
     value_sum[...] = jnp.zeros_like(value_sum)
     owned_sum = jnp.zeros((1, 256), f32)
     other_sum = jnp.zeros((1, 256), f32)
-    dq[:128] = jnp.zeros((128, 128), bf16)
-    dq[640:768] = jnp.zeros((128, 128), bf16)
+    grads[0, :128] = jnp.zeros((128, 128), bf16)
+    grads[0, 640:768] = jnp.zeros((128, 128), bf16)
     for j in range(4):
         low = 128 * j
         query = stack_heads(q[128 + low : 256 + low, :] * 0.125)
@@ -504,7 +528,7 @@
         key_sum[768:, :] += dot_nn(far_d, query)
         value_sum[768:, :] += dot_nn(far.astype(bf16), back)
         got = dot_nn(keys[:, low : low + 384], near_d) + dot_nn(keys[:, 768:], far_d)
-        dq[128 + low : 256 + low, :] = (merge_heads(got) * 0.125).astype(bf16)
+        grads[0, 128 + low : 256 + low, :] = (merge_heads(got) * 0.125).astype(bf16)
         band_sum[...] += near_d.astype(f32)
         far_d = far_d.astype(f32)
         owned_sum += jnp.sum(jnp.where(owned, far_d, 0.0), 0, keepdims=True)
@@ -534,12 +558,12 @@
     key_sum[768:, :] += dot_nn(far_d, query)
     value_sum[768:, :] += dot_nn(far.astype(bf16), back)
     got = dot_nn(keys[:, 128:640], near_d) + dot_nn(keys[:, 768:], far_d)
-    dq[768:, :] = (merge_heads(got) * 0.125).astype(bf16)
+    grads[0, 768:, :] = (merge_heads(got) * 0.125).astype(bf16)
     near_d = near_d.astype(f32)
     owned_sum += jnp.sum(jnp.where(owned, near_d, 0.0), 0, keepdims=True)
     other_sum += jnp.sum(jnp.where(owned, 0.0, near_d), 0, keepdims=True)
-    dk[...] = key_sum[...].astype(bf16)
-    dv[...] = value_sum[...].astype(bf16)
+    grads[1] = key_sum[...].astype(bf16)
+    grads[2] = value_sum[...].astype(bf16)
     rel[0] = jnp.zeros((8, 512), f32)
     for head in range(2):
         lanes = slice(128 * head, 128 * head + 128)
@@ -567,15 +591,11 @@
             pl.BlockSpec((1, 1, 256), lambda h: (h, 0, 0)),
         ],
         out_specs=[
-            column(EXT, 0),
-            column(EXT, 0),
-            column(EXT, 0),
+            pl.BlockSpec((3, EXT, 128), lambda h: (0, 0, h)),
             pl.BlockSpec((1, 8, 512), lambda h: (h, 0, 0)),
         ],
         out_shape=(
-            jax.ShapeDtypeStruct((EXT, D), bf16),
-            jax.ShapeDtypeStruct((EXT, D), bf16),
-            jax.ShapeDtypeStruct((EXT, D), bf16),
+            jax.ShapeDtypeStruct((3, EXT, D), bf16),
             jax.ShapeDtypeStruct((6, 8, 512), f32),
         ),
         scratch_shapes=[
@@ -613,8 +633,7 @@
     wattn_grad,
     win_send,
     win_keep,
-    wout_send,
-    wout_keep,
+    wout_grad,
     norm_grads,
     mixed,
     acts,
@@ -729,11 +748,9 @@
             win_keep[0] = part
 
         part = dot_tn(hidden[chunk], jnp.where(keep_rows, grad_z[...], zeros))
-        part = part.reshape(8, 2, 2, 24, D)
-        for p in range(2):
-            even, odd = part[:, p, 0], part[:, p, 1]
-            wout_keep[p] = jnp.where(core == 0, even, odd).astype(bf16)
-            wout_send[p] = jnp.where(core == 0, odd, even).astype(bf16)
+        part = part.reshape(2, 16, 24, D).astype(bf16)
+        for i in range(2):
+            wout_grad[:, i] = part[i]
 
     @pl.when(step == 7)
     def _():
@@ -798,8 +815,7 @@
                 fixed((D, D)),
                 pl.BlockSpec((1, D, D), lambda t, place: (jnp.clip(t - 4, 0, 1), 0, 0)),
                 pl.BlockSpec((1, D, D), lambda t, place: (jnp.clip(t - 6, 0, 1), 0, 0)),
-                pl.BlockSpec((2, 8, 24, D), lambda t, place: (0, back_chunk(t, place), 0, 0)),
-                pl.BlockSpec((2, 8, 24, D), lambda t, place: (0, back_chunk(t, place), 0, 0)),
+                pl.BlockSpec((16, 2, 24, D), lambda t, place: (0, back_chunk(t, place), 0, 0)),
                 fixed((8, D)),
             ],
             scratch_shapes=[
@@ -827,8 +843,7 @@
             jax.ShapeDtypeStruct((D, D), bf16),
             jax.ShapeDtypeStruct((2, D, D), bf16),
             jax.ShapeDtypeStruct((2, D, D), bf16),
-            jax.ShapeDtypeStruct((2, 32, 24, D), bf16),
-            jax.ShapeDtypeStruct((2, 32, 24, D), bf16),
+            jax.ShapeDtypeStruct((16, 8, 24, D), bf16),
             jax.ShapeDtypeStruct((8, D), f32),
         ),
         compiler_params=params(60),
@@ -837,78 +852,140 @@
     )(place, coef, rows, long_out, parts, shares, packed, globs, norms, *weights)
 
 
-def project_back_kernel(
-    place, rows, acts, dq, dk, dv, norms, middle_grad, wattn_grad, rel, norm_two, loss,
-    mine, other, send, keep, nat, left, right, globs, w, sems, small,
+def input_grad_kernel(
+    place, rows, grads, norms, middle_grad, rel, norm_two, loss, mine, other,
+    nat, left, right, globs, totals, w, sems, grad, small,
 ):
+    step = pl.program_id(0)
     core = place[1]
-    copies = load_quarters(core, mine, other, w, sems, 4)
-    both = acts[...]
-    grads = [dot_tn(both, ref[...]).reshape(32, 24, D).astype(bf16) for ref in (dq, dk, dv)]
-    grads.append(wattn_grad[...].astype(f32).reshape(32, 24, D).astype(bf16))
-    first, second = slice(0, 32), slice(32, 64)
-
-    @pl.when(core == 0)
+
+    @pl.when(step == 0)
     def _():
-        keep[first], keep[second], send[first], send[second] = grads[0], grads[2], grads[1], grads[3]
-
-    @pl.when(core == 1)
+        load_quarters(core, mine, other, w, sems, 4)
+        grad[...] = jnp.zeros_like(grad)
+        small[2:4, :] = norm_two[0:2, :]
+        for n in range(HEADS):
+            low = 256 * (n % 3)
+            small[4 + n // 3 : 5 + n // 3, low : low + 256] = rel[n // 2, n % 2 : n % 2 + 1, :256]
+        lane = lax.broadcasted_iota(jnp.int32, (1, 128), 1)
+        line = jnp.where(lane == 24, loss[0:1, :], small[4:5, :128])
+        for n in range(2 * HEADS):
+            head, row = n % HEADS, 2 + 2 * (n // HEADS)
+            part = rel[head // 2, row + head % 2 : row + head % 2 + 1, :128]
+            line = jnp.where(lane == n, jnp.sum(part, 1, keepdims=True), line)
+        small[4:5, :128] = line
+
+    quarter_copy(step, core, mine, w, sems).wait()
+    grad[...] += dot_nt(grads[0], w[step])
+
+    @pl.when(step == 2)
     def _():
-        keep[first], keep[second], send[first], send[second] = grads[1], grads[3], grads[0], grads[2]
-
-    for copy in copies:
-        copy.wait()
-    grad = dot_nt(dq[...], w[0]) + dot_nt(dk[...], w[1]) + dot_nt(dv[...], w[2])
-    base, factor = normalise(rows[...].astype(f32))
-    small[0:1, :] = jnp.sum(grad * base, 0, keepdims=True)
-    small[1:2, :] = jnp.sum(grad, 0, keepdims=True)
-    small[2:4, :] = norm_two[0:2, :]
-    for n in range(HEADS):
-        low = 256 * (n % 3)
-        small[4 + n // 3 : 5 + n // 3, low : low + 256] = rel[n // 2, n % 2 : n % 2 + 1, :256]
-    lane = lax.broadcasted_iota(jnp.int32, (1, 128), 1)
-    line = jnp.where(lane == 24, loss[0:1, :], small[4:5, :128])
-    for n in range(2 * HEADS):
-        head, row = n % HEADS, 2 + 2 * (n // HEADS)
-        part = rel[head // 2, row + head % 2 : row + head % 2 + 1, :128]
-        line = jnp.where(lane == n, jnp.sum(part, 1, keepdims=True), line)
-    small[4:5, :128] = line
-    high, low = encode(small[...])
-    for ref in (keep, send):
-        ref[64, :8] = high
-        ref[64, 8:16] = low
-        ref[64, 16:] = jnp.zeros((8, D), bf16)
-    scaled = grad * norms[0:1]
-    first = jnp.mean(scaled, -1, keepdims=True)
-    second = jnp.mean(scaled * base, -1, keepdims=True)
-    back = factor * (scaled - first - base * second)
-    nat[...] = back[128:640] + middle_grad[:ROWS]
-    left[...] = back[:128].astype(bf16)
-    right[...] = back[640:768].astype(bf16)
-    globs[...] = back[768:]
-
-
-def project_back(*operands):
-    vm = pl.BlockSpec(memory_space=pltpu.VMEM)
+        quarter_copy(step + 1, core, mine, w, sems).wait()
+        base, factor = normalise(rows[...].astype(f32))
+        total = grad[...]
+        small[0:1, :] = jnp.sum(total * base, 0, keepdims=True)
+        small[1:2, :] = jnp.sum(total, 0, keepdims=True)
+        high, low = encode(small[...])
+        totals[0, :8] = high
+        totals[0, 8:16] = low
+        totals[0, 16:] = jnp.zeros((8, D), bf16)
+        scaled = total * norms[0:1]
+        first = jnp.mean(scaled, -1, keepdims=True)
+        second = jnp.mean(scaled * base, -1, keepdims=True)
+        back = factor * (scaled - first - base * second)
+        nat[...] = back[128:640] + middle_grad[:ROWS]
+        left[...] = back[:128].astype(bf16)
+        right[...] = back[640:768].astype(bf16)
+        globs[...] = back[768:]
+
+
+def input_grad(*operands):
     return pl.pallas_call(
-        project_back_kernel,
-        in_specs=[SCALARS] + [vm] * 11 + [ANY] * 2,
+        input_grad_kernel,
+        grid=(3,),
+        in_specs=[
+            SCALARS,
+            whole((EXT, D)),
+            pl.BlockSpec((1, EXT, D), lambda i: (i, 0, 0)),
+            whole((8, D)),
+            whole((640, D)),
+            whole((6, 8, 512)),
+            whole((8, D)),
+            whole((8, 128)),
+            ANY,
+            ANY,
+        ],
+        out_specs=[
+            whole((ROWS, D)),
+            whole((128, D)),
+            whole((128, D)),
+            whole((128, D)),
+            whole((1, 24, D)),
+        ],
         scratch_shapes=[
             pltpu.VMEM((4, D, D), bf16),
             pltpu.SemaphoreType.DMA((4,)),
+            pltpu.VMEM((EXT, D), f32),
             pltpu.VMEM((8, D), f32),
         ],
         out_shape=(
-            jax.ShapeDtypeStruct((65, 24, D), bf16),
-            jax.ShapeDtypeStruct((65, 24, D), bf16),
             jax.ShapeDtypeStruct((ROWS, D), f32),
             jax.ShapeDtypeStruct((128, D), bf16),
             jax.ShapeDtypeStruct((128, D), bf16),
             jax.ShapeDtypeStruct((128, D), f32),
+            jax.ShapeDtypeStruct((1, 24, D), bf16),
         ),
         compiler_params=params(56),
-        cost_estimate=cost(15),
-        name="project_back",
+        cost_estimate=cost(60),
+        name="input_grad",
+    )(*operands)
+
+
+def weight_grad_kernel(place, acts, grads, wattn_grad, totals, send, keep):
+    step = pl.program_id(0)
+    ours = step % 2 == place[1]
+    part = dot_tn(acts[...], grads[0]).reshape(32, 24, D).astype(bf16)
+    chunks = pl.ds(32 * (step // 2), 32)
+
+    @pl.when(ours)
+    def _():
+        keep[chunks] = part
+
+    @pl.when(jnp.logical_not(ours))
+    def _():
+        send[chunks] = part
+
+    @pl.when(step == 2)
+    def _():
+        send[64] = totals[0]
+        keep[64] = totals[0]
+        rest = wattn_grad[...].astype(f32).reshape(32, 24, D).astype(bf16)
+
+        @pl.when(ours)
+        def _():
+            send[32:64] = rest
+
+        @pl.when(jnp.logical_not(ours))
+        def _():
+            keep[32:64] = rest
+
+
+def weight_grad(*operands):
+    return pl.pallas_call(
+        weight_grad_kernel,
+        grid=(3,),
+        in_specs=[
+            SCALARS,
+            whole((EXT, D)),
+            pl.BlockSpec((1, EXT, D), lambda i: (i, 0, 0)),
+            whole((D, D)),
+            whole((1, 24, D)),
+        ],
+        out_specs=[whole((65, 24, D))] * 2,
+        out_shape=[jax.ShapeDtypeStruct((65, 24, D), bf16)] * 2,
+        compiler_params=params(48),
+        cost_estimate=cost(0.1),
+        name="weight_grad",
     )(*operands)
 
 
@@ -1018,6 +1095,7 @@
     first, second, natural, key_mask, self_mask, line = lax.optimization_barrier(
         (first, second, natural, key_mask, self_mask, line)
     )
+    wout = lax.all_gather(after(wout, natural), "dp", axis=0, tiled=True)
     left = lax.ppermute(natural[ROWS - BLOCK :], "fsdp", TO_RIGHT)
     right = lax.ppermute(natural[:BLOCK], "fsdp", TO_LEFT)
     first = first.reshape(2, 2, 4, 24, EXT)
@@ -1041,7 +1119,6 @@
     )
     first = first.reshape(2, D, EXT)
     first_other = swap(first)
-    wout = lax.all_gather(after(wout, first), "dp", axis=0, tiled=True)
     second = after(second.reshape(16, 24, D), first_other)
     second_parts = [second] + relay([second] * 3, "y")
     side = first[0, :, D:].astype(f32)
@@ -1057,8 +1134,9 @@
         [part_out, split3(part_lse.reshape(HEADS, 128)), jnp.zeros((12, 128), bf16)], 0
     )
     packed = after(packed, long_out)
-    got = exchange(jnp.broadcast_to(after(sent, packed)[None], (4, 816, 128)), "fsdp", QUADS)
-    *second_parts, _ = lax.optimization_barrier((*second_parts, long_out))
+    sent = jnp.broadcast_to(after(sent, packed)[None], (4, 816, 128))
+    second_parts = lax.optimization_barrier((*second_parts, sent))[:-1]
+    got = exchange(sent, "fsdp", QUADS)
     (second,) = place_parts(
         spot["y"],
         second_parts,
@@ -1085,8 +1163,7 @@
         wattn_grad,
         win_send,
         win_keep,
-        wout_send,
-        wout_keep,
+        wout_grad,
         norm_two,
     ) = feed(
         place,
@@ -1104,34 +1181,22 @@
         second,
         second_other,
     )
-    dq, dk, dv, rel = attend_back(
+    (two,) = add_pairs([(win_keep, swap(win_send))], "add_cores")
+    grads, rel = attend_back(
         place, table, line, key_mask, self_mask, proj, grad_mixed, long_lse, glob_out, glob_lse
     )
-    (two,) = add_pairs([(win_keep, swap(win_send))], "add_cores")
-    three = fold_parts(
-        spot["z"],
-        [wout_keep.reshape(64, 24, D), swap(wout_send).reshape(64, 24, D)],
-        lambda s: [((g // 4 * 2 + (s >> 1)) * 4 + g % 4) * 4 + (s & 1) * 2 for g in range(8)],
-        2,
-        "three_z",
-    )
-    dq, two, *three = lax.optimization_barrier((dq, two, *three))
+    grads, two = lax.optimization_barrier((grads, two))
     two = exchange(two.reshape(64, 24, D), BOTH, SAME_CORE)
-    one_send, one_keep, grad_nat, back_left, back_right, back_glob = project_back(
-        place,
-        rows,
-        acts,
-        dq,
-        dk,
-        dv,
-        norms,
-        grad_middle,
-        wattn_grad,
-        rel,
-        norm_two,
-        loss_sum,
-        first,
-        first_other,
+    grad_nat, back_left, back_right, back_glob, totals = input_grad(
+        place, rows, grads, norms, grad_middle, rel, norm_two, loss_sum, first, first_other
+    )
+    from_left = lax.ppermute(back_right, "fsdp", TO_RIGHT)
+    from_right = lax.ppermute(back_left, "fsdp", TO_LEFT)
+    both = pack_rows(result, grad_nat, from_left, from_right)
+    one_send, one_keep = weight_grad(place, acts, grads, wattn_grad, totals)
+    one_send, one_keep, two, both = lax.optimization_barrier((one_send, one_keep, two, both))
+    out_grad = lax.psum_scatter(
+        wout_grad.reshape(4 * D, D), "fsdp", scatter_dimension=0, tiled=True
     )
     one = scatter_axis(
         spot["x"],
@@ -1141,22 +1206,25 @@
         4,
         "one_x",
     )
-    *three, _ = lax.optimization_barrier((*three, one[0]))
-    three = [three[0]] + relay(three[1:], "z")
-    three = scatter_axis(spot["x"], three, "x", lambda s: [s * 2, (4 + s) * 2], 2, "three_x")
-    three = scatter_axis(spot["y"], three, "y", lambda s: [(s & 1) * 2 + (s >> 1)], 1, "three_y")
-    out_grad = total_of(three)[0]
-    from_left = lax.ppermute(back_right, "fsdp", TO_RIGHT)
-    from_right = lax.ppermute(back_left, "fsdp", TO_LEFT)
-    both = pack_rows(result, grad_nat, from_left, from_right)
-    both = exchange(after(both, two), "fsdp")
-    out_long, grad_long = unpack_rows(exchange(both[order], "fsdp"))
+    both = exchange(both, "fsdp")[order]
+    out_grad = after(out_grad, both).reshape(2, 4, 24, D)
+    cut = [
+        lax.dynamic_index_in_dim(out_grad, spot["x"][0] ^ k, 1, keepdims=False) for k in range(4)
+    ]
+    out_grad = total_of([cut[0]] + relay(cut[1:], "x"))
+    z_hi = spot["z"][0] >> 1
+    far = lax.dynamic_index_in_dim(out_grad, 1 - z_hi, 0, keepdims=False).astype(bf16)
+    near = lax.dynamic_index_in_dim(out_grad, z_hi, 0, keepdims=False)
+    out_grad = near + lax.ppermute(far, BOTH, PARTNERS["z"][1]).astype(f32)
+    *one, both = lax.optimization_barrier((*one, both))
+    out_long, grad_long = unpack_rows(exchange(both, "fsdp"))
     two = jnp.sum(two.astype(f32), 0)
     out_glob = lax.dynamic_slice_in_dim(result, ROWS + quarter * 32, 32, 0)
     one = scatter_axis(
         spot["z"], one, "z", lambda s: [s * 2, (4 + s) * 2], 2, "one_z"
     )
     one = scatter_axis(spot["y"], one, "y", lambda s: [(s & 1) * 2 + (s >> 1)], 1, "one_y")
+    one = lax.optimization_barrier((*one, out_long, out_grad))[:4]
     small = [part[1, :8].astype(f32) + part[1, 8:16].astype(f32) for part in one]
     small = (small[0] + small[1]) + (small[2] + small[3])
     one = [part[0] for part in one]

time: 480 us -> 463 us (0.965)
  waiting for transfers between devices: 136 us -> 120 us
  local copies, waits for them, and re-layouts: 44.6 us -> 49.5 us
    all_to_all x10, waiting for transfers between devices: 16.8 us -> 31.6 us  [exchange(): lax.all_to_all(value, axis, 0, 0, axis_index_groups=groups, tiled=True)]
    ppermute x36 -> x30, waiting for transfers between devices: 81.3 us -> 66.6 us  [relay(): lax.ppermute(value, BOTH, pairs)]
    ppermute x36 -> x30, starting transfers between devices: 58.2 us -> 43.9 us  [relay(): lax.ppermute(value, BOTH, pairs)]
    ppermute x1, waiting for transfers between devices: 16 us -> 5.27 us  [shards(): from_left = lax.ppermute(back_right, 'fsdp', TO_RIGHT)]
    all_gather x1, waiting for transfers between devices: 8.31 us -> 0.01 us  [shards(): wout = lax.all_gather(after(wout, natural), 'dp', axis=0, tiled=True)]
    ppermute x5 -> x4, starting transfers between devices: 5.11 us -> 12.8 us  [swap(): return lax.ppermute(value, 'fsdp', SWAP)]
    unnamed x102 -> x100, local copies, waits for them, and re-layouts: 17.4 us -> 23.5 us
    all_to_all x10, starting transfers between devices: 52.6 us -> 57.6 us  [exchange(): lax.all_to_all(value, axis, 0, 0, axis_index_groups=groups, tiled=True)]
  transfers between devices with their start and end apart: 57 -> 52, of which waited for: 25 -> 22; matrix products, arithmetic and copies ran while one was open for 8% -> 8% of each run, Pallas kernels for 12% -> 17%
where the time goes in v4:
time: 463 us; the launch traced here: 457 us
  starting transfers between devices  126 us (27%)
  waiting for transfers between devices  120 us (26%)
  Pallas kernels  118 us (25%)
  local copies, waits for them, and re-layouts  49.5 us (11%)
  other arithmetic  23.3 us (5%)
  between operations  20.6 us (4%)
    ppermute x30, waiting for transfers between devices, relay(): lax.ppermute(value, BOTH, pairs)  66.6 us
    all_to_all x10, starting transfers between devices, exchange(): lax.all_to_all(value, axis, 0, 0, axis_index_groups=groups, tiled=True)  57.6 us
    ppermute x30, starting transfers between devices, relay(): lax.ppermute(value, BOTH, pairs)  43.9 us
    pallas_call x1, Pallas kernels, feed(): pl.pallas_call(feed_kernel, grid_spec=pltpu.PrefetchScalarGridSpec(num_sc...  41.2 us
    all_to_all x10, waiting for transfers between devices, exchange(): lax.all_to_all(value, axis, 0, 0, axis_index_groups=groups, tiled=True)  31.6 us
    unnamed x100, local copies, waits for them, and re-layouts  23.5 us
    pallas_call x1, Pallas kernels, attend_back(): pl.pallas_call(attend_back_kernel, grid=(6,), in_specs=[SCALARS, SCALARS,...  20.7 us
    pallas_call x1, Pallas kernels, attend(): pl.pallas_call(attend_kernel, grid=(6,), in_specs=[SCALARS, SCALARS, pl.B...  15.6 us
  transfers between devices with their start and end apart: 52, of which 22 were waited for; matrix products, arithmetic and copies ran while one was open for 8% of the time, Pallas kernels for 17%

profile of v4, /device:TPU:1, one launch (start us, length us, event | category | flops | bytes accessed | tf_op | source)
XLA Modules:
  0.0 457.4 jit_solution(10712795622471146540)
XLA Ops:
  18.6 4.9 %all-to-all-start = ((bf16[4,88,768]{2,1,0:T(8,128)(2,1)}), bf16[4,88,768]{2,1,0:T(8,128)(2,1)S(1)}, u32[]{:S(2)}, u32[]{:S(2)}) async-start(bf16[4,88,768]{2,1,0:T(8,128)(2,1)} %pad_maximum_fusion.1), calls=%async_computation | async-start | bytes 1081344 | tf_op jit(solution)/shard_map/all_to_all | solution.py:47
  26.2 5.5 %all-to-all-done = bf16[4,88,768]{2,1,0:T(8,128)(2,1)S(1)} async-done(((bf16[4,88,768]{2,1,0:T(8,128)(2,1)}), bf16[4,88,768]{2,1,0:T(8,128)(2,1)S(1)}, u32[]{:S(2)}, u32[]{:S(2)}) %all-to-all-start) | async-done | bytes 540704 | tf_op jit(solution)/shard_map/all_to_all | solution.py:47
  32.7 6.8 %all-to-all-start.1 = ((bf16[64,8,768]{2,1,0:T(8,128)(2,1)}), bf16[64,8,768]{2,1,0:T(8,128)(2,1)S(1)}, u32[]{:S(2)}, u32[]{:S(2)}) async-start(bf16[64,8,768]{2,1,0:T(8,128)(2,1)} %bitcast.15), calls=%async_computation.1 | async-start | bytes 1572864 | tf_op jit(solution)/shard_map/all_to_all | solution.py:47
  41.7 3.3 collective-permute-start.4
  46.4 2.4 collective-permute-start.1
  49.3 6.4 %collective-permute-start.2 = (bf16[24,896]{1,0:T(8,128)(2,1)S(1)}, bf16[24,896]{1,0:T(8,128)(2,1)S(1)}, u32[]{:S(2)}, u32[]{:S(2)}) collective-permute-start(bf16[24,896]{1,0:T(8,128)(2,1)S(1)} %constant_dynamic-update-slice_fusion.refs_0_), channel_id=1, source_target_pairs={{0,6},{1,7},{2,4},{3,5},{4,2},{5,3},{6,0},{7,1},{8,14},{9,15},{10,... | collective-permute-start | bytes 129032 | tf_op jit(solution)/shard_map/ppermute | solution.py:55
  57.7 5.2 %all-to-all-start.2 = ((bf16[64,8,768]{2,1,0:T(8,128)(2,1)}), bf16[64,8,768]{2,1,0:T(8,128)(2,1)S(1)}, u32[]{:S(2)}, u32[]{:S(2)}) async-start(bf16[64,8,768]{2,1,0:T(8,128)(2,1)} %gather_fusion), calls=%async_computation.2 | async-start | bytes 1572864 | tf_op jit(solution)/shard_map/all_to_all | solution.py:47
  64.4 2.6 collective-permute-start.10
  70.0 2.5 collective-permute-start.7
  74.2 2.5 collective-permute-done.11.refs_3_
  78.6 5.3 %collective-permute-done.7.refs_2_ = bf16[2,2,24,896]{3,2,1,0:T(8,128)(2,1)S(1)} collective-permute-done((bf16[2,2,24,896]{3,2,1,0:T(8,128)(2,1)S(1)}, bf16[2,2,24,896]{3,2,1,0:T(8,128)(2,1)S(1)}, u32[]{:S(2)}, u32[]{:S(2)}) %collective-permute-start.7) | collective-permute-done | bytes 172064 | tf_op jit(solution)/shard_map/ppermute | solution.py:55
  86.7 5.0 %all-to-all-start.3 = ((bf16[64,8,1664]{2,1,0:T(8,128)(2,1)}), bf16[64,8,1664]{2,1,0:T(8,128)(2,1)}, u32[]{:S(2)}, u32[]{:S(2)}) async-start(bf16[64,8,1664]{2,1,0:T(8,128)(2,1)} %bitcast.117), calls=%async_computation.3 | async-start | bytes 3407872 | tf_op jit(solution)/shard_map/all_to_all | solution.py:47
  92.5 3.0 collective-permute-start.13
  96.4 4.4 collective-permute-start.15
  104.7 11.8 %collective-permute-done.15.left = bf16[128,768]{1,0:T(8,128)(2,1)S(1)} collective-permute-done((bf16[128,768]{1,0:T(8,128)(2,1)}, bf16[128,768]{1,0:T(8,128)(2,1)S(1)}, u32[]{:S(2)}, u32[]{:S(2)}) %collective-permute-start.15) | collective-permute-done | bytes 196640 | tf_op jit(solution)/shard_map/ppermute | solution.py:1099
  116.7 14.6 %collective-permute-done.13.refs_2_ = bf16[2,2,4,24,896]{4,3,2,1,0:T(8,128)(2,1)} collective-permute-done((bf16[2,2,4,24,896]{4,3,2,1,0:T(8,128)(2,1)S(1)}, bf16[2,2,4,24,896]{4,3,2,1,0:T(8,128)(2,1)}, u32[]{:S(2)}, u32[]{:S(2)}) %collective-permute-start.13) | collective-permute-done | bytes 688160 | tf_op jit(solution)/shard_map/ppermute | solution.py:55
  131.3 3.0 first_x.1
  139.3 3.4 gather_fusion.1
  142.7 5.8 %all-to-all-start.4 = ((bf16[64,8,1664]{2,1,0:T(8,128)(2,1)}), bf16[64,8,1664]{2,1,0:T(8,128)(2,1)}, u32[]{:S(2)}, u32[]{:S(2)}) async-start(bf16[64,8,1664]{2,1,0:T(8,128)(2,1)} %gather_fusion.1), calls=%async_computation.4 | async-start | bytes 3407872 | tf_op jit(solution)/shard_map/all_to_all | solution.py:47
  153.7 8.0 %project.1 = (bf16[896,768]{1,0:T(8,128)(2,1)S(1)}, bf16[896,768]{1,0:T(8,128)(2,1)}, bf16[896,2304]{1,0:T(8,128)(2,1)}) custom-call(s32[2]{0:T(128)S(1)} %pad_add_fusion.place, bf16[128,768]{1,0:T(8,128)(2,1)S(1)} %copy-done.22, bf16[512,768]{1,0:T(8,128)(2,1)S(1)} %bitcast.101, bf16[128,768]{1,0:T(8,128)(2,1)} %collective-permute-done.16.right, ...), custom_call_target="tpu_custom_call" | custom-call | flops 9900000256 | bytes 32400000 | tf_op jit(solution)/shard_map/project/pallas_call | solution.py:316
  161.8 2.7 copy-done.29
  164.4 15.6 %attend.1 = (bf16[512,768]{1,0:T(8,128)(2,1)S(1)}, f32[6,4,256]{2,1,0:T(4,128)S(1)}, bf16[768,128]{1,0:T(8,128)(2,1)S(1)}, f32[6,1,256]{2,1,0:T(1,128)S(1)}) custom-call(s32[2]{0:T(128)S(1)} %pad_add_fusion.place, f32[2,12]{1,0:T(2,128)S(1)} %copy.75.table, f32[6,2,512]{2,1,0:T(2,128)S(1)} %reshape.350.line, f32[896,256]{1,0:T(8,128)S(1)} %broadcast_in_dim.129.key_mask, ...), custom_call_target="tpu_custom_call" | custom-call | flops 16499999744 | bytes 54000000 | tf_op jit(solution)/shard_map/attend/pallas_call | solution.py:434
  184.4 11.9 %collective-permute-done.19.refs_2_ = bf16[16,24,768]{2,1,0:T(8,128)(2,1)} collective-permute-done((bf16[16,24,768]{2,1,0:T(8,128)(2,1)S(1)}, bf16[16,24,768]{2,1,0:T(8,128)(2,1)}, u32[]{:S(2)}, u32[]{:S(2)}) %collective-permute-start.19) | collective-permute-done | bytes 589856 | tf_op jit(solution)/shard_map/ppermute | solution.py:55
  201.8 4.2 all-to-all-start.5
  208.9 2.8 copy.70
  211.7 5.7 %all-to-all-done.5.parts = bf16[4,816,128]{2,1,0:T(8,128)(2,1)} async-done(((bf16[4,816,128]{2,1,0:T(8,128)(2,1)}), bf16[4,816,128]{2,1,0:T(8,128)(2,1)}, u32[]{:S(2)}, u32[]{:S(2)}) %all-to-all-start.5) | async-done | bytes 835616 | tf_op jit(solution)/shard_map/all_to_all | solution.py:47
  219.0 41.2 %feed.1 = (bf16[640,768]{1,0:T(8,128)(2,1)}, f32[8,128]{1,0:T(8,128)}, bf16[768,128]{1,0:T(8,128)(2,1)}, f32[640,768]{1,0:T(8,128)}, bf16[640,768]{1,0:T(8,128)(...) custom-call(s32[2]{0:T(128)} %copy-done.6, ...), custom_call_target="tpu_custom_call" | custom-call | flops 47300001792 | bytes 154800000 | tf_op jit(solution)/shard_map/feed/pallas_call | solution.py:789
  260.1 10.1 %collective-permute-start.22 = (bf16[2,768,768]{2,1,0:T(8,128)(2,1)}, bf16[2,768,768]{2,1,0:T(8,128)(2,1)S(1)}, u32[]{:S(2)}, u32[]{:S(2)}) collective-permute-start(bf16[2,768,768]{2,1,0:T(8,128)(2,1)} %get-tuple-element.130), channel_id=1, source_target_pairs={{0,1},{1,0},{2,3},{3,2},{4,5},{5,4},{6,7},{7,6},{8,9},{9,8},{10,11... | collective-permute-start | bytes 7077896 | tf_op jit(solution)/shard_map/ppermute | solution.py:51
  273.0 20.7 %attend_back.1 = (bf16[3,896,768]{2,1,0:T(8,128)(2,1)}, f32[6,8,512]{2,1,0:T(8,128)S(1)}) custom-call(s32[2]{0:T(128)S(1)} %copy-done.7, f32[2,12]{1,0:T(2,128)S(1)} %copy.75.table, f32[6,2,512]{2,1,0:T(2,128)S(1)} %reshape.350.line, f32[896,256]{1,0:T(8,128)S(1)} %broadcast_in_dim.129.key_mask, f32[128,256]{1,0:T(8,128)S(1)} %broadcast_in_dim.132.self_mask, ...), custom_call_target="tpu_custom_call" | custom-call | flops 23100000256 | bytes 75600000 | tf_op jit(solution)/shard_map/attend_back/pallas_call | solution.py:576
  296.0 6.8 %all-to-all-start.6 = ((bf16[64,24,768]{2,1,0:T(8,128)(2,1)}), bf16[64,24,768]{2,1,0:T(8,128)(2,1)}, u32[]{:S(2)}, u32[]{:S(2)}) async-start(bf16[64,24,768]{2,1,0:T(8,128)(2,1)} %bitcast.42), calls=%async_computation.6 | async-start | bytes 4718592 | tf_op jit(solution)/shard_map/all_to_all | solution.py:47
  302.9 11.7 %input_grad.1 = (f32[512,768]{1,0:T(8,128)}, bf16[128,768]{1,0:T(8,128)(2,1)}, bf16[128,768]{1,0:T(8,128)(2,1)}, f32[128,768]{1,0:T(8,128)}, bf16[1,24,768]{2,1,0:T(8,128)(2,1)}) custom-call(s32[2]{0:T(128)} %copy-done.6, bf16[896,768]{1,0:T(8,128)(2,1)} %copy-done.30, bf16[3,896,768]{2,1,0:T(8,128)(2,1)} %get-tuple-element.131.grads, f32[8,768]{1,0:T(8,128)} %copy-done.4, ...), custom_call_target="tpu_custom_call" | custom-call | flops 65999998976 | bytes 216000000 | tf_op jit(solution)/shard_map/input_grad/pallas_call | solution.py:903
  314.6 3.1 collective-permute-start.23
  320.4 7.8 %weight_grad.1 = (bf16[65,24,768]{2,1,0:T(8,128)(2,1)S(1)}, bf16[65,24,768]{2,1,0:T(8,128)(2,1)}) custom-call(s32[2]{0:T(128)S(1)} %copy-done.8, bf16[896,768]{1,0:T(8,128)(2,1)S(1)} %copy-done, bf16[3,896,768]{2,1,0:T(8,128)(2,1)} %get-tuple-element.131.grads, bf16[768,768]{1,0:T(8,128)(2,1)S(1)} %copy-done.1, bf16[1,24,768]{2,1,0:T(8,128)(2,1)S(1)} %copy-done.3), custom_call_target="tpu_custom_call" | custom-call | flops 110000000 | bytes 360000 | tf_op jit(solution)/shard_map/weight_grad/pallas_call | solution.py:974
  329.6 5.3 %collective-permute-done.23.left_ref = bf16[128,768]{1,0:T(8,128)(2,1)S(1)} collective-permute-done((bf16[128,768]{1,0:T(8,128)(2,1)}, bf16[128,768]{1,0:T(8,128)(2,1)S(1)}, u32[]{:S(2)}, u32[]{:S(2)}) %collective-permute-start.23) | collective-permute-done | bytes 196640 | tf_op jit(solution)/shard_map/ppermute | solution.py:1193
  337.3 6.0 %all-to-all-start.7 = ((bf16[64,8,1536]{2,1,0:T(8,128)(2,1)}), bf16[64,8,1536]{2,1,0:T(8,128)(2,1)}, u32[]{:S(2)}, u32[]{:S(2)}) async-start(bf16[64,8,1536]{2,1,0:T(8,128)(2,1)} %pack_rows.1), calls=%async_computation.7 | async-start | bytes 3145728 | tf_op jit(solution)/shard_map/all_to_all | solution.py:47
  345.0 3.3 one_x.1
  349.9 2.8 collective-permute-start.27
  353.0 15.4 %all-to-all-done.7 = bf16[64,8,1536]{2,1,0:T(8,128)(2,1)} async-done(((bf16[64,8,1536]{2,1,0:T(8,128)(2,1)}), bf16[64,8,1536]{2,1,0:T(8,128)(2,1)}, u32[]{:S(2)}, u32[]{:S(2)}) %all-to-all-start.7) | async-done | bytes 1572896 | tf_op jit(solution)/shard_map/all_to_all | solution.py:47
  368.4 3.2 gather_fusion.2
  371.6 8.9 %collective-permute-done.27.refs_2_ = bf16[17,24,768]{2,1,0:T(8,128)(2,1)S(1)} collective-permute-done((bf16[17,24,768]{2,1,0:T(8,128)(2,1)}, bf16[17,24,768]{2,1,0:T(8,128)(2,1)S(1)}, u32[]{:S(2)}, u32[]{:S(2)}) %collective-permute-start.27) | collective-permute-done | bytes 626720 | tf_op jit(solution)/shard_map/ppermute | solution.py:55
  383.4 6.9 %all-to-all-start.8 = ((bf16[64,8,1536]{2,1,0:T(8,128)(2,1)}), bf16[64,8,1536]{2,1,0:T(8,128)(2,1)S(1)}, u32[]{:S(2)}, u32[]{:S(2)}) async-start(bf16[64,8,1536]{2,1,0:T(8,128)(2,1)} %gather_fusion.2), calls=%async_computation.8 | async-start | bytes 3145728 | tf_op jit(solution)/shard_map/all_to_all | solution.py:47
  396.8 3.4 collective-permute-start.30
  403.4 10.0 %collective-permute-done.29.refs_1_ = bf16[5,24,768]{2,1,0:T(8,128)(2,1)S(1)} collective-permute-done((bf16[5,24,768]{2,1,0:T(8,128)(2,1)S(1)}, bf16[5,24,768]{2,1,0:T(8,128)(2,1)S(1)}, u32[]{:S(2)}, u32[]{:S(2)}) %collective-permute-start.29) | collective-permute-done | bytes 184352 | tf_op jit(solution)/shard_map/ppermute | solution.py:55
  413.4 6.2 %collective-permute-done.30.refs_2_ = bf16[5,24,768]{2,1,0:T(8,128)(2,1)S(1)} collective-permute-done((bf16[5,24,768]{2,1,0:T(8,128)(2,1)S(1)}, bf16[5,24,768]{2,1,0:T(8,128)(2,1)S(1)}, u32[]{:S(2)}, u32[]{:S(2)}) %collective-permute-start.30) | collective-permute-done | bytes 184352 | tf_op jit(solution)/shard_map/ppermute | solution.py:55
  420.9 2.4 collective-permute-start.33
  426.3 2.7 collective-permute-done.38
  431.4 6.0 %all-to-all-start.9 = ((f32[4,48,768]{2,1,0:T(8,128)}), f32[4,48,768]{2,1,0:T(8,128)S(1)}, u32[]{:S(2)}, u32[]{:S(2)}) async-start(f32[4,48,768]{2,1,0:T(8,128)} %maximum_maximum_fusion), calls=%async_computation.10 | async-start | bytes 1179648 | tf_op jit(solution)/shard_map/all_to_all | solution.py:47
  441.1 5.0 %all-to-all-done.9 = f32[4,48,768]{2,1,0:T(8,128)S(1)} async-done(((f32[4,48,768]{2,1,0:T(8,128)}), f32[4,48,768]{2,1,0:T(8,128)S(1)}, u32[]{:S(2)}, u32[]{:S(2)}) %all-to-all-start.9) | async-done | bytes 589856 | tf_op jit(solution)/shard_map/all_to_all | solution.py:47
  (272 shorter events, 98.7 us)
Async XLA Ops:
  18.6 13.0 %all-to-all-start = ((bf16[4,88,768]{2,1,0:T(8,128)(2,1)}), bf16[4,88,768]{2,1,0:T(8,128)(2,1)S(1)}, u32[]{:S(2)}, u32[]{:S(2)}) async-start(bf16[4,88,768]{2,1,0:T(8,128)(2,1)} %pad_maximum_fusion.1), calls=%async_computation | async-start | bytes 1081344 | tf_op jit(solution)/shard_map/all_to_all | solution.py:47
  23.5 79.3 %all-gather.3.cloned.1.call-start = ((), (), s32[]{:S(2)}) async-start(), calls=%async_computation.11 | async-start | bytes 1253376 | tf_op jit(solution)/shard_map/all_gather | solution.py:1052
  32.7 23.5 %all-to-all-start.1 = ((bf16[64,8,768]{2,1,0:T(8,128)(2,1)}), bf16[64,8,768]{2,1,0:T(8,128)(2,1)S(1)}, u32[]{:S(2)}, u32[]{:S(2)}) async-start(bf16[64,8,768]{2,1,0:T(8,128)(2,1)} %bitcast.15), calls=%async_computation.1 | async-start | bytes 1572864 | tf_op jit(solution)/shard_map/all_to_all | solution.py:47
  40.2 9.1 %collective-permute-start.3 = (bf16[24,768]{1,0:T(8,128)(2,1)S(1)}, bf16[24,768]{1,0:T(8,128)(2,1)S(1)}, u32[]{:S(2)}, u32[]{:S(2)}) collective-permute-start(bf16[24,768]{1,0:T(8,128)(2,1)S(1)} %reshape.345.refs_0_), channel_id=1, source_target_pairs={{0,8},{1,9},{2,10},{3,11},{4,12},{5,13},{6,14},{7,15},{8,0},{9,1},... | collective-permute-start | bytes 110600 | tf_op jit(solution)/shard_map/ppermute | solution.py:55
  41.7 14.5 %collective-permute-start.4 = (bf16[24,768]{1,0:T(8,128)(2,1)S(1)}, bf16[24,768]{1,0:T(8,128)(2,1)S(1)}, u32[]{:S(2)}, u32[]{:S(2)}) collective-permute-start(bf16[24,768]{1,0:T(8,128)(2,1)S(1)} %reshape.345.refs_0_), channel_id=1, source_target_pairs={{0,64},{1,65},{2,66},{3,67},{4,68},{5,69},{6,70},{7,71},{8,72},{9,... | collective-permute-start | bytes 110600 | tf_op jit(solution)/shard_map/ppermute | solution.py:55
  45.0 11.2 %collective-permute-start.5 = (bf16[24,768]{1,0:T(8,128)(2,1)S(1)}, bf16[24,768]{1,0:T(8,128)(2,1)S(1)}, u32[]{:S(2)}, u32[]{:S(2)}) collective-permute-start(bf16[24,768]{1,0:T(8,128)(2,1)S(1)} %reshape.345.refs_0_), channel_id=1, source_target_pairs={{0,72},{1,73},{2,74},{3,75},{4,76},{5,77},{6,78},{7,79},{8,64},{9,... | collective-permute-start | bytes 110600 | tf_op jit(solution)/shard_map/ppermute | solution.py:55
  45.1 17.8 %collective-permute-start = (bf16[24,896]{1,0:T(8,128)(2,1)S(1)}, bf16[24,896]{1,0:T(8,128)(2,1)S(1)}, u32[]{:S(2)}, u32[]{:S(2)}) collective-permute-start(bf16[24,896]{1,0:T(8,128)(2,1)S(1)} %constant_dynamic-update-slice_fusion.refs_0_), channel_id=1, source_target_pairs={{0,2},{1,3},{2,0},{3,1},{4,6},{5,7},{6,4},{7,5},{8,10},{9,11},{10,... | collective-permute-start | bytes 129032 | tf_op jit(solution)/shard_map/ppermute | solution.py:55
  46.4 16.6 %collective-permute-start.1 = (bf16[24,896]{1,0:T(8,128)(2,1)S(1)}, bf16[24,896]{1,0:T(8,128)(2,1)S(1)}, u32[]{:S(2)}, u32[]{:S(2)}) collective-permute-start(bf16[24,896]{1,0:T(8,128)(2,1)S(1)} %constant_dynamic-update-slice_fusion.refs_0_), channel_id=1, source_target_pairs={{0,4},{1,5},{2,6},{3,7},{4,0},{5,1},{6,2},{7,3},{8,12},{9,13},{10,... | collective-permute-start | bytes 129032 | tf_op jit(solution)/shard_map/ppermute | solution.py:55
  49.3 13.6 %collective-permute-start.2 = (bf16[24,896]{1,0:T(8,128)(2,1)S(1)}, bf16[24,896]{1,0:T(8,128)(2,1)S(1)}, u32[]{:S(2)}, u32[]{:S(2)}) collective-permute-start(bf16[24,896]{1,0:T(8,128)(2,1)S(1)} %constant_dynamic-update-slice_fusion.refs_0_), channel_id=1, source_target_pairs={{0,6},{1,7},{2,4},{3,5},{4,2},{5,3},{6,0},{7,1},{8,14},{9,15},{10,... | collective-permute-start | bytes 129032 | tf_op jit(solution)/shard_map/ppermute | solution.py:55
  57.7 26.3 %all-to-all-start.2 = ((bf16[64,8,768]{2,1,0:T(8,128)(2,1)}), bf16[64,8,768]{2,1,0:T(8,128)(2,1)S(1)}, u32[]{:S(2)}, u32[]{:S(2)}) async-start(bf16[64,8,768]{2,1,0:T(8,128)(2,1)} %gather_fusion), calls=%async_computation.2 | async-start | bytes 1572864 | tf_op jit(solution)/shard_map/all_to_all | solution.py:47
  63.0 9.5 %collective-permute-start.9 = (bf16[2,2,24,768]{3,2,1,0:T(8,128)(2,1)S(1)}, bf16[2,2,24,768]{3,2,1,0:T(8,128)(2,1)S(1)}, u32[]{:S(2)}, u32[]{:S(2)}) collective-permute-start(bf16[2,2,24,768]{3,2,1,0:T(8,128)(2,1)S(1)} %second_z.1.refs_0_), channel_id=1, source_target_pairs={{0,16},{1,17},{2,18},{3,19},{4,20},{5,21},{6,22},{7,23},{8,24},{9,... | collective-permute-start | bytes 442376 | tf_op jit(solution)/shard_map/ppermute | solution.py:55
  64.4 9.8 %collective-permute-start.10 = (bf16[2,2,24,768]{3,2,1,0:T(8,128)(2,1)S(1)}, bf16[2,2,24,768]{3,2,1,0:T(8,128)(2,1)S(1)}, u32[]{:S(2)}, u32[]{:S(2)}) collective-permute-start(bf16[2,2,24,768]{3,2,1,0:T(8,128)(2,1)S(1)} %second_z.1.refs_0_), channel_id=1, source_target_pairs={{0,32},{1,33},{2,34},{3,35},{4,36},{5,37},{6,38},{7,39},{8,40},{9,... | collective-permute-start | bytes 442376 | tf_op jit(solution)/shard_map/ppermute | solution.py:55
  67.0 9.6 %collective-permute-start.11 = (bf16[2,2,24,768]{3,2,1,0:T(8,128)(2,1)S(1)}, bf16[2,2,24,768]{3,2,1,0:T(8,128)(2,1)S(1)}, u32[]{:S(2)}, u32[]{:S(2)}) collective-permute-start(bf16[2,2,24,768]{3,2,1,0:T(8,128)(2,1)S(1)} %second_z.1.refs_0_), channel_id=1, source_target_pairs={{0,48},{1,49},{2,50},{3,51},{4,52},{5,53},{6,54},{7,55},{8,56},{9,... | collective-permute-start | bytes 442376 | tf_op jit(solution)/shard_map/ppermute | solution.py:55
  68.6 10.0 %collective-permute-start.6 = (bf16[2,2,24,896]{3,2,1,0:T(8,128)(2,1)S(1)}, bf16[2,2,24,896]{3,2,1,0:T(8,128)(2,1)S(1)}, u32[]{:S(2)}, u32[]{:S(2)}) collective-permute-start(bf16[2,2,24,896]{3,2,1,0:T(8,128)(2,1)S(1)} %first_y.1.refs_0_), channel_id=1, source_target_pairs={{0,8},{1,9},{2,10},{3,11},{4,12},{5,13},{6,14},{7,15},{8,0},{9,1},... | collective-permute-start | bytes 516104 | tf_op jit(solution)/shard_map/ppermute | solution.py:55
  70.0 13.9 %collective-permute-start.7 = (bf16[2,2,24,896]{3,2,1,0:T(8,128)(2,1)S(1)}, bf16[2,2,24,896]{3,2,1,0:T(8,128)(2,1)S(1)}, u32[]{:S(2)}, u32[]{:S(2)}) collective-permute-start(bf16[2,2,24,896]{3,2,1,0:T(8,128)(2,1)S(1)} %first_y.1.refs_0_), channel_id=1, source_target_pairs={{0,64},{1,65},{2,66},{3,67},{4,68},{5,69},{6,70},{7,71},{8,72},{9,... | collective-permute-start | bytes 516104 | tf_op jit(solution)/shard_map/ppermute | solution.py:55
  72.5 11.4 %collective-permute-start.8 = (bf16[2,2,24,896]{3,2,1,0:T(8,128)(2,1)S(1)}, bf16[2,2,24,896]{3,2,1,0:T(8,128)(2,1)S(1)}, u32[]{:S(2)}, u32[]{:S(2)}) collective-permute-start(bf16[2,2,24,896]{3,2,1,0:T(8,128)(2,1)S(1)} %first_y.1.refs_0_), channel_id=1, source_target_pairs={{0,72},{1,73},{2,74},{3,75},{4,76},{5,77},{6,78},{7,79},{8,64},{9,... | collective-permute-start | bytes 516104 | tf_op jit(solution)/shard_map/ppermute | solution.py:55
  86.7 44.6 %all-to-all-start.3 = ((bf16[64,8,1664]{2,1,0:T(8,128)(2,1)}), bf16[64,8,1664]{2,1,0:T(8,128)(2,1)}, u32[]{:S(2)}, u32[]{:S(2)}) async-start(bf16[64,8,1664]{2,1,0:T(8,128)(2,1)} %bitcast.117), calls=%async_computation.3 | async-start | bytes 3407872 | tf_op jit(solution)/shard_map/all_to_all | solution.py:47
  91.7 127.3 %all-gather.5.cloned.1.call-start = ((), (), s32[]{:S(2)}) async-start(), calls=%async_computation.12 | async-start | bytes 5308416 | tf_op jit(solution)/shard_map/all_gather | solution.py:1098
  91.7 25.0 %collective-permute-start.12 = (bf16[2,2,4,24,896]{4,3,2,1,0:T(8,128)(2,1)S(1)}, bf16[2,2,4,24,896]{4,3,2,1,0:T(8,128)(2,1)S(1)}, u32[]{:S(2)}, u32[]{:S(2)}) collective-permute-start(bf16[2,2,4,24,896]{4,3,2,1,0:T(8,128)(2,1)S(1)} %bitcast.107), channel_id=1, source_target_pairs={{0,16},{1,17},{2,18},{3,19},{4,20},{5,21},{6,22},{7,23},{8,24},{9,... | collective-permute-start | bytes 2064392 | tf_op jit(solution)/shard_map/ppermute | solution.py:55
  92.5 38.8 %collective-permute-start.13 = (bf16[2,2,4,24,896]{4,3,2,1,0:T(8,128)(2,1)S(1)}, bf16[2,2,4,24,896]{4,3,2,1,0:T(8,128)(2,1)}, u32[]{:S(2)}, u32[]{:S(2)}) collective-permute-start(bf16[2,2,4,24,896]{4,3,2,1,0:T(8,128)(2,1)S(1)} %bitcast.108), channel_id=1, source_target_pairs={{0,32},{1,33},{2,34},{3,35},{4,36},{5,37},{6,38},{7,39},{8,40},{9,... | collective-permute-start | bytes 2064392 | tf_op jit(solution)/shard_map/ppermute | solution.py:55
  95.5 35.8 %collective-permute-start.14 = (bf16[2,2,4,24,896]{4,3,2,1,0:T(8,128)(2,1)S(1)}, bf16[2,2,4,24,896]{4,3,2,1,0:T(8,128)(2,1)}, u32[]{:S(2)}, u32[]{:S(2)}) collective-permute-start(bf16[2,2,4,24,896]{4,3,2,1,0:T(8,128)(2,1)S(1)} %bitcast.109), channel_id=1, source_target_pairs={{0,48},{1,49},{2,50},{3,51},{4,52},{5,53},{6,54},{7,55},{8,56},{9,... | collective-permute-start | bytes 2064392 | tf_op jit(solution)/shard_map/ppermute | solution.py:55
  96.4 20.1 %collective-permute-start.15 = (bf16[128,768]{1,0:T(8,128)(2,1)}, bf16[128,768]{1,0:T(8,128)(2,1)S(1)}, u32[]{:S(2)}, u32[]{:S(2)}) collective-permute-start(bf16[128,768]{1,0:T(8,128)(2,1)} %get-tuple-element.185), channel_id=1, source_target_pairs={{0,1},{1,2},{2,3},{4,5},{5,6},{6,7},{8,9},{9,10},{10,11},{12,13},{... | collective-permute-start | bytes 589832 | tf_op jit(solution)/shard_map/ppermute | solution.py:1099
  100.8 15.9 %collective-permute-start.16 = (bf16[128,768]{1,0:T(8,128)(2,1)}, bf16[128,768]{1,0:T(8,128)(2,1)}, u32[]{:S(2)}, u32[]{:S(2)}) collective-permute-start(bf16[128,768]{1,0:T(8,128)(2,1)} %get-tuple-element.184), channel_id=1, source_target_pairs={{1,0},{2,1},{3,2},{5,4},{6,5},{7,6},{9,8},{10,9},{11,10},{13,12},{... | collective-permute-start | bytes 589832 | tf_op jit(solution)/shard_map/ppermute | solution.py:1100
  134.3 14.2 %collective-permute-start.17 = (bf16[2,768,896]{2,1,0:T(8,128)(2,1)}, bf16[2,768,896]{2,1,0:T(8,128)(2,1)}, u32[]{:S(2)}, u32[]{:S(2)}) collective-permute-start(bf16[2,768,896]{2,1,0:T(8,128)(2,1)} %bitcast.28.mine.first_mine), channel_id=1, source_target_pairs={{0,1},{1,0},{2,3},{3,2},{4,5},{5,4},{6,7},{7,6},{8,9},{9,8},{10,11... | collective-permute-start | bytes 8257544 | tf_op jit(solution)/shard_map/ppermute | solution.py:51
  142.7 38.3 %all-to-all-start.4 = ((bf16[64,8,1664]{2,1,0:T(8,128)(2,1)}), bf16[64,8,1664]{2,1,0:T(8,128)(2,1)}, u32[]{:S(2)}, u32[]{:S(2)}) async-start(bf16[64,8,1664]{2,1,0:T(8,128)(2,1)} %gather_fusion.1), calls=%async_computation.4 | async-start | bytes 3407872 | tf_op jit(solution)/shard_map/all_to_all | solution.py:47
  148.6 35.0 %collective-permute-start.18 = (bf16[16,24,768]{2,1,0:T(8,128)(2,1)S(1)}, bf16[16,24,768]{2,1,0:T(8,128)(2,1)S(1)}, u32[]{:S(2)}, u32[]{:S(2)}) collective-permute-start(bf16[16,24,768]{2,1,0:T(8,128)(2,1)S(1)} %bitcast.111), channel_id=1, source_target_pairs={{0,2},{1,3},{2,0},{3,1},{4,6},{5,7},{6,4},{7,5},{8,10},{9,11},{10,... | collective-permute-start | bytes 1769480 | tf_op jit(solution)/shard_map/ppermute | solution.py:55
  150.0 46.3 %collective-permute-start.19 = (bf16[16,24,768]{2,1,0:T(8,128)(2,1)S(1)}, bf16[16,24,768]{2,1,0:T(8,128)(2,1)}, u32[]{:S(2)}, u32[]{:S(2)}) collective-permute-start(bf16[16,24,768]{2,1,0:T(8,128)(2,1)S(1)} %bitcast.112), channel_id=1, source_target_pairs={{0,4},{1,5},{2,6},{3,7},{4,0},{5,1},{6,2},{7,3},{8,12},{9,13},{10,... | collective-permute-start | bytes 1769480 | tf_op jit(solution)/shard_map/ppermute | solution.py:55
  152.4 43.9 %collective-permute-start.20 = (bf16[16,24,768]{2,1,0:T(8,128)(2,1)S(1)}, bf16[16,24,768]{2,1,0:T(8,128)(2,1)}, u32[]{:S(2)}, u32[]{:S(2)}) collective-permute-start(bf16[16,24,768]{2,1,0:T(8,128)(2,1)S(1)} %bitcast.113), channel_id=1, source_target_pairs={{0,6},{1,7},{2,4},{3,5},{4,2},{5,3},{6,0},{7,1},{8,14},{9,15},{10,... | collective-permute-start | bytes 1769480 | tf_op jit(solution)/shard_map/ppermute | solution.py:55
  200.9 18.1 %collective-permute-start.21 = (bf16[2,768,768]{2,1,0:T(8,128)(2,1)S(1)}, bf16[2,768,768]{2,1,0:T(8,128)(2,1)}, u32[]{:S(2)}, u32[]{:S(2)}) collective-permute-start(bf16[2,768,768]{2,1,0:T(8,128)(2,1)S(1)} %bitcast.104), channel_id=1, source_target_pairs={{0,1},{1,0},{2,3},{3,2},{4,5},{5,4},{6,7},{7,6},{8,9},{9,8},{10,11... | collective-permute-start | bytes 7077896 | tf_op jit(solution)/shard_map/ppermute | solution.py:51
  201.8 15.6 %all-to-all-start.5 = ((bf16[4,816,128]{2,1,0:T(8,128)(2,1)}), bf16[4,816,128]{2,1,0:T(8,128)(2,1)}, u32[]{:S(2)}, u32[]{:S(2)}) async-start(bf16[4,816,128]{2,1,0:T(8,128)(2,1)} %broadcast_in_dim.137), calls=%async_computation.5 | async-start | bytes 1671168 | tf_op jit(solution)/shard_map/all_to_all | solution.py:47
  206.0 196.2 %reduce-scatter.2.cloned.1.call-start = ((), (), s32[]{:S(2)}) async-start(), calls=%async_computation.13 | async-start | bytes 5013504 | tf_op jit(solution)/shard_map/reduce_scatter | solution.py:1198
  260.1 33.6 %collective-permute-start.22 = (bf16[2,768,768]{2,1,0:T(8,128)(2,1)}, bf16[2,768,768]{2,1,0:T(8,128)(2,1)S(1)}, u32[]{:S(2)}, u32[]{:S(2)}) collective-permute-start(bf16[2,768,768]{2,1,0:T(8,128)(2,1)} %get-tuple-element.130), channel_id=1, source_target_pairs={{0,1},{1,0},{2,3},{3,2},{4,5},{5,4},{6,7},{7,6},{8,9},{9,8},{10,11... | collective-permute-start | bytes 7077896 | tf_op jit(solution)/shard_map/ppermute | solution.py:51
  296.0 41.3 %all-to-all-start.6 = ((bf16[64,24,768]{2,1,0:T(8,128)(2,1)}), bf16[64,24,768]{2,1,0:T(8,128)(2,1)}, u32[]{:S(2)}, u32[]{:S(2)}) async-start(bf16[64,24,768]{2,1,0:T(8,128)(2,1)} %bitcast.42), calls=%async_computation.6 | async-start | bytes 4718592 | tf_op jit(solution)/shard_map/all_to_all | solution.py:47
  314.6 20.3 %collective-permute-start.23 = (bf16[128,768]{1,0:T(8,128)(2,1)}, bf16[128,768]{1,0:T(8,128)(2,1)S(1)}, u32[]{:S(2)}, u32[]{:S(2)}) collective-permute-start(bf16[128,768]{1,0:T(8,128)(2,1)} %get-tuple-element.143), channel_id=1, source_target_pairs={{0,1},{1,2},{2,3},{4,5},{5,6},{6,7},{8,9},{9,10},{10,11},{12,13},{... | collective-permute-start | bytes 589832 | tf_op jit(solution)/shard_map/ppermute | solution.py:1193
  317.7 18.3 %collective-permute-start.24 = (bf16[128,768]{1,0:T(8,128)(2,1)}, bf16[128,768]{1,0:T(8,128)(2,1)S(1)}, u32[]{:S(2)}, u32[]{:S(2)}) collective-permute-start(bf16[128,768]{1,0:T(8,128)(2,1)} %get-tuple-element.144), channel_id=1, source_target_pairs={{1,0},{2,1},{3,2},{5,4},{6,5},{7,6},{9,8},{10,9},{11,10},{13,12},{... | collective-permute-start | bytes 589832 | tf_op jit(solution)/shard_map/ppermute | solution.py:1194
  337.3 31.1 %all-to-all-start.7 = ((bf16[64,8,1536]{2,1,0:T(8,128)(2,1)}), bf16[64,8,1536]{2,1,0:T(8,128)(2,1)}, u32[]{:S(2)}, u32[]{:S(2)}) async-start(bf16[64,8,1536]{2,1,0:T(8,128)(2,1)} %pack_rows.1), calls=%async_computation.7 | async-start | bytes 3145728 | tf_op jit(solution)/shard_map/all_to_all | solution.py:47
  349.2 22.5 %collective-permute-start.26 = (bf16[17,24,768]{2,1,0:T(8,128)(2,1)}, bf16[17,24,768]{2,1,0:T(8,128)(2,1)S(1)}, u32[]{:S(2)}, u32[]{:S(2)}) collective-permute-start(bf16[17,24,768]{2,1,0:T(8,128)(2,1)} %get-tuple-element.148), channel_id=1, source_target_pairs={{0,16},{1,17},{2,18},{3,19},{4,20},{5,21},{6,22},{7,23},{8,24},{9,... | collective-permute-start | bytes 1880072 | tf_op jit(solution)/shard_map/ppermute | solution.py:55
  349.9 30.6 %collective-permute-start.27 = (bf16[17,24,768]{2,1,0:T(8,128)(2,1)}, bf16[17,24,768]{2,1,0:T(8,128)(2,1)S(1)}, u32[]{:S(2)}, u32[]{:S(2)}) collective-permute-start(bf16[17,24,768]{2,1,0:T(8,128)(2,1)} %get-tuple-element.149), channel_id=1, source_target_pairs={{0,32},{1,33},{2,34},{3,35},{4,36},{5,37},{6,38},{7,39},{8,40},{9,... | collective-permute-start | bytes 1880072 | tf_op jit(solution)/shard_map/ppermute | solution.py:55
  352.8 29.8 %collective-permute-start.28 = (bf16[17,24,768]{2,1,0:T(8,128)(2,1)}, bf16[17,24,768]{2,1,0:T(8,128)(2,1)S(1)}, u32[]{:S(2)}, u32[]{:S(2)}) collective-permute-start(bf16[17,24,768]{2,1,0:T(8,128)(2,1)} %get-tuple-element.150), channel_id=1, source_target_pairs={{0,48},{1,49},{2,50},{3,51},{4,52},{5,53},{6,54},{7,55},{8,56},{9,... | collective-permute-start | bytes 1880072 | tf_op jit(solution)/shard_map/ppermute | solution.py:55
  383.4 41.3 %all-to-all-start.8 = ((bf16[64,8,1536]{2,1,0:T(8,128)(2,1)}), bf16[64,8,1536]{2,1,0:T(8,128)(2,1)S(1)}, u32[]{:S(2)}, u32[]{:S(2)}) async-start(bf16[64,8,1536]{2,1,0:T(8,128)(2,1)} %gather_fusion.2), calls=%async_computation.8 | async-start | bytes 3145728 | tf_op jit(solution)/shard_map/all_to_all | solution.py:47
  395.2 18.2 %collective-permute-start.29 = (bf16[5,24,768]{2,1,0:T(8,128)(2,1)S(1)}, bf16[5,24,768]{2,1,0:T(8,128)(2,1)S(1)}, u32[]{:S(2)}, u32[]{:S(2)}) collective-permute-start(bf16[5,24,768]{2,1,0:T(8,128)(2,1)S(1)} %get-tuple-element.159), channel_id=1, source_target_pairs={{0,8},{1,9},{2,10},{3,11},{4,12},{5,13},{6,14},{7,15},{8,0},{9,1},... | collective-permute-start | bytes 552968 | tf_op jit(solution)/shard_map/ppermute | solution.py:55
  396.8 22.8 %collective-permute-start.30 = (bf16[5,24,768]{2,1,0:T(8,128)(2,1)S(1)}, bf16[5,24,768]{2,1,0:T(8,128)(2,1)S(1)}, u32[]{:S(2)}, u32[]{:S(2)}) collective-permute-start(bf16[5,24,768]{2,1,0:T(8,128)(2,1)S(1)} %get-tuple-element.160), channel_id=1, source_target_pairs={{0,64},{1,65},{2,66},{3,67},{4,68},{5,69},{6,70},{7,71},{8,72},{9,... | collective-permute-start | bytes 552968 | tf_op jit(solution)/shard_map/ppermute | solution.py:55
  400.2 19.4 %collective-permute-start.31 = (bf16[5,24,768]{2,1,0:T(8,128)(2,1)S(1)}, bf16[5,24,768]{2,1,0:T(8,128)(2,1)S(1)}, u32[]{:S(2)}, u32[]{:S(2)}) collective-permute-start(bf16[5,24,768]{2,1,0:T(8,128)(2,1)S(1)} %get-tuple-element.161), channel_id=1, source_target_pairs={{0,72},{1,73},{2,74},{3,75},{4,76},{5,77},{6,78},{7,79},{8,64},{9,... | collective-permute-start | bytes 552968 | tf_op jit(solution)/shard_map/ppermute | solution.py:55
  403.2 20.1 %collective-permute-start.37 = (bf16[2,24,768]{2,1,0:T(8,128)(2,1)S(1)}, bf16[2,24,768]{2,1,0:T(8,128)(2,1)S(1)}, u32[]{:S(2)}, u32[]{:S(2)}) collective-permute-start(bf16[2,24,768]{2,1,0:T(8,128)(2,1)S(1)} %get-tuple-element.191), channel_id=1, source_target_pairs={{0,48},{1,49},{2,50},{3,51},{4,52},{5,53},{6,54},{7,55},{8,56},{9,... | collective-permute-start | bytes 221192 | tf_op jit(solution)/shard_map/ppermute | solution.py:55
  403.3 20.3 %collective-permute-start.36 = (bf16[2,24,768]{2,1,0:T(8,128)(2,1)S(1)}, bf16[2,24,768]{2,1,0:T(8,128)(2,1)S(1)}, u32[]{:S(2)}, u32[]{:S(2)}) collective-permute-start(bf16[2,24,768]{2,1,0:T(8,128)(2,1)S(1)} %get-tuple-element.192), channel_id=1, source_target_pairs={{0,32},{1,33},{2,34},{3,35},{4,36},{5,37},{6,38},{7,39},{8,40},{9,... | collective-permute-start | bytes 221192 | tf_op jit(solution)/shard_map/ppermute | solution.py:55
  413.4 10.2 %collective-permute-start.35 = (bf16[2,24,768]{2,1,0:T(8,128)(2,1)S(1)}, bf16[2,24,768]{2,1,0:T(8,128)(2,1)S(1)}, u32[]{:S(2)}, u32[]{:S(2)}) collective-permute-start(bf16[2,24,768]{2,1,0:T(8,128)(2,1)S(1)} %get-tuple-element.190), channel_id=1, source_target_pairs={{0,16},{1,17},{2,18},{3,19},{4,20},{5,21},{6,22},{7,23},{8,24},{9,... | collective-permute-start | bytes 221192 | tf_op jit(solution)/shard_map/ppermute | solution.py:55
  419.7 9.9 %collective-permute-start.32 = (bf16[2,24,768]{2,1,0:T(8,128)(2,1)S(1)}, bf16[2,24,768]{2,1,0:T(8,128)(2,1)S(1)}, u32[]{:S(2)}, u32[]{:S(2)}) collective-permute-start(bf16[2,24,768]{2,1,0:T(8,128)(2,1)S(1)} %get-tuple-element.163), channel_id=1, source_target_pairs={{0,2},{1,3},{2,0},{3,1},{4,6},{5,7},{6,4},{7,5},{8,10},{9,11},{10,... | collective-permute-start | bytes 221192 | tf_op jit(solution)/shard_map/ppermute | solution.py:55
  431.4 14.7 %all-to-all-start.9 = ((f32[4,48,768]{2,1,0:T(8,128)}), f32[4,48,768]{2,1,0:T(8,128)S(1)}, u32[]{:S(2)}, u32[]{:S(2)}) async-start(f32[4,48,768]{2,1,0:T(8,128)} %maximum_maximum_fusion), calls=%async_computation.10 | async-start | bytes 1179648 | tf_op jit(solution)/shard_map/all_to_all | solution.py:47
  (52 other events, 409.0 us)
Sparse Core Ops, SparseCore 0:
  26.6 40.8 all-gather.2
  104.8 99.4 all-gather.4
  270.4 90.4 reduce-scatter.1

commit v5 on v4

--- a/solution.py
+++ b/solution.py
@@ -1085,12 +1085,12 @@
         "first_z",
     )
     (second,) = gather_axis(
-        spot["x"],
+        spot["y"],
         second,
-        "x",
-        [(2, 4, 2, 24, D)],
-        lambda s: [(..., 0, (every, s))],
-        "second_x",
+        "y",
+        [(2, 2, 2, 2, 24, D)],
+        lambda s: [(..., 0, (s & 1, every, every, s >> 1))],
+        "second_y",
     )
     first, second, natural, key_mask, self_mask, line = lax.optimization_barrier(
         (first, second, natural, key_mask, self_mask, line)
@@ -1119,8 +1119,8 @@
     )
     first = first.reshape(2, D, EXT)
     first_other = swap(first)
-    second = after(second.reshape(16, 24, D), first_other)
-    second_parts = [second] + relay([second] * 3, "y")
+    second = after(second.reshape(2, 2, 4, 24, D), first_other)
+    second_parts = [second] + relay([second] * 3, "x")
     side = first[0, :, D:].astype(f32)
     whole_count = side[:, 4] * 16.0 + side[:, 5]
     count = jnp.sum(jnp.where(jnp.arange(D) % 6 == 0, whole_count, 0.0))
@@ -1138,11 +1138,11 @@
     second_parts = lax.optimization_barrier((*second_parts, sent))[:-1]
     got = exchange(sent, "fsdp", QUADS)
     (second,) = place_parts(
-        spot["y"],
+        spot["x"],
         second_parts,
-        [(2, 16, 2, 24, D)],
-        lambda s: [(..., 0, (s & 1, every, s >> 1))],
-        "second_y",
+        [(2, 2, 4, 4, 24, D)],
+        lambda s: [(..., 0, (every, every, s))],
+        "second_x",
     )
     second = second.reshape(2, D, D)
     second_other = swap(second)

time: 463 us -> 454 us (0.981)
  waiting for transfers between devices: 120 us -> 108 us
    ppermute x30, waiting for transfers between devices: 66.6 us -> 54.9 us  [relay(): lax.ppermute(value, BOTH, pairs)]
  transfers between devices with their start and end apart: 52 -> 52, of which waited for: 22 -> 21; matrix products, arithmetic and copies ran while one was open for 8% -> 8% of each run, Pallas kernels for 17% -> 17%
where the time goes in v5:
time: 454 us; the launch traced here: 449 us
  starting transfers between devices  129 us (28%)
  Pallas kernels  118 us (26%)
  waiting for transfers between devices  108 us (24%)
  local copies, waits for them, and re-layouts  49.5 us (11%)
  other arithmetic  23.3 us (5%)
  between operations  20.7 us (5%)
    all_to_all x10, starting transfers between devices, exchange(): lax.all_to_all(value, axis, 0, 0, axis_index_groups=groups, tiled=True)  58.1 us
    ppermute x30, waiting for transfers between devices, relay(): lax.ppermute(value, BOTH, pairs)  54.9 us
    ppermute x30, starting transfers between devices, relay(): lax.ppermute(value, BOTH, pairs)  46.5 us
    pallas_call x1, Pallas kernels, feed(): pl.pallas_call(feed_kernel, grid_spec=pltpu.PrefetchScalarGridSpec(num_sc...  41.2 us
    all_to_all x10, waiting for transfers between devices, exchange(): lax.all_to_all(value, axis, 0, 0, axis_index_groups=groups, tiled=True)  31.5 us
    unnamed x100, local copies, waits for them, and re-layouts  23.5 us
    pallas_call x1, Pallas kernels, attend_back(): pl.pallas_call(attend_back_kernel, grid=(6,), in_specs=[SCALARS, SCALARS,...  20.7 us
    pallas_call x1, Pallas kernels, attend(): pl.pallas_call(attend_kernel, grid=(6,), in_specs=[SCALARS, SCALARS, pl.B...  15.6 us
  transfers between devices with their start and end apart: 52, of which 21 were waited for; matrix products, arithmetic and copies ran while one was open for 8% of the time, Pallas kernels for 17%

profile of v5, /device:TPU:1, one launch (start us, length us, event | category | flops | bytes accessed | tf_op | source)
XLA Modules:
  0.0 449.4 jit_solution(2815929353188564220)
XLA Ops:
  18.6 4.9 %all-to-all-start = ((bf16[4,88,768]{2,1,0:T(8,128)(2,1)}), bf16[4,88,768]{2,1,0:T(8,128)(2,1)S(1)}, u32[]{:S(2)}, u32[]{:S(2)}) async-start(bf16[4,88,768]{2,1,0:T(8,128)(2,1)} %pad_maximum_fusion.1), calls=%async_computation | async-start | bytes 1081344 | tf_op jit(solution)/shard_map/all_to_all | solution.py:47
  26.2 5.5 %all-to-all-done = bf16[4,88,768]{2,1,0:T(8,128)(2,1)S(1)} async-done(((bf16[4,88,768]{2,1,0:T(8,128)(2,1)}), bf16[4,88,768]{2,1,0:T(8,128)(2,1)S(1)}, u32[]{:S(2)}, u32[]{:S(2)}) %all-to-all-start) | async-done | bytes 540704 | tf_op jit(solution)/shard_map/all_to_all | solution.py:47
  32.7 6.8 %all-to-all-start.1 = ((bf16[64,8,768]{2,1,0:T(8,128)(2,1)}), bf16[64,8,768]{2,1,0:T(8,128)(2,1)S(1)}, u32[]{:S(2)}, u32[]{:S(2)}) async-start(bf16[64,8,768]{2,1,0:T(8,128)(2,1)} %bitcast.15), calls=%async_computation.1 | async-start | bytes 1572864 | tf_op jit(solution)/shard_map/all_to_all | solution.py:47
  41.7 3.3 collective-permute-start.4
  46.4 2.4 collective-permute-start.1
  49.3 6.4 %collective-permute-start.2 = (bf16[24,896]{1,0:T(8,128)(2,1)S(1)}, bf16[24,896]{1,0:T(8,128)(2,1)S(1)}, u32[]{:S(2)}, u32[]{:S(2)}) collective-permute-start(bf16[24,896]{1,0:T(8,128)(2,1)S(1)} %constant_dynamic-update-slice_fusion.refs_0_), channel_id=1, source_target_pairs={{0,6},{1,7},{2,4},{3,5},{4,2},{5,3},{6,0},{7,1},{8,14},{9,15},{10,... | collective-permute-start | bytes 129032 | tf_op jit(solution)/shard_map/ppermute | solution.py:55
  57.7 5.2 %all-to-all-start.2 = ((bf16[64,8,768]{2,1,0:T(8,128)(2,1)}), bf16[64,8,768]{2,1,0:T(8,128)(2,1)S(1)}, u32[]{:S(2)}, u32[]{:S(2)}) async-start(bf16[64,8,768]{2,1,0:T(8,128)(2,1)} %gather_fusion), calls=%async_computation.2 | async-start | bytes 1572864 | tf_op jit(solution)/shard_map/all_to_all | solution.py:47
  64.4 2.4 collective-permute-start.10
  69.9 2.6 collective-permute-start.7
  72.5 4.4 collective-permute-done.9.refs_1_
  76.9 2.6 collective-permute-start.8
  83.9 3.5 collective-permute-done.8.refs_3_
  90.3 4.6 %all-to-all-start.3 = ((bf16[64,8,1664]{2,1,0:T(8,128)(2,1)}), bf16[64,8,1664]{2,1,0:T(8,128)(2,1)}, u32[]{:S(2)}, u32[]{:S(2)}) async-start(bf16[64,8,1664]{2,1,0:T(8,128)(2,1)} %bitcast.117), calls=%async_computation.3 | async-start | bytes 3407872 | tf_op jit(solution)/shard_map/all_to_all | solution.py:47
  96.3 2.4 collective-permute-start.13
  99.7 4.4 collective-permute-start.15
  107.9 11.6 %collective-permute-done.15.left = bf16[128,768]{1,0:T(8,128)(2,1)S(1)} collective-permute-done((bf16[128,768]{1,0:T(8,128)(2,1)}, bf16[128,768]{1,0:T(8,128)(2,1)S(1)}, u32[]{:S(2)}, u32[]{:S(2)}) %collective-permute-start.15) | collective-permute-done | bytes 196640 | tf_op jit(solution)/shard_map/ppermute | solution.py:1099
  120.0 14.3 %collective-permute-done.13.refs_2_ = bf16[2,2,4,24,896]{4,3,2,1,0:T(8,128)(2,1)} collective-permute-done((bf16[2,2,4,24,896]{4,3,2,1,0:T(8,128)(2,1)S(1)}, bf16[2,2,4,24,896]{4,3,2,1,0:T(8,128)(2,1)}, u32[]{:S(2)}, u32[]{:S(2)}) %collective-permute-start.13) | collective-permute-done | bytes 688160 | tf_op jit(solution)/shard_map/ppermute | solution.py:55
  134.3 3.0 first_x.1
  142.7 3.4 gather_fusion.1
  146.0 5.8 %all-to-all-start.4 = ((bf16[64,8,1664]{2,1,0:T(8,128)(2,1)}), bf16[64,8,1664]{2,1,0:T(8,128)(2,1)}, u32[]{:S(2)}, u32[]{:S(2)}) async-start(bf16[64,8,1664]{2,1,0:T(8,128)(2,1)} %gather_fusion.1), calls=%async_computation.4 | async-start | bytes 3407872 | tf_op jit(solution)/shard_map/all_to_all | solution.py:47
  153.3 2.8 collective-permute-start.20
  157.0 8.0 %project.1 = (bf16[896,768]{1,0:T(8,128)(2,1)S(1)}, bf16[896,768]{1,0:T(8,128)(2,1)}, bf16[896,2304]{1,0:T(8,128)(2,1)}) custom-call(s32[2]{0:T(128)S(1)} %pad_add_fusion.place, bf16[128,768]{1,0:T(8,128)(2,1)S(1)} %copy-done.22, bf16[512,768]{1,0:T(8,128)(2,1)S(1)} %bitcast.101, bf16[128,768]{1,0:T(8,128)(2,1)} %collective-permute-done.16.right, ...), custom_call_target="tpu_custom_call" | custom-call | flops 9900000256 | bytes 32400000 | tf_op jit(solution)/shard_map/project/pallas_call | solution.py:316
  165.0 2.7 copy-done.29
  167.7 15.6 %attend.1 = (bf16[512,768]{1,0:T(8,128)(2,1)S(1)}, f32[6,4,256]{2,1,0:T(4,128)S(1)}, bf16[768,128]{1,0:T(8,128)(2,1)S(1)}, f32[6,1,256]{2,1,0:T(1,128)S(1)}) custom-call(s32[2]{0:T(128)S(1)} %pad_add_fusion.place, f32[2,12]{1,0:T(2,128)S(1)} %copy.75.table, f32[6,2,512]{2,1,0:T(2,128)S(1)} %reshape.350.line, f32[896,256]{1,0:T(8,128)S(1)} %broadcast_in_dim.129.key_mask, ...), custom_call_target="tpu_custom_call" | custom-call | flops 16499999744 | bytes 54000000 | tf_op jit(solution)/shard_map/attend/pallas_call | solution.py:434
  192.7 4.2 all-to-all-start.5
  199.8 2.8 copy.70
  202.6 5.7 %all-to-all-done.5.parts = bf16[4,816,128]{2,1,0:T(8,128)(2,1)} async-done(((bf16[4,816,128]{2,1,0:T(8,128)(2,1)}), bf16[4,816,128]{2,1,0:T(8,128)(2,1)}, u32[]{:S(2)}, u32[]{:S(2)}) %all-to-all-start.5) | async-done | bytes 835616 | tf_op jit(solution)/shard_map/all_to_all | solution.py:47
  209.8 41.2 %feed.1 = (bf16[640,768]{1,0:T(8,128)(2,1)}, f32[8,128]{1,0:T(8,128)}, bf16[768,128]{1,0:T(8,128)(2,1)}, f32[640,768]{1,0:T(8,128)}, bf16[640,768]{1,0:T(8,128)(...) custom-call(s32[2]{0:T(128)} %copy-done.6, ...), custom_call_target="tpu_custom_call" | custom-call | flops 47300001792 | bytes 154800000 | tf_op jit(solution)/shard_map/feed/pallas_call | solution.py:789
  251.0 10.1 %collective-permute-start.22 = (bf16[2,768,768]{2,1,0:T(8,128)(2,1)}, bf16[2,768,768]{2,1,0:T(8,128)(2,1)S(1)}, u32[]{:S(2)}, u32[]{:S(2)}) collective-permute-start(bf16[2,768,768]{2,1,0:T(8,128)(2,1)} %get-tuple-element.130), channel_id=1, source_target_pairs={{0,1},{1,0},{2,3},{3,2},{4,5},{5,4},{6,7},{7,6},{8,9},{9,8},{10,11... | collective-permute-start | bytes 7077896 | tf_op jit(solution)/shard_map/ppermute | solution.py:51
  263.9 20.7 %attend_back.1 = (bf16[3,896,768]{2,1,0:T(8,128)(2,1)}, f32[6,8,512]{2,1,0:T(8,128)S(1)}) custom-call(s32[2]{0:T(128)S(1)} %copy-done.7, f32[2,12]{1,0:T(2,128)S(1)} %copy.75.table, f32[6,2,512]{2,1,0:T(2,128)S(1)} %reshape.350.line, f32[896,256]{1,0:T(8,128)S(1)} %broadcast_in_dim.129.key_mask, f32[128,256]{1,0:T(8,128)S(1)} %broadcast_in_dim.132.self_mask, ...), custom_call_target="tpu_custom_call" | custom-call | flops 23100000256 | bytes 75600000 | tf_op jit(solution)/shard_map/attend_back/pallas_call | solution.py:576
  286.8 7.9 %all-to-all-start.6 = ((bf16[64,24,768]{2,1,0:T(8,128)(2,1)}), bf16[64,24,768]{2,1,0:T(8,128)(2,1)}, u32[]{:S(2)}, u32[]{:S(2)}) async-start(bf16[64,24,768]{2,1,0:T(8,128)(2,1)} %bitcast.42), calls=%async_computation.6 | async-start | bytes 4718592 | tf_op jit(solution)/shard_map/all_to_all | solution.py:47
  294.8 11.7 %input_grad.1 = (f32[512,768]{1,0:T(8,128)}, bf16[128,768]{1,0:T(8,128)(2,1)}, bf16[128,768]{1,0:T(8,128)(2,1)}, f32[128,768]{1,0:T(8,128)}, bf16[1,24,768]{2,1,0:T(8,128)(2,1)}) custom-call(s32[2]{0:T(128)} %copy-done.6, bf16[896,768]{1,0:T(8,128)(2,1)} %copy-done.30, bf16[3,896,768]{2,1,0:T(8,128)(2,1)} %get-tuple-element.131.grads, f32[8,768]{1,0:T(8,128)} %copy-done.4, ...), custom_call_target="tpu_custom_call" | custom-call | flops 65999998976 | bytes 216000000 | tf_op jit(solution)/shard_map/input_grad/pallas_call | solution.py:903
  306.5 3.1 collective-permute-start.23
  312.3 7.8 %weight_grad.1 = (bf16[65,24,768]{2,1,0:T(8,128)(2,1)S(1)}, bf16[65,24,768]{2,1,0:T(8,128)(2,1)}) custom-call(s32[2]{0:T(128)S(1)} %copy-done.8, bf16[896,768]{1,0:T(8,128)(2,1)S(1)} %copy-done, bf16[3,896,768]{2,1,0:T(8,128)(2,1)} %get-tuple-element.131.grads, bf16[768,768]{1,0:T(8,128)(2,1)S(1)} %copy-done.1, bf16[1,24,768]{2,1,0:T(8,128)(2,1)S(1)} %copy-done.3), custom_call_target="tpu_custom_call" | custom-call | flops 110000000 | bytes 360000 | tf_op jit(solution)/shard_map/weight_grad/pallas_call | solution.py:974
  321.5 5.3 %collective-permute-done.23.left_ref = bf16[128,768]{1,0:T(8,128)(2,1)S(1)} collective-permute-done((bf16[128,768]{1,0:T(8,128)(2,1)}, bf16[128,768]{1,0:T(8,128)(2,1)S(1)}, u32[]{:S(2)}, u32[]{:S(2)}) %collective-permute-start.23) | collective-permute-done | bytes 196640 | tf_op jit(solution)/shard_map/ppermute | solution.py:1193
  329.2 5.9 %all-to-all-start.7 = ((bf16[64,8,1536]{2,1,0:T(8,128)(2,1)}), bf16[64,8,1536]{2,1,0:T(8,128)(2,1)}, u32[]{:S(2)}, u32[]{:S(2)}) async-start(bf16[64,8,1536]{2,1,0:T(8,128)(2,1)} %pack_rows.1), calls=%async_computation.7 | async-start | bytes 3145728 | tf_op jit(solution)/shard_map/all_to_all | solution.py:47
  336.8 3.3 one_x.1
  341.8 3.1 collective-permute-start.27
  344.9 15.3 %all-to-all-done.7 = bf16[64,8,1536]{2,1,0:T(8,128)(2,1)} async-done(((bf16[64,8,1536]{2,1,0:T(8,128)(2,1)}), bf16[64,8,1536]{2,1,0:T(8,128)(2,1)}, u32[]{:S(2)}, u32[]{:S(2)}) %all-to-all-start.7) | async-done | bytes 1572896 | tf_op jit(solution)/shard_map/all_to_all | solution.py:47
  360.2 3.2 gather_fusion.2
  363.4 9.2 %collective-permute-done.27.refs_2_ = bf16[17,24,768]{2,1,0:T(8,128)(2,1)S(1)} collective-permute-done((bf16[17,24,768]{2,1,0:T(8,128)(2,1)}, bf16[17,24,768]{2,1,0:T(8,128)(2,1)S(1)}, u32[]{:S(2)}, u32[]{:S(2)}) %collective-permute-start.27) | collective-permute-done | bytes 626720 | tf_op jit(solution)/shard_map/ppermute | solution.py:55
  375.5 6.7 %all-to-all-start.8 = ((bf16[64,8,1536]{2,1,0:T(8,128)(2,1)}), bf16[64,8,1536]{2,1,0:T(8,128)(2,1)S(1)}, u32[]{:S(2)}, u32[]{:S(2)}) async-start(bf16[64,8,1536]{2,1,0:T(8,128)(2,1)} %gather_fusion.2), calls=%async_computation.8 | async-start | bytes 3145728 | tf_op jit(solution)/shard_map/all_to_all | solution.py:47
  388.8 3.4 collective-permute-start.30
  395.4 10.0 %collective-permute-done.29.refs_1_ = bf16[5,24,768]{2,1,0:T(8,128)(2,1)S(1)} collective-permute-done((bf16[5,24,768]{2,1,0:T(8,128)(2,1)S(1)}, bf16[5,24,768]{2,1,0:T(8,128)(2,1)S(1)}, u32[]{:S(2)}, u32[]{:S(2)}) %collective-permute-start.29) | collective-permute-done | bytes 184352 | tf_op jit(solution)/shard_map/ppermute | solution.py:55
  405.4 6.2 %collective-permute-done.30.refs_2_ = bf16[5,24,768]{2,1,0:T(8,128)(2,1)S(1)} collective-permute-done((bf16[5,24,768]{2,1,0:T(8,128)(2,1)S(1)}, bf16[5,24,768]{2,1,0:T(8,128)(2,1)S(1)}, u32[]{:S(2)}, u32[]{:S(2)}) %collective-permute-start.30) | collective-permute-done | bytes 184352 | tf_op jit(solution)/shard_map/ppermute | solution.py:55
  418.3 2.7 collective-permute-done.38
  423.3 6.0 %all-to-all-start.9 = ((f32[4,48,768]{2,1,0:T(8,128)}), f32[4,48,768]{2,1,0:T(8,128)S(1)}, u32[]{:S(2)}, u32[]{:S(2)}) async-start(f32[4,48,768]{2,1,0:T(8,128)} %maximum_maximum_fusion), calls=%async_computation.10 | async-start | bytes 1179648 | tf_op jit(solution)/shard_map/all_to_all | solution.py:47
  433.0 5.0 %all-to-all-done.9 = f32[4,48,768]{2,1,0:T(8,128)S(1)} async-done(((f32[4,48,768]{2,1,0:T(8,128)}), f32[4,48,768]{2,1,0:T(8,128)S(1)}, u32[]{:S(2)}, u32[]{:S(2)}) %all-to-all-start.9) | async-done | bytes 589856 | tf_op jit(solution)/shard_map/all_to_all | solution.py:47
  (272 shorter events, 99.7 us)
Async XLA Ops:
  18.6 13.0 %all-to-all-start = ((bf16[4,88,768]{2,1,0:T(8,128)(2,1)}), bf16[4,88,768]{2,1,0:T(8,128)(2,1)S(1)}, u32[]{:S(2)}, u32[]{:S(2)}) async-start(bf16[4,88,768]{2,1,0:T(8,128)(2,1)} %pad_maximum_fusion.1), calls=%async_computation | async-start | bytes 1081344 | tf_op jit(solution)/shard_map/all_to_all | solution.py:47
  23.5 82.5 %all-gather.3.cloned.1.call-start = ((), (), s32[]{:S(2)}) async-start(), calls=%async_computation.11 | async-start | bytes 1253376 | tf_op jit(solution)/shard_map/all_gather | solution.py:1052
  32.7 23.5 %all-to-all-start.1 = ((bf16[64,8,768]{2,1,0:T(8,128)(2,1)}), bf16[64,8,768]{2,1,0:T(8,128)(2,1)S(1)}, u32[]{:S(2)}, u32[]{:S(2)}) async-start(bf16[64,8,768]{2,1,0:T(8,128)(2,1)} %bitcast.15), calls=%async_computation.1 | async-start | bytes 1572864 | tf_op jit(solution)/shard_map/all_to_all | solution.py:47
  40.2 9.1 %collective-permute-start.3 = (bf16[24,768]{1,0:T(8,128)(2,1)S(1)}, bf16[24,768]{1,0:T(8,128)(2,1)S(1)}, u32[]{:S(2)}, u32[]{:S(2)}) collective-permute-start(bf16[24,768]{1,0:T(8,128)(2,1)S(1)} %reshape.345.refs_0_), channel_id=1, source_target_pairs={{0,8},{1,9},{2,10},{3,11},{4,12},{5,13},{6,14},{7,15},{8,0},{9,1},... | collective-permute-start | bytes 110600 | tf_op jit(solution)/shard_map/ppermute | solution.py:55
  41.7 14.5 %collective-permute-start.4 = (bf16[24,768]{1,0:T(8,128)(2,1)S(1)}, bf16[24,768]{1,0:T(8,128)(2,1)S(1)}, u32[]{:S(2)}, u32[]{:S(2)}) collective-permute-start(bf16[24,768]{1,0:T(8,128)(2,1)S(1)} %reshape.345.refs_0_), channel_id=1, source_target_pairs={{0,64},{1,65},{2,66},{3,67},{4,68},{5,69},{6,70},{7,71},{8,72},{9,... | collective-permute-start | bytes 110600 | tf_op jit(solution)/shard_map/ppermute | solution.py:55
  45.0 11.2 %collective-permute-start.5 = (bf16[24,768]{1,0:T(8,128)(2,1)S(1)}, bf16[24,768]{1,0:T(8,128)(2,1)S(1)}, u32[]{:S(2)}, u32[]{:S(2)}) collective-permute-start(bf16[24,768]{1,0:T(8,128)(2,1)S(1)} %reshape.345.refs_0_), channel_id=1, source_target_pairs={{0,72},{1,73},{2,74},{3,75},{4,76},{5,77},{6,78},{7,79},{8,64},{9,... | collective-permute-start | bytes 110600 | tf_op jit(solution)/shard_map/ppermute | solution.py:55
  45.1 17.8 %collective-permute-start = (bf16[24,896]{1,0:T(8,128)(2,1)S(1)}, bf16[24,896]{1,0:T(8,128)(2,1)S(1)}, u32[]{:S(2)}, u32[]{:S(2)}) collective-permute-start(bf16[24,896]{1,0:T(8,128)(2,1)S(1)} %constant_dynamic-update-slice_fusion.refs_0_), channel_id=1, source_target_pairs={{0,2},{1,3},{2,0},{3,1},{4,6},{5,7},{6,4},{7,5},{8,10},{9,11},{10,... | collective-permute-start | bytes 129032 | tf_op jit(solution)/shard_map/ppermute | solution.py:55
  46.4 16.6 %collective-permute-start.1 = (bf16[24,896]{1,0:T(8,128)(2,1)S(1)}, bf16[24,896]{1,0:T(8,128)(2,1)S(1)}, u32[]{:S(2)}, u32[]{:S(2)}) collective-permute-start(bf16[24,896]{1,0:T(8,128)(2,1)S(1)} %constant_dynamic-update-slice_fusion.refs_0_), channel_id=1, source_target_pairs={{0,4},{1,5},{2,6},{3,7},{4,0},{5,1},{6,2},{7,3},{8,12},{9,13},{10,... | collective-permute-start | bytes 129032 | tf_op jit(solution)/shard_map/ppermute | solution.py:55
  49.3 13.6 %collective-permute-start.2 = (bf16[24,896]{1,0:T(8,128)(2,1)S(1)}, bf16[24,896]{1,0:T(8,128)(2,1)S(1)}, u32[]{:S(2)}, u32[]{:S(2)}) collective-permute-start(bf16[24,896]{1,0:T(8,128)(2,1)S(1)} %constant_dynamic-update-slice_fusion.refs_0_), channel_id=1, source_target_pairs={{0,6},{1,7},{2,4},{3,5},{4,2},{5,3},{6,0},{7,1},{8,14},{9,15},{10,... | collective-permute-start | bytes 129032 | tf_op jit(solution)/shard_map/ppermute | solution.py:55
  57.7 29.8 %all-to-all-start.2 = ((bf16[64,8,768]{2,1,0:T(8,128)(2,1)}), bf16[64,8,768]{2,1,0:T(8,128)(2,1)S(1)}, u32[]{:S(2)}, u32[]{:S(2)}) async-start(bf16[64,8,768]{2,1,0:T(8,128)(2,1)} %gather_fusion), calls=%async_computation.2 | async-start | bytes 1572864 | tf_op jit(solution)/shard_map/all_to_all | solution.py:47
  63.0 13.9 %collective-permute-start.9 = (bf16[2,2,24,768]{3,2,1,0:T(8,128)(2,1)S(1)}, bf16[2,2,24,768]{3,2,1,0:T(8,128)(2,1)S(1)}, u32[]{:S(2)}, u32[]{:S(2)}) collective-permute-start(bf16[2,2,24,768]{3,2,1,0:T(8,128)(2,1)S(1)} %second_z.1.refs_0_), channel_id=1, source_target_pairs={{0,2},{1,3},{2,0},{3,1},{4,6},{5,7},{6,4},{7,5},{8,10},{9,11},{10,... | collective-permute-start | bytes 442376 | tf_op jit(solution)/shard_map/ppermute | solution.py:55
  64.4 17.1 %collective-permute-start.10 = (bf16[2,2,24,768]{3,2,1,0:T(8,128)(2,1)S(1)}, bf16[2,2,24,768]{3,2,1,0:T(8,128)(2,1)S(1)}, u32[]{:S(2)}, u32[]{:S(2)}) collective-permute-start(bf16[2,2,24,768]{3,2,1,0:T(8,128)(2,1)S(1)} %second_z.1.refs_0_), channel_id=1, source_target_pairs={{0,4},{1,5},{2,6},{3,7},{4,0},{5,1},{6,2},{7,3},{8,12},{9,13},{10,... | collective-permute-start | bytes 442376 | tf_op jit(solution)/shard_map/ppermute | solution.py:55
  66.8 14.7 %collective-permute-start.11 = (bf16[2,2,24,768]{3,2,1,0:T(8,128)(2,1)S(1)}, bf16[2,2,24,768]{3,2,1,0:T(8,128)(2,1)S(1)}, u32[]{:S(2)}, u32[]{:S(2)}) collective-permute-start(bf16[2,2,24,768]{3,2,1,0:T(8,128)(2,1)S(1)} %second_z.1.refs_0_), channel_id=1, source_target_pairs={{0,6},{1,7},{2,4},{3,5},{4,2},{5,3},{6,0},{7,1},{8,14},{9,15},{10,... | collective-permute-start | bytes 442376 | tf_op jit(solution)/shard_map/ppermute | solution.py:55
  68.5 13.9 %collective-permute-start.6 = (bf16[2,2,24,896]{3,2,1,0:T(8,128)(2,1)S(1)}, bf16[2,2,24,896]{3,2,1,0:T(8,128)(2,1)S(1)}, u32[]{:S(2)}, u32[]{:S(2)}) collective-permute-start(bf16[2,2,24,896]{3,2,1,0:T(8,128)(2,1)S(1)} %first_y.1.refs_0_), channel_id=1, source_target_pairs={{0,8},{1,9},{2,10},{3,11},{4,12},{5,13},{6,14},{7,15},{8,0},{9,1},... | collective-permute-start | bytes 516104 | tf_op jit(solution)/shard_map/ppermute | solution.py:55
  69.9 14.0 %collective-permute-start.7 = (bf16[2,2,24,896]{3,2,1,0:T(8,128)(2,1)S(1)}, bf16[2,2,24,896]{3,2,1,0:T(8,128)(2,1)S(1)}, u32[]{:S(2)}, u32[]{:S(2)}) collective-permute-start(bf16[2,2,24,896]{3,2,1,0:T(8,128)(2,1)S(1)} %first_y.1.refs_0_), channel_id=1, source_target_pairs={{0,64},{1,65},{2,66},{3,67},{4,68},{5,69},{6,70},{7,71},{8,72},{9,... | collective-permute-start | bytes 516104 | tf_op jit(solution)/shard_map/ppermute | solution.py:55
  76.9 10.5 %collective-permute-start.8 = (bf16[2,2,24,896]{3,2,1,0:T(8,128)(2,1)S(1)}, bf16[2,2,24,896]{3,2,1,0:T(8,128)(2,1)S(1)}, u32[]{:S(2)}, u32[]{:S(2)}) collective-permute-start(bf16[2,2,24,896]{3,2,1,0:T(8,128)(2,1)S(1)} %first_y.1.refs_0_), channel_id=1, source_target_pairs={{0,72},{1,73},{2,74},{3,75},{4,76},{5,77},{6,78},{7,79},{8,64},{9,... | collective-permute-start | bytes 516104 | tf_op jit(solution)/shard_map/ppermute | solution.py:55
  90.3 44.0 %all-to-all-start.3 = ((bf16[64,8,1664]{2,1,0:T(8,128)(2,1)}), bf16[64,8,1664]{2,1,0:T(8,128)(2,1)}, u32[]{:S(2)}, u32[]{:S(2)}) async-start(bf16[64,8,1664]{2,1,0:T(8,128)(2,1)} %bitcast.117), calls=%async_computation.3 | async-start | bytes 3407872 | tf_op jit(solution)/shard_map/all_to_all | solution.py:47
  94.9 114.9 %all-gather.5.cloned.1.call-start = ((), (), s32[]{:S(2)}) async-start(), calls=%async_computation.12 | async-start | bytes 5308416 | tf_op jit(solution)/shard_map/all_gather | solution.py:1098
  94.9 25.0 %collective-permute-start.12 = (bf16[2,2,4,24,896]{4,3,2,1,0:T(8,128)(2,1)S(1)}, bf16[2,2,4,24,896]{4,3,2,1,0:T(8,128)(2,1)S(1)}, u32[]{:S(2)}, u32[]{:S(2)}) collective-permute-start(bf16[2,2,4,24,896]{4,3,2,1,0:T(8,128)(2,1)S(1)} %bitcast.107), channel_id=1, source_target_pairs={{0,16},{1,17},{2,18},{3,19},{4,20},{5,21},{6,22},{7,23},{8,24},{9,... | collective-permute-start | bytes 2064392 | tf_op jit(solution)/shard_map/ppermute | solution.py:55
  96.3 38.0 %collective-permute-start.13 = (bf16[2,2,4,24,896]{4,3,2,1,0:T(8,128)(2,1)S(1)}, bf16[2,2,4,24,896]{4,3,2,1,0:T(8,128)(2,1)}, u32[]{:S(2)}, u32[]{:S(2)}) collective-permute-start(bf16[2,2,4,24,896]{4,3,2,1,0:T(8,128)(2,1)S(1)} %bitcast.108), channel_id=1, source_target_pairs={{0,32},{1,33},{2,34},{3,35},{4,36},{5,37},{6,38},{7,39},{8,40},{9,... | collective-permute-start | bytes 2064392 | tf_op jit(solution)/shard_map/ppermute | solution.py:55
  98.7 35.5 %collective-permute-start.14 = (bf16[2,2,4,24,896]{4,3,2,1,0:T(8,128)(2,1)S(1)}, bf16[2,2,4,24,896]{4,3,2,1,0:T(8,128)(2,1)}, u32[]{:S(2)}, u32[]{:S(2)}) collective-permute-start(bf16[2,2,4,24,896]{4,3,2,1,0:T(8,128)(2,1)S(1)} %bitcast.109), channel_id=1, source_target_pairs={{0,48},{1,49},{2,50},{3,51},{4,52},{5,53},{6,54},{7,55},{8,56},{9,... | collective-permute-start | bytes 2064392 | tf_op jit(solution)/shard_map/ppermute | solution.py:55
  99.7 19.9 %collective-permute-start.15 = (bf16[128,768]{1,0:T(8,128)(2,1)}, bf16[128,768]{1,0:T(8,128)(2,1)S(1)}, u32[]{:S(2)}, u32[]{:S(2)}) collective-permute-start(bf16[128,768]{1,0:T(8,128)(2,1)} %get-tuple-element.185), channel_id=1, source_target_pairs={{0,1},{1,2},{2,3},{4,5},{5,6},{6,7},{8,9},{9,10},{10,11},{12,13},{... | collective-permute-start | bytes 589832 | tf_op jit(solution)/shard_map/ppermute | solution.py:1099
  104.0 15.9 %collective-permute-start.16 = (bf16[128,768]{1,0:T(8,128)(2,1)}, bf16[128,768]{1,0:T(8,128)(2,1)}, u32[]{:S(2)}, u32[]{:S(2)}) collective-permute-start(bf16[128,768]{1,0:T(8,128)(2,1)} %get-tuple-element.184), channel_id=1, source_target_pairs={{1,0},{2,1},{3,2},{5,4},{6,5},{7,6},{9,8},{10,9},{11,10},{13,12},{... | collective-permute-start | bytes 589832 | tf_op jit(solution)/shard_map/ppermute | solution.py:1100
  137.3 14.5 %collective-permute-start.17 = (bf16[2,768,896]{2,1,0:T(8,128)(2,1)}, bf16[2,768,896]{2,1,0:T(8,128)(2,1)}, u32[]{:S(2)}, u32[]{:S(2)}) collective-permute-start(bf16[2,768,896]{2,1,0:T(8,128)(2,1)} %bitcast.28.mine.first_mine), channel_id=1, source_target_pairs={{0,1},{1,0},{2,3},{3,2},{4,5},{5,4},{6,7},{7,6},{8,9},{9,8},{10,11... | collective-permute-start | bytes 8257544 | tf_op jit(solution)/shard_map/ppermute | solution.py:51
  146.0 38.2 %all-to-all-start.4 = ((bf16[64,8,1664]{2,1,0:T(8,128)(2,1)}), bf16[64,8,1664]{2,1,0:T(8,128)(2,1)}, u32[]{:S(2)}, u32[]{:S(2)}) async-start(bf16[64,8,1664]{2,1,0:T(8,128)(2,1)} %gather_fusion.1), calls=%async_computation.4 | async-start | bytes 3407872 | tf_op jit(solution)/shard_map/all_to_all | solution.py:47
  151.9 32.8 %collective-permute-start.18 = (bf16[2,2,4,24,768]{4,3,2,1,0:T(8,128)(2,1)S(1)}, bf16[2,2,4,24,768]{4,3,2,1,0:T(8,128)(2,1)S(1)}, u32[]{:S(2)}, u32[]{:S(2)}) collective-permute-start(bf16[2,2,4,24,768]{4,3,2,1,0:T(8,128)(2,1)S(1)} %bitcast.111), channel_id=1, source_target_pairs={{0,16},{1,17},{2,18},{3,19},{4,20},{5,21},{6,22},{7,23},{8,24},{9,... | collective-permute-start | bytes 1769480 | tf_op jit(solution)/shard_map/ppermute | solution.py:55
  152.0 34.9 %collective-permute-start.19 = (bf16[2,2,4,24,768]{4,3,2,1,0:T(8,128)(2,1)S(1)}, bf16[2,2,4,24,768]{4,3,2,1,0:T(8,128)(2,1)}, u32[]{:S(2)}, u32[]{:S(2)}) collective-permute-start(bf16[2,2,4,24,768]{4,3,2,1,0:T(8,128)(2,1)S(1)} %bitcast.112), channel_id=1, source_target_pairs={{0,32},{1,33},{2,34},{3,35},{4,36},{5,37},{6,38},{7,39},{8,40},{9,... | collective-permute-start | bytes 1769480 | tf_op jit(solution)/shard_map/ppermute | solution.py:55
  153.3 33.6 %collective-permute-start.20 = (bf16[2,2,4,24,768]{4,3,2,1,0:T(8,128)(2,1)S(1)}, bf16[2,2,4,24,768]{4,3,2,1,0:T(8,128)(2,1)}, u32[]{:S(2)}, u32[]{:S(2)}) collective-permute-start(bf16[2,2,4,24,768]{4,3,2,1,0:T(8,128)(2,1)S(1)} %bitcast.113), channel_id=1, source_target_pairs={{0,48},{1,49},{2,50},{3,51},{4,52},{5,53},{6,54},{7,55},{8,56},{9,... | collective-permute-start | bytes 1769480 | tf_op jit(solution)/shard_map/ppermute | solution.py:55
  191.4 18.4 %collective-permute-start.21 = (bf16[2,768,768]{2,1,0:T(8,128)(2,1)S(1)}, bf16[2,768,768]{2,1,0:T(8,128)(2,1)}, u32[]{:S(2)}, u32[]{:S(2)}) collective-permute-start(bf16[2,768,768]{2,1,0:T(8,128)(2,1)S(1)} %bitcast.104), channel_id=1, source_target_pairs={{0,1},{1,0},{2,3},{3,2},{4,5},{5,4},{6,7},{7,6},{8,9},{9,8},{10,11... | collective-permute-start | bytes 7077896 | tf_op jit(solution)/shard_map/ppermute | solution.py:51
  192.7 15.6 %all-to-all-start.5 = ((bf16[4,816,128]{2,1,0:T(8,128)(2,1)}), bf16[4,816,128]{2,1,0:T(8,128)(2,1)}, u32[]{:S(2)}, u32[]{:S(2)}) async-start(bf16[4,816,128]{2,1,0:T(8,128)(2,1)} %broadcast_in_dim.137), calls=%async_computation.5 | async-start | bytes 1671168 | tf_op jit(solution)/shard_map/all_to_all | solution.py:47
  196.9 197.3 %reduce-scatter.2.cloned.1.call-start = ((), (), s32[]{:S(2)}) async-start(), calls=%async_computation.13 | async-start | bytes 5013504 | tf_op jit(solution)/shard_map/reduce_scatter | solution.py:1198
  251.0 33.6 %collective-permute-start.22 = (bf16[2,768,768]{2,1,0:T(8,128)(2,1)}, bf16[2,768,768]{2,1,0:T(8,128)(2,1)S(1)}, u32[]{:S(2)}, u32[]{:S(2)}) collective-permute-start(bf16[2,768,768]{2,1,0:T(8,128)(2,1)} %get-tuple-element.130), channel_id=1, source_target_pairs={{0,1},{1,0},{2,3},{3,2},{4,5},{5,4},{6,7},{7,6},{8,9},{9,8},{10,11... | collective-permute-start | bytes 7077896 | tf_op jit(solution)/shard_map/ppermute | solution.py:51
  286.8 42.3 %all-to-all-start.6 = ((bf16[64,24,768]{2,1,0:T(8,128)(2,1)}), bf16[64,24,768]{2,1,0:T(8,128)(2,1)}, u32[]{:S(2)}, u32[]{:S(2)}) async-start(bf16[64,24,768]{2,1,0:T(8,128)(2,1)} %bitcast.42), calls=%async_computation.6 | async-start | bytes 4718592 | tf_op jit(solution)/shard_map/all_to_all | solution.py:47
  306.5 20.3 %collective-permute-start.23 = (bf16[128,768]{1,0:T(8,128)(2,1)}, bf16[128,768]{1,0:T(8,128)(2,1)S(1)}, u32[]{:S(2)}, u32[]{:S(2)}) collective-permute-start(bf16[128,768]{1,0:T(8,128)(2,1)} %get-tuple-element.143), channel_id=1, source_target_pairs={{0,1},{1,2},{2,3},{4,5},{5,6},{6,7},{8,9},{9,10},{10,11},{12,13},{... | collective-permute-start | bytes 589832 | tf_op jit(solution)/shard_map/ppermute | solution.py:1193
  309.6 18.3 %collective-permute-start.24 = (bf16[128,768]{1,0:T(8,128)(2,1)}, bf16[128,768]{1,0:T(8,128)(2,1)S(1)}, u32[]{:S(2)}, u32[]{:S(2)}) collective-permute-start(bf16[128,768]{1,0:T(8,128)(2,1)} %get-tuple-element.144), channel_id=1, source_target_pairs={{1,0},{2,1},{3,2},{5,4},{6,5},{7,6},{9,8},{10,9},{11,10},{13,12},{... | collective-permute-start | bytes 589832 | tf_op jit(solution)/shard_map/ppermute | solution.py:1194
  329.2 31.1 %all-to-all-start.7 = ((bf16[64,8,1536]{2,1,0:T(8,128)(2,1)}), bf16[64,8,1536]{2,1,0:T(8,128)(2,1)}, u32[]{:S(2)}, u32[]{:S(2)}) async-start(bf16[64,8,1536]{2,1,0:T(8,128)(2,1)} %pack_rows.1), calls=%async_computation.7 | async-start | bytes 3145728 | tf_op jit(solution)/shard_map/all_to_all | solution.py:47
  341.0 22.5 %collective-permute-start.26 = (bf16[17,24,768]{2,1,0:T(8,128)(2,1)}, bf16[17,24,768]{2,1,0:T(8,128)(2,1)S(1)}, u32[]{:S(2)}, u32[]{:S(2)}) collective-permute-start(bf16[17,24,768]{2,1,0:T(8,128)(2,1)} %get-tuple-element.148), channel_id=1, source_target_pairs={{0,16},{1,17},{2,18},{3,19},{4,20},{5,21},{6,22},{7,23},{8,24},{9,... | collective-permute-start | bytes 1880072 | tf_op jit(solution)/shard_map/ppermute | solution.py:55
  341.8 30.9 %collective-permute-start.27 = (bf16[17,24,768]{2,1,0:T(8,128)(2,1)}, bf16[17,24,768]{2,1,0:T(8,128)(2,1)S(1)}, u32[]{:S(2)}, u32[]{:S(2)}) collective-permute-start(bf16[17,24,768]{2,1,0:T(8,128)(2,1)} %get-tuple-element.149), channel_id=1, source_target_pairs={{0,32},{1,33},{2,34},{3,35},{4,36},{5,37},{6,38},{7,39},{8,40},{9,... | collective-permute-start | bytes 1880072 | tf_op jit(solution)/shard_map/ppermute | solution.py:55
  344.9 29.8 %collective-permute-start.28 = (bf16[17,24,768]{2,1,0:T(8,128)(2,1)}, bf16[17,24,768]{2,1,0:T(8,128)(2,1)S(1)}, u32[]{:S(2)}, u32[]{:S(2)}) collective-permute-start(bf16[17,24,768]{2,1,0:T(8,128)(2,1)} %get-tuple-element.150), channel_id=1, source_target_pairs={{0,48},{1,49},{2,50},{3,51},{4,52},{5,53},{6,54},{7,55},{8,56},{9,... | collective-permute-start | bytes 1880072 | tf_op jit(solution)/shard_map/ppermute | solution.py:55
  375.5 41.2 %all-to-all-start.8 = ((bf16[64,8,1536]{2,1,0:T(8,128)(2,1)}), bf16[64,8,1536]{2,1,0:T(8,128)(2,1)S(1)}, u32[]{:S(2)}, u32[]{:S(2)}) async-start(bf16[64,8,1536]{2,1,0:T(8,128)(2,1)} %gather_fusion.2), calls=%async_computation.8 | async-start | bytes 3145728 | tf_op jit(solution)/shard_map/all_to_all | solution.py:47
  387.2 18.2 %collective-permute-start.29 = (bf16[5,24,768]{2,1,0:T(8,128)(2,1)S(1)}, bf16[5,24,768]{2,1,0:T(8,128)(2,1)S(1)}, u32[]{:S(2)}, u32[]{:S(2)}) collective-permute-start(bf16[5,24,768]{2,1,0:T(8,128)(2,1)S(1)} %get-tuple-element.159), channel_id=1, source_target_pairs={{0,8},{1,9},{2,10},{3,11},{4,12},{5,13},{6,14},{7,15},{8,0},{9,1},... | collective-permute-start | bytes 552968 | tf_op jit(solution)/shard_map/ppermute | solution.py:55
  388.8 22.8 %collective-permute-start.30 = (bf16[5,24,768]{2,1,0:T(8,128)(2,1)S(1)}, bf16[5,24,768]{2,1,0:T(8,128)(2,1)S(1)}, u32[]{:S(2)}, u32[]{:S(2)}) collective-permute-start(bf16[5,24,768]{2,1,0:T(8,128)(2,1)S(1)} %get-tuple-element.160), channel_id=1, source_target_pairs={{0,64},{1,65},{2,66},{3,67},{4,68},{5,69},{6,70},{7,71},{8,72},{9,... | collective-permute-start | bytes 552968 | tf_op jit(solution)/shard_map/ppermute | solution.py:55
  392.1 19.4 %collective-permute-start.31 = (bf16[5,24,768]{2,1,0:T(8,128)(2,1)S(1)}, bf16[5,24,768]{2,1,0:T(8,128)(2,1)S(1)}, u32[]{:S(2)}, u32[]{:S(2)}) collective-permute-start(bf16[5,24,768]{2,1,0:T(8,128)(2,1)S(1)} %get-tuple-element.161), channel_id=1, source_target_pairs={{0,72},{1,73},{2,74},{3,75},{4,76},{5,77},{6,78},{7,79},{8,64},{9,... | collective-permute-start | bytes 552968 | tf_op jit(solution)/shard_map/ppermute | solution.py:55
  395.2 20.1 %collective-permute-start.37 = (bf16[2,24,768]{2,1,0:T(8,128)(2,1)S(1)}, bf16[2,24,768]{2,1,0:T(8,128)(2,1)S(1)}, u32[]{:S(2)}, u32[]{:S(2)}) collective-permute-start(bf16[2,24,768]{2,1,0:T(8,128)(2,1)S(1)} %get-tuple-element.191), channel_id=1, source_target_pairs={{0,48},{1,49},{2,50},{3,51},{4,52},{5,53},{6,54},{7,55},{8,56},{9,... | collective-permute-start | bytes 221192 | tf_op jit(solution)/shard_map/ppermute | solution.py:55
  395.3 20.3 %collective-permute-start.36 = (bf16[2,24,768]{2,1,0:T(8,128)(2,1)S(1)}, bf16[2,24,768]{2,1,0:T(8,128)(2,1)S(1)}, u32[]{:S(2)}, u32[]{:S(2)}) collective-permute-start(bf16[2,24,768]{2,1,0:T(8,128)(2,1)S(1)} %get-tuple-element.192), channel_id=1, source_target_pairs={{0,32},{1,33},{2,34},{3,35},{4,36},{5,37},{6,38},{7,39},{8,40},{9,... | collective-permute-start | bytes 221192 | tf_op jit(solution)/shard_map/ppermute | solution.py:55
  405.4 10.2 %collective-permute-start.35 = (bf16[2,24,768]{2,1,0:T(8,128)(2,1)S(1)}, bf16[2,24,768]{2,1,0:T(8,128)(2,1)S(1)}, u32[]{:S(2)}, u32[]{:S(2)}) collective-permute-start(bf16[2,24,768]{2,1,0:T(8,128)(2,1)S(1)} %get-tuple-element.190), channel_id=1, source_target_pairs={{0,16},{1,17},{2,18},{3,19},{4,20},{5,21},{6,22},{7,23},{8,24},{9,... | collective-permute-start | bytes 221192 | tf_op jit(solution)/shard_map/ppermute | solution.py:55
  411.7 9.9 %collective-permute-start.32 = (bf16[2,24,768]{2,1,0:T(8,128)(2,1)S(1)}, bf16[2,24,768]{2,1,0:T(8,128)(2,1)S(1)}, u32[]{:S(2)}, u32[]{:S(2)}) collective-permute-start(bf16[2,24,768]{2,1,0:T(8,128)(2,1)S(1)} %get-tuple-element.163), channel_id=1, source_target_pairs={{0,2},{1,3},{2,0},{3,1},{4,6},{5,7},{6,4},{7,5},{8,10},{9,11},{10,... | collective-permute-start | bytes 221192 | tf_op jit(solution)/shard_map/ppermute | solution.py:55
  423.3 14.7 %all-to-all-start.9 = ((f32[4,48,768]{2,1,0:T(8,128)}), f32[4,48,768]{2,1,0:T(8,128)S(1)}, u32[]{:S(2)}, u32[]{:S(2)}) async-start(f32[4,48,768]{2,1,0:T(8,128)} %maximum_maximum_fusion), calls=%async_computation.10 | async-start | bytes 1179648 | tf_op jit(solution)/shard_map/all_to_all | solution.py:47
  (52 other events, 409.0 us)
Sparse Core Ops, SparseCore 0:
  26.6 40.8 all-gather.2
  108.1 99.5 all-gather.4
  261.2 91.4 reduce-scatter.1

commit v6 on v5

--- a/solution.py
+++ b/solution.py
@@ -1194,7 +1194,7 @@
     from_right = lax.ppermute(back_left, "fsdp", TO_LEFT)
     both = pack_rows(result, grad_nat, from_left, from_right)
     one_send, one_keep = weight_grad(place, acts, grads, wattn_grad, totals)
-    one_send, one_keep, two, both = lax.optimization_barrier((one_send, one_keep, two, both))
+    one_keep, two = lax.optimization_barrier((one_keep, two))
     out_grad = lax.psum_scatter(
         wout_grad.reshape(4 * D, D), "fsdp", scatter_dimension=0, tiled=True
     )
@@ -1206,7 +1206,7 @@
         4,
         "one_x",
     )
-    both = exchange(both, "fsdp")[order]
+    both = exchange(after(both, two), "fsdp")[order]
     out_grad = after(out_grad, both).reshape(2, 4, 24, D)
     cut = [
         lax.dynamic_index_in_dim(out_grad, spot["x"][0] ^ k, 1, keepdims=False) for k in range(4)
@@ -1237,7 +1237,7 @@
         ],
         1,
     )
-    closing = exchange(after(closing, out_long), "fsdp", QUADS)
+    closing = exchange(after(closing.astype(bf16), out_long), "fsdp", QUADS).astype(f32)
     grad_glob = lax.dynamic_slice_in_dim(grad_middle, ROWS + quarter * 32, 32, 0) + jnp.sum(
         closing[:, :32], 0
     )

time: 454 us -> 448 us (0.987)
  local copies, waits for them, and re-layouts: 49.5 us -> 42.6 us
  Pallas kernels: 118 us -> 123 us
    unnamed x100 -> x98, local copies, waits for them, and re-layouts: 23.5 us -> 15 us
  transfers between devices with their start and end apart: 52 -> 52, of which waited for: 21 -> 21; matrix products, arithmetic and copies ran while one was open for 8% -> 8% of each run, Pallas kernels for 17% -> 19%
where the time goes in v6:
time: 448 us; the launch traced here: 443 us
  starting transfers between devices  131 us (29%)
  Pallas kernels  123 us (27%)
  waiting for transfers between devices  104 us (23%)
  local copies, waits for them, and re-layouts  42.6 us (10%)
  other arithmetic  21.2 us (5%)
  between operations  20.5 us (5%)
    all_to_all x10, starting transfers between devices, exchange(): lax.all_to_all(value, axis, 0, 0, axis_index_groups=groups, tiled=True)  58.2 us
    ppermute x30, waiting for transfers between devices, relay(): lax.ppermute(value, BOTH, pairs)  54.5 us
    ppermute x30, starting transfers between devices, relay(): lax.ppermute(value, BOTH, pairs)  47.1 us
    pallas_call x1, Pallas kernels, feed(): pl.pallas_call(feed_kernel, grid_spec=pltpu.PrefetchScalarGridSpec(num_sc...  41.1 us
    all_to_all x10, waiting for transfers between devices, exchange(): lax.all_to_all(value, axis, 0, 0, axis_index_groups=groups, tiled=True)  29.5 us
    pallas_call x1, Pallas kernels, attend_back(): pl.pallas_call(attend_back_kernel, grid=(6,), in_specs=[SCALARS, SCALARS,...  20.7 us
    pallas_call x1, Pallas kernels, attend(): pl.pallas_call(attend_kernel, grid=(6,), in_specs=[SCALARS, SCALARS, pl.B...  15.6 us
    unnamed x98, local copies, waits for them, and re-layouts  15 us
  transfers between devices with their start and end apart: 52, of which 21 were waited for; matrix products, arithmetic and copies ran while one was open for 8% of the time, Pallas kernels for 19%

profile of v6, /device:TPU:1, one launch (start us, length us, event | category | flops | bytes accessed | tf_op | source)
XLA Modules:
  0.0 443.2 jit_solution(8241032361847091328)
XLA Ops:
  18.6 4.9 %all-to-all-start = ((bf16[4,88,768]{2,1,0:T(8,128)(2,1)}), bf16[4,88,768]{2,1,0:T(8,128)(2,1)S(1)}, u32[]{:S(2)}, u32[]{:S(2)}) async-start(bf16[4,88,768]{2,1,0:T(8,128)(2,1)} %pad_maximum_fusion.1), calls=%async_computation | async-start | bytes 1081344 | tf_op jit(solution)/shard_map/all_to_all | solution.py:47
  26.2 5.5 %all-to-all-done = bf16[4,88,768]{2,1,0:T(8,128)(2,1)S(1)} async-done(((bf16[4,88,768]{2,1,0:T(8,128)(2,1)}), bf16[4,88,768]{2,1,0:T(8,128)(2,1)S(1)}, u32[]{:S(2)}, u32[]{:S(2)}) %all-to-all-start) | async-done | bytes 540704 | tf_op jit(solution)/shard_map/all_to_all | solution.py:47
  32.7 6.8 %all-to-all-start.1 = ((bf16[64,8,768]{2,1,0:T(8,128)(2,1)}), bf16[64,8,768]{2,1,0:T(8,128)(2,1)S(1)}, u32[]{:S(2)}, u32[]{:S(2)}) async-start(bf16[64,8,768]{2,1,0:T(8,128)(2,1)} %bitcast.15), calls=%async_computation.1 | async-start | bytes 1572864 | tf_op jit(solution)/shard_map/all_to_all | solution.py:47
  41.7 3.3 collective-permute-start.4
  49.3 6.4 %collective-permute-start.2 = (bf16[24,896]{1,0:T(8,128)(2,1)S(1)}, bf16[24,896]{1,0:T(8,128)(2,1)S(1)}, u32[]{:S(2)}, u32[]{:S(2)}) collective-permute-start(bf16[24,896]{1,0:T(8,128)(2,1)S(1)} %constant_dynamic-update-slice_fusion.refs_0_), channel_id=1, source_target_pairs={{0,6},{1,7},{2,4},{3,5},{4,2},{5,3},{6,0},{7,1},{8,14},{9,15},{10,... | collective-permute-start | bytes 129032 | tf_op jit(solution)/shard_map/ppermute | solution.py:55
  57.7 5.2 %all-to-all-start.2 = ((bf16[64,8,768]{2,1,0:T(8,128)(2,1)}), bf16[64,8,768]{2,1,0:T(8,128)(2,1)}, u32[]{:S(2)}, u32[]{:S(2)}) async-start(bf16[64,8,768]{2,1,0:T(8,128)(2,1)} %gather_fusion), calls=%async_computation.2 | async-start | bytes 1572864 | tf_op jit(solution)/shard_map/all_to_all | solution.py:47
  69.9 3.2 collective-permute-start.7
  73.1 3.8 collective-permute-done.9.refs_1_
  76.9 3.2 collective-permute-start.8
  81.6 2.9 collective-permute-done.7.refs_2_
  84.5 3.5 collective-permute-done.8.refs_3_
  91.1 4.6 %all-to-all-start.3 = ((bf16[64,8,1664]{2,1,0:T(8,128)(2,1)}), bf16[64,8,1664]{2,1,0:T(8,128)(2,1)}, u32[]{:S(2)}, u32[]{:S(2)}) async-start(bf16[64,8,1664]{2,1,0:T(8,128)(2,1)} %bitcast.114), calls=%async_computation.3 | async-start | bytes 3407872 | tf_op jit(solution)/shard_map/all_to_all | solution.py:47
  97.2 2.4 collective-permute-start.13
  100.5 4.4 collective-permute-start.15
  108.8 11.6 %collective-permute-done.15.left = bf16[128,768]{1,0:T(8,128)(2,1)S(1)} collective-permute-done((bf16[128,768]{1,0:T(8,128)(2,1)}, bf16[128,768]{1,0:T(8,128)(2,1)S(1)}, u32[]{:S(2)}, u32[]{:S(2)}) %collective-permute-start.15) | collective-permute-done | bytes 196640 | tf_op jit(solution)/shard_map/ppermute | solution.py:1099
  120.8 14.4 %collective-permute-done.13.refs_2_ = bf16[2,2,4,24,896]{4,3,2,1,0:T(8,128)(2,1)} collective-permute-done((bf16[2,2,4,24,896]{4,3,2,1,0:T(8,128)(2,1)S(1)}, bf16[2,2,4,24,896]{4,3,2,1,0:T(8,128)(2,1)}, u32[]{:S(2)}, u32[]{:S(2)}) %collective-permute-start.13) | collective-permute-done | bytes 688160 | tf_op jit(solution)/shard_map/ppermute | solution.py:55
  135.2 3.2 first_x.1
  143.9 3.4 gather_fusion.1
  147.3 5.8 %all-to-all-start.4 = ((bf16[64,8,1664]{2,1,0:T(8,128)(2,1)}), bf16[64,8,1664]{2,1,0:T(8,128)(2,1)}, u32[]{:S(2)}, u32[]{:S(2)}) async-start(bf16[64,8,1664]{2,1,0:T(8,128)(2,1)} %gather_fusion.1), calls=%async_computation.4 | async-start | bytes 3407872 | tf_op jit(solution)/shard_map/all_to_all | solution.py:47
  154.5 2.8 collective-permute-start.20
  157.3 7.6 %project.1 = (bf16[896,768]{1,0:T(8,128)(2,1)S(1)}, bf16[896,768]{1,0:T(8,128)(2,1)}, bf16[896,2304]{1,0:T(8,128)(2,1)}) custom-call(s32[2]{0:T(128)S(1)} %pad_add_fusion.place, bf16[128,768]{1,0:T(8,128)(2,1)S(1)} %copy-done.15, bf16[512,768]{1,0:T(8,128)(2,1)S(1)} %bitcast.101, bf16[128,768]{1,0:T(8,128)(2,1)S(1)} %copy-done.17, ...), custom_call_target="tpu_custom_call" | custom-call | flops 9900000256 | bytes 32400000 | tf_op jit(solution)/shard_map/project/pallas_call | solution.py:316
  165.0 2.7 copy-done.24
  167.6 15.6 %attend.1 = (bf16[512,768]{1,0:T(8,128)(2,1)S(1)}, f32[6,4,256]{2,1,0:T(4,128)S(1)}, bf16[768,128]{1,0:T(8,128)(2,1)S(1)}, f32[6,1,256]{2,1,0:T(1,128)S(1)}) custom-call(s32[2]{0:T(128)S(1)} %pad_add_fusion.place, f32[2,12]{1,0:T(2,128)S(1)} %copy.75.table, f32[6,2,512]{2,1,0:T(2,128)S(1)} %reshape.353.line, f32[896,256]{1,0:T(8,128)S(1)} %broadcast_in_dim.129.key_mask, ...), custom_call_target="tpu_custom_call" | custom-call | flops 16499999744 | bytes 54000000 | tf_op jit(solution)/shard_map/attend/pallas_call | solution.py:434
  184.6 2.9 collective-permute-done.19.refs_2_
  188.5 3.0 second_x.1
  192.5 3.6 all-to-all-start.5
  197.7 2.9 copy.70
  200.6 6.9 %all-to-all-done.5.parts = bf16[4,816,128]{2,1,0:T(8,128)(2,1)S(1)} async-done(((bf16[4,816,128]{2,1,0:T(8,128)(2,1)}), bf16[4,816,128]{2,1,0:T(8,128)(2,1)S(1)}, u32[]{:S(2)}, u32[]{:S(2)}) %all-to-all-start.5) | async-done | bytes 835616 | tf_op jit(solution)/shard_map/all_to_all | solution.py:47
  208.4 41.1 %feed.1 = (bf16[640,768]{1,0:T(8,128)(2,1)}, f32[8,128]{1,0:T(8,128)}, bf16[768,128]{1,0:T(8,128)(2,1)}, f32[640,768]{1,0:T(8,128)}, bf16[640,768]{1,0:T(8,128)(...) custom-call(s32[2]{0:T(128)} %copy-done.6, ...), custom_call_target="tpu_custom_call" | custom-call | flops 47300001792 | bytes 154800000 | tf_op jit(solution)/shard_map/feed/pallas_call | solution.py:789
  249.6 10.0 %collective-permute-start.22 = (bf16[2,768,768]{2,1,0:T(8,128)(2,1)}, bf16[2,768,768]{2,1,0:T(8,128)(2,1)}, u32[]{:S(2)}, u32[]{:S(2)}) collective-permute-start(bf16[2,768,768]{2,1,0:T(8,128)(2,1)} %get-tuple-element.129), channel_id=1, source_target_pairs={{0,1},{1,0},{2,3},{3,2},{4,5},{5,4},{6,7},{7,6},{8,9},{9,8},{10,11... | collective-permute-start | bytes 7077896 | tf_op jit(solution)/shard_map/ppermute | solution.py:51
  260.8 20.7 %attend_back.1 = (bf16[3,896,768]{2,1,0:T(8,128)(2,1)}, f32[6,8,512]{2,1,0:T(8,128)S(1)}) custom-call(s32[2]{0:T(128)S(1)} %copy-done.7, f32[2,12]{1,0:T(2,128)S(1)} %copy.75.table, f32[6,2,512]{2,1,0:T(2,128)S(1)} %reshape.353.line, f32[896,256]{1,0:T(8,128)S(1)} %broadcast_in_dim.129.key_mask, f32[128,256]{1,0:T(8,128)S(1)} %broadcast_in_dim.132.self_mask, ...), custom_call_target="tpu_custom_call" | custom-call | flops 23100000256 | bytes 75600000 | tf_op jit(solution)/shard_map/attend_back/pallas_call | solution.py:576
  281.6 4.2 add_cores.1
  285.8 7.9 %all-to-all-start.6 = ((bf16[64,24,768]{2,1,0:T(8,128)(2,1)}), bf16[64,24,768]{2,1,0:T(8,128)(2,1)}, u32[]{:S(2)}, u32[]{:S(2)}) async-start(bf16[64,24,768]{2,1,0:T(8,128)(2,1)} %bitcast.42), calls=%async_computation.6 | async-start | bytes 4718592 | tf_op jit(solution)/shard_map/all_to_all | solution.py:47
  293.7 11.7 %input_grad.1 = (f32[512,768]{1,0:T(8,128)}, bf16[128,768]{1,0:T(8,128)(2,1)}, bf16[128,768]{1,0:T(8,128)(2,1)}, f32[128,768]{1,0:T(8,128)}, bf16[1,24,768]{2,1,0:T(8,128)(2,1)}) custom-call(s32[2]{0:T(128)} %copy-done.6, bf16[896,768]{1,0:T(8,128)(2,1)} %copy-done.25, bf16[3,896,768]{2,1,0:T(8,128)(2,1)} %get-tuple-element.130.grads, f32[8,768]{1,0:T(8,128)} %copy-done.4, ...), custom_call_target="tpu_custom_call" | custom-call | flops 65999998976 | bytes 216000000 | tf_op jit(solution)/shard_map/input_grad/pallas_call | solution.py:903
  306.3 8.6 %weight_grad.1 = (bf16[65,24,768]{2,1,0:T(8,128)(2,1)}, bf16[65,24,768]{2,1,0:T(8,128)(2,1)}) custom-call(s32[2]{0:T(128)S(1)} %copy-done.8, bf16[896,768]{1,0:T(8,128)(2,1)S(1)} %copy-done, bf16[3,896,768]{2,1,0:T(8,128)(2,1)} %get-tuple-element.130.grads, bf16[768,768]{1,0:T(8,128)(2,1)S(1)} %copy-done.1, bf16[1,24,768]{2,1,0:T(8,128)(2,1)S(1)} %copy-done.3), custom_call_target="tpu_custom_call" | custom-call | flops 110000000 | bytes 360000 | tf_op jit(solution)/shard_map/weight_grad/pallas_call | solution.py:974
  314.9 3.4 collective-permute-start.27
  320.2 5.4 %collective-permute-done.27.left_ref = bf16[128,768]{1,0:T(8,128)(2,1)S(1)} collective-permute-done((bf16[128,768]{1,0:T(8,128)(2,1)S(1)}, bf16[128,768]{1,0:T(8,128)(2,1)S(1)}, u32[]{:S(2)}, u32[]{:S(2)}) %collective-permute-start.27) | collective-permute-done | bytes 196640 | tf_op jit(solution)/shard_map/ppermute | solution.py:1193
  327.8 6.4 %all-to-all-start.7 = ((bf16[64,8,1536]{2,1,0:T(8,128)(2,1)}), bf16[64,8,1536]{2,1,0:T(8,128)(2,1)}, u32[]{:S(2)}, u32[]{:S(2)}) async-start(bf16[64,8,1536]{2,1,0:T(8,128)(2,1)} %pack_rows.1), calls=%async_computation.7 | async-start | bytes 3145728 | tf_op jit(solution)/shard_map/all_to_all | solution.py:47
  335.9 3.3 one_x.1
  340.9 2.7 collective-permute-start.25
  344.0 15.2 %all-to-all-done.7 = bf16[64,8,1536]{2,1,0:T(8,128)(2,1)} async-done(((bf16[64,8,1536]{2,1,0:T(8,128)(2,1)}), bf16[64,8,1536]{2,1,0:T(8,128)(2,1)}, u32[]{:S(2)}, u32[]{:S(2)}) %all-to-all-start.7) | async-done | bytes 1572896 | tf_op jit(solution)/shard_map/all_to_all | solution.py:47
  359.1 3.2 gather_fusion.2
  362.3 9.0 %collective-permute-done.25.refs_2_ = bf16[17,24,768]{2,1,0:T(8,128)(2,1)S(1)} collective-permute-done((bf16[17,24,768]{2,1,0:T(8,128)(2,1)}, bf16[17,24,768]{2,1,0:T(8,128)(2,1)S(1)}, u32[]{:S(2)}, u32[]{:S(2)}) %collective-permute-start.25) | collective-permute-done | bytes 626720 | tf_op jit(solution)/shard_map/ppermute | solution.py:55
  374.2 7.0 %all-to-all-start.8 = ((bf16[64,8,1536]{2,1,0:T(8,128)(2,1)}), bf16[64,8,1536]{2,1,0:T(8,128)(2,1)S(1)}, u32[]{:S(2)}, u32[]{:S(2)}) async-start(bf16[64,8,1536]{2,1,0:T(8,128)(2,1)} %gather_fusion.2), calls=%async_computation.8 | async-start | bytes 3145728 | tf_op jit(solution)/shard_map/all_to_all | solution.py:47
  394.4 9.9 %collective-permute-done.29.refs_1_ = bf16[5,24,768]{2,1,0:T(8,128)(2,1)S(1)} collective-permute-done((bf16[5,24,768]{2,1,0:T(8,128)(2,1)}, bf16[5,24,768]{2,1,0:T(8,128)(2,1)S(1)}, u32[]{:S(2)}, u32[]{:S(2)}) %collective-permute-start.29) | collective-permute-done | bytes 184352 | tf_op jit(solution)/shard_map/ppermute | solution.py:55
  404.3 4.3 collective-permute-done.30.refs_2_
  409.9 2.4 collective-permute-start.33
  420.3 6.0 %all-to-all-start.9 = ((bf16[4,48,768]{2,1,0:T(8,128)(2,1)}), bf16[4,48,768]{2,1,0:T(8,128)(2,1)S(1)}, u32[]{:S(2)}, u32[]{:S(2)}) async-start(bf16[4,48,768]{2,1,0:T(8,128)(2,1)} %maximum_maximum_fusion), calls=%async_computation.10 | async-start | bytes 589824 | tf_op jit(solution)/shard_map/all_to_all | solution.py:47
  (272 shorter events, 93.7 us)
Async XLA Ops:
  18.6 13.0 %all-to-all-start = ((bf16[4,88,768]{2,1,0:T(8,128)(2,1)}), bf16[4,88,768]{2,1,0:T(8,128)(2,1)S(1)}, u32[]{:S(2)}, u32[]{:S(2)}) async-start(bf16[4,88,768]{2,1,0:T(8,128)(2,1)} %pad_maximum_fusion.1), calls=%async_computation | async-start | bytes 1081344 | tf_op jit(solution)/shard_map/all_to_all | solution.py:47
  23.5 83.3 %all-gather.3.cloned.1.call-start = ((), (), s32[]{:S(2)}) async-start(), calls=%async_computation.11 | async-start | bytes 1253376 | tf_op jit(solution)/shard_map/all_gather | solution.py:1052
  32.7 23.5 %all-to-all-start.1 = ((bf16[64,8,768]{2,1,0:T(8,128)(2,1)}), bf16[64,8,768]{2,1,0:T(8,128)(2,1)S(1)}, u32[]{:S(2)}, u32[]{:S(2)}) async-start(bf16[64,8,768]{2,1,0:T(8,128)(2,1)} %bitcast.15), calls=%async_computation.1 | async-start | bytes 1572864 | tf_op jit(solution)/shard_map/all_to_all | solution.py:47
  40.2 9.1 %collective-permute-start.3 = (bf16[24,768]{1,0:T(8,128)(2,1)S(1)}, bf16[24,768]{1,0:T(8,128)(2,1)S(1)}, u32[]{:S(2)}, u32[]{:S(2)}) collective-permute-start(bf16[24,768]{1,0:T(8,128)(2,1)S(1)} %reshape.348.refs_0_), channel_id=1, source_target_pairs={{0,8},{1,9},{2,10},{3,11},{4,12},{5,13},{6,14},{7,15},{8,0},{9,1},... | collective-permute-start | bytes 110600 | tf_op jit(solution)/shard_map/ppermute | solution.py:55
  41.7 14.5 %collective-permute-start.4 = (bf16[24,768]{1,0:T(8,128)(2,1)S(1)}, bf16[24,768]{1,0:T(8,128)(2,1)S(1)}, u32[]{:S(2)}, u32[]{:S(2)}) collective-permute-start(bf16[24,768]{1,0:T(8,128)(2,1)S(1)} %reshape.348.refs_0_), channel_id=1, source_target_pairs={{0,64},{1,65},{2,66},{3,67},{4,68},{5,69},{6,70},{7,71},{8,72},{9,... | collective-permute-start | bytes 110600 | tf_op jit(solution)/shard_map/ppermute | solution.py:55
  45.0 11.2 %collective-permute-start.5 = (bf16[24,768]{1,0:T(8,128)(2,1)S(1)}, bf16[24,768]{1,0:T(8,128)(2,1)S(1)}, u32[]{:S(2)}, u32[]{:S(2)}) collective-permute-start(bf16[24,768]{1,0:T(8,128)(2,1)S(1)} %reshape.348.refs_0_), channel_id=1, source_target_pairs={{0,72},{1,73},{2,74},{3,75},{4,76},{5,77},{6,78},{7,79},{8,64},{9,... | collective-permute-start | bytes 110600 | tf_op jit(solution)/shard_map/ppermute | solution.py:55
  45.1 17.8 %collective-permute-start = (bf16[24,896]{1,0:T(8,128)(2,1)S(1)}, bf16[24,896]{1,0:T(8,128)(2,1)S(1)}, u32[]{:S(2)}, u32[]{:S(2)}) collective-permute-start(bf16[24,896]{1,0:T(8,128)(2,1)S(1)} %constant_dynamic-update-slice_fusion.refs_0_), channel_id=1, source_target_pairs={{0,2},{1,3},{2,0},{3,1},{4,6},{5,7},{6,4},{7,5},{8,10},{9,11},{10,... | collective-permute-start | bytes 129032 | tf_op jit(solution)/shard_map/ppermute | solution.py:55
  46.4 16.6 %collective-permute-start.1 = (bf16[24,896]{1,0:T(8,128)(2,1)S(1)}, bf16[24,896]{1,0:T(8,128)(2,1)S(1)}, u32[]{:S(2)}, u32[]{:S(2)}) collective-permute-start(bf16[24,896]{1,0:T(8,128)(2,1)S(1)} %constant_dynamic-update-slice_fusion.refs_0_), channel_id=1, source_target_pairs={{0,4},{1,5},{2,6},{3,7},{4,0},{5,1},{6,2},{7,3},{8,12},{9,13},{10,... | collective-permute-start | bytes 129032 | tf_op jit(solution)/shard_map/ppermute | solution.py:55
  49.3 13.6 %collective-permute-start.2 = (bf16[24,896]{1,0:T(8,128)(2,1)S(1)}, bf16[24,896]{1,0:T(8,128)(2,1)S(1)}, u32[]{:S(2)}, u32[]{:S(2)}) collective-permute-start(bf16[24,896]{1,0:T(8,128)(2,1)S(1)} %constant_dynamic-update-slice_fusion.refs_0_), channel_id=1, source_target_pairs={{0,6},{1,7},{2,4},{3,5},{4,2},{5,3},{6,0},{7,1},{8,14},{9,15},{10,... | collective-permute-start | bytes 129032 | tf_op jit(solution)/shard_map/ppermute | solution.py:55
  57.7 30.4 %all-to-all-start.2 = ((bf16[64,8,768]{2,1,0:T(8,128)(2,1)}), bf16[64,8,768]{2,1,0:T(8,128)(2,1)}, u32[]{:S(2)}, u32[]{:S(2)}) async-start(bf16[64,8,768]{2,1,0:T(8,128)(2,1)} %gather_fusion), calls=%async_computation.2 | async-start | bytes 1572864 | tf_op jit(solution)/shard_map/all_to_all | solution.py:47
  63.0 13.9 %collective-permute-start.9 = (bf16[2,2,24,768]{3,2,1,0:T(8,128)(2,1)S(1)}, bf16[2,2,24,768]{3,2,1,0:T(8,128)(2,1)S(1)}, u32[]{:S(2)}, u32[]{:S(2)}) collective-permute-start(bf16[2,2,24,768]{3,2,1,0:T(8,128)(2,1)S(1)} %second_z.1.refs_0_), channel_id=1, source_target_pairs={{0,2},{1,3},{2,0},{3,1},{4,6},{5,7},{6,4},{7,5},{8,10},{9,11},{10,... | collective-permute-start | bytes 442376 | tf_op jit(solution)/shard_map/ppermute | solution.py:55
  64.4 17.1 %collective-permute-start.10 = (bf16[2,2,24,768]{3,2,1,0:T(8,128)(2,1)S(1)}, bf16[2,2,24,768]{3,2,1,0:T(8,128)(2,1)S(1)}, u32[]{:S(2)}, u32[]{:S(2)}) collective-permute-start(bf16[2,2,24,768]{3,2,1,0:T(8,128)(2,1)S(1)} %second_z.1.refs_0_), channel_id=1, source_target_pairs={{0,4},{1,5},{2,6},{3,7},{4,0},{5,1},{6,2},{7,3},{8,12},{9,13},{10,... | collective-permute-start | bytes 442376 | tf_op jit(solution)/shard_map/ppermute | solution.py:55
  66.8 14.7 %collective-permute-start.11 = (bf16[2,2,24,768]{3,2,1,0:T(8,128)(2,1)S(1)}, bf16[2,2,24,768]{3,2,1,0:T(8,128)(2,1)S(1)}, u32[]{:S(2)}, u32[]{:S(2)}) collective-permute-start(bf16[2,2,24,768]{3,2,1,0:T(8,128)(2,1)S(1)} %second_z.1.refs_0_), channel_id=1, source_target_pairs={{0,6},{1,7},{2,4},{3,5},{4,2},{5,3},{6,0},{7,1},{8,14},{9,15},{10,... | collective-permute-start | bytes 442376 | tf_op jit(solution)/shard_map/ppermute | solution.py:55
  68.4 13.1 %collective-permute-start.6 = (bf16[2,2,24,896]{3,2,1,0:T(8,128)(2,1)S(1)}, bf16[2,2,24,896]{3,2,1,0:T(8,128)(2,1)S(1)}, u32[]{:S(2)}, u32[]{:S(2)}) collective-permute-start(bf16[2,2,24,896]{3,2,1,0:T(8,128)(2,1)S(1)} %first_y.1.refs_0_), channel_id=1, source_target_pairs={{0,8},{1,9},{2,10},{3,11},{4,12},{5,13},{6,14},{7,15},{8,0},{9,1},... | collective-permute-start | bytes 516104 | tf_op jit(solution)/shard_map/ppermute | solution.py:55
  69.9 14.6 %collective-permute-start.7 = (bf16[2,2,24,896]{3,2,1,0:T(8,128)(2,1)S(1)}, bf16[2,2,24,896]{3,2,1,0:T(8,128)(2,1)S(1)}, u32[]{:S(2)}, u32[]{:S(2)}) collective-permute-start(bf16[2,2,24,896]{3,2,1,0:T(8,128)(2,1)S(1)} %first_y.1.refs_0_), channel_id=1, source_target_pairs={{0,64},{1,65},{2,66},{3,67},{4,68},{5,69},{6,70},{7,71},{8,72},{9,... | collective-permute-start | bytes 516104 | tf_op jit(solution)/shard_map/ppermute | solution.py:55
  76.9 11.1 %collective-permute-start.8 = (bf16[2,2,24,896]{3,2,1,0:T(8,128)(2,1)S(1)}, bf16[2,2,24,896]{3,2,1,0:T(8,128)(2,1)S(1)}, u32[]{:S(2)}, u32[]{:S(2)}) collective-permute-start(bf16[2,2,24,896]{3,2,1,0:T(8,128)(2,1)S(1)} %first_y.1.refs_0_), channel_id=1, source_target_pairs={{0,72},{1,73},{2,74},{3,75},{4,76},{5,77},{6,78},{7,79},{8,64},{9,... | collective-permute-start | bytes 516104 | tf_op jit(solution)/shard_map/ppermute | solution.py:55
  91.1 44.1 %all-to-all-start.3 = ((bf16[64,8,1664]{2,1,0:T(8,128)(2,1)}), bf16[64,8,1664]{2,1,0:T(8,128)(2,1)}, u32[]{:S(2)}, u32[]{:S(2)}) async-start(bf16[64,8,1664]{2,1,0:T(8,128)(2,1)} %bitcast.114), calls=%async_computation.3 | async-start | bytes 3407872 | tf_op jit(solution)/shard_map/all_to_all | solution.py:47
  95.8 112.6 %all-gather.5.cloned.1.call-start = ((), (), s32[]{:S(2)}) async-start(), calls=%async_computation.12 | async-start | bytes 5308416 | tf_op jit(solution)/shard_map/all_gather | solution.py:1098
  95.8 25.0 %collective-permute-start.12 = (bf16[2,2,4,24,896]{4,3,2,1,0:T(8,128)(2,1)S(1)}, bf16[2,2,4,24,896]{4,3,2,1,0:T(8,128)(2,1)}, u32[]{:S(2)}, u32[]{:S(2)}) collective-permute-start(bf16[2,2,4,24,896]{4,3,2,1,0:T(8,128)(2,1)S(1)} %bitcast.104), channel_id=1, source_target_pairs={{0,16},{1,17},{2,18},{3,19},{4,20},{5,21},{6,22},{7,23},{8,24},{9,... | collective-permute-start | bytes 2064392 | tf_op jit(solution)/shard_map/ppermute | solution.py:55
  97.2 38.1 %collective-permute-start.13 = (bf16[2,2,4,24,896]{4,3,2,1,0:T(8,128)(2,1)S(1)}, bf16[2,2,4,24,896]{4,3,2,1,0:T(8,128)(2,1)}, u32[]{:S(2)}, u32[]{:S(2)}) collective-permute-start(bf16[2,2,4,24,896]{4,3,2,1,0:T(8,128)(2,1)S(1)} %bitcast.105), channel_id=1, source_target_pairs={{0,32},{1,33},{2,34},{3,35},{4,36},{5,37},{6,38},{7,39},{8,40},{9,... | collective-permute-start | bytes 2064392 | tf_op jit(solution)/shard_map/ppermute | solution.py:55
  99.6 35.6 %collective-permute-start.14 = (bf16[2,2,4,24,896]{4,3,2,1,0:T(8,128)(2,1)S(1)}, bf16[2,2,4,24,896]{4,3,2,1,0:T(8,128)(2,1)}, u32[]{:S(2)}, u32[]{:S(2)}) collective-permute-start(bf16[2,2,4,24,896]{4,3,2,1,0:T(8,128)(2,1)S(1)} %bitcast.106), channel_id=1, source_target_pairs={{0,48},{1,49},{2,50},{3,51},{4,52},{5,53},{6,54},{7,55},{8,56},{9,... | collective-permute-start | bytes 2064392 | tf_op jit(solution)/shard_map/ppermute | solution.py:55
  100.5 19.9 %collective-permute-start.15 = (bf16[128,768]{1,0:T(8,128)(2,1)}, bf16[128,768]{1,0:T(8,128)(2,1)S(1)}, u32[]{:S(2)}, u32[]{:S(2)}) collective-permute-start(bf16[128,768]{1,0:T(8,128)(2,1)} %get-tuple-element.183), channel_id=1, source_target_pairs={{0,1},{1,2},{2,3},{4,5},{5,6},{6,7},{8,9},{9,10},{10,11},{12,13},{... | collective-permute-start | bytes 589832 | tf_op jit(solution)/shard_map/ppermute | solution.py:1099
  104.9 15.9 %collective-permute-start.16 = (bf16[128,768]{1,0:T(8,128)(2,1)}, bf16[128,768]{1,0:T(8,128)(2,1)S(1)}, u32[]{:S(2)}, u32[]{:S(2)}) collective-permute-start(bf16[128,768]{1,0:T(8,128)(2,1)} %get-tuple-element.182), channel_id=1, source_target_pairs={{1,0},{2,1},{3,2},{5,4},{6,5},{7,6},{9,8},{10,9},{11,10},{13,12},{... | collective-permute-start | bytes 589832 | tf_op jit(solution)/shard_map/ppermute | solution.py:1100
  138.5 14.7 %collective-permute-start.17 = (bf16[2,768,896]{2,1,0:T(8,128)(2,1)}, bf16[2,768,896]{2,1,0:T(8,128)(2,1)}, u32[]{:S(2)}, u32[]{:S(2)}) collective-permute-start(bf16[2,768,896]{2,1,0:T(8,128)(2,1)} %bitcast.28.mine.first_mine), channel_id=1, source_target_pairs={{0,1},{1,0},{2,3},{3,2},{4,5},{5,4},{6,7},{7,6},{8,9},{9,8},{10,11... | collective-permute-start | bytes 8257544 | tf_op jit(solution)/shard_map/ppermute | solution.py:51
  147.3 36.9 %all-to-all-start.4 = ((bf16[64,8,1664]{2,1,0:T(8,128)(2,1)}), bf16[64,8,1664]{2,1,0:T(8,128)(2,1)}, u32[]{:S(2)}, u32[]{:S(2)}) async-start(bf16[64,8,1664]{2,1,0:T(8,128)(2,1)} %gather_fusion.1), calls=%async_computation.4 | async-start | bytes 3407872 | tf_op jit(solution)/shard_map/all_to_all | solution.py:47
  153.2 31.4 %collective-permute-start.18 = (bf16[2,2,4,24,768]{4,3,2,1,0:T(8,128)(2,1)S(1)}, bf16[2,2,4,24,768]{4,3,2,1,0:T(8,128)(2,1)}, u32[]{:S(2)}, u32[]{:S(2)}) collective-permute-start(bf16[2,2,4,24,768]{4,3,2,1,0:T(8,128)(2,1)S(1)} %bitcast.108), channel_id=1, source_target_pairs={{0,16},{1,17},{2,18},{3,19},{4,20},{5,21},{6,22},{7,23},{8,24},{9,... | collective-permute-start | bytes 1769480 | tf_op jit(solution)/shard_map/ppermute | solution.py:55
  153.2 34.2 %collective-permute-start.19 = (bf16[2,2,4,24,768]{4,3,2,1,0:T(8,128)(2,1)S(1)}, bf16[2,2,4,24,768]{4,3,2,1,0:T(8,128)(2,1)}, u32[]{:S(2)}, u32[]{:S(2)}) collective-permute-start(bf16[2,2,4,24,768]{4,3,2,1,0:T(8,128)(2,1)S(1)} %bitcast.109), channel_id=1, source_target_pairs={{0,32},{1,33},{2,34},{3,35},{4,36},{5,37},{6,38},{7,39},{8,40},{9,... | collective-permute-start | bytes 1769480 | tf_op jit(solution)/shard_map/ppermute | solution.py:55
  154.5 33.0 %collective-permute-start.20 = (bf16[2,2,4,24,768]{4,3,2,1,0:T(8,128)(2,1)S(1)}, bf16[2,2,4,24,768]{4,3,2,1,0:T(8,128)(2,1)}, u32[]{:S(2)}, u32[]{:S(2)}) collective-permute-start(bf16[2,2,4,24,768]{4,3,2,1,0:T(8,128)(2,1)S(1)} %bitcast.110), channel_id=1, source_target_pairs={{0,48},{1,49},{2,50},{3,51},{4,52},{5,53},{6,54},{7,55},{8,56},{9,... | collective-permute-start | bytes 1769480 | tf_op jit(solution)/shard_map/ppermute | solution.py:55
  191.5 16.9 %collective-permute-start.21 = (bf16[2,768,768]{2,1,0:T(8,128)(2,1)}, bf16[2,768,768]{2,1,0:T(8,128)(2,1)}, u32[]{:S(2)}, u32[]{:S(2)}) collective-permute-start(bf16[2,768,768]{2,1,0:T(8,128)(2,1)} %bitcast.39.in_mine), channel_id=1, source_target_pairs={{0,1},{1,0},{2,3},{3,2},{4,5},{5,4},{6,7},{7,6},{8,9},{9,8},{10,11... | collective-permute-start | bytes 7077896 | tf_op jit(solution)/shard_map/ppermute | solution.py:51
  192.5 15.0 %all-to-all-start.5 = ((bf16[4,816,128]{2,1,0:T(8,128)(2,1)}), bf16[4,816,128]{2,1,0:T(8,128)(2,1)S(1)}, u32[]{:S(2)}, u32[]{:S(2)}) async-start(bf16[4,816,128]{2,1,0:T(8,128)(2,1)} %broadcast_in_dim.137), calls=%async_computation.5 | async-start | bytes 1671168 | tf_op jit(solution)/shard_map/all_to_all | solution.py:47
  196.1 196.9 %reduce-scatter.2.cloned.1.call-start = ((), (), s32[]{:S(2)}) async-start(), calls=%async_computation.13 | async-start | bytes 5013504 | tf_op jit(solution)/shard_map/reduce_scatter | solution.py:1198
  249.6 32.0 %collective-permute-start.22 = (bf16[2,768,768]{2,1,0:T(8,128)(2,1)}, bf16[2,768,768]{2,1,0:T(8,128)(2,1)}, u32[]{:S(2)}, u32[]{:S(2)}) collective-permute-start(bf16[2,768,768]{2,1,0:T(8,128)(2,1)} %get-tuple-element.129), channel_id=1, source_target_pairs={{0,1},{1,0},{2,3},{3,2},{4,5},{5,4},{6,7},{7,6},{8,9},{9,8},{10,11... | collective-permute-start | bytes 7077896 | tf_op jit(solution)/shard_map/ppermute | solution.py:51
  285.8 42.1 %all-to-all-start.6 = ((bf16[64,24,768]{2,1,0:T(8,128)(2,1)}), bf16[64,24,768]{2,1,0:T(8,128)(2,1)}, u32[]{:S(2)}, u32[]{:S(2)}) async-start(bf16[64,24,768]{2,1,0:T(8,128)(2,1)} %bitcast.42), calls=%async_computation.6 | async-start | bytes 4718592 | tf_op jit(solution)/shard_map/all_to_all | solution.py:47
  314.9 19.3 %collective-permute-start.23 = (bf16[65,24,768]{2,1,0:T(8,128)(2,1)}, bf16[65,24,768]{2,1,0:T(8,128)(2,1)}, u32[]{:S(2)}, u32[]{:S(2)}) collective-permute-start(bf16[65,24,768]{2,1,0:T(8,128)(2,1)} %get-tuple-element.140), channel_id=1, source_target_pairs={{0,1},{1,0},{2,3},{3,2},{4,5},{5,4},{6,7},{7,6},{8,9},{9,8},{10,11... | collective-permute-start | bytes 7188488 | tf_op jit(solution)/shard_map/ppermute | solution.py:51
  314.9 10.7 %collective-permute-start.27 = (bf16[128,768]{1,0:T(8,128)(2,1)S(1)}, bf16[128,768]{1,0:T(8,128)(2,1)S(1)}, u32[]{:S(2)}, u32[]{:S(2)}) collective-permute-start(bf16[128,768]{1,0:T(8,128)(2,1)S(1)} %copy-done.44), channel_id=1, source_target_pairs={{0,1},{1,2},{2,3},{4,5},{5,6},{6,7},{8,9},{9,10},{10,11},{12,13},{... | collective-permute-start | bytes 589832 | tf_op jit(solution)/shard_map/ppermute | solution.py:1193
  327.8 31.3 %all-to-all-start.7 = ((bf16[64,8,1536]{2,1,0:T(8,128)(2,1)}), bf16[64,8,1536]{2,1,0:T(8,128)(2,1)}, u32[]{:S(2)}, u32[]{:S(2)}) async-start(bf16[64,8,1536]{2,1,0:T(8,128)(2,1)} %pack_rows.1), calls=%async_computation.7 | async-start | bytes 3145728 | tf_op jit(solution)/shard_map/all_to_all | solution.py:47
  340.1 22.2 %collective-permute-start.24 = (bf16[17,24,768]{2,1,0:T(8,128)(2,1)}, bf16[17,24,768]{2,1,0:T(8,128)(2,1)S(1)}, u32[]{:S(2)}, u32[]{:S(2)}) collective-permute-start(bf16[17,24,768]{2,1,0:T(8,128)(2,1)} %get-tuple-element.142), channel_id=1, source_target_pairs={{0,16},{1,17},{2,18},{3,19},{4,20},{5,21},{6,22},{7,23},{8,24},{9,... | collective-permute-start | bytes 1880072 | tf_op jit(solution)/shard_map/ppermute | solution.py:55
  340.9 30.5 %collective-permute-start.25 = (bf16[17,24,768]{2,1,0:T(8,128)(2,1)}, bf16[17,24,768]{2,1,0:T(8,128)(2,1)S(1)}, u32[]{:S(2)}, u32[]{:S(2)}) collective-permute-start(bf16[17,24,768]{2,1,0:T(8,128)(2,1)} %get-tuple-element.143), channel_id=1, source_target_pairs={{0,32},{1,33},{2,34},{3,35},{4,36},{5,37},{6,38},{7,39},{8,40},{9,... | collective-permute-start | bytes 1880072 | tf_op jit(solution)/shard_map/ppermute | solution.py:55
  343.6 29.8 %collective-permute-start.26 = (bf16[17,24,768]{2,1,0:T(8,128)(2,1)}, bf16[17,24,768]{2,1,0:T(8,128)(2,1)S(1)}, u32[]{:S(2)}, u32[]{:S(2)}) collective-permute-start(bf16[17,24,768]{2,1,0:T(8,128)(2,1)} %get-tuple-element.144), channel_id=1, source_target_pairs={{0,48},{1,49},{2,50},{3,51},{4,52},{5,53},{6,54},{7,55},{8,56},{9,... | collective-permute-start | bytes 1880072 | tf_op jit(solution)/shard_map/ppermute | solution.py:55
  374.2 41.0 %all-to-all-start.8 = ((bf16[64,8,1536]{2,1,0:T(8,128)(2,1)}), bf16[64,8,1536]{2,1,0:T(8,128)(2,1)S(1)}, u32[]{:S(2)}, u32[]{:S(2)}) async-start(bf16[64,8,1536]{2,1,0:T(8,128)(2,1)} %gather_fusion.2), calls=%async_computation.8 | async-start | bytes 3145728 | tf_op jit(solution)/shard_map/all_to_all | solution.py:47
  386.1 18.3 %collective-permute-start.29 = (bf16[5,24,768]{2,1,0:T(8,128)(2,1)}, bf16[5,24,768]{2,1,0:T(8,128)(2,1)S(1)}, u32[]{:S(2)}, u32[]{:S(2)}) collective-permute-start(bf16[5,24,768]{2,1,0:T(8,128)(2,1)} %get-tuple-element.158), channel_id=1, source_target_pairs={{0,8},{1,9},{2,10},{3,11},{4,12},{5,13},{6,14},{7,15},{8,0},{9,1},... | collective-permute-start | bytes 552968 | tf_op jit(solution)/shard_map/ppermute | solution.py:55
  387.7 20.9 %collective-permute-start.30 = (bf16[5,24,768]{2,1,0:T(8,128)(2,1)S(1)}, bf16[5,24,768]{2,1,0:T(8,128)(2,1)S(1)}, u32[]{:S(2)}, u32[]{:S(2)}) collective-permute-start(bf16[5,24,768]{2,1,0:T(8,128)(2,1)S(1)} %get-tuple-element.159), channel_id=1, source_target_pairs={{0,64},{1,65},{2,66},{3,67},{4,68},{5,69},{6,70},{7,71},{8,72},{9,... | collective-permute-start | bytes 552968 | tf_op jit(solution)/shard_map/ppermute | solution.py:55
  389.2 19.5 %collective-permute-start.31 = (bf16[5,24,768]{2,1,0:T(8,128)(2,1)S(1)}, bf16[5,24,768]{2,1,0:T(8,128)(2,1)S(1)}, u32[]{:S(2)}, u32[]{:S(2)}) collective-permute-start(bf16[5,24,768]{2,1,0:T(8,128)(2,1)S(1)} %get-tuple-element.160), channel_id=1, source_target_pairs={{0,72},{1,73},{2,74},{3,75},{4,76},{5,77},{6,78},{7,79},{8,64},{9,... | collective-permute-start | bytes 552968 | tf_op jit(solution)/shard_map/ppermute | solution.py:55
  394.0 18.4 %collective-permute-start.37 = (bf16[2,24,768]{2,1,0:T(8,128)(2,1)S(1)}, bf16[2,24,768]{2,1,0:T(8,128)(2,1)S(1)}, u32[]{:S(2)}, u32[]{:S(2)}) collective-permute-start(bf16[2,24,768]{2,1,0:T(8,128)(2,1)S(1)} %get-tuple-element.189), channel_id=1, source_target_pairs={{0,48},{1,49},{2,50},{3,51},{4,52},{5,53},{6,54},{7,55},{8,56},{9,... | collective-permute-start | bytes 221192 | tf_op jit(solution)/shard_map/ppermute | solution.py:55
  394.4 18.3 %collective-permute-start.36 = (bf16[2,24,768]{2,1,0:T(8,128)(2,1)S(1)}, bf16[2,24,768]{2,1,0:T(8,128)(2,1)S(1)}, u32[]{:S(2)}, u32[]{:S(2)}) collective-permute-start(bf16[2,24,768]{2,1,0:T(8,128)(2,1)S(1)} %get-tuple-element.190), channel_id=1, source_target_pairs={{0,32},{1,33},{2,34},{3,35},{4,36},{5,37},{6,38},{7,39},{8,40},{9,... | collective-permute-start | bytes 221192 | tf_op jit(solution)/shard_map/ppermute | solution.py:55
  408.8 9.9 %collective-permute-start.32 = (bf16[2,24,768]{2,1,0:T(8,128)(2,1)S(1)}, bf16[2,24,768]{2,1,0:T(8,128)(2,1)S(1)}, u32[]{:S(2)}, u32[]{:S(2)}) collective-permute-start(bf16[2,24,768]{2,1,0:T(8,128)(2,1)S(1)} %get-tuple-element.162), channel_id=1, source_target_pairs={{0,2},{1,3},{2,0},{3,1},{4,6},{5,7},{6,4},{7,5},{8,10},{9,11},{10,... | collective-permute-start | bytes 221192 | tf_op jit(solution)/shard_map/ppermute | solution.py:55
  409.9 8.8 %collective-permute-start.33 = (bf16[2,24,768]{2,1,0:T(8,128)(2,1)S(1)}, bf16[2,24,768]{2,1,0:T(8,128)(2,1)S(1)}, u32[]{:S(2)}, u32[]{:S(2)}) collective-permute-start(bf16[2,24,768]{2,1,0:T(8,128)(2,1)S(1)} %get-tuple-element.163), channel_id=1, source_target_pairs={{0,4},{1,5},{2,6},{3,7},{4,0},{5,1},{6,2},{7,3},{8,12},{9,13},{10,... | collective-permute-start | bytes 221192 | tf_op jit(solution)/shard_map/ppermute | solution.py:55
  420.3 11.5 %all-to-all-start.9 = ((bf16[4,48,768]{2,1,0:T(8,128)(2,1)}), bf16[4,48,768]{2,1,0:T(8,128)(2,1)S(1)}, u32[]{:S(2)}, u32[]{:S(2)}) async-start(bf16[4,48,768]{2,1,0:T(8,128)(2,1)} %maximum_maximum_fusion), calls=%async_computation.10 | async-start | bytes 589824 | tf_op jit(solution)/shard_map/all_to_all | solution.py:47
  (51 other events, 436.3 us)
Sparse Core Ops, SparseCore 0:
  26.6 40.8 all-gather.2
  108.9 99.4 all-gather.4
  259.7 95.7 reduce-scatter.1
